TPU v7x, 128 devices: a whole 4x4x4 slice. The times are simulated.
128 devices in a mesh: batch: 4 (over y_lo, core), tensor: 8 (over x, y_hi), latent: 4 (over z).
Axes of the slice: x: 4, y: 4 (y_hi: 2, y_lo: 2; y = y_hi * 2 + y_lo), z: 4, core: 2. Of those that a mesh axis runs over, the one named last changes fastest.
Arguments:
- residual: bfloat16 [1024, 3584], P('batch', ('tensor', 'latent')), may hold values from -6 to 6
- target: bfloat16 [1024, 3584], P('batch', ('tensor', 'latent')), may hold values from -6 to 6
- encoder_weight: bfloat16 [3584, 32768], P(None, ('tensor', 'latent')), may hold values from -0.09375 to 0.09375
- encoder_bias: bfloat16 [32768], P(('tensor', 'latent')), may hold values from -0.59765625 to 0.29882812
- decoder_weight: bfloat16 [32768, 3584], P(('tensor', 'latent')), may hold values from -0.09375 to 0.09375
- decoder_bias: bfloat16 [3584], replicated, may hold values from -3 to 3
- first_gain: bfloat16 [3584], replicated, may hold values from 0.5 to 1.5
- second_gain: bfloat16 [3584], replicated, may hold values from 0.5 to 1.5
- gate_weight: bfloat16 [3584, 7168], P(None, ('tensor', 'latent')), may hold values from -0.09375 to 0.09375
- up_weight: bfloat16 [3584, 7168], P(None, ('tensor', 'latent')), may hold values from -0.09375 to 0.09375
- down_weight: bfloat16 [7168, 3584], P(('tensor', 'latent')), may hold values from -0.125 to 0.125
Outputs:
- encoder_grad: bfloat16 [3584, 32768], P('batch', ('tensor', 'latent'))
- decoder_grad: bfloat16 [32768, 3584], P(('tensor', 'latent'), 'batch')
All inputs are finite; a program needn't handle non-finite values.
Results may differ from a plain program's by a relative error of at most 0.012.
The roundings to bfloat16 on the way count: a program that leaves them out, or rounds other values in their place, can miss the bound.
Values may be sent and summed in bfloat16 or wider, within the bound.
No kernel may reach another device: no remote copies, remote signals or barrier semaphores. Data moves between devices by JAX's collectives and lax.ppermute only.
A program may use at most 128 MiB of HBM per device.

v0:
```python
import jax
import jax.numpy as jnp
from jax import lax
from jax.sharding import Mesh
from jax.sharding import PartitionSpec as P

TENSOR_LATENT = ("tensor_0", "tensor_1", "latent")


epsilon = 1e-06


def rows_for(lines, count):
    spare = -len(lines) % count
    return jnp.pad(lines, [(0, spare)] + [(0, 0)] * (lines.ndim - 1))


def copy_for_each(shard, axis):
    copies = jnp.broadcast_to(shard, (lax.axis_size(axis), *shard.shape))
    return lax.all_to_all(copies, axis, split_axis=0, concat_axis=0, tiled=True)


def laid_out(pieces, dim):
    pieces = jnp.moveaxis(pieces, 0, dim)
    lengths = pieces.shape
    return pieces.reshape(*lengths[:dim], lengths[dim] * lengths[dim + 1], *lengths[dim + 2 :])


def whole_of(shard, axes, dim):
    far, near = axes
    initial = copy_for_each(shard, far)
    pieces = jnp.swapaxes(copy_for_each(initial, near), 0, 1)
    return laid_out(pieces.reshape(-1, *shard.shape), dim)


def split_up(shard, dim, count):
    lengths = shard.shape
    pieces = shard.reshape(*lengths[:dim], count, lengths[dim] // count, *lengths[dim + 1 :])
    return jnp.moveaxis(pieces, dim, 0)


def sum_at_owner(shard, axis, dim):
    pieces = split_up(shard, dim, lax.axis_size(axis))
    arrived = lax.all_to_all(pieces, axis, split_axis=0, concat_axis=0, tiled=True)
    return arrived.astype(jnp.float32).sum(axis=0)


def summed_rows(shard, axes, dim):
    far, near = axes
    own = sum_at_owner(split_up(shard, dim, lax.axis_size(far)), near, dim + 1)
    return jnp.sum(
        lax.all_to_all(own.astype(jnp.bfloat16), far, 0, 0, tiled=True).astype(jnp.float32), axis=0
    )


def total_of(shard, axes):
    lines = shard.reshape(-1, shard.shape[-1])
    padded = rows_for(lines, lax.axis_size(axes[0]) * lax.axis_size(axes[1]))
    whole = whole_of(summed_rows(padded, axes, 0).astype(jnp.bfloat16), axes, 0)
    return lax.slice_in_dim(whole, 0, len(lines)).reshape(shard.shape).astype(jnp.float32)


def sum_in_order(pieces, axes, order):
    inside = pieces.shape[1:]
    pieces = pieces.reshape(*(lax.axis_size(a) for a in axes), *inside)
    pieces = jnp.moveaxis(pieces, order, range(len(axes))).reshape(-1, *inside)
    for k in order:
        pieces = lax.psum_scatter(pieces, axes[k], scatter_dimension=0, tiled=True)
    return pieces[0]


def summed_rows_2(shard, axes, order, dim):
    count = lax.axis_size(axes)
    return sum_in_order(split_up(shard, dim, count), axes, order)


def over_copies(shard, axis):
    return copy_for_each(shard, axis).sum(axis=0)


def in_one_piece(arrays, axis, dim, along):
    both = jnp.concatenate(arrays, axis=along)
    out, at, gathered = (lax.all_gather(both, axis, axis=dim, tiled=True), 0, [])
    for a in arrays:
        gathered.append(lax.slice_in_dim(out, at, at + a.shape[along], axis=along))
        at += a.shape[along]
    return tuple(gathered)


def per_device(
    residual,
    target,
    encoder_weight,
    encoder_bias,
    decoder_weight,
    decoder_bias,
    first_gain,
    second_gain,
    gate_weight,
    up_weight,
    down_weight,
):
    f32 = jnp.float32
    bf16 = jnp.bfloat16
    contract_last = (((1,), (1,)), ((), ()))
    contract_first = (((0,), (0,)), ((), ()))
    share_width = residual.shape[1]
    model_width = share_width * lax.axis_size(TENSOR_LATENT)
    offset = lax.axis_index(TENSOR_LATENT) * share_width
    token_count = residual.shape[0] * lax.axis_size("batch")
    bias_share = lax.dynamic_slice_in_dim(decoder_bias.astype(f32), offset, share_width)
    first_share = lax.dynamic_slice_in_dim(first_gain.astype(f32), offset, share_width)
    second_share = lax.dynamic_slice_in_dim(second_gain.astype(f32), offset, share_width)
    centered_share = (residual.astype(f32) - bias_share).astype(bf16)
    centered = lax.all_gather(centered_share, TENSOR_LATENT, axis=1, tiled=True)
    preact = jnp.dot(centered, encoder_weight, preferred_element_type=f32) + encoder_bias.astype(
        f32
    )
    latents = jnp.maximum(preact, 0.0).astype(bf16)
    partial_recon = jnp.dot(latents, decoder_weight, preferred_element_type=f32)
    recon_full = total_of(
        partial_recon.astype(jnp.bfloat16), (("tensor_0", "tensor_1"), "latent")
    ) + decoder_bias.astype(f32)
    scale_in = lax.rsqrt(
        jnp.sum(recon_full * recon_full, axis=1, keepdims=True) / model_width + epsilon
    )
    normed_input = (recon_full * scale_in * first_gain.astype(f32)).astype(bf16)
    recon = lax.dynamic_slice_in_dim(recon_full, offset, share_width, 1)
    gate_value = jnp.dot(normed_input, gate_weight, preferred_element_type=f32)
    up_value = jnp.dot(normed_input, up_weight, preferred_element_type=f32)
    gelu_value, gelu_back = jax.vjp(lambda v: jax.nn.gelu(v, approximate=True), gate_value)
    hidden = (gelu_value * up_value).astype(bf16)
    partial_out = jnp.dot(hidden, down_weight, preferred_element_type=f32)
    output = summed_rows_2(partial_out.astype(jnp.bfloat16), TENSOR_LATENT, (0, 2, 1), 1).astype(
        jnp.float32
    )
    out_squares = over_copies(jnp.sum(output * output, axis=1), TENSOR_LATENT)
    scale_out = lax.rsqrt(out_squares[:, None] / model_width + epsilon)
    normed_out = output * scale_out
    result = recon + normed_out * second_share
    grad_result = 2.0 * (result - target.astype(f32)) / token_count
    grad_normed = grad_result * second_share
    inner_out = over_copies(jnp.sum(grad_normed * normed_out, axis=1), TENSOR_LATENT) / model_width
    grad_share = (scale_out * (grad_normed - normed_out * inner_out[:, None])).astype(bf16)
    grad_output = lax.all_gather(grad_share, TENSOR_LATENT, axis=1, tiled=True)
    grad_hidden = lax.dot_general(
        grad_output, down_weight, contract_last, preferred_element_type=f32
    )
    grad_gate = gelu_back(grad_hidden * up_value)[0].astype(bf16)
    grad_up = (grad_hidden * gelu_value).astype(bf16)
    partial_input = lax.dot_general(
        grad_gate, gate_weight, contract_last, preferred_element_type=f32
    )
    partial_input = partial_input + lax.dot_general(
        grad_up, up_weight, contract_last, preferred_element_type=f32
    )
    grad_normed_in = sum_at_owner(partial_input.astype(jnp.bfloat16), TENSOR_LATENT, 1)
    unit = recon * scale_in
    grad_unit = grad_normed_in * first_share
    inner_in = over_copies(jnp.sum(grad_unit * unit, axis=1), TENSOR_LATENT) / model_width
    recon_share = (grad_result + scale_in * (grad_unit - unit * inner_in[:, None])).astype(bf16)
    grad_recon = lax.all_gather(recon_share, TENSOR_LATENT, axis=1, tiled=True)
    grad_latent = lax.dot_general(
        grad_recon, decoder_weight, contract_last, preferred_element_type=f32
    )
    grad_preact = jnp.where(preact > 0, grad_latent, 0.0).astype(bf16)
    centered_block, recon_block = (
        lax.all_to_all(centered, "batch", split_axis=1, concat_axis=0, tiled=True),
        lax.all_to_all(grad_recon, "batch", split_axis=1, concat_axis=0, tiled=True),
    )
    latents_all, preact_all = in_one_piece((latents, grad_preact), "batch", 0, 1)
    encoder_grad = lax.dot_general(
        centered_block, preact_all, contract_first, preferred_element_type=f32
    )
    decoder_grad = lax.dot_general(
        latents_all, recon_block, contract_first, preferred_element_type=f32
    )
    return (encoder_grad.astype(bf16), decoder_grad.astype(bf16))


def solution(mesh):
    split = Mesh(
        mesh.devices.reshape(mesh.shape["batch"], 4, 2, mesh.shape["latent"]),
        ("batch", "tensor_0", "tensor_1", "latent"),
    )
    in_specs = (
        P("batch", TENSOR_LATENT),
        P("batch", TENSOR_LATENT),
        P(None, TENSOR_LATENT),
        P(TENSOR_LATENT),
        P(TENSOR_LATENT, None),
        P(),
        P(),
        P(),
        P(None, TENSOR_LATENT),
        P(None, TENSOR_LATENT),
        P(TENSOR_LATENT, None),
    )
    out_specs = (P("batch", TENSOR_LATENT), P(TENSOR_LATENT, "batch"))
    return jax.shard_map(
        per_device, mesh=split, in_specs=in_specs, out_specs=out_specs, check_vma=False
    )
```

profile of v0, /device:TPU:14, one launch (start us, length us, event | category | flops | bytes accessed | tf_op | source)
XLA Modules:
  0.0 580.4 jit_solution(9790143516048892075)
XLA Ops:
  7.2 0.9 dynamic_slice.12
  8.1 1.5 subtract_convert_fusion
  10.3 70.5 %all-gather.5.cloned.1.call-done = bf16[256,3584]{0,1:T(8,128)(2,1)} async-done(((bf16[256,112]{0,1:T(8,128)(2,1)}), bf16[256,3584]{0,1:T(8,128)(2,1)}) %all-gather.5.cloned.1.call-update) | async-done | bytes 1835024 | tf_op jit(solution)/shard_map/all_gather | solution.py:115
  80.9 6.7 %maximum_convert_fusion = (bf16[256,1024]{1,0:T(8,128)(2,1)S(1)}, f32[256,1024]{1,0:T(8,128)}) fusion(f32[1024]{0:T(1024)S(1)} %convert_element_type.91, bf16[256,3584]{0,1:T(8,128)(2,1)} %all-gather.5.cloned.1.call-done, bf16[3584,1024]{1,0:T(8,128)(2,1)} %param.13), kind=kOutput, calls=%fused_computation.20 | convolution fusion | flops 1879834624 | bytes 10752000 | tf_op jit(solution)/shard_map/dot_general | solution.py:116
  87.6 5.3 convolution_convert_fusion
  93.1 25.3 %all_to_all.81 = bf16[4,8,8,3584]{3,2,1,0:T(8,128)(2,1)S(1)} all-to-all(bf16[4,8,8,3584]{3,2,1,0:T(8,128)(2,1)S(1)} %bitcast.58), channel_id=1, replica_groups=mesh['batch'=4,'tensor_0'=4,'tensor_1'=2,'latent'=4] {'latent'}, dimensions={0} | all-to-all | bytes 3670016 | tf_op jit(solution)/shard_map/all_to_all | solution.py:44
  118.4 1.1 reduce_sum.98
  119.6 12.9 %all_to_all.82 = bf16[8,8,3584]{2,1,0:T(8,128)(2,1)S(1)} all-to-all(bf16[8,8,3584]{2,1,0:T(8,128)(2,1)} %reduce_sum.98), channel_id=1, replica_groups=mesh['batch'=4,'tensor_0'=4,'tensor_1'=2,'latent'=4] {'tensor_0','tensor..., dimensions={0} | all-to-all | bytes 917504 | tf_op jit(solution)/shard_map/all_to_all | solution.py:52
  132.5 12.4 %all_to_all.83 = bf16[8,8,3584]{2,1,0:T(8,128)(2,1)S(1)} all-to-all(bf16[8,8,3584]{2,1,0:T(8,128)(2,1)S(1)} %broadcast_in_dim.11), channel_id=1, replica_groups=mesh['batch'=4,'tensor_0'=4,'tensor_1'=2,'latent'=4] {'tensor_0','tensor..., dimensions={0} | all-to-all | bytes 917504 | tf_op jit(solution)/shard_map/all_to_all | solution.py:20
  144.9 1.4 broadcast_in_dim.12
  146.3 3.7 all-to-all-start.4
  150.1 18.4 %all-to-all-done.4 = bf16[4,8,8,3584]{3,2,1,0:T(8,128)(2,1)S(1)} async-done(((bf16[4,8,8,3584]{3,2,1,0:T(8,128)(2,1)}), bf16[4,8,8,3584]{3,2,1,0:T(8,128)(2,1)S(1)}, u32[]{:S(2)}, u32[]{:S(2)}) %all-to-all-start.4) | async-done | bytes 1835040 | tf_op jit(solution)/shard_map/all_to_all | solution.py:20
  168.5 2.2 copy_convert_fusion
  170.7 5.1 copy.51
  175.8 4.4 broadcast_add_fusion
  181.0 3.4 fusion.51
  186.5 1.9 convolution_convert_fusion.1
  188.5 2.9 copy.52
  191.3 1.4 copy.53
  192.8 24.1 %reduce-scatter.4.cloned.1.call-done = bf16[8,256,112]{1,2,0:T(8,128)(2,1)} async-done(((bf16[32,256,112]{1,2,0:T(8,128)(2,1)}), bf16[8,256,112]{1,2,0:T(8,128)(2,1)}) %reduce-scatter.4.cloned.1.call-update) | async-done | bytes 458768 | tf_op jit(solution)/shard_map/reduce_scatter | solution.py:68
  217.0 25.1 %reduce-scatter.6.cloned.1.call-done = bf16[2,256,112]{1,2,0:T(8,128)(2,1)} async-done(((bf16[8,256,112]{1,2,0:T(8,128)(2,1)}), bf16[2,256,112]{1,2,0:T(8,128)(2,1)}) %reduce-scatter.6.cloned.1.call-update) | async-done | bytes 114704 | tf_op jit(solution)/shard_map/reduce_scatter | solution.py:68
  242.1 15.2 %reduce-scatter.8.cloned.1.call-done = bf16[1,256,112]{1,2,0:T(8,128)(2,1)} async-done(((bf16[2,256,112]{1,2,0:T(8,128)(2,1)}), bf16[1,256,112]{1,2,0:T(8,128)(2,1)}) %reduce-scatter.8.cloned.1.call-update) | async-done | bytes 57360 | tf_op jit(solution)/shard_map/reduce_scatter | solution.py:68
  257.3 0.8 fusion.28
  258.7 8.4 %all-to-all-start.5 = ((f32[32,1,256]{2,1,0:T(1,128)}), f32[32,1,256]{2,1,0:T(1,128)S(1)}, u32[]{:S(2)}, u32[]{:S(2)}) async-start(f32[32,1,256]{2,1,0:T(1,128)} %broadcast_in_dim.13), calls=%async_computation.8 | async-start | bytes 65536 | tf_op jit(solution)/shard_map/all_to_all | solution.py:20
  268.0 7.2 %all-to-all-done.5 = f32[32,1,256]{2,1,0:T(1,128)S(1)} async-done(((f32[32,1,256]{2,1,0:T(1,128)}), f32[32,1,256]{2,1,0:T(1,128)S(1)}, u32[]{:S(2)}, u32[]{:S(2)}) %all-to-all-start.5) | async-done | bytes 32800 | tf_op jit(solution)/shard_map/all_to_all | solution.py:20
  275.2 1.1 fusion.24
  276.3 13.2 %all_to_all.84 = f32[32,1,256]{2,1,0:T(1,128)S(1)} all-to-all(f32[32,1,256]{2,1,0:T(1,128)S(1)} %broadcast_in_dim.14), channel_id=1, replica_groups=mesh['batch'=4,'tensor_0'=4,'tensor_1'=2,'latent'=4] {'tensor_0','tensor..., dimensions={0} | all-to-all | bytes 65536 | tf_op jit(solution)/shard_map/all_to_all | solution.py:20
  289.6 1.7 fusion.27
  291.3 64.6 %all-gather.7.cloned.1.call-done = bf16[256,3584]{0,1:T(8,128)(2,1)} async-done(((bf16[256,112]{0,1:T(8,128)(2,1)}), bf16[256,3584]{0,1:T(8,128)(2,1)}) %all-gather.7.cloned.1.call-update) | async-done | bytes 1835024 | tf_op jit(solution)/shard_map/all_gather | solution.py:145
  355.9 2.1 fusion.53
  358.0 0.8 fusion.29
  360.1 2.3 copy.56
  362.4 7.7 %all-to-all-start.7 = ((bf16[32,256,112]{1,2,0:T(8,128)(2,1)}), bf16[32,256,112]{1,2,0:T(8,128)(2,1)S(1)}, u32[]{:S(2)}, u32[]{:S(2)}) async-start(bf16[32,256,112]{1,2,0:T(8,128)(2,1)} %bitcast.16), calls=%async_computation.10 | async-start | bytes 3670016 | tf_op jit(solution)/shard_map/all_to_all | solution.py:44
  370.2 24.2 %all-to-all-done.7 = bf16[32,256,112]{1,2,0:T(8,128)(2,1)S(1)} async-done(((bf16[32,256,112]{1,2,0:T(8,128)(2,1)}), bf16[32,256,112]{1,2,0:T(8,128)(2,1)S(1)}, u32[]{:S(2)}, u32[]{:S(2)}) %all-to-all-start.7) | async-done | bytes 1835040 | tf_op jit(solution)/shard_map/all_to_all | solution.py:44
  394.7 1.0 multiply_reduce_fusion.1
  395.7 13.0 %all_to_all.85 = f32[32,1,256]{2,1,0:T(1,128)S(1)} all-to-all(f32[32,1,256]{2,1,0:T(1,128)S(1)} %broadcast_in_dim.15), channel_id=1, replica_groups=mesh['batch'=4,'tensor_0'=4,'tensor_1'=2,'latent'=4] {'tensor_0','tensor..., dimensions={0} | all-to-all | bytes 65536 | tf_op jit(solution)/shard_map/all_to_all | solution.py:20
  408.8 1.6 add_convert_fusion
  410.5 64.5 %all-gather.9.cloned.1.call-done = bf16[256,3584]{0,1:T(8,128)(2,1)} async-done(((bf16[256,112]{0,1:T(8,128)(2,1)}), bf16[256,3584]{0,1:T(8,128)(2,1)}) %all-gather.9.cloned.1.call-update) | async-done | bytes 1835024 | tf_op jit(solution)/shard_map/all_gather | solution.py:162
  475.0 5.8 %fusion.11 = bf16[256,1024]{1,0:T(8,128)(2,1)S(1)} fusion(bf16[256,3584]{0,1:T(8,128)(2,1)} %all-gather.9.cloned.1.call-done, bf16[1024,3584]{1,0:T(8,128)(2,1)} %param.15, f32[256,1024]{1,0:T(8,128)S(1)} %copy-done.15), kind=kOutput, calls=%fused_computation.18 | convolution fusion | flops 1879834624 | bytes 10747904 | tf_op jit(solution)/shard_map/dot_general | solution.py:163
  480.9 1.1 pad_maximum_fusion
  482.0 0.8 copy-done.3
  482.8 40.7 %all_to_all.86 = bf16[256,4,896]{0,2,1:T(8,128)(2,1)} all-to-all(bf16[256,4,896]{0,2,1:T(8,128)(2,1)S(1)} %bitcast.54), channel_id=1, replica_groups=mesh['batch'=4,'tensor_0'=4,'tensor_1'=2,'latent'=4] {'batch'}, dimensions={1} | all-to-all | bytes 3670016 | tf_op jit(solution)/shard_map/all_to_all | solution.py:168
  523.4 5.7 all-to-all-start.9
  529.1 3.5 copy.48
  532.6 29.3 %all-to-all-done.9 = bf16[256,4,896]{0,2,1:T(8,128)(2,1)S(1)} async-done(((bf16[256,4,896]{0,2,1:T(8,128)(2,1)}), bf16[256,4,896]{0,2,1:T(8,128)(2,1)S(1)}, u32[]{:S(2)}, u32[]{:S(2)}) %all-to-all-start.9) | async-done | bytes 1835040 | tf_op jit(solution)/shard_map/all_to_all | solution.py:169
  561.9 2.4 copy.58
  564.3 5.9 %fusion.8 = bf16[1024,896]{1,0:T(8,128)(2,1)} fusion(bf16[1024,896]{1,0:T(8,128)(2,1)} %bitcast.62, bf16[1024,2048]{1,0:T(8,128)(2,1)} %all-gather.11.cloned.1.call-done), kind=kOutput, calls=%fused_computation.15 | convolution fusion | flops 1879965696 | bytes 5767168 | tf_op jit(solution)/shard_map/dot_general | solution.py:175
  570.2 3.4 fusion.5
  (79 shorter events, 7.4 us)
Async XLA Ops:
  7.2 179.4 %copy-start = (bf16[224,3584]{1,0:T(8,128)(2,1)S(1)}, bf16[224,3584]{1,0:T(8,128)(2,1)}, u32[]{:S(2)}) copy-start(bf16[224,3584]{1,0:T(8,128)(2,1)} %param.21) | copy-start | bytes 4816900
  7.2 73.7 %all-gather.5.cloned.1.call-start = ((), (), s32[]{:S(2)}) async-start(), calls=%async_computation.13 | async-start | bytes 1892352 | tf_op jit(solution)/shard_map/all_gather | solution.py:115
  87.6 5.4 copy-start.10
  146.3 3.8 copy-start.18
  146.3 3.8 copy-start.19
  146.3 22.2 %all-to-all-start.4 = ((bf16[4,8,8,3584]{3,2,1,0:T(8,128)(2,1)}), bf16[4,8,8,3584]{3,2,1,0:T(8,128)(2,1)S(1)}, u32[]{:S(2)}, u32[]{:S(2)}) async-start(bf16[4,8,8,3584]{3,2,1,0:T(8,128)(2,1)} %broadcast_in_dim.12), calls=%async_computation.4 | async-start | bytes 3670016 | tf_op jit(solution)/shard_map/all_to_all | solution.py:20
  150.0 66.9 %reduce-scatter.4.cloned.1.call-start = ((), (), s32[]{:S(2)}) async-start(), calls=%async_computation.14 | async-start | bytes 2293760 | tf_op jit(solution)/shard_map/reduce_scatter | solution.py:68
  180.9 3.6 copy-start.2
  180.9 4.1 copy-start.5
  185.0 0.8 copy-start.7
  185.8 0.7 copy-start.12
  192.8 82.4 %copy-start.17 = (bf16[256,112]{0,1:T(8,128)(2,1)S(1)}, bf16[256,112]{0,1:T(8,128)(2,1)}, u32[]{:S(2)}) copy-start(bf16[256,112]{0,1:T(8,128)(2,1)} %param.12) | copy-start | bytes 172036
  192.8 49.3 %reduce-scatter.6.cloned.1.call-start = ((), (), s32[]{:S(2)}) async-start(), calls=%async_computation.15 | async-start | bytes 573440 | tf_op jit(solution)/shard_map/reduce_scatter | solution.py:68
  216.9 40.3 %reduce-scatter.8.cloned.1.call-start = ((), (), s32[]{:S(2)}) async-start(), calls=%async_computation.16 | async-start | bytes 172032 | tf_op jit(solution)/shard_map/reduce_scatter | solution.py:68
  258.7 16.4 %all-to-all-start.5 = ((f32[32,1,256]{2,1,0:T(1,128)}), f32[32,1,256]{2,1,0:T(1,128)S(1)}, u32[]{:S(2)}, u32[]{:S(2)}) async-start(f32[32,1,256]{2,1,0:T(1,128)} %broadcast_in_dim.13), calls=%async_computation.8 | async-start | bytes 65536 | tf_op jit(solution)/shard_map/all_to_all | solution.py:20
  267.2 88.7 %all-gather.7.cloned.1.call-start = ((), (), s32[]{:S(2)}) async-start(), calls=%async_computation.17 | async-start | bytes 1892352 | tf_op jit(solution)/shard_map/all_gather | solution.py:145
  291.3 66.7 %copy-start.4 = (bf16[3584,224]{0,1:T(8,128)(2,1)S(1)}, bf16[3584,224]{0,1:T(8,128)(2,1)}, u32[]{:S(2)}) copy-start(bf16[3584,224]{0,1:T(8,128)(2,1)} %param.19) | copy-start | bytes 4816900
  291.3 66.7 %copy-start.8 = (f32[256,224]{0,1:T(8,128)S(1)}, f32[256,224]{0,1:T(8,128)}, u32[]{:S(2)}) copy-start(f32[256,224]{0,1:T(8,128)} %copy-done.7) | copy-start | bytes 688132
  355.9 2.2 copy-start.13
  358.0 1.4 copy-start.6
  358.0 1.4 copy-start.9
  362.4 32.0 %all-to-all-start.7 = ((bf16[32,256,112]{1,2,0:T(8,128)(2,1)}), bf16[32,256,112]{1,2,0:T(8,128)(2,1)S(1)}, u32[]{:S(2)}, u32[]{:S(2)}) async-start(bf16[32,256,112]{1,2,0:T(8,128)(2,1)} %bitcast.16), calls=%async_computation.10 | async-start | bytes 3670016 | tf_op jit(solution)/shard_map/all_to_all | solution.py:44
  370.1 38.7 %copy-start.16 = (bf16[1,256,112]{1,2,0:T(8,128)(2,1)S(1)}, bf16[1,256,112]{1,2,0:T(8,128)(2,1)}, u32[]{:S(2)}) copy-start(bf16[1,256,112]{1,2,0:T(8,128)(2,1)} %reduce-scatter.8.cloned.1.call-done) | copy-start | bytes 172036
  370.1 105.0 %copy-start.15 = (f32[256,1024]{1,0:T(8,128)S(1)}, f32[256,1024]{1,0:T(8,128)}, u32[]{:S(2)}) copy-start(f32[256,1024]{1,0:T(8,128)} %get-tuple-element.5) | copy-start | bytes 3145732
  370.1 104.9 %all-gather.9.cloned.1.call-start = ((), (), s32[]{:S(2)}) async-start(), calls=%async_computation.18 | async-start | bytes 1892352 | tf_op jit(solution)/shard_map/all_gather | solution.py:162
  410.4 153.8 %all-gather.11.cloned.1.call-start = ((), (), s32[]{:S(2)}) async-start(), calls=%async_computation.19 | async-start | bytes 5242880 | tf_op jit(solution)/shard_map/all_gather | solution.py:83
  475.0 5.8 %copy-start.11 = (bf16[256,1024]{1,0:T(8,128)(2,1)S(1)}, bf16[256,1024]{1,0:T(8,128)(2,1)}, u32[]{:S(2)}) copy-start(bf16[256,1024]{1,0:T(8,128)(2,1)} %copy-done.10) | copy-start | bytes 1572868
  480.9 1.9 copy-start.3
  523.4 38.5 %all-to-all-start.9 = ((bf16[256,4,896]{0,2,1:T(8,128)(2,1)}), bf16[256,4,896]{0,2,1:T(8,128)(2,1)S(1)}, u32[]{:S(2)}, u32[]{:S(2)}) async-start(bf16[256,4,896]{0,2,1:T(8,128)(2,1)} %bitcast.60), calls=%async_computation.12 | async-start | bytes 3670016 | tf_op jit(solution)/shard_map/all_to_all | solution.py:169
  564.3 5.9 %copy-start.14 = (bf16[4,256,896]{2,1,0:T(8,128)(2,1)S(1)}, bf16[4,256,896]{2,1,0:T(8,128)(2,1)}, u32[]{:S(2)}) copy-start(bf16[4,256,896]{2,1,0:T(8,128)(2,1)} %copy.48) | copy-start | bytes 5505028
  564.3 5.9 %copy-start.20 = (bf16[1024,2048]{1,0:T(8,128)(2,1)S(1)}, bf16[1024,2048]{1,0:T(8,128)(2,1)}, u32[]{:S(2)}) copy-start(bf16[1024,2048]{1,0:T(8,128)(2,1)} %all-gather.11.cloned.1.call-done) | copy-start | bytes 12582916
  570.2 3.4 copy-start.1
Sparse Core Ops, SparseCore 0:
  11.7 69.1 all-gather.4
  192.9 23.9 reduce-scatter.3
  219.3 22.7 reduce-scatter.5
  244.3 12.8 reduce-scatter.7
  291.4 64.4 all-gather.6
  410.6 64.4 all-gather.8
  482.1 71.5 all-gather.10
where the time goes:
time: 586 us; the launch traced here: 580 us
  waiting for transfers between devices  343 us (59%)
  blocking collectives  117 us (20%)
  matrix products  36.9 us (6%)
  starting transfers between devices  25.7 us (4%)
  local copies, waits for them, and re-layouts  23.7 us (4%)
  other arithmetic  19.1 us (3%)
  between operations  14.5 us (2%)
    all_gather x1, waiting for transfers between devices, per_device(): centered = lax.all_gather(centered_share, TENSOR_LATENT, axis=1, tiled=True)  70.5 us
    all_gather x1, waiting for transfers between devices, per_device(): grad_output = lax.all_gather(grad_share, TENSOR_LATENT, axis=1, tiled=True)  64.6 us
    all_gather x1, waiting for transfers between devices, per_device(): grad_recon = lax.all_gather(recon_share, TENSOR_LATENT, axis=1, tiled=True)  64.5 us
    reduce_scatter x3, waiting for transfers between devices, sum_in_order(): pieces = lax.psum_scatter(pieces, axes[k], scatter_dimension=0, tiled=True)  64.3 us
    all_to_all x1, blocking collectives, per_device(): lax.all_to_all(centered, 'batch', split_axis=1, concat_axis=0, tiled=True)  40.7 us
    all_to_all x3, blocking collectives, copy_for_each(): return lax.all_to_all(copies, axis, split_axis=0, concat_axis=0, tiled=True)  38.6 us
    all_to_all x1, waiting for transfers between devices, per_device(): lax.all_to_all(grad_recon, 'batch', split_axis=1, concat_axis=0, tiled=True)  29.3 us
    all_to_all x2, waiting for transfers between devices, copy_for_each(): return lax.all_to_all(copies, axis, split_axis=0, concat_axis=0, tiled=True)  25.5 us
  transfers between devices with their start and end apart: 11, of which 10 were waited for; matrix products, arithmetic and copies ran while one was open for 1% of the time, Pallas kernels for 0%

commit v1 on v0

v1 whole, which is shorter than its diff:
```python
import jax
import jax.numpy as jnp
from jax import lax
from jax.sharding import Mesh
from jax.sharding import PartitionSpec as P

SHARDS = ("tensor_0", "tensor_1", "latent")
BATCH = ("batch_0", "batch_1")

epsilon = 1e-06


def exchange(pieces, axes):
    return lax.all_to_all(pieces, axes, split_axis=0, concat_axis=0, tiled=True)


def to_everyone(shard, axes):
    return exchange(jnp.broadcast_to(shard, (lax.axis_size(axes), *shard.shape)), axes)


def per_device(
    residual,
    target,
    encoder_weight,
    encoder_bias,
    decoder_weight,
    decoder_bias,
    first_gain,
    second_gain,
    gate_weight,
    up_weight,
    down_weight,
):
    f32 = jnp.float32
    bf16 = jnp.bfloat16
    contract_last = (((1,), (1,)), ((), ()))
    contract_first = (((0,), (0,)), ((), ()))
    tokens, share_width = residual.shape
    shards = lax.axis_size(SHARDS)
    copies = lax.axis_size(BATCH)
    width = share_width * shards
    own_tokens = tokens // shards
    token_count = tokens * copies
    offset = lax.axis_index(SHARDS) * share_width
    bias = decoder_bias.astype(f32)
    gain_in = first_gain.astype(f32)
    gain_out = second_gain.astype(f32)

    def sum_of_own_tokens(partial):
        pieces = partial.astype(bf16).reshape(shards, own_tokens, width)
        return exchange(pieces, SHARDS).astype(f32).sum(axis=0)

    def all_tokens(own):
        return to_everyone(own, SHARDS).reshape(tokens, width)

    bias_share = lax.dynamic_slice_in_dim(bias, offset, share_width)
    centered_share = (residual.astype(f32) - bias_share).astype(bf16)
    centered = to_everyone(centered_share.T, SHARDS).reshape(width, tokens)
    preact = lax.dot_general(centered, encoder_weight, contract_first, preferred_element_type=f32)
    preact = preact + encoder_bias.astype(f32)
    latents = jnp.maximum(preact, 0.0).astype(bf16)
    partial_recon = jnp.dot(latents, decoder_weight, preferred_element_type=f32)

    own_target = exchange(target.reshape(shards, own_tokens, share_width), SHARDS)
    own_target = jnp.moveaxis(own_target, 0, 1).reshape(own_tokens, width).astype(f32)
    recon = sum_of_own_tokens(partial_recon) + bias
    scale_in = lax.rsqrt(jnp.sum(recon * recon, axis=1, keepdims=True) / width + epsilon)
    unit = recon * scale_in
    normed_input = all_tokens((unit * gain_in).astype(bf16))

    latents_all = lax.all_gather(latents, BATCH, axis=0, tiled=True)
    centered_block = exchange(centered.reshape(copies, width // copies, tokens), BATCH)
    centered_block = jnp.moveaxis(centered_block, 0, 1).reshape(width // copies, token_count)

    gate_value = jnp.dot(normed_input, gate_weight, preferred_element_type=f32)
    up_value = jnp.dot(normed_input, up_weight, preferred_element_type=f32)
    gelu_value, gelu_back = jax.vjp(lambda v: jax.nn.gelu(v, approximate=True), gate_value)
    hidden = (gelu_value * up_value).astype(bf16)
    partial_out = jnp.dot(hidden, down_weight, preferred_element_type=f32)

    output = sum_of_own_tokens(partial_out)
    scale_out = lax.rsqrt(jnp.sum(output * output, axis=1, keepdims=True) / width + epsilon)
    normed_out = output * scale_out
    result = recon + normed_out * gain_out
    grad_result = 2.0 * (result - own_target) / token_count
    grad_normed = grad_result * gain_out
    inner_out = jnp.sum(grad_normed * normed_out, axis=1, keepdims=True) / width
    grad_output = all_tokens((scale_out * (grad_normed - normed_out * inner_out)).astype(bf16))

    grad_hidden = lax.dot_general(
        grad_output, down_weight, contract_last, preferred_element_type=f32
    )
    grad_gate = gelu_back(grad_hidden * up_value)[0].astype(bf16)
    grad_up = (grad_hidden * gelu_value).astype(bf16)
    partial_input = lax.dot_general(
        grad_gate, gate_weight, contract_last, preferred_element_type=f32
    )
    partial_input = partial_input + lax.dot_general(
        grad_up, up_weight, contract_last, preferred_element_type=f32
    )

    grad_unit = sum_of_own_tokens(partial_input) * gain_in
    inner_in = jnp.sum(grad_unit * unit, axis=1, keepdims=True) / width
    grad_recon = all_tokens((grad_result + scale_in * (grad_unit - unit * inner_in)).astype(bf16))

    grad_latent = lax.dot_general(
        grad_recon, decoder_weight, contract_last, preferred_element_type=f32
    )
    grad_preact = jnp.where(preact > 0, grad_latent, 0.0).astype(bf16)
    recon_block = lax.all_to_all(grad_recon, BATCH, split_axis=1, concat_axis=0, tiled=True)
    decoder_grad = lax.dot_general(
        latents_all, recon_block, contract_first, preferred_element_type=f32
    )
    preact_all = to_everyone(grad_preact, BATCH).reshape(token_count, -1)
    encoder_grad = jnp.dot(centered_block, preact_all, preferred_element_type=f32)
    return (encoder_grad.astype(bf16), decoder_grad.astype(bf16))


def solution(mesh):
    batch, latent = mesh.shape["batch"], mesh.shape["latent"]
    split = Mesh(
        mesh.devices.reshape(2, batch // 2, mesh.shape["tensor"] // 2, 2, latent),
        BATCH + SHARDS,
    )
    in_specs = (
        P(BATCH, SHARDS),
        P(BATCH, SHARDS),
        P(None, SHARDS),
        P(SHARDS),
        P(SHARDS, None),
        P(),
        P(),
        P(),
        P(None, SHARDS),
        P(None, SHARDS),
        P(SHARDS, None),
    )
    out_specs = (P(BATCH, SHARDS), P(SHARDS, BATCH))
    return jax.shard_map(
        per_device, mesh=split, in_specs=in_specs, out_specs=out_specs, check_vma=False
    )
```

time: 586 us -> 386 us (0.66)
  waiting for transfers between devices: 343 us -> 148 us
  starting transfers between devices: 25.7 us -> 55.9 us
  blocking collectives: 117 us -> 89.4 us
  other arithmetic: 19.1 us -> 12.2 us
    all_gather x4 -> x1, waiting for transfers between devices: 200 us -> 0.01 us  [per_device(): latents_all = lax.all_gather(latents, BATCH, axis=0, tiled=True)]
    all_to_all x4 -> x8, waiting for transfers between devices: 79 us -> 147 us  [the longest x7 131 us: exchange(): return lax.all_to_all(pieces, axes, split_axis=0, concat_axis=0, tiled=True)]
    reduce_scatter x3 -> x0, waiting for transfers between devices: 64.3 us -> none  [sum_in_order(): pieces = lax.psum_scatter(pieces, axes[k], scatter_dimension=0, tiled=True)]
    all_to_all x4 -> x8, starting transfers between devices: 25.5 us -> 55.9 us  [the longest x7 49.3 us: exchange(): return lax.all_to_all(pieces, axes, split_axis=0, concat_axis=0, tiled=True)]
    all_to_all x6 -> x3, blocking collectives: 117 us -> 89.4 us  [exchange(): return lax.all_to_all(pieces, axes, split_axis=0, concat_axis=0, tiled=True)]
    convert_element_type x3 -> x2, local copies, waits for them, and re-layouts: 10.3 us -> 2.35 us  [per_device(): jnp.moveaxis(own_target, 0, 1).reshape(own_tokens, width).astype(f32)]
  transfers between devices with their start and end apart: 11 -> 9, of which waited for: 10 -> 8; matrix products, arithmetic and copies ran while one was open for 1% -> 9% of each run, Pallas kernels for 0% -> 0%
where the time goes in v1:
time: 386 us; the launch traced here: 379 us
  waiting for transfers between devices  148 us (38%)
  blocking collectives  89.4 us (23%)
  starting transfers between devices  55.9 us (14%)
  matrix products  36.8 us (10%)
  local copies, waits for them, and re-layouts  21.9 us (6%)
  between operations  14.3 us (4%)
  other arithmetic  12.2 us (3%)
    all_to_all x7, waiting for transfers between devices, exchange(): return lax.all_to_all(pieces, axes, split_axis=0, concat_axis=0, tiled=True)  131 us
    all_to_all x3, blocking collectives, exchange(): return lax.all_to_all(pieces, axes, split_axis=0, concat_axis=0, tiled=True)  89.4 us
    all_to_all x7, starting transfers between devices, exchange(): return lax.all_to_all(pieces, axes, split_axis=0, concat_axis=0, tiled=True)  49.3 us
    all_to_all x1, waiting for transfers between devices, per_device(): lax.all_to_all(grad_recon, BATCH, split_axis=1, concat_axis=0, tiled=True)  16.2 us
  transfers between devices with their start and end apart: 9, of which 8 were waited for; matrix products, arithmetic and copies ran while one was open for 9% of the time, Pallas kernels for 0%

profile of v1, /device:TPU:14, one launch (start us, length us, event | category | flops | bytes accessed | tf_op | source)
XLA Modules:
  0.0 378.7 jit_solution(10255153200037055870)
XLA Ops:
  7.2 0.9 dynamic_slice.3
  8.1 0.9 fusion.39
  9.0 1.3 broadcast_in_dim.11
  10.3 10.4 %all-to-all-start = ((bf16[32,112,256]{2,1,0:T(8,128)(2,1)}), bf16[32,112,256]{2,1,0:T(8,128)(2,1)}, u32[]{:S(2)}, u32[]{:S(2)}) async-start(bf16[32,112,256]{2,1,0:T(8,128)(2,1)} %broadcast_in_dim.11), calls=%async_computation | async-start | bytes 3670016 | tf_op jit(solution)/shard_map/all_to_all | solution.py:14
  20.7 24.5 %all-to-all-done = bf16[32,112,256]{2,1,0:T(8,128)(2,1)} async-done(((bf16[32,112,256]{2,1,0:T(8,128)(2,1)}), bf16[32,112,256]{2,1,0:T(8,128)(2,1)}, u32[]{:S(2)}, u32[]{:S(2)}) %all-to-all-start) | async-done | bytes 1835040 | tf_op jit(solution)/shard_map/all_to_all | solution.py:14
  45.2 6.7 %maximum_convert_fusion = (bf16[256,1024]{1,0:T(8,128)(2,1)S(1)}, f32[256,1024]{1,0:T(8,128)}) fusion(f32[1024]{0:T(1024)S(1)} %convert_element_type.82, bf16[3584,256]{1,0:T(8,128)(2,1)} %bitcast.3, bf16[3584,1024]{1,0:T(8,128)(2,1)} %param.13), kind=kOutput, calls=%fused_computation.24 | convolution fusion | flops 1879834624 | bytes 10752000 | tf_op jit(solution)/shard_map/dot_general | solution.py:59
  51.9 6.6 %fusion.3 = bf16[32,8,3584]{2,1,0:T(8,128)(2,1)} fusion(bf16[256,1024]{1,0:T(8,128)(2,1)S(1)} %get-tuple-element.2, bf16[1024,3584]{1,0:T(8,128)(2,1)} %param.15), kind=kOutput, calls=%fused_computation.6 | convolution fusion | flops 1879965696 | bytes 9699328 | tf_op jit(solution)/shard_map/dot_general | solution.py:62
  58.5 7.3 %all-to-all-start.2 = ((bf16[32,8,3584]{2,1,0:T(8,128)(2,1)}), bf16[32,8,3584]{2,1,0:T(8,128)(2,1)S(1)}, u32[]{:S(2)}, u32[]{:S(2)}) async-start(bf16[32,8,3584]{2,1,0:T(8,128)(2,1)} %fusion.3), calls=%async_computation.2 | async-start | bytes 3670016 | tf_op jit(solution)/shard_map/all_to_all | solution.py:14
  67.0 23.4 %all-to-all-done.2 = bf16[32,8,3584]{2,1,0:T(8,128)(2,1)S(1)} async-done(((bf16[32,8,3584]{2,1,0:T(8,128)(2,1)}), bf16[32,8,3584]{2,1,0:T(8,128)(2,1)S(1)}, u32[]{:S(2)}, u32[]{:S(2)}) %all-to-all-start.2) | async-done | bytes 1835040 | tf_op jit(solution)/shard_map/all_to_all | solution.py:14
  92.0 1.3 broadcast_in_dim.12
  93.4 5.2 %all-to-all-start.3 = ((bf16[32,8,3584]{2,1,0:T(8,128)(2,1)}), bf16[32,8,3584]{2,1,0:T(8,128)(2,1)S(1)}, u32[]{:S(2)}, u32[]{:S(2)}) async-start(bf16[32,8,3584]{2,1,0:T(8,128)(2,1)} %broadcast_in_dim.12), calls=%async_computation.3 | async-start | bytes 3670016 | tf_op jit(solution)/shard_map/all_to_all | solution.py:14
  98.6 1.6 copy.22
  100.2 23.3 %all-to-all-done.3 = bf16[32,8,3584]{2,1,0:T(8,128)(2,1)S(1)} async-done(((bf16[32,8,3584]{2,1,0:T(8,128)(2,1)}), bf16[32,8,3584]{2,1,0:T(8,128)(2,1)S(1)}, u32[]{:S(2)}, u32[]{:S(2)}) %all-to-all-start.3) | async-done | bytes 1835040 | tf_op jit(solution)/shard_map/all_to_all | solution.py:14
  123.5 5.4 %all-to-all-start.5 = ((bf16[32,8,112]{2,1,0:T(8,128)(2,1)}), bf16[32,8,112]{2,1,0:T(8,128)(2,1)}, u32[]{:S(2)}, u32[]{:S(2)}) async-start(bf16[32,8,112]{2,1,0:T(8,128)(2,1)} %bitcast.52), calls=%async_computation.5 | async-start | bytes 131072 | tf_op jit(solution)/shard_map/all_to_all | solution.py:14
  128.9 2.2 fusion.10
  132.6 1.9 fusion.1
  134.6 2.5 all-to-all-done.5
  137.1 7.3 %all-to-all-start.4 = ((bf16[32,8,3584]{2,1,0:T(8,128)(2,1)}), bf16[32,8,3584]{2,1,0:T(8,128)(2,1)S(1)}, u32[]{:S(2)}, u32[]{:S(2)}) async-start(bf16[32,8,3584]{2,1,0:T(8,128)(2,1)} %fusion.1), calls=%async_computation.4 | async-start | bytes 3670016 | tf_op jit(solution)/shard_map/all_to_all | solution.py:14
  144.4 1.4 add.79
  145.8 1.4 mul.200
  147.1 1.3 convert_element_type.91
  148.4 1.3 broadcast_multiply_fusion.1
  149.7 1.3 broadcast_multiply_fusion
  151.1 0.8 convert_bitcast_fusion
  152.6 1.7 reshape.93
  154.3 0.8 reduce_sum.71
  155.0 13.7 %all-to-all-done.4 = bf16[32,8,3584]{2,1,0:T(8,128)(2,1)S(1)} async-done(((bf16[32,8,3584]{2,1,0:T(8,128)(2,1)}), bf16[32,8,3584]{2,1,0:T(8,128)(2,1)S(1)}, u32[]{:S(2)}, u32[]{:S(2)}) %all-to-all-start.4) | async-done | bytes 1835040 | tf_op jit(solution)/shard_map/all_to_all | solution.py:14
  168.7 0.9 convert_reduce_fusion.1
  169.6 1.0 reduce_sum.72
  170.6 1.0 multiply_reduce_fusion.1
  171.7 1.2 fusion.30
  172.9 1.1 multiply_convert_fusion.4
  174.1 30.0 %all_to_all.69 = bf16[32,8,3584]{2,1,0:T(8,128)(2,1)S(1)} all-to-all(bf16[32,8,3584]{2,1,0:T(8,128)(2,1)S(1)} %broadcast_in_dim.13), channel_id=1, replica_groups=mesh['batch_0'=2,'batch_1'=2,'tensor_0'=4,'tensor_1'=2,'latent'=4] {'ten..., dimensions={0} | all-to-all | bytes 3670016 | tf_op jit(solution)/shard_map/all_to_all | solution.py:14
  205.6 0.8 fusion.31
  207.7 29.3 %all_to_all.70 = bf16[32,8,3584]{2,1,0:T(8,128)(2,1)S(1)} all-to-all(bf16[32,8,3584]{2,1,0:T(8,128)(2,1)S(1)} %fusion.2), channel_id=1, replica_groups=mesh['batch_0'=2,'batch_1'=2,'tensor_0'=4,'tensor_1'=2,'latent'=4] {'ten..., dimensions={0} | all-to-all | bytes 3670016 | tf_op jit(solution)/shard_map/all_to_all | solution.py:14
  238.3 30.1 %all_to_all.71 = bf16[32,8,3584]{2,1,0:T(8,128)(2,1)S(1)} all-to-all(bf16[32,8,3584]{2,1,0:T(8,128)(2,1)S(1)} %broadcast_in_dim.14), channel_id=1, replica_groups=mesh['batch_0'=2,'batch_1'=2,'tensor_0'=4,'tensor_1'=2,'latent'=4] {'ten..., dimensions={0} | all-to-all | bytes 3670016 | tf_op jit(solution)/shard_map/all_to_all | solution.py:14
  268.4 7.6 %all-to-all-start.1 = ((bf16[4,896,256]{2,1,0:T(8,128)(2,1)}), bf16[4,896,256]{2,1,0:T(8,128)(2,1)}, u32[]{:S(2)}, u32[]{:S(2)}) async-start(bf16[4,896,256]{2,1,0:T(8,128)(2,1)} %bitcast.1), calls=%async_computation.1 | async-start | bytes 3670016 | tf_op jit(solution)/shard_map/all_to_all | solution.py:14
  276.7 1.5 all_to_all.54
  278.1 2.9 copy.26
  281.1 25.5 %all-to-all-done.1 = bf16[4,896,256]{2,1,0:T(8,128)(2,1)} async-done(((bf16[4,896,256]{2,1,0:T(8,128)(2,1)}), bf16[4,896,256]{2,1,0:T(8,128)(2,1)}, u32[]{:S(2)}, u32[]{:S(2)}) %all-to-all-start.1) | async-done | bytes 1835040 | tf_op jit(solution)/shard_map/all_to_all | solution.py:14
  306.6 6.5 %all-to-all-start.10 = ((bf16[256,4,896]{2,0,1:T(8,128)(2,1)}), bf16[256,4,896]{2,0,1:T(8,128)(2,1)}, u32[]{:S(2)}, u32[]{:S(2)}) async-start(bf16[256,4,896]{2,0,1:T(8,128)(2,1)} %copy.26), calls=%async_computation.10 | async-start | bytes 3670016 | tf_op jit(solution)/shard_map/all_to_all | solution.py:110
  313.1 5.2 %fusion.16 = bf16[256,1024]{1,0:T(8,128)(2,1)S(1)} fusion(bf16[1024,3584]{1,0:T(8,128)(2,1)} %param.15, bf16[32,8,3584]{2,1,0:T(8,128)(2,1)S(1)} %all_to_all.71, f32[256,1024]{1,0:T(8,128)S(1)} %copy-done.11), kind=kOutput, calls=%fused_computation.23 | convolution fusion | flops 1879834624 | bytes 10747904 | tf_op jit(solution)/shard_map/dot_general | solution.py:106
  318.3 16.2 %all-to-all-done.10 = bf16[256,4,896]{2,0,1:T(8,128)(2,1)} async-done(((bf16[256,4,896]{2,0,1:T(8,128)(2,1)}), bf16[256,4,896]{2,0,1:T(8,128)(2,1)}, u32[]{:S(2)}, u32[]{:S(2)}) %all-to-all-start.10) | async-done | bytes 1835040 | tf_op jit(solution)/shard_map/all_to_all | solution.py:110
  334.4 1.6 broadcast_in_dim.15
  336.0 6.1 %all-to-all-start.9 = ((bf16[4,256,1024]{2,1,0:T(8,128)(2,1)}), bf16[4,256,1024]{2,1,0:T(8,128)(2,1)}, u32[]{:S(2)}, u32[]{:S(2)}) async-start(bf16[4,256,1024]{2,1,0:T(8,128)(2,1)} %broadcast_in_dim.15), calls=%async_computation.9 | async-start | bytes 4194304 | tf_op jit(solution)/shard_map/all_to_all | solution.py:14
  342.1 5.7 %convolution_convert_fusion.2 = bf16[1024,896]{1,0:T(8,128)(2,1)} fusion(bf16[1024,1024]{1,0:T(8,128)(2,1)} %all-gather.2.cloned.1.call-done, bf16[1024,896]{1,0:T(8,128)(2,1)} %bitcast.14), kind=kOutput, calls=%fused_computation.20 | convolution fusion | flops 1879965696 | bytes 5767168 | tf_op jit(solution)/shard_map/dot_general | solution.py:111
  347.9 18.4 %all-to-all-done.9 = bf16[4,256,1024]{2,1,0:T(8,128)(2,1)} async-done(((bf16[4,256,1024]{2,1,0:T(8,128)(2,1)}), bf16[4,256,1024]{2,1,0:T(8,128)(2,1)}, u32[]{:S(2)}, u32[]{:S(2)}) %all-to-all-start.9) | async-done | bytes 2097184 | tf_op jit(solution)/shard_map/all_to_all | solution.py:14
  366.2 5.6 %bitcast_convert_fusion = bf16[896,1024]{1,0:T(8,128)(2,1)} fusion(bf16[4,256,1024]{2,1,0:T(8,128)(2,1)} %all-to-all-done.9, bf16[4,896,256]{2,1,0:T(8,128)(2,1)} %all-to-all-done.1), kind=kOutput, calls=%fused_computation.7 | convolution fusion | flops 1879965696 | bytes 5767168 | tf_op jit(solution)/shard_map/dot_general | solution.py:115
  (68 shorter events, 9.7 us)
Async XLA Ops:
  7.2 125.5 %copy-start = (bf16[224,3584]{1,0:T(8,128)(2,1)S(1)}, bf16[224,3584]{1,0:T(8,128)(2,1)}, u32[]{:S(2)}) copy-start(bf16[224,3584]{1,0:T(8,128)(2,1)} %param.21) | copy-start | bytes 4816900
  10.3 10.4 %copy-start.22 = (bf16[1024]{0:T(1024)(128)(2,1)S(1)}, bf16[1024]{0:T(1024)(128)(2,1)}, u32[]{:S(2)}) copy-start(bf16[1024]{0:T(1024)(128)(2,1)} %param.14) | copy-start | bytes 6148
  10.3 34.9 %all-to-all-start = ((bf16[32,112,256]{2,1,0:T(8,128)(2,1)}), bf16[32,112,256]{2,1,0:T(8,128)(2,1)}, u32[]{:S(2)}, u32[]{:S(2)}) async-start(bf16[32,112,256]{2,1,0:T(8,128)(2,1)} %broadcast_in_dim.11), calls=%async_computation | async-start | bytes 3670016 | tf_op jit(solution)/shard_map/all_to_all | solution.py:14
  51.9 6.6 %copy-start.8 = (bf16[256,1024]{1,0:T(8,128)(2,1)}, bf16[256,1024]{1,0:T(8,128)(2,1)S(1)}, u32[]{:S(2)}) copy-start(bf16[256,1024]{1,0:T(8,128)(2,1)S(1)} %get-tuple-element.2) | copy-start | bytes 1572868
  58.5 7.3 %copy-start.18 = (bf16[3584]{0:T(1024)(128)(2,1)S(1)}, bf16[3584]{0:T(1024)(128)(2,1)}, u32[]{:S(2)}) copy-start(bf16[3584]{0:T(1024)(128)(2,1)} %param.16) | copy-start | bytes 21508
  58.5 8.0 %copy-start.19 = (bf16[3584]{0:T(1024)(128)(2,1)S(1)}, bf16[3584]{0:T(1024)(128)(2,1)}, u32[]{:S(2)}) copy-start(bf16[3584]{0:T(1024)(128)(2,1)} %param.17) | copy-start | bytes 21508
  58.5 32.0 %all-to-all-start.2 = ((bf16[32,8,3584]{2,1,0:T(8,128)(2,1)}), bf16[32,8,3584]{2,1,0:T(8,128)(2,1)S(1)}, u32[]{:S(2)}, u32[]{:S(2)}) async-start(bf16[32,8,3584]{2,1,0:T(8,128)(2,1)} %fusion.3), calls=%async_computation.2 | async-start | bytes 3670016 | tf_op jit(solution)/shard_map/all_to_all | solution.py:14
  90.5 0.7 copy-start.13
  90.5 1.5 copy-start.15
  91.3 0.6 copy-start.20
  93.4 30.1 %all-to-all-start.3 = ((bf16[32,8,3584]{2,1,0:T(8,128)(2,1)}), bf16[32,8,3584]{2,1,0:T(8,128)(2,1)S(1)}, u32[]{:S(2)}, u32[]{:S(2)}) async-start(bf16[32,8,3584]{2,1,0:T(8,128)(2,1)} %broadcast_in_dim.12), calls=%async_computation.3 | async-start | bytes 3670016 | tf_op jit(solution)/shard_map/all_to_all | solution.py:14
  123.5 13.6 %all-to-all-start.5 = ((bf16[32,8,112]{2,1,0:T(8,128)(2,1)}), bf16[32,8,112]{2,1,0:T(8,128)(2,1)}, u32[]{:S(2)}, u32[]{:S(2)}) async-start(bf16[32,8,112]{2,1,0:T(8,128)(2,1)} %bitcast.52), calls=%async_computation.5 | async-start | bytes 131072 | tf_op jit(solution)/shard_map/all_to_all | solution.py:14
  128.9 2.3 copy-start.3
  131.2 0.7 copy-start.5
  131.9 0.7 copy-start.9
  137.1 31.6 %all-to-all-start.4 = ((bf16[32,8,3584]{2,1,0:T(8,128)(2,1)}), bf16[32,8,3584]{2,1,0:T(8,128)(2,1)S(1)}, u32[]{:S(2)}, u32[]{:S(2)}) async-start(bf16[32,8,3584]{2,1,0:T(8,128)(2,1)} %fusion.1), calls=%async_computation.4 | async-start | bytes 3670016 | tf_op jit(solution)/shard_map/all_to_all | solution.py:14
  204.1 1.4 copy-start.2
  204.1 1.4 copy-start.6
  204.1 1.5 copy-start.10
  205.6 1.4 copy-start.4
  237.1 0.7 copy-start.14
  237.1 0.7 copy-start.16
  237.1 0.7 copy-start.21
  237.1 1.0 copy-start.7
  237.1 1.0 copy-start.12
  237.1 1.0 copy-start.17
  268.4 38.2 %all-to-all-start.1 = ((bf16[4,896,256]{2,1,0:T(8,128)(2,1)}), bf16[4,896,256]{2,1,0:T(8,128)(2,1)}, u32[]{:S(2)}, u32[]{:S(2)}) async-start(bf16[4,896,256]{2,1,0:T(8,128)(2,1)} %bitcast.1), calls=%async_computation.1 | async-start | bytes 3670016 | tf_op jit(solution)/shard_map/all_to_all | solution.py:14
  276.0 66.1 %all-gather.2.cloned.1.call-start = ((), (), s32[]{:S(2)}) async-start(), calls=%async_computation.11 | async-start | bytes 2621440 | tf_op jit(solution)/shard_map/all_gather | solution.py:71
  281.1 32.0 %copy-start.11 = (f32[256,1024]{1,0:T(8,128)S(1)}, f32[256,1024]{1,0:T(8,128)}, u32[]{:S(2)}) copy-start(f32[256,1024]{1,0:T(8,128)} %get-tuple-element.3) | copy-start | bytes 3145732
  306.6 27.8 %all-to-all-start.10 = ((bf16[256,4,896]{2,0,1:T(8,128)(2,1)}), bf16[256,4,896]{2,0,1:T(8,128)(2,1)}, u32[]{:S(2)}, u32[]{:S(2)}) async-start(bf16[256,4,896]{2,0,1:T(8,128)(2,1)} %copy.26), calls=%async_computation.10 | async-start | bytes 3670016 | tf_op jit(solution)/shard_map/all_to_all | solution.py:110
  336.0 30.2 %all-to-all-start.9 = ((bf16[4,256,1024]{2,1,0:T(8,128)(2,1)}), bf16[4,256,1024]{2,1,0:T(8,128)(2,1)}, u32[]{:S(2)}, u32[]{:S(2)}) async-start(bf16[4,256,1024]{2,1,0:T(8,128)(2,1)} %broadcast_in_dim.15), calls=%async_computation.9 | async-start | bytes 4194304 | tf_op jit(solution)/shard_map/all_to_all | solution.py:14
  366.2 5.6 %copy-start.1 = (bf16[224,3584]{1,0:T(8,128)(2,1)S(1)}, bf16[224,3584]{1,0:T(8,128)(2,1)}, u32[]{:S(2)}) copy-start(bf16[224,3584]{1,0:T(8,128)(2,1)} %param.21) | copy-start | bytes 4816900
Sparse Core Ops, SparseCore 0:
  278.4 35.7 all-gather.1

commit v2 on v1

v2 whole, which is shorter than its diff:
```python
import functools

import jax
import jax.numpy as jnp
from jax import lax
from jax.experimental import pallas as pl
from jax.experimental.pallas import tpu as pltpu
from jax.sharding import Mesh
from jax.sharding import PartitionSpec as P

SHARDS = ("tensor_0", "tensor_1", "latent")
BATCH = ("batch_0", "batch_1")

epsilon = 1e-06

f32 = jnp.float32
bf16 = jnp.bfloat16
LAST = (((1,), (1,)), ((), ()))
WHOLE = pl.BlockSpec(memory_space=pltpu.VMEM)
LIMIT = 40 * 1024 * 1024


def exchange(pieces, axes):
    return lax.all_to_all(pieces, axes, split_axis=0, concat_axis=0, tiled=True)


def swap(block, axes):
    for_all = lax.axis_size(axes)
    return lax.ppermute(block, axes, [(i, for_all - 1 - i) for i in range(for_all)])


def copies_of_all(block):
    near = swap(block, BATCH[1])
    far = swap(block, BATCH[0])
    return [block, near, far, swap(far, BATCH[1])]


def blocks_of_all(block_at):
    own = lax.axis_index(BATCH)
    steps = ((1, BATCH[1]), (2, BATCH[0]), (3, BATCH))
    return [block_at(own)] + [swap(block_at(own ^ step), axes) for step, axes in steps]


def call(body, outs, flops, args, **more):
    moved = sum(a.size * a.dtype.itemsize for a in [*args, *jax.tree.leaves(outs)])
    cost = pl.CostEstimate(flops=flops, bytes_accessed=moved, transcendentals=0)
    return pl.pallas_call(
        body,
        out_shape=outs,
        cost_estimate=cost,
        compiler_params=pltpu.CompilerParams(vmem_limit_bytes=LIMIT),
        **more,
    )(*args)


def array(shape, dtype=bf16):
    return jax.ShapeDtypeStruct(shape, dtype)


def product(left, right):
    return jnp.dot(left, right, preferred_element_type=f32)


def product_t(left, right):
    return lax.dot_general(left, right, LAST, preferred_element_type=f32)


def encode_kernel(centered_ref, weight_ref, bias_ref, latents_ref, turned_ref, rows_ref):
    width = centered_ref.shape[0]

    @pl.when(pl.program_id(0) == 0)
    def _():
        for at in range(0, width, 256):
            rows_ref[:, at : at + 256] = centered_ref[at : at + 256, :].T

    preact = product(rows_ref[...], weight_ref[...]) + bias_ref[...].astype(f32)
    latents = jnp.maximum(preact, 0.0).astype(bf16)
    latents_ref[...] = latents
    turned_ref[...] = latents.T


def encode(centered, weight, bias, tile):
    width, tokens = centered.shape
    count = weight.shape[1]
    return call(
        encode_kernel,
        [array((tokens, count)), array((count, tokens))],
        2 * tokens * width * count,
        [centered, weight, bias.reshape(1, count)],
        grid=(count // tile,),
        in_specs=[
            WHOLE,
            pl.BlockSpec((width, tile), lambda j: (0, j)),
            pl.BlockSpec((1, tile), lambda j: (0, j)),
        ],
        out_specs=[
            pl.BlockSpec((tokens, tile), lambda j: (0, j)),
            pl.BlockSpec((tile, tokens), lambda j: (j, 0)),
        ],
        scratch_shapes=[pltpu.VMEM((tokens, width), bf16)],
    )


def decode_kernel(latents_ref, weight_ref, target_ref, out_ref):
    tile = weight_ref.shape[1]
    step = pl.program_id(0)
    at = pl.multiple_of(step * tile, tile)
    out_ref[:, pl.ds(at, tile)] = product(latents_ref[...], weight_ref[...]).astype(bf16)

    @pl.when(step == 0)
    def _():
        rows, tokens = target_ref.shape
        spare = -rows % 128
        padded = jnp.concatenate([target_ref[...], jnp.zeros((spare, tokens), bf16)], axis=0)
        out_ref[:, out_ref.shape[1] - rows - spare :] = padded.T


def decode(latents, weight, turned_target, room):
    tokens, count = latents.shape
    width = weight.shape[1]
    tile = width // 7
    return call(
        decode_kernel,
        array((tokens, width + room)),
        2 * tokens * width * count,
        [latents, weight, turned_target],
        grid=(7,),
        in_specs=[WHOLE, pl.BlockSpec((count, tile), lambda j: (0, j)), WHOLE],
        out_specs=WHOLE,
    )


def total_of(pieces_ref, width):
    total = pieces_ref[0, :, :width].astype(f32)
    for k in range(1, pieces_ref.shape[0]):
        total += pieces_ref[k, :, :width].astype(f32)
    return total


def send_to_all(out_ref, rows):
    for k in range(out_ref.shape[0]):
        out_ref[k] = rows


def mean_of(values):
    return jnp.sum(values, axis=1, keepdims=True) / values.shape[1]


def recon_kernel(pieces_ref, bias_ref, gain_ref, out_ref, recon_ref):
    recon = total_of(pieces_ref, recon_ref.shape[1]) + bias_ref[...].astype(f32)
    recon_ref[...] = recon
    scale_in = lax.rsqrt(mean_of(recon * recon) + epsilon)
    send_to_all(out_ref, (recon * scale_in * gain_ref[...].astype(f32)).astype(bf16))


def output_kernel(token_count, pieces_ref, recon_ref, target_ref, gain_ref, out_ref, grad_ref):
    gain = gain_ref[...].astype(f32)
    output = total_of(pieces_ref, recon_ref.shape[1])
    scale_out = lax.rsqrt(mean_of(output * output) + epsilon)
    normed_out = output * scale_out
    result = recon_ref[...] + normed_out * gain
    grad_result = 2.0 * (result - target_ref[...].astype(f32)) / token_count
    grad_ref[...] = grad_result
    grad_normed = grad_result * gain
    inner = mean_of(grad_normed * normed_out)
    send_to_all(out_ref, (scale_out * (grad_normed - normed_out * inner)).astype(bf16))


def input_kernel(pieces_ref, recon_ref, grad_ref, gain_ref, out_ref):
    recon = recon_ref[...]
    scale_in = lax.rsqrt(mean_of(recon * recon) + epsilon)
    unit = recon * scale_in
    grad_unit = total_of(pieces_ref, recon_ref.shape[1]) * gain_ref[...].astype(f32)
    inner = mean_of(grad_unit * unit)
    send_to_all(out_ref, (grad_ref[...] + scale_in * (grad_unit - unit * inner)).astype(bf16))


def local(body, outs, args):
    return call(body, outs, 0, args, in_specs=[WHOLE] * len(args), out_specs=[WHOLE] * len(outs))


def forward_kernel(rows_ref, gate_ref, up_ref, down_ref, out_ref, gelu_ref, slope_ref):
    gate_value = product_t(rows_ref[...], gate_ref[...])
    up_value = product_t(rows_ref[...], up_ref[...])
    root = 0.7978845608028654
    cube = 0.044715
    square = gate_value * gate_value
    curve = jnp.tanh(root * gate_value * (1.0 + cube * square))
    half = 0.5 * (1.0 + curve)
    gelu_value = gate_value * half
    rise = 0.5 * gate_value * (1.0 - curve * curve) * root * (1.0 + 3.0 * cube * square)
    gelu_ref[...] = gelu_value
    slope_ref[...] = up_value * (half + rise)
    hidden = (gelu_value * up_value).astype(bf16)
    for at in range(0, out_ref.shape[1], 512):
        out_ref[:, at : at + 512] = product(hidden, down_ref[:, at : at + 512]).astype(bf16)


def backward_kernel(
    rows_ref, gate_ref, up_ref, down_ref, gelu_ref, slope_ref, out_ref
):
    grad_hidden = product_t(rows_ref[...], down_ref[...])
    grad_gate = (grad_hidden * slope_ref[...]).astype(bf16)
    grad_up = (grad_hidden * gelu_ref[...]).astype(bf16)
    for at in range(0, out_ref.shape[1], 512):
        part = product(grad_gate, gate_ref[:, at : at + 512])
        part += product(grad_up, up_ref[:, at : at + 512])
        out_ref[:, at : at + 512] = part.astype(bf16)


def latent_kernel(rows_ref, weight_ref, latents_ref, out_ref):
    grad_latent = product_t(rows_ref[...], weight_ref[...])
    out_ref[...] = jnp.where(latents_ref[...].astype(f32) > 0, grad_latent, 0.0).astype(bf16)


def grad_of_preact(rows, weight, latents, tile):
    tokens, width = rows.shape
    count = weight.shape[0]
    return call(
        latent_kernel,
        array((tokens, count)),
        2 * tokens * width * count,
        [rows, weight, latents],
        grid=(count // tile,),
        in_specs=[
            WHOLE,
            pl.BlockSpec((tile, width), lambda j: (j, 0)),
            pl.BlockSpec((tokens, tile), lambda j: (0, j)),
        ],
        out_specs=pl.BlockSpec((tokens, tile), lambda j: (0, j)),
    )


def products_kernel(*refs):
    count = len(refs) // 2
    out_ref = refs[-1]
    total = product(refs[0][...], refs[count][...])
    for k in range(1, count):
        total += product(refs[k][...], refs[count + k][...])
    out_ref[...] = total.astype(bf16)


def sum_of_products(left, right, tile):
    rows, depth = left[0].shape
    columns = right[0].shape[1]
    return call(
        products_kernel,
        array((rows, columns)),
        2 * rows * depth * columns * len(left),
        [*left, *right],
        grid=(columns // tile,),
        in_specs=[pl.BlockSpec((rows, depth), lambda j: (0, 0))] * len(left)
        + [pl.BlockSpec((depth, tile), lambda j: (0, j))] * len(right),
        out_specs=pl.BlockSpec((rows, tile), lambda j: (0, j)),
    )


def per_device(
    residual,
    target,
    encoder_weight,
    encoder_bias,
    decoder_weight,
    decoder_bias,
    first_gain,
    second_gain,
    gate_weight,
    up_weight,
    down_weight,
):
    tokens, share_width = residual.shape
    shards = lax.axis_size(SHARDS)
    copies = lax.axis_size(BATCH)
    width = share_width * shards
    block = width // copies
    own_tokens = tokens // shards
    token_count = tokens * copies
    offset = lax.axis_index(SHARDS) * share_width
    bias, gain_in, gain_out = (a.reshape(1, width) for a in (decoder_bias, first_gain, second_gain))
    gate, up = gate_weight.T, up_weight.T
    everyone = array((shards, own_tokens, width))
    own_rows = array((own_tokens, width), f32)

    def to_owners(partial):
        return exchange(partial.reshape(shards, own_tokens, -1), SHARDS)

    def all_tokens(pieces):
        return exchange(pieces, SHARDS).reshape(tokens, width)

    bias_share = lax.dynamic_slice_in_dim(decoder_bias.astype(f32), offset, share_width)
    centered_share = (residual.astype(f32) - bias_share).astype(bf16).T
    pieces = jnp.broadcast_to(centered_share, (shards, share_width, tokens))
    centered = exchange(pieces, SHARDS).reshape(width, tokens)

    centered_blocks = blocks_of_all(
        lambda b: lax.dynamic_slice_in_dim(centered, b * block, block, axis=0)
    )
    latents, turned_latents = encode(centered, encoder_weight, encoder_bias, 256)
    partial_recon = decode(latents, decoder_weight, target.T, 128)
    partial_recon, *centered_blocks = lax.optimization_barrier((partial_recon, *centered_blocks))

    pieces = to_owners(partial_recon)
    own_target = pieces[:, :, width : width + share_width]
    own_target = jnp.moveaxis(own_target, 0, 1).reshape(own_tokens, width)
    pieces, recon = local(recon_kernel, [everyone, own_rows], [pieces, bias, gain_in])

    normed_input = all_tokens(pieces)
    latent_blocks = copies_of_all(turned_latents)
    hidden = array((tokens, gate.shape[0]), f32)
    partial_out, gelu_value, slope = local(
        forward_kernel,
        [array((tokens, width)), hidden, hidden],
        [normed_input, gate, up, down_weight],
    )
    partial_out, *latent_blocks = lax.optimization_barrier((partial_out, *latent_blocks))

    pieces, grad_result = local(
        functools.partial(output_kernel, token_count),
        [everyone, own_rows],
        [to_owners(partial_out), recon, own_target, gain_out],
    )
    grad_output = all_tokens(pieces)
    (partial_input,) = local(
        backward_kernel,
        [array((tokens, width))],
        [grad_output, gate, up, down_weight, gelu_value, slope],
    )
    (pieces,) = local(
        input_kernel, [everyone], [to_owners(partial_input), recon, grad_result, gain_in]
    )
    grad_recon = all_tokens(pieces)

    recon_blocks = blocks_of_all(
        lambda b: lax.dynamic_slice_in_dim(grad_recon, b * block, block, axis=1)
    )
    grad_preact = grad_of_preact(grad_recon, decoder_weight, latents, 256)
    decoder_grad = sum_of_products(latent_blocks, recon_blocks, 128)
    encoder_grad = sum_of_products(centered_blocks, copies_of_all(grad_preact), 256)
    return encoder_grad, decoder_grad


def solution(mesh):
    batch, latent = mesh.shape["batch"], mesh.shape["latent"]
    split = Mesh(
        mesh.devices.reshape(2, batch // 2, mesh.shape["tensor"] // 2, 2, latent),
        BATCH + SHARDS,
    )
    in_specs = (
        P(BATCH, SHARDS),
        P(BATCH, SHARDS),
        P(None, SHARDS),
        P(SHARDS),
        P(SHARDS, None),
        P(),
        P(),
        P(),
        P(None, SHARDS),
        P(None, SHARDS),
        P(SHARDS, None),
    )
    out_specs = (P(BATCH, SHARDS), P(SHARDS, BATCH))
    return jax.shard_map(
        per_device, mesh=split, in_specs=in_specs, out_specs=out_specs, check_vma=False
    )
```

time: 386 us -> 332 us (0.86)
  matrix products: 36.8 us -> 0 us
  Pallas kernels: 0 us -> 32.7 us
  starting transfers between devices: 55.9 us -> 40.5 us
  between operations: 14.3 us -> 1.12 us
  other arithmetic: 12.2 us -> 1.67 us
  waiting for transfers between devices: 148 us -> 142 us
    ppermute x0 -> x12, waiting for transfers between devices: none -> 63.1 us  [swap(): lax.ppermute(block, axes, [(i, for_all - 1 - i) for i in range(for_all)])]
    all_to_all x7 -> x4, waiting for transfers between devices: 131 us -> 79.3 us  [exchange(): return lax.all_to_all(pieces, axes, split_axis=0, concat_axis=0, tiled=True)]
    dot_general x11 -> x0, matrix products: 36.8 us -> none  [the longest x1 6.71 us: per_device(): lax.dot_general(centered, encoder_weight, contract_first, preferred_eleme...]
    pallas_call x0 -> x10, Pallas kernels: none -> 32.7 us  [call(): pl.pallas_call(body, out_shape=outs, cost_estimate=cost, compiler_params=...]
    all_to_all x7 -> x4, starting transfers between devices: 49.3 us -> 31.9 us  [exchange(): return lax.all_to_all(pieces, axes, split_axis=0, concat_axis=0, tiled=True)]
    all_to_all x1 -> x0, waiting for transfers between devices: 16.2 us -> none  [per_device(): lax.all_to_all(grad_recon, BATCH, split_axis=1, concat_axis=0, tiled=True)]
    unnamed x47 -> x72, local copies, waits for them, and re-layouts: 5.23 us -> 15 us
    ppermute x0 -> x12, starting transfers between devices: none -> 8.57 us  [swap(): lax.ppermute(block, axes, [(i, for_all - 1 - i) for i in range(for_all)])]
  transfers between devices with their start and end apart: 9 -> 16, of which waited for: 8 -> 8; matrix products, arithmetic and copies ran while one was open for 9% -> 0% of each run, Pallas kernels for 0% -> 6%
where the time goes in v2:
time: 332 us; the launch traced here: 328 us
  waiting for transfers between devices  142 us (43%)
  blocking collectives  90.7 us (27%)
  starting transfers between devices  40.5 us (12%)
  Pallas kernels  32.7 us (10%)
  local copies, waits for them, and re-layouts  19.1 us (6%)
    all_to_all x3, blocking collectives, exchange(): return lax.all_to_all(pieces, axes, split_axis=0, concat_axis=0, tiled=True)  90.7 us
    all_to_all x4, waiting for transfers between devices, exchange(): return lax.all_to_all(pieces, axes, split_axis=0, concat_axis=0, tiled=True)  79.3 us
    ppermute x12, waiting for transfers between devices, swap(): lax.ppermute(block, axes, [(i, for_all - 1 - i) for i in range(for_all)])  63.1 us
    pallas_call x10, Pallas kernels, call(): pl.pallas_call(body, out_shape=outs, cost_estimate=cost, compiler_params=...  32.7 us
    all_to_all x4, starting transfers between devices, exchange(): return lax.all_to_all(pieces, axes, split_axis=0, concat_axis=0, tiled=True)  31.9 us
    unnamed x72, local copies, waits for them, and re-layouts  15 us
    ppermute x12, starting transfers between devices, swap(): lax.ppermute(block, axes, [(i, for_all - 1 - i) for i in range(for_all)])  8.57 us
  transfers between devices with their start and end apart: 16, of which 8 were waited for; matrix products, arithmetic and copies ran while one was open for 0% of the time, Pallas kernels for 6%

profile of v2, /device:TPU:14, one launch (start us, length us, event | category | flops | bytes accessed | tf_op | source)
XLA Modules:
  0.0 328.2 jit_solution(4912875190221637633)
XLA Ops:
  0.6 0.8 dynamic-slice_convert_fusion
  1.4 0.9 fusion
  2.3 1.3 broadcast_in_dim.4
  3.7 10.5 %all-to-all-start = ((bf16[32,112,256]{2,1,0:T(8,128)(2,1)}), bf16[32,112,256]{2,1,0:T(8,128)(2,1)}, u32[]{:S(2)}, u32[]{:S(2)}) async-start(bf16[32,112,256]{2,1,0:T(8,128)(2,1)} %broadcast_in_dim.4), calls=%async_computation | async-start | bytes 3670016 | tf_op jit(solution)/shard_map/all_to_all | solution.py:24
  14.2 24.5 %all-to-all-done = bf16[32,112,256]{2,1,0:T(8,128)(2,1)} async-done(((bf16[32,112,256]{2,1,0:T(8,128)(2,1)}), bf16[32,112,256]{2,1,0:T(8,128)(2,1)}, u32[]{:S(2)}, u32[]{:S(2)}) %all-to-all-start) | async-done | bytes 1835040 | tf_op jit(solution)/shard_map/all_to_all | solution.py:24
  38.7 2.4 constant_dynamic-slice_fusion.4
  41.0 0.9 collective-permute-start.1
  41.9 0.9 collective-permute-start
  42.9 3.1 copy-done.1
  46.0 5.8 %shard_map.122 = (bf16[256,1024]{1,0:T(8,128)(2,1)S(1)}, bf16[1024,256]{1,0:T(8,128)(2,1)S(1)}) custom-call(bf16[3584,256]{1,0:T(8,128)(2,1)} %bitcast.1.centered_ref, bf16[3584,1024]{1,0:T(8,128)(2,1)S(1)} %copy-done.1, bf16[1,1024]{1,0:T(2,128)(2,1)S(1)} %reshape.42.bias_ref), custom_call_target="tpu_custom_call" | custom-call | flops 1879048192 | bytes 10225664 | tf_op jit(solution)/shard_map/pallas_call | solution.py:47
  51.8 3.7 %shard_map.123 = bf16[256,3712]{1,0:T(8,128)(2,1)S(1)} custom-call(bf16[256,1024]{1,0:T(8,128)(2,1)S(1)} %get-tuple-element.21.latents_ref, bf16[1024,3584]{1,0:T(8,128)(2,1)S(1)} %bitcast.15, bf16[112,256]{1,0:T(8,128)(2,1)S(1)} %bitcast.28), custom_call_target="tpu_custom_call" | custom-call | flops 1879048192 | bytes 9822208 | tf_op jit(solution)/shard_map/pallas_call | solution.py:47
  55.5 1.3 copy-done
  56.8 0.8 copy-done.22
  57.6 5.0 %collective-permute-done.1.refs_2_ = bf16[896,256]{1,0:T(8,128)(2,1)S(1)} collective-permute-done((bf16[896,256]{1,0:T(8,128)(2,1)S(1)}, bf16[896,256]{1,0:T(8,128)(2,1)S(1)}, u32[]{:S(2)}, u32[]{:S(2)}) %collective-permute-start.1) | collective-permute-done | bytes 458784 | tf_op jit(solution)/shard_map/ppermute | solution.py:29
  62.6 0.8 copy-done.24
  63.4 0.8 copy-done.26
  64.2 7.3 %all-to-all-start.1 = ((bf16[32,8,3712]{2,1,0:T(8,128)(2,1)}), bf16[32,8,3712]{2,1,0:T(8,128)(2,1)S(1)}, u32[]{:S(2)}, u32[]{:S(2)}) async-start(bf16[32,8,3712]{2,1,0:T(8,128)(2,1)} %bitcast.20), calls=%async_computation.1 | async-start | bytes 3801088 | tf_op jit(solution)/shard_map/all_to_all | solution.py:24
  71.6 27.8 %all-to-all-done.1.pieces_ref = bf16[32,8,3712]{2,1,0:T(8,128)(2,1)S(1)} async-done(((bf16[32,8,3712]{2,1,0:T(8,128)(2,1)}), bf16[32,8,3712]{2,1,0:T(8,128)(2,1)S(1)}, u32[]{:S(2)}, u32[]{:S(2)}) %all-to-all-start.1) | async-done | bytes 1900576 | tf_op jit(solution)/shard_map/all_to_all | solution.py:24
  99.4 0.5 shard_map.124
  99.9 1.2 copy-done.9
  101.1 0.6 copy-done.12
  101.8 5.3 %all-to-all-start.2 = ((bf16[32,8,3584]{2,1,0:T(8,128)(2,1)}), bf16[32,8,3584]{2,1,0:T(8,128)(2,1)}, u32[]{:S(2)}, u32[]{:S(2)}) async-start(bf16[32,8,3584]{2,1,0:T(8,128)(2,1)} %copy-done.9), calls=%async_computation.2 | async-start | bytes 3670016 | tf_op jit(solution)/shard_map/all_to_all | solution.py:24
  107.0 1.8 collective-permute-start.4
  108.8 31.1 %collective-permute-done.4.refs_2_ = bf16[1024,256]{1,0:T(8,128)(2,1)} collective-permute-done((bf16[1024,256]{1,0:T(8,128)(2,1)}, bf16[1024,256]{1,0:T(8,128)(2,1)}, u32[]{:S(2)}, u32[]{:S(2)}) %collective-permute-start.4) | collective-permute-done | bytes 524320 | tf_op jit(solution)/shard_map/ppermute | solution.py:29
  140.0 1.4 copy-done.3
  141.4 1.4 copy-done.5
  142.8 3.3 %shard_map.125 = (bf16[256,3584]{1,0:T(8,128)(2,1)S(1)}, f32[256,224]{1,0:T(8,128)S(1)}, f32[256,224]{1,0:T(8,128)S(1)}) custom-call(bf16[256,3584]{1,0:T(8,128)(2,1)} %bitcast.4.rows_ref, bf16[224,3584]{1,0:T(8,128)(2,1)S(1)} %bitcast.23, bf16[224,3584]{1,0:T(8,128)(2,1)S(1)} %bitcast.25, bf16[224,3584]{1,0:T(8,128)(2,1)S(1)} %copy-done.5), custom_call_target="tpu_custom_call" | custom-call | bytes 8945664 | tf_op jit(solution)/shard_map/pallas_call | solution.py:47
  146.1 1.2 copy-done.10
  147.3 0.7 copy-done.15
  148.0 0.7 copy-done.17
  148.8 8.9 %all-to-all-start.3 = ((bf16[32,8,3584]{2,1,0:T(8,128)(2,1)}), bf16[32,8,3584]{2,1,0:T(8,128)(2,1)}, u32[]{:S(2)}, u32[]{:S(2)}) async-start(bf16[32,8,3584]{2,1,0:T(8,128)(2,1)} %bitcast.27), calls=%async_computation.3 | async-start | bytes 3670016 | tf_op jit(solution)/shard_map/all_to_all | solution.py:24
  157.8 27.1 %all-to-all-done.3.pieces_ref = bf16[32,8,3584]{2,1,0:T(8,128)(2,1)} async-done(((bf16[32,8,3584]{2,1,0:T(8,128)(2,1)}), bf16[32,8,3584]{2,1,0:T(8,128)(2,1)}, u32[]{:S(2)}, u32[]{:S(2)}) %all-to-all-start.3) | async-done | bytes 1835040 | tf_op jit(solution)/shard_map/all_to_all | solution.py:24
  184.9 0.9 copy-done.13
  185.8 2.2 shard_map.126
  188.0 29.6 %all_to_all.35 = bf16[32,8,3584]{2,1,0:T(8,128)(2,1)S(1)} all-to-all(bf16[32,8,3584]{2,1,0:T(8,128)(2,1)S(1)} %get-tuple-element.32), channel_id=1, replica_groups=mesh['batch_0'=2,'batch_1'=2,'tensor_0'=4,'tensor_1'=2,'latent'=4] {'ten..., dimensions={0} | all-to-all | bytes 3670016 | tf_op jit(solution)/shard_map/all_to_all | solution.py:24
  217.6 2.5 shard_map.127
  220.2 30.9 %all_to_all.36.pieces_ref = bf16[32,8,3584]{2,1,0:T(8,128)(2,1)S(1)} all-to-all(bf16[32,8,3584]{2,1,0:T(8,128)(2,1)S(1)} %bitcast.22), channel_id=1, replica_groups=mesh['batch_0'=2,'batch_1'=2,'tensor_0'=4,'tensor_1'=2,'latent'=4] {'ten..., dimensions={0} | all-to-all | bytes 3670016 | tf_op jit(solution)/shard_map/all_to_all | solution.py:24
  251.1 0.5 shard_map.128
  251.6 30.2 %all_to_all.37 = bf16[32,8,3584]{2,1,0:T(8,128)(2,1)S(1)} all-to-all(bf16[32,8,3584]{2,1,0:T(8,128)(2,1)S(1)} %shard_map.128), channel_id=1, replica_groups=mesh['batch_0'=2,'batch_1'=2,'tensor_0'=4,'tensor_1'=2,'latent'=4] {'ten..., dimensions={0} | all-to-all | bytes 3670016 | tf_op jit(solution)/shard_map/all_to_all | solution.py:24
  281.8 2.9 shard_map.129.refs_4_
  284.7 3.0 collective-permute-start.7
  287.7 0.1 constant_dynamic-slice_fusion
  288.1 1.7 collective-permute-start.9
  289.8 10.7 %collective-permute-done.7.refs_6_ = bf16[256,1024]{1,0:T(8,128)(2,1)S(1)} collective-permute-done((bf16[256,1024]{1,0:T(8,128)(2,1)S(1)}, bf16[256,1024]{1,0:T(8,128)(2,1)S(1)}, u32[]{:S(2)}, u32[]{:S(2)}) %collective-permute-start.7) | collective-permute-done | bytes 524320 | tf_op jit(solution)/shard_map/ppermute | solution.py:29
  300.5 9.4 %collective-permute-done.11.refs_7_ = bf16[256,896]{1,0:T(8,128)(2,1)S(1)} collective-permute-done((bf16[256,896]{1,0:T(8,128)(2,1)S(1)}, bf16[256,896]{1,0:T(8,128)(2,1)S(1)}, u32[]{:S(2)}, u32[]{:S(2)}) %collective-permute-start.11) | collective-permute-done | bytes 458784 | tf_op jit(solution)/shard_map/ppermute | solution.py:29
  309.9 6.9 %collective-permute-done.10.refs_6_ = bf16[256,896]{1,0:T(8,128)(2,1)S(1)} collective-permute-done((bf16[256,896]{1,0:T(8,128)(2,1)S(1)}, bf16[256,896]{1,0:T(8,128)(2,1)S(1)}, u32[]{:S(2)}, u32[]{:S(2)}) %collective-permute-start.10) | collective-permute-done | bytes 458784 | tf_op jit(solution)/shard_map/ppermute | solution.py:29
  316.8 7.6 %shard_map.131 = bf16[1024,896]{1,0:T(8,128)(2,1)} custom-call(bf16[1024,256]{1,0:T(8,128)(2,1)S(1)} %copy-done.21, bf16[1024,256]{1,0:T(8,128)(2,1)} %collective-permute-done.3.refs_1_, bf16[1024,256]{1,0:T(8,128)(2,1)} %collective-permute-done.4.refs_2_, bf16[1024,256]{1,0:T(8,128)(2,1)} %collective-permute-done.5.refs_3_, ...), custom_call_target="tpu_custom_call" | custom-call | flops 1879048192 | bytes 5767168 | tf_op jit(solution)/shard_map/pallas_call | solution.py:47
  324.5 3.7 %shard_map.130 = bf16[896,1024]{1,0:T(8,128)(2,1)} custom-call(bf16[896,256]{1,0:T(8,128)(2,1)S(1)} %copy-done.11, bf16[896,256]{1,0:T(8,128)(2,1)S(1)} %copy-done.27, bf16[896,256]{1,0:T(8,128)(2,1)S(1)} %copy-done.25, bf16[896,256]{1,0:T(8,128)(2,1)S(1)} %copy-done.23, bf16[256,1024]{1,0:T(8,128)(2,1)S(1)} %shard_map.129.refs_4_, ...), custom_call_target="tpu_custom_call" | custom-call | flops 1879048192 | bytes 5767168 | tf_op jit(solution)/shard_map/pallas_call | solution.py:47
  (83 shorter events, 0.6 us)
Async XLA Ops:
  3.7 48.1 %slice-start = ((s8[7340032]{0:T(1024)(128)(4,1)}), s8[3145728]{0:T(1024)(128)(4,1)S(1)}, s32[]{:S(2)}) async-start(s8[7340032]{0:T(1024)(128)(4,1)} %bitcast.14), calls=%async_computation.7 | async-start | bytes 6291456
  3.7 35.0 %all-to-all-start = ((bf16[32,112,256]{2,1,0:T(8,128)(2,1)}), bf16[32,112,256]{2,1,0:T(8,128)(2,1)}, u32[]{:S(2)}, u32[]{:S(2)}) async-start(bf16[32,112,256]{2,1,0:T(8,128)(2,1)} %broadcast_in_dim.4), calls=%async_computation | async-start | bytes 3670016 | tf_op jit(solution)/shard_map/all_to_all | solution.py:24
  38.7 4.2 %copy-start.31 = (bf16[1024]{0:T(1024)(128)(2,1)S(1)}, bf16[1024]{0:T(1024)(128)(2,1)}, u32[]{:S(2)}) copy-start(bf16[1024]{0:T(1024)(128)(2,1)} %param.14) | copy-start | bytes 6148
  41.0 15.8 %collective-permute-start.2 = (bf16[896,256]{1,0:T(8,128)(2,1)S(1)}, bf16[896,256]{1,0:T(8,128)(2,1)S(1)}, u32[]{:S(2)}, u32[]{:S(2)}) collective-permute-start(bf16[896,256]{1,0:T(8,128)(2,1)S(1)} %get-tuple-element.44), channel_id=1, source_target_pairs={{0,96},{32,64},{64,32},{96,0},{1,97},{33,65},{65,33},{97,1},{2,98}... | collective-permute-start | bytes 1376264 | tf_op jit(solution)/shard_map/ppermute | solution.py:29
  41.0 21.6 %collective-permute-start.1 = (bf16[896,256]{1,0:T(8,128)(2,1)S(1)}, bf16[896,256]{1,0:T(8,128)(2,1)S(1)}, u32[]{:S(2)}, u32[]{:S(2)}) collective-permute-start(bf16[896,256]{1,0:T(8,128)(2,1)S(1)} %get-tuple-element.45), channel_id=1, source_target_pairs={{0,64},{64,0},{1,65},{65,1},{2,66},{66,2},{3,67},{67,3},{4,68},{68... | collective-permute-start | bytes 1376264 | tf_op jit(solution)/shard_map/ppermute | solution.py:29
  41.9 21.5 %collective-permute-start = (bf16[896,256]{1,0:T(8,128)(2,1)S(1)}, bf16[896,256]{1,0:T(8,128)(2,1)S(1)}, u32[]{:S(2)}, u32[]{:S(2)}) collective-permute-start(bf16[896,256]{1,0:T(8,128)(2,1)S(1)} %get-tuple-element.46), channel_id=1, source_target_pairs={{0,32},{32,0},{1,33},{33,1},{2,34},{34,2},{3,35},{35,3},{4,36},{36... | collective-permute-start | bytes 1376264 | tf_op jit(solution)/shard_map/ppermute | solution.py:29
  42.9 3.1 copy-start.1
  46.0 5.8 %slice-start.1 = ((s8[7340032]{0:T(1024)(128)(4,1)}), s8[4194304]{0:T(1024)(128)(4,1)S(1)}, s32[]{:S(2)}) async-start(s8[7340032]{0:T(1024)(128)(4,1)} %bitcast.14), calls=%async_computation.8 | async-start | bytes 8388608
  46.0 5.8 %copy-start.19 = (bf16[256,112]{0,1:T(8,128)(2,1)S(1)}, bf16[256,112]{0,1:T(8,128)(2,1)}, u32[]{:S(2)}) copy-start(bf16[256,112]{0,1:T(8,128)(2,1)} %param.12) | copy-start | bytes 172036
  51.8 3.7 %copy-start.7 = (bf16[256,1024]{1,0:T(8,128)(2,1)}, bf16[256,1024]{1,0:T(8,128)(2,1)S(1)}, u32[]{:S(2)}) copy-start(bf16[256,1024]{1,0:T(8,128)(2,1)S(1)} %get-tuple-element.21.latents_ref) | copy-start | bytes 1572868
  51.8 3.7 %copy-start.20 = (bf16[1024,256]{1,0:T(8,128)(2,1)}, bf16[1024,256]{1,0:T(8,128)(2,1)S(1)}, u32[]{:S(2)}) copy-start(bf16[1024,256]{1,0:T(8,128)(2,1)S(1)} %get-tuple-element.36.refs_0_) | copy-start | bytes 1572868
  55.5 1.3 copy-start
  56.8 0.8 copy-start.22
  62.6 0.8 copy-start.24
  64.2 7.3 %copy-start.28 = (bf16[3584]{0:T(1024)(128)(2,1)S(1)}, bf16[3584]{0:T(1024)(128)(2,1)}, u32[]{:S(2)}) copy-start(bf16[3584]{0:T(1024)(128)(2,1)} %param.16) | copy-start | bytes 21508
  64.2 7.3 %copy-start.29 = (bf16[3584]{0:T(1024)(128)(2,1)S(1)}, bf16[3584]{0:T(1024)(128)(2,1)}, u32[]{:S(2)}) copy-start(bf16[3584]{0:T(1024)(128)(2,1)} %param.17) | copy-start | bytes 21508
  64.2 35.1 %all-to-all-start.1 = ((bf16[32,8,3712]{2,1,0:T(8,128)(2,1)}), bf16[32,8,3712]{2,1,0:T(8,128)(2,1)S(1)}, u32[]{:S(2)}, u32[]{:S(2)}) async-start(bf16[32,8,3712]{2,1,0:T(8,128)(2,1)} %bitcast.20), calls=%async_computation.1 | async-start | bytes 3801088 | tf_op jit(solution)/shard_map/all_to_all | solution.py:24
  99.9 1.2 copy-start.9
  101.8 38.2 %copy-start.2 = (bf16[3584,224]{0,1:T(8,128)(2,1)S(1)}, bf16[3584,224]{0,1:T(8,128)(2,1)}, u32[]{:S(2)}) copy-start(bf16[3584,224]{0,1:T(8,128)(2,1)} %param.19) | copy-start | bytes 4816900
  101.8 38.2 %all-to-all-start.2 = ((bf16[32,8,3584]{2,1,0:T(8,128)(2,1)}), bf16[32,8,3584]{2,1,0:T(8,128)(2,1)}, u32[]{:S(2)}, u32[]{:S(2)}) async-start(bf16[32,8,3584]{2,1,0:T(8,128)(2,1)} %copy-done.9), calls=%async_computation.2 | async-start | bytes 3670016 | tf_op jit(solution)/shard_map/all_to_all | solution.py:24
  107.0 32.9 %collective-permute-start.4 = (bf16[1024,256]{1,0:T(8,128)(2,1)}, bf16[1024,256]{1,0:T(8,128)(2,1)}, u32[]{:S(2)}, u32[]{:S(2)}) collective-permute-start(bf16[1024,256]{1,0:T(8,128)(2,1)} %copy-done.20), channel_id=1, source_target_pairs={{0,64},{64,0},{1,65},{65,1},{2,66},{66,2},{3,67},{67,3},{4,68},{68... | collective-permute-start | bytes 1572872 | tf_op jit(solution)/shard_map/ppermute | solution.py:29
  108.8 39.9 %collective-permute-start.3 = (bf16[1024,256]{1,0:T(8,128)(2,1)}, bf16[1024,256]{1,0:T(8,128)(2,1)}, u32[]{:S(2)}, u32[]{:S(2)}) collective-permute-start(bf16[1024,256]{1,0:T(8,128)(2,1)} %copy-done.20), channel_id=1, source_target_pairs={{0,32},{32,0},{1,33},{33,1},{2,34},{34,2},{3,35},{35,3},{4,36},{36... | collective-permute-start | bytes 1572872 | tf_op jit(solution)/shard_map/ppermute | solution.py:29
  139.9 8.8 %collective-permute-start.5 = (bf16[1024,256]{1,0:T(8,128)(2,1)}, bf16[1024,256]{1,0:T(8,128)(2,1)}, u32[]{:S(2)}, u32[]{:S(2)}) collective-permute-start(bf16[1024,256]{1,0:T(8,128)(2,1)} %collective-permute-done.4.refs_2_), channel_id=1, source_target_pairs={{0,32},{32,0},{1,33},{33,1},{2,34},{34,2},{3,35},{35,3},{4,36},{36... | collective-permute-start | bytes 1572872 | tf_op jit(solution)/shard_map/ppermute | solution.py:29
  139.9 1.4 copy-start.3
  141.4 1.4 copy-start.5
  146.1 1.2 copy-start.10
  148.7 8.9 %copy-start.30 = (bf16[3584]{0:T(1024)(128)(2,1)S(1)}, bf16[3584]{0:T(1024)(128)(2,1)}, u32[]{:S(2)}) copy-start(bf16[3584]{0:T(1024)(128)(2,1)} %param.18) | copy-start | bytes 21508
  148.8 36.1 %all-to-all-start.3 = ((bf16[32,8,3584]{2,1,0:T(8,128)(2,1)}), bf16[32,8,3584]{2,1,0:T(8,128)(2,1)}, u32[]{:S(2)}, u32[]{:S(2)}) async-start(bf16[32,8,3584]{2,1,0:T(8,128)(2,1)} %bitcast.27), calls=%async_computation.3 | async-start | bytes 3670016 | tf_op jit(solution)/shard_map/all_to_all | solution.py:24
  184.9 0.9 copy-start.13
  185.8 31.8 %copy-start.18 = (f32[256,224]{1,0:T(8,128)S(1)}, f32[256,224]{1,0:T(8,128)}, u32[]{:S(2)}) copy-start(f32[256,224]{1,0:T(8,128)} %copy-done.17) | copy-start | bytes 688132
  188.0 29.6 %copy-start.4 = (bf16[3584,224]{0,1:T(8,128)(2,1)S(1)}, bf16[3584,224]{0,1:T(8,128)(2,1)}, u32[]{:S(2)}) copy-start(bf16[3584,224]{0,1:T(8,128)(2,1)} %param.20) | copy-start | bytes 4816900
  188.0 29.6 %copy-start.6 = (bf16[224,3584]{1,0:T(8,128)(2,1)S(1)}, bf16[224,3584]{1,0:T(8,128)(2,1)}, u32[]{:S(2)}) copy-start(bf16[224,3584]{1,0:T(8,128)(2,1)} %down_ref.3) | copy-start | bytes 4816900
  188.0 29.6 %copy-start.16 = (f32[256,224]{1,0:T(8,128)S(1)}, f32[256,224]{1,0:T(8,128)}, u32[]{:S(2)}) copy-start(f32[256,224]{1,0:T(8,128)} %copy-done.15) | copy-start | bytes 688132
  217.6 64.2 %slice-start.2 = ((s8[7340032]{0:T(1024)(128)(4,1)}), s8[4194304]{0:T(1024)(128)(4,1)S(1)}, s32[]{:S(2)}) async-start(s8[7340032]{0:T(1024)(128)(4,1)} %bitcast.16), calls=%async_computation.9 | async-start | bytes 8388608
  220.1 30.9 %copy-start.14 = (f32[8,3584]{1,0:T(8,128)S(1)}, f32[8,3584]{1,0:T(8,128)}, u32[]{:S(2)}) copy-start(f32[8,3584]{1,0:T(8,128)} %copy-done.12) | copy-start | bytes 344068
  220.1 61.7 %slice-start.3 = ((s8[7340032]{0:T(1024)(128)(4,1)}), s8[3145728]{0:T(1024)(128)(4,1)S(1)}, s32[]{:S(2)}) async-start(s8[7340032]{0:T(1024)(128)(4,1)} %bitcast.16), calls=%async_computation.10 | async-start | bytes 6291456
  251.6 30.2 %copy-start.8 = (bf16[256,1024]{1,0:T(8,128)(2,1)S(1)}, bf16[256,1024]{1,0:T(8,128)(2,1)}, u32[]{:S(2)}) copy-start(bf16[256,1024]{1,0:T(8,128)(2,1)} %copy-done.7) | copy-start | bytes 1572868
  284.7 32.1 %copy-start.21 = (bf16[1024,256]{1,0:T(8,128)(2,1)S(1)}, bf16[1024,256]{1,0:T(8,128)(2,1)}, u32[]{:S(2)}) copy-start(bf16[1024,256]{1,0:T(8,128)(2,1)} %copy-done.20) | copy-start | bytes 1572868
  284.7 15.8 %collective-permute-start.7 = (bf16[256,1024]{1,0:T(8,128)(2,1)S(1)}, bf16[256,1024]{1,0:T(8,128)(2,1)S(1)}, u32[]{:S(2)}, u32[]{:S(2)}) collective-permute-start(bf16[256,1024]{1,0:T(8,128)(2,1)S(1)} %shard_map.129.refs_4_), channel_id=1, source_target_pairs={{0,64},{64,0},{1,65},{65,1},{2,66},{66,2},{3,67},{67,3},{4,68},{68... | collective-permute-start | bytes 1572872 | tf_op jit(solution)/shard_map/ppermute | solution.py:29
  287.9 22.1 %collective-permute-start.11 = (bf16[256,896]{1,0:T(8,128)(2,1)S(1)}, bf16[256,896]{1,0:T(8,128)(2,1)S(1)}, u32[]{:S(2)}, u32[]{:S(2)}) collective-permute-start(bf16[256,896]{1,0:T(8,128)(2,1)S(1)} %get-tuple-element.40), channel_id=1, source_target_pairs={{0,96},{32,64},{64,32},{96,0},{1,97},{33,65},{65,33},{97,1},{2,98}... | collective-permute-start | bytes 1376264 | tf_op jit(solution)/shard_map/ppermute | solution.py:29
  287.9 28.8 %collective-permute-start.10 = (bf16[256,896]{1,0:T(8,128)(2,1)S(1)}, bf16[256,896]{1,0:T(8,128)(2,1)S(1)}, u32[]{:S(2)}, u32[]{:S(2)}) collective-permute-start(bf16[256,896]{1,0:T(8,128)(2,1)S(1)} %get-tuple-element.41), channel_id=1, source_target_pairs={{0,64},{64,0},{1,65},{65,1},{2,66},{66,2},{3,67},{67,3},{4,68},{68... | collective-permute-start | bytes 1376264 | tf_op jit(solution)/shard_map/ppermute | solution.py:29
  288.1 28.7 %collective-permute-start.9 = (bf16[256,896]{1,0:T(8,128)(2,1)S(1)}, bf16[256,896]{1,0:T(8,128)(2,1)S(1)}, u32[]{:S(2)}, u32[]{:S(2)}) collective-permute-start(bf16[256,896]{1,0:T(8,128)(2,1)S(1)} %get-tuple-element.42), channel_id=1, source_target_pairs={{0,32},{32,0},{1,33},{33,1},{2,34},{34,2},{3,35},{35,3},{4,36},{36... | collective-permute-start | bytes 1376264 | tf_op jit(solution)/shard_map/ppermute | solution.py:29
  289.8 34.6 %collective-permute-start.6 = (bf16[256,1024]{1,0:T(8,128)(2,1)S(1)}, bf16[256,1024]{1,0:T(8,128)(2,1)S(1)}, u32[]{:S(2)}, u32[]{:S(2)}) collective-permute-start(bf16[256,1024]{1,0:T(8,128)(2,1)S(1)} %shard_map.129.refs_4_), channel_id=1, source_target_pairs={{0,32},{32,0},{1,33},{33,1},{2,34},{34,2},{3,35},{35,3},{4,36},{36... | collective-permute-start | bytes 1572872 | tf_op jit(solution)/shard_map/ppermute | solution.py:29
  300.5 23.9 %collective-permute-start.8 = (bf16[256,1024]{1,0:T(8,128)(2,1)S(1)}, bf16[256,1024]{1,0:T(8,128)(2,1)S(1)}, u32[]{:S(2)}, u32[]{:S(2)}) collective-permute-start(bf16[256,1024]{1,0:T(8,128)(2,1)S(1)} %collective-permute-done.7.refs_6_), channel_id=1, source_target_pairs={{0,32},{32,0},{1,33},{33,1},{2,34},{34,2},{3,35},{35,3},{4,36},{36... | collective-permute-start | bytes 1572872 | tf_op jit(solution)/shard_map/ppermute | solution.py:29
  316.8 7.7 %copy-start.11 = (bf16[896,256]{1,0:T(8,128)(2,1)S(1)}, bf16[896,256]{1,0:T(8,128)(2,1)}, u32[]{:S(2)}) copy-start(bf16[896,256]{1,0:T(8,128)(2,1)} %get-tuple-element.22.refs_0_) | copy-start | bytes 1376260
  316.8 7.7 %copy-start.23 = (bf16[896,256]{1,0:T(8,128)(2,1)S(1)}, bf16[896,256]{1,0:T(8,128)(2,1)}, u32[]{:S(2)}) copy-start(bf16[896,256]{1,0:T(8,128)(2,1)} %copy-done.22) | copy-start | bytes 1376260
  316.8 7.7 %copy-start.25 = (bf16[896,256]{1,0:T(8,128)(2,1)S(1)}, bf16[896,256]{1,0:T(8,128)(2,1)}, u32[]{:S(2)}) copy-start(bf16[896,256]{1,0:T(8,128)(2,1)} %copy-done.24) | copy-start | bytes 1376260
  316.8 7.7 %copy-start.27 = (bf16[896,256]{1,0:T(8,128)(2,1)S(1)}, bf16[896,256]{1,0:T(8,128)(2,1)}, u32[]{:S(2)}) copy-start(bf16[896,256]{1,0:T(8,128)(2,1)} %copy-done.26) | copy-start | bytes 1376260
  (4 other events, 2.8 us)

commit v3 on v2

--- a/solution.py
+++ b/solution.py
@@ -10,6 +10,8 @@
 
 SHARDS = ("tensor_0", "tensor_1", "latent")
 BATCH = ("batch_0", "batch_1")
+HALF = ("tensor_0", "latent")
+OTHER_HALF = ("batch_0", "tensor_1")
 
 epsilon = 1e-06
 
@@ -179,33 +181,48 @@
     return call(body, outs, 0, args, in_specs=[WHOLE] * len(args), out_specs=[WHOLE] * len(outs))
 
 
-def forward_kernel(rows_ref, gate_ref, up_ref, down_ref, out_ref, gelu_ref, slope_ref):
-    gate_value = product_t(rows_ref[...], gate_ref[...])
-    up_value = product_t(rows_ref[...], up_ref[...])
+def parts_of(own, near, far):
+    return [own, [near.at[k] for k in range(3)], [far.at[k] for k in range(3)]]
+
+
+def forward_kernel(rows_ref, gate_ref, up_ref, down_ref, near_ref, far_ref, out_ref, *saved):
     root = 0.7978845608028654
     cube = 0.044715
-    square = gate_value * gate_value
-    curve = jnp.tanh(root * gate_value * (1.0 + cube * square))
-    half = 0.5 * (1.0 + curve)
-    gelu_value = gate_value * half
-    rise = 0.5 * gate_value * (1.0 - curve * curve) * root * (1.0 + 3.0 * cube * square)
-    gelu_ref[...] = gelu_value
-    slope_ref[...] = up_value * (half + rise)
-    hidden = (gelu_value * up_value).astype(bf16)
+    rows = rows_ref[...]
+    parts = parts_of([gate_ref, up_ref, down_ref], near_ref, far_ref)
+    hidden = []
+    for (gate, up, _), gelu_ref, slope_ref in zip(parts, saved[0::2], saved[1::2]):
+        gate_value = product_t(rows, gate[...])
+        up_value = product_t(rows, up[...])
+        square = gate_value * gate_value
+        curve = jnp.tanh(root * gate_value * (1.0 + cube * square))
+        half = 0.5 * (1.0 + curve)
+        gelu_value = gate_value * half
+        rise = 0.5 * gate_value * (1.0 - curve * curve) * root * (1.0 + 3.0 * cube * square)
+        gelu_ref[...] = gelu_value
+        slope_ref[...] = up_value * (half + rise)
+        hidden.append((gelu_value * up_value).astype(bf16))
     for at in range(0, out_ref.shape[1], 512):
-        out_ref[:, at : at + 512] = product(hidden, down_ref[:, at : at + 512]).astype(bf16)
-
-
-def backward_kernel(
-    rows_ref, gate_ref, up_ref, down_ref, gelu_ref, slope_ref, out_ref
-):
-    grad_hidden = product_t(rows_ref[...], down_ref[...])
-    grad_gate = (grad_hidden * slope_ref[...]).astype(bf16)
-    grad_up = (grad_hidden * gelu_ref[...]).astype(bf16)
+        span = slice(at, at + 512)
+        terms = [product(h, down[:, span]) for h, (_, _, down) in zip(hidden, parts)]
+        out_ref[:, span] = sum(terms[1:], terms[0]).astype(bf16)
+
+
+def backward_kernel(rows_ref, gate_ref, up_ref, down_ref, near_ref, far_ref, *refs):
+    saved, out_ref = refs[:-1], refs[-1]
+    rows = rows_ref[...]
+    parts = parts_of([gate_ref, up_ref, down_ref], near_ref, far_ref)
+    grads = []
+    for (_, _, down), gelu_ref, slope_ref in zip(parts, saved[0::2], saved[1::2]):
+        grad_hidden = product_t(rows, down[...])
+        grad_gate = (grad_hidden * slope_ref[...]).astype(bf16)
+        grads.append((grad_gate, (grad_hidden * gelu_ref[...]).astype(bf16)))
     for at in range(0, out_ref.shape[1], 512):
-        part = product(grad_gate, gate_ref[:, at : at + 512])
-        part += product(grad_up, up_ref[:, at : at + 512])
-        out_ref[:, at : at + 512] = part.astype(bf16)
+        span = slice(at, at + 512)
+        terms = []
+        for (grad_gate, grad_up), (gate, up, _) in zip(grads, parts):
+            terms += [product(grad_gate, gate[:, span]), product(grad_up, up[:, span])]
+        out_ref[:, span] = sum(terms[1:], terms[0]).astype(bf16)
 
 
 def latent_kernel(rows_ref, weight_ref, latents_ref, out_ref):
@@ -279,13 +296,22 @@
     bias, gain_in, gain_out = (a.reshape(1, width) for a in (decoder_bias, first_gain, second_gain))
     gate, up = gate_weight.T, up_weight.T
     everyone = array((shards, own_tokens, width))
+    half = lax.axis_size(HALF)
+    half_of_them = array((half, own_tokens, width))
     own_rows = array((own_tokens, width), f32)
 
-    def to_owners(partial):
-        return exchange(partial.reshape(shards, own_tokens, -1), SHARDS)
-
-    def all_tokens(pieces):
-        return exchange(pieces, SHARDS).reshape(tokens, width)
+    def to_owners(partial, axes):
+        return exchange(partial.reshape(lax.axis_size(axes), own_tokens, -1), axes)
+
+    def all_tokens(pieces, axes):
+        return exchange(pieces, axes).reshape(-1, width)
+
+    units = gate.shape[0] // 2
+    at = lax.axis_index(BATCH[1]) * units
+    weights = [gate, up, down_weight]
+    sent = jnp.stack([lax.dynamic_slice_in_dim(w, at, units, axis=0) for w in weights])
+    near = swap(sent, OTHER_HALF)
+    far = swap(near, BATCH[1])
 
     bias_share = lax.dynamic_slice_in_dim(decoder_bias.astype(f32), offset, share_width)
     centered_share = (residual.astype(f32) - bias_share).astype(bf16).T
@@ -299,36 +325,37 @@
     partial_recon = decode(latents, decoder_weight, target.T, 128)
     partial_recon, *centered_blocks = lax.optimization_barrier((partial_recon, *centered_blocks))
 
-    pieces = to_owners(partial_recon)
+    pieces = to_owners(partial_recon, SHARDS)
     own_target = pieces[:, :, width : width + share_width]
     own_target = jnp.moveaxis(own_target, 0, 1).reshape(own_tokens, width)
-    pieces, recon = local(recon_kernel, [everyone, own_rows], [pieces, bias, gain_in])
-
-    normed_input = all_tokens(pieces)
+    pieces, recon = local(recon_kernel, [half_of_them, own_rows], [pieces, bias, gain_in])
+
+    normed_input = all_tokens(pieces, HALF)
     latent_blocks = copies_of_all(turned_latents)
-    hidden = array((tokens, gate.shape[0]), f32)
-    partial_out, gelu_value, slope = local(
+    rows = half * own_tokens
+    saved = [array((rows, n), f32) for n in (2 * units, 2 * units, units, units, units, units)]
+    partial_out, *saved = local(
         forward_kernel,
-        [array((tokens, width)), hidden, hidden],
-        [normed_input, gate, up, down_weight],
+        [array((rows, width)), *saved],
+        [normed_input, *weights, near, far],
     )
     partial_out, *latent_blocks = lax.optimization_barrier((partial_out, *latent_blocks))
 
     pieces, grad_result = local(
         functools.partial(output_kernel, token_count),
-        [everyone, own_rows],
-        [to_owners(partial_out), recon, own_target, gain_out],
-    )
-    grad_output = all_tokens(pieces)
+        [half_of_them, own_rows],
+        [to_owners(partial_out, HALF), recon, own_target, gain_out],
+    )
+    grad_output = all_tokens(pieces, HALF)
     (partial_input,) = local(
         backward_kernel,
-        [array((tokens, width))],
-        [grad_output, gate, up, down_weight, gelu_value, slope],
+        [array((rows, width))],
+        [grad_output, *weights, near, far, *saved],
     )
     (pieces,) = local(
-        input_kernel, [everyone], [to_owners(partial_input), recon, grad_result, gain_in]
-    )
-    grad_recon = all_tokens(pieces)
+        input_kernel, [everyone], [to_owners(partial_input, HALF), recon, grad_result, gain_in]
+    )
+    grad_recon = all_tokens(pieces, SHARDS)
 
     recon_blocks = blocks_of_all(
         lambda b: lax.dynamic_slice_in_dim(grad_recon, b * block, block, axis=1)

time: 332 us -> 281 us (0.85)
  waiting for transfers between devices: 142 us -> 111 us
  blocking collectives: 90.7 us -> 62.5 us
  Pallas kernels: 32.7 us -> 39.8 us
    all_to_all x4, waiting for transfers between devices: 79.3 us -> 39.6 us  [exchange(): return lax.all_to_all(pieces, axes, split_axis=0, concat_axis=0, tiled=True)]
    all_to_all x3, blocking collectives: 90.7 us -> 62.5 us  [exchange(): return lax.all_to_all(pieces, axes, split_axis=0, concat_axis=0, tiled=True)]
    ppermute x12 -> x14, waiting for transfers between devices: 63.1 us -> 71.8 us  [swap(): lax.ppermute(block, axes, [(i, for_all - 1 - i) for i in range(for_all)])]
    pallas_call x10, Pallas kernels: 32.7 us -> 39.8 us  [call(): pl.pallas_call(body, out_shape=outs, cost_estimate=cost, compiler_params=...]
    unnamed x72 -> x76, local copies, waits for them, and re-layouts: 15 us -> 13.3 us
    ppermute x12 -> x14, starting transfers between devices: 8.57 us -> 8.08 us  [swap(): lax.ppermute(block, axes, [(i, for_all - 1 - i) for i in range(for_all)])]
  transfers between devices with their start and end apart: 16 -> 18, of which waited for: 8 -> 9; matrix products, arithmetic and copies ran while one was open for 0% -> 3% of each run, Pallas kernels for 6% -> 9%
where the time goes in v3:
time: 281 us; the launch traced here: 278 us
  waiting for transfers between devices  111 us (40%)
  blocking collectives  62.5 us (22%)
  Pallas kernels  39.8 us (14%)
  starting transfers between devices  39.2 us (14%)
  local copies, waits for them, and re-layouts  20.9 us (7%)
  other arithmetic  3.35 us (1%)
    ppermute x14, waiting for transfers between devices, swap(): lax.ppermute(block, axes, [(i, for_all - 1 - i) for i in range(for_all)])  71.8 us
    all_to_all x3, blocking collectives, exchange(): return lax.all_to_all(pieces, axes, split_axis=0, concat_axis=0, tiled=True)  62.5 us
    pallas_call x10, Pallas kernels, call(): pl.pallas_call(body, out_shape=outs, cost_estimate=cost, compiler_params=...  39.8 us
    all_to_all x4, waiting for transfers between devices, exchange(): return lax.all_to_all(pieces, axes, split_axis=0, concat_axis=0, tiled=True)  39.6 us
    all_to_all x4, starting transfers between devices, exchange(): return lax.all_to_all(pieces, axes, split_axis=0, concat_axis=0, tiled=True)  31.1 us
    unnamed x76, local copies, waits for them, and re-layouts  13.3 us
    ppermute x14, starting transfers between devices, swap(): lax.ppermute(block, axes, [(i, for_all - 1 - i) for i in range(for_all)])  8.08 us
  transfers between devices with their start and end apart: 18, of which 9 were waited for; matrix products, arithmetic and copies ran while one was open for 3% of the time, Pallas kernels for 9%

profile of v3, /device:TPU:14, one launch (start us, length us, event | category | flops | bytes accessed | tf_op | source)
XLA Modules:
  0.0 278.2 jit_solution(3803168888906858778)
XLA Ops:
  0.6 0.8 dynamic-slice_convert_fusion
  1.4 0.9 fusion
  2.3 1.3 broadcast_in_dim.4
  3.7 10.5 %all-to-all-start = ((bf16[32,112,256]{2,1,0:T(8,128)(2,1)}), bf16[32,112,256]{2,1,0:T(8,128)(2,1)}, u32[]{:S(2)}, u32[]{:S(2)}) async-start(bf16[32,112,256]{2,1,0:T(8,128)(2,1)} %broadcast_in_dim.4), calls=%async_computation | async-start | bytes 3670016 | tf_op jit(solution)/shard_map/all_to_all | solution.py:26
  14.2 1.2 dynamic-slice_bitcast_fusion
  15.5 1.7 pad_maximum_fusion
  17.2 2.3 collective-permute-start.3
  19.5 19.2 %all-to-all-done = bf16[32,112,256]{2,1,0:T(8,128)(2,1)} async-done(((bf16[32,112,256]{2,1,0:T(8,128)(2,1)}), bf16[32,112,256]{2,1,0:T(8,128)(2,1)}, u32[]{:S(2)}, u32[]{:S(2)}) %all-to-all-start) | async-done | bytes 1835040 | tf_op jit(solution)/shard_map/all_to_all | solution.py:26
  38.7 2.3 constant_dynamic-slice_fusion.4
  41.0 1.0 collective-permute-start.1
  42.0 0.9 collective-permute-start
  42.9 3.1 %copy-done.7 = bf16[3584,1024]{1,0:T(8,128)(2,1)S(1)} copy-done((bf16[3584,1024]{1,0:T(8,128)(2,1)S(1)}, bf16[3584,1024]{1,0:T(8,128)(2,1)}, u32[]{:S(2)}) %copy-start.7) | copy-done | bytes 7340056
  46.0 6.4 %shard_map.122 = (bf16[256,1024]{1,0:T(8,128)(2,1)S(1)}, bf16[1024,256]{1,0:T(8,128)(2,1)}) custom-call(bf16[3584,256]{1,0:T(8,128)(2,1)} %bitcast.1.centered_ref, bf16[3584,1024]{1,0:T(8,128)(2,1)S(1)} %copy-done.7, bf16[1,1024]{1,0:T(2,128)(2,1)S(1)} %reshape.42.bias_ref), custom_call_target="tpu_custom_call" | custom-call | flops 1879048192 | bytes 10225664 | tf_op jit(solution)/shard_map/pallas_call | solution.py:49
  52.5 3.7 %shard_map.123 = bf16[256,3712]{1,0:T(8,128)(2,1)S(1)} custom-call(bf16[256,1024]{1,0:T(8,128)(2,1)S(1)} %get-tuple-element.25.latents_ref, bf16[1024,3584]{1,0:T(8,128)(2,1)S(1)} %bitcast.25, bf16[112,256]{1,0:T(8,128)(2,1)S(1)} %bitcast.38), custom_call_target="tpu_custom_call" | custom-call | flops 1879048192 | bytes 9822208 | tf_op jit(solution)/shard_map/pallas_call | solution.py:49
  56.2 1.3 copy-done.6
  57.5 0.8 copy-done.24
  58.3 4.5 %collective-permute-done.1.refs_2_ = bf16[896,256]{1,0:T(8,128)(2,1)S(1)} collective-permute-done((bf16[896,256]{1,0:T(8,128)(2,1)S(1)}, bf16[896,256]{1,0:T(8,128)(2,1)S(1)}, u32[]{:S(2)}, u32[]{:S(2)}) %collective-permute-start.1) | collective-permute-done | bytes 458784 | tf_op jit(solution)/shard_map/ppermute | solution.py:31
  62.8 0.8 copy-done.26
  63.6 0.8 copy-done.28
  64.4 7.1 %all-to-all-start.1 = ((bf16[32,8,3712]{2,1,0:T(8,128)(2,1)}), bf16[32,8,3712]{2,1,0:T(8,128)(2,1)}, u32[]{:S(2)}, u32[]{:S(2)}) async-start(bf16[32,8,3712]{2,1,0:T(8,128)(2,1)} %bitcast.34), calls=%async_computation.1 | async-start | bytes 3801088 | tf_op jit(solution)/shard_map/all_to_all | solution.py:26
  71.5 38.1 %collective-permute-done.3.near_ref = bf16[3,112,3584]{2,1,0:T(8,128)(2,1)} collective-permute-done((bf16[3,112,3584]{2,1,0:T(8,128)(2,1)}, bf16[3,112,3584]{2,1,0:T(8,128)(2,1)}, u32[]{:S(2)}, u32[]{:S(2)}) %collective-permute-start.3) | collective-permute-done | bytes 2408480 | tf_op jit(solution)/shard_map/ppermute | solution.py:31
  109.6 1.2 collective-permute-start.6
  110.9 2.1 shard_map.124
  113.0 0.9 copy-done.11
  113.9 6.8 %all-to-all-start.2 = ((bf16[16,8,3584]{2,1,0:T(8,128)(2,1)}), bf16[16,8,3584]{2,1,0:T(8,128)(2,1)}, u32[]{:S(2)}, u32[]{:S(2)}) async-start(bf16[16,8,3584]{2,1,0:T(8,128)(2,1)} %copy-done.11), calls=%async_computation.2 | async-start | bytes 1835008 | tf_op jit(solution)/shard_map/all_to_all | solution.py:26
  120.8 3.5 %collective-permute-done.6.refs_2_ = bf16[1024,256]{1,0:T(8,128)(2,1)} collective-permute-done((bf16[1024,256]{1,0:T(8,128)(2,1)}, bf16[1024,256]{1,0:T(8,128)(2,1)}, u32[]{:S(2)}, u32[]{:S(2)}) %collective-permute-start.6) | collective-permute-done | bytes 524320 | tf_op jit(solution)/shard_map/ppermute | solution.py:31
  124.3 10.8 %all-to-all-done.2 = bf16[16,8,3584]{2,1,0:T(8,128)(2,1)} async-done(((bf16[16,8,3584]{2,1,0:T(8,128)(2,1)}), bf16[16,8,3584]{2,1,0:T(8,128)(2,1)}, u32[]{:S(2)}, u32[]{:S(2)}) %all-to-all-start.2) | async-done | bytes 917536 | tf_op jit(solution)/shard_map/all_to_all | solution.py:26
  135.0 1.4 copy-done.4
  136.4 5.6 %shard_map.125 = (bf16[128,3584]{1,0:T(8,128)(2,1)S(1)}, f32[128,224]{1,0:T(8,128)S(1)}, f32[128,224]{1,0:T(8,128)S(1)}, f32[128,112]{1,0:T(8,128)S(1)}, f32[128...) custom-call(bf16[128,3584]{1,0:T(8,128)(2,1)} %bitcast.4.rows_ref, ...), custom_call_target="tpu_custom_call" | custom-call | bytes 11927552 | tf_op jit(solution)/shard_map/pallas_call | solution.py:49
  142.1 0.9 copy-done.10
  143.0 0.7 copy-done.13
  146.2 6.7 %all-to-all-start.3 = ((bf16[16,8,3584]{2,1,0:T(8,128)(2,1)}), bf16[16,8,3584]{2,1,0:T(8,128)(2,1)}, u32[]{:S(2)}, u32[]{:S(2)}) async-start(bf16[16,8,3584]{2,1,0:T(8,128)(2,1)} %bitcast.37), calls=%async_computation.3 | async-start | bytes 1835008 | tf_op jit(solution)/shard_map/all_to_all | solution.py:26
  152.8 0.8 slice_bitcast_fusion
  153.7 0.6 copy.13
  154.3 1.0 reshape.48.target_ref
  155.3 9.6 %all-to-all-done.3.pieces_ref = bf16[16,8,3584]{2,1,0:T(8,128)(2,1)} async-done(((bf16[16,8,3584]{2,1,0:T(8,128)(2,1)}), bf16[16,8,3584]{2,1,0:T(8,128)(2,1)}, u32[]{:S(2)}, u32[]{:S(2)}) %all-to-all-start.3) | async-done | bytes 917536 | tf_op jit(solution)/shard_map/all_to_all | solution.py:26
  165.0 1.7 shard_map.126
  166.7 17.7 %all_to_all.35 = bf16[16,8,3584]{2,1,0:T(8,128)(2,1)S(1)} all-to-all(bf16[16,8,3584]{2,1,0:T(8,128)(2,1)S(1)} %get-tuple-element.36), channel_id=1, replica_groups=mesh['batch_0'=2,'batch_1'=2,'tensor_0'=4,'tensor_1'=2,'latent'=4] {'ten..., dimensions={0} | all-to-all | bytes 1835008 | tf_op jit(solution)/shard_map/all_to_all | solution.py:26
  184.6 5.3 %shard_map.127 = bf16[128,3584]{1,0:T(8,128)(2,1)S(1)} custom-call(bf16[128,3584]{1,0:T(8,128)(2,1)S(1)} %bitcast.35, bf16[224,3584]{1,0:T(8,128)(2,1)S(1)} %bitcast.31, bf16[224,3584]{1,0:T(8,128)(2,1)S(1)} %bitcast.33, bf16[224,3584]{1,0:T(8,128)(2,1)S(1)} %copy-done.5, bf16[3,112,3584]{2,1,0:T(8,128)(2,1)} %collective-permute-done.3.near_ref, ...), custom_call_target="tpu_custom_call" | custom-call | bytes 11927552 | tf_op jit(solution)/shard_map/pallas_call | solution.py:49
  189.9 16.3 %all_to_all.36.pieces_ref = bf16[16,8,3584]{2,1,0:T(8,128)(2,1)S(1)} all-to-all(bf16[16,8,3584]{2,1,0:T(8,128)(2,1)S(1)} %bitcast.36), channel_id=1, replica_groups=mesh['batch_0'=2,'batch_1'=2,'tensor_0'=4,'tensor_1'=2,'latent'=4] {'ten..., dimensions={0} | all-to-all | bytes 1835008 | tf_op jit(solution)/shard_map/all_to_all | solution.py:26
  206.6 28.5 %all_to_all.37 = bf16[32,8,3584]{2,1,0:T(8,128)(2,1)S(1)} all-to-all(bf16[32,8,3584]{2,1,0:T(8,128)(2,1)S(1)} %shard_map.128), channel_id=1, replica_groups=mesh['batch_0'=2,'batch_1'=2,'tensor_0'=4,'tensor_1'=2,'latent'=4] {'ten..., dimensions={0} | all-to-all | bytes 3670016 | tf_op jit(solution)/shard_map/all_to_all | solution.py:26
  235.1 2.9 %shard_map.129.refs_4_ = bf16[256,1024]{1,0:T(8,128)(2,1)S(1)} custom-call(bf16[256,3584]{1,0:T(8,128)(2,1)S(1)} %bitcast.28, bf16[1024,3584]{1,0:T(8,128)(2,1)S(1)} %bitcast.27, bf16[256,1024]{1,0:T(8,128)(2,1)S(1)} %copy-done.9), custom_call_target="tpu_custom_call" | custom-call | flops 1879048192 | bytes 10223616 | tf_op jit(solution)/shard_map/pallas_call | solution.py:49
  238.4 2.1 collective-permute-start.12
  240.9 11.9 %collective-permute-done.9.refs_6_ = bf16[256,1024]{1,0:T(8,128)(2,1)S(1)} collective-permute-done((bf16[256,1024]{1,0:T(8,128)(2,1)S(1)}, bf16[256,1024]{1,0:T(8,128)(2,1)S(1)}, u32[]{:S(2)}, u32[]{:S(2)}) %collective-permute-start.9) | collective-permute-done | bytes 524320 | tf_op jit(solution)/shard_map/ppermute | solution.py:31
  252.9 5.6 %collective-permute-done.13.refs_7_ = bf16[256,896]{1,0:T(8,128)(2,1)S(1)} collective-permute-done((bf16[256,896]{1,0:T(8,128)(2,1)S(1)}, bf16[256,896]{1,0:T(8,128)(2,1)S(1)}, u32[]{:S(2)}, u32[]{:S(2)}) %collective-permute-start.13) | collective-permute-done | bytes 458784 | tf_op jit(solution)/shard_map/ppermute | solution.py:31
  258.5 8.1 %collective-permute-done.12.refs_6_ = bf16[256,896]{1,0:T(8,128)(2,1)S(1)} collective-permute-done((bf16[256,896]{1,0:T(8,128)(2,1)S(1)}, bf16[256,896]{1,0:T(8,128)(2,1)S(1)}, u32[]{:S(2)}, u32[]{:S(2)}) %collective-permute-start.12) | collective-permute-done | bytes 458784 | tf_op jit(solution)/shard_map/ppermute | solution.py:31
  266.6 7.8 %shard_map.131 = bf16[1024,896]{1,0:T(8,128)(2,1)} custom-call(bf16[1024,256]{1,0:T(8,128)(2,1)} %get-tuple-element.44.refs_0_, bf16[1024,256]{1,0:T(8,128)(2,1)} %collective-permute-done.5.refs_1_, bf16[1024,256]{1,0:T(8,128)(2,1)} %collective-permute-done.6.refs_2_, bf16[1024,256]{1,0:T(8,128)(2,1)} %collective-permute-done.7.refs_3_, ...), custom_call_target="tpu_custom_call" | custom-call | flops 1879048192 | bytes 5767168 | tf_op jit(solution)/shard_map/pallas_call | solution.py:49
  274.5 3.7 %shard_map.130 = bf16[896,1024]{1,0:T(8,128)(2,1)} custom-call(bf16[896,256]{1,0:T(8,128)(2,1)S(1)} %copy-done.12, bf16[896,256]{1,0:T(8,128)(2,1)S(1)} %copy-done.29, bf16[896,256]{1,0:T(8,128)(2,1)S(1)} %copy-done.27, bf16[896,256]{1,0:T(8,128)(2,1)S(1)} %copy-done.25, bf16[256,1024]{1,0:T(8,128)(2,1)S(1)} %shard_map.129.refs_4_, ...), custom_call_target="tpu_custom_call" | custom-call | flops 1879048192 | bytes 5767168 | tf_op jit(solution)/shard_map/pallas_call | solution.py:49
  (94 shorter events, 4.0 us)
Async XLA Ops:
  3.7 11.7 %copy-start = (bf16[3584,224]{0,1:T(8,128)(2,1)S(1)}, bf16[3584,224]{0,1:T(8,128)(2,1)}, u32[]{:S(2)}) copy-start(bf16[3584,224]{0,1:T(8,128)(2,1)} %param.19) | copy-start | bytes 4816900
  3.7 11.7 %copy-start.2 = (bf16[3584,224]{0,1:T(8,128)(2,1)S(1)}, bf16[3584,224]{0,1:T(8,128)(2,1)}, u32[]{:S(2)}) copy-start(bf16[3584,224]{0,1:T(8,128)(2,1)} %param.20) | copy-start | bytes 4816900
  3.7 35.0 %all-to-all-start = ((bf16[32,112,256]{2,1,0:T(8,128)(2,1)}), bf16[32,112,256]{2,1,0:T(8,128)(2,1)}, u32[]{:S(2)}, u32[]{:S(2)}) async-start(bf16[32,112,256]{2,1,0:T(8,128)(2,1)} %broadcast_in_dim.4), calls=%async_computation | async-start | bytes 3670016 | tf_op jit(solution)/shard_map/all_to_all | solution.py:26
  15.5 36.9 %slice-start = ((s8[7340032]{0:T(1024)(128)(4,1)}), s8[3145728]{0:T(1024)(128)(4,1)S(1)}, s32[]{:S(2)}) async-start(s8[7340032]{0:T(1024)(128)(4,1)} %bitcast.24), calls=%async_computation.7 | async-start | bytes 6291456
  17.2 92.4 %collective-permute-start.3 = (bf16[3,112,3584]{2,1,0:T(8,128)(2,1)}, bf16[3,112,3584]{2,1,0:T(8,128)(2,1)}, u32[]{:S(2)}, u32[]{:S(2)}) collective-permute-start(bf16[3,112,3584]{2,1,0:T(8,128)(2,1)} %pad_maximum_fusion), channel_id=1, source_target_pairs={{0,68},{4,64},{64,4},{68,0},{1,69},{5,65},{65,5},{69,1},{2,70},{6,... | collective-permute-start | bytes 7225352 | tf_op jit(solution)/shard_map/ppermute | solution.py:31
  38.7 4.2 %copy-start.33 = (bf16[1024]{0:T(1024)(128)(2,1)S(1)}, bf16[1024]{0:T(1024)(128)(2,1)}, u32[]{:S(2)}) copy-start(bf16[1024]{0:T(1024)(128)(2,1)} %param.14) | copy-start | bytes 6148
  41.0 16.5 %collective-permute-start.2 = (bf16[896,256]{1,0:T(8,128)(2,1)S(1)}, bf16[896,256]{1,0:T(8,128)(2,1)S(1)}, u32[]{:S(2)}, u32[]{:S(2)}) collective-permute-start(bf16[896,256]{1,0:T(8,128)(2,1)S(1)} %get-tuple-element.52), channel_id=1, source_target_pairs={{0,96},{32,64},{64,32},{96,0},{1,97},{33,65},{65,33},{97,1},{2,98}... | collective-permute-start | bytes 1376264 | tf_op jit(solution)/shard_map/ppermute | solution.py:31
  41.0 21.7 %collective-permute-start.1 = (bf16[896,256]{1,0:T(8,128)(2,1)S(1)}, bf16[896,256]{1,0:T(8,128)(2,1)S(1)}, u32[]{:S(2)}, u32[]{:S(2)}) collective-permute-start(bf16[896,256]{1,0:T(8,128)(2,1)S(1)} %get-tuple-element.53), channel_id=1, source_target_pairs={{0,64},{64,0},{1,65},{65,1},{2,66},{66,2},{3,67},{67,3},{4,68},{68... | collective-permute-start | bytes 1376264 | tf_op jit(solution)/shard_map/ppermute | solution.py:31
  42.0 21.5 %collective-permute-start = (bf16[896,256]{1,0:T(8,128)(2,1)S(1)}, bf16[896,256]{1,0:T(8,128)(2,1)S(1)}, u32[]{:S(2)}, u32[]{:S(2)}) collective-permute-start(bf16[896,256]{1,0:T(8,128)(2,1)S(1)} %get-tuple-element.54), channel_id=1, source_target_pairs={{0,32},{32,0},{1,33},{33,1},{2,34},{34,2},{3,35},{35,3},{4,36},{36... | collective-permute-start | bytes 1376264 | tf_op jit(solution)/shard_map/ppermute | solution.py:31
  42.9 3.1 %copy-start.7 = (bf16[3584,1024]{1,0:T(8,128)(2,1)S(1)}, bf16[3584,1024]{1,0:T(8,128)(2,1)}, u32[]{:S(2)}) copy-start(bf16[3584,1024]{1,0:T(8,128)(2,1)} %weight_ref.3) | copy-start | bytes 22020100
  46.0 6.4 %slice-start.1 = ((s8[7340032]{0:T(1024)(128)(4,1)}), s8[4194304]{0:T(1024)(128)(4,1)S(1)}, s32[]{:S(2)}) async-start(s8[7340032]{0:T(1024)(128)(4,1)} %bitcast.24), calls=%async_computation.8 | async-start | bytes 8388608
  46.0 6.5 %copy-start.23 = (bf16[256,112]{0,1:T(8,128)(2,1)S(1)}, bf16[256,112]{0,1:T(8,128)(2,1)}, u32[]{:S(2)}) copy-start(bf16[256,112]{0,1:T(8,128)(2,1)} %param.12) | copy-start | bytes 172036
  52.4 3.7 %copy-start.8 = (bf16[256,1024]{1,0:T(8,128)(2,1)}, bf16[256,1024]{1,0:T(8,128)(2,1)S(1)}, u32[]{:S(2)}) copy-start(bf16[256,1024]{1,0:T(8,128)(2,1)S(1)} %get-tuple-element.25.latents_ref) | copy-start | bytes 1572868
  56.1 1.4 copy-start.6
  64.3 46.4 %copy-start.30 = (bf16[3584]{0:T(1024)(128)(2,1)S(1)}, bf16[3584]{0:T(1024)(128)(2,1)}, u32[]{:S(2)}) copy-start(bf16[3584]{0:T(1024)(128)(2,1)} %param.16) | copy-start | bytes 21508
  64.3 46.4 %copy-start.31 = (bf16[3584]{0:T(1024)(128)(2,1)S(1)}, bf16[3584]{0:T(1024)(128)(2,1)}, u32[]{:S(2)}) copy-start(bf16[3584]{0:T(1024)(128)(2,1)} %param.17) | copy-start | bytes 21508
  64.4 46.5 %all-to-all-start.1 = ((bf16[32,8,3712]{2,1,0:T(8,128)(2,1)}), bf16[32,8,3712]{2,1,0:T(8,128)(2,1)}, u32[]{:S(2)}, u32[]{:S(2)}) async-start(bf16[32,8,3712]{2,1,0:T(8,128)(2,1)} %bitcast.34), calls=%async_computation.1 | async-start | bytes 3801088 | tf_op jit(solution)/shard_map/all_to_all | solution.py:26
  109.6 14.7 %collective-permute-start.4 = (bf16[3,112,3584]{2,1,0:T(8,128)(2,1)}, bf16[3,112,3584]{2,1,0:T(8,128)(2,1)}, u32[]{:S(2)}, u32[]{:S(2)}) collective-permute-start(bf16[3,112,3584]{2,1,0:T(8,128)(2,1)} %collective-permute-done.3.near_ref), channel_id=1, source_target_pairs={{0,32},{32,0},{1,33},{33,1},{2,34},{34,2},{3,35},{35,3},{4,36},{36... | collective-permute-start | bytes 7225352 | tf_op jit(solution)/shard_map/ppermute | solution.py:31
  109.6 14.7 %collective-permute-start.6 = (bf16[1024,256]{1,0:T(8,128)(2,1)}, bf16[1024,256]{1,0:T(8,128)(2,1)}, u32[]{:S(2)}, u32[]{:S(2)}) collective-permute-start(bf16[1024,256]{1,0:T(8,128)(2,1)} %get-tuple-element.44.refs_0_), channel_id=1, source_target_pairs={{0,64},{64,0},{1,65},{65,1},{2,66},{66,2},{3,67},{67,3},{4,68},{68... | collective-permute-start | bytes 1572872 | tf_op jit(solution)/shard_map/ppermute | solution.py:31
  110.8 24.2 %copy-start.1 = (bf16[3584,224]{0,1:T(8,128)(2,1)S(1)}, bf16[3584,224]{0,1:T(8,128)(2,1)}, u32[]{:S(2)}) copy-start(bf16[3584,224]{0,1:T(8,128)(2,1)} %param.19) | copy-start | bytes 4816900
  110.8 24.2 %copy-start.3 = (bf16[3584,224]{0,1:T(8,128)(2,1)S(1)}, bf16[3584,224]{0,1:T(8,128)(2,1)}, u32[]{:S(2)}) copy-start(bf16[3584,224]{0,1:T(8,128)(2,1)} %param.20) | copy-start | bytes 4816900
  113.0 0.9 copy-start.11
  113.9 21.1 %all-to-all-start.2 = ((bf16[16,8,3584]{2,1,0:T(8,128)(2,1)}), bf16[16,8,3584]{2,1,0:T(8,128)(2,1)}, u32[]{:S(2)}, u32[]{:S(2)}) async-start(bf16[16,8,3584]{2,1,0:T(8,128)(2,1)} %copy-done.11), calls=%async_computation.2 | async-start | bytes 1835008 | tf_op jit(solution)/shard_map/all_to_all | solution.py:26
  120.7 25.4 %collective-permute-start.5 = (bf16[1024,256]{1,0:T(8,128)(2,1)}, bf16[1024,256]{1,0:T(8,128)(2,1)}, u32[]{:S(2)}, u32[]{:S(2)}) collective-permute-start(bf16[1024,256]{1,0:T(8,128)(2,1)} %get-tuple-element.44.refs_0_), channel_id=1, source_target_pairs={{0,32},{32,0},{1,33},{33,1},{2,34},{34,2},{3,35},{35,3},{4,36},{36... | collective-permute-start | bytes 1572872 | tf_op jit(solution)/shard_map/ppermute | solution.py:31
  124.2 21.9 %collective-permute-start.7 = (bf16[1024,256]{1,0:T(8,128)(2,1)}, bf16[1024,256]{1,0:T(8,128)(2,1)}, u32[]{:S(2)}, u32[]{:S(2)}) collective-permute-start(bf16[1024,256]{1,0:T(8,128)(2,1)} %collective-permute-done.6.refs_2_), channel_id=1, source_target_pairs={{0,32},{32,0},{1,33},{33,1},{2,34},{34,2},{3,35},{35,3},{4,36},{36... | collective-permute-start | bytes 1572872 | tf_op jit(solution)/shard_map/ppermute | solution.py:31
  135.0 1.4 copy-start.4
  142.1 0.9 copy-start.10
  146.2 6.7 %copy-start.32 = (bf16[3584]{0:T(1024)(128)(2,1)S(1)}, bf16[3584]{0:T(1024)(128)(2,1)}, u32[]{:S(2)}) copy-start(bf16[3584]{0:T(1024)(128)(2,1)} %param.18) | copy-start | bytes 21508
  146.2 18.8 %all-to-all-start.3 = ((bf16[16,8,3584]{2,1,0:T(8,128)(2,1)}), bf16[16,8,3584]{2,1,0:T(8,128)(2,1)}, u32[]{:S(2)}, u32[]{:S(2)}) async-start(bf16[16,8,3584]{2,1,0:T(8,128)(2,1)} %bitcast.37), calls=%async_computation.3 | async-start | bytes 1835008 | tf_op jit(solution)/shard_map/all_to_all | solution.py:26
  164.9 19.6 %copy-start.5 = (bf16[224,3584]{1,0:T(8,128)(2,1)S(1)}, bf16[224,3584]{1,0:T(8,128)(2,1)}, u32[]{:S(2)}) copy-start(bf16[224,3584]{1,0:T(8,128)(2,1)} %down_ref.3) | copy-start | bytes 4816900
  165.0 19.6 %copy-start.14 = (f32[128,224]{1,0:T(8,128)S(1)}, f32[128,224]{1,0:T(8,128)}, u32[]{:S(2)}) copy-start(f32[128,224]{1,0:T(8,128)} %copy-done.13) | copy-start | bytes 344068
  165.0 19.6 %copy-start.16 = (f32[128,112]{1,0:T(8,128)S(1)}, f32[128,112]{1,0:T(8,128)}, u32[]{:S(2)}) copy-start(f32[128,112]{1,0:T(8,128)} %copy-done.15) | copy-start | bytes 172036
  165.0 19.6 %copy-start.18 = (f32[128,112]{1,0:T(8,128)S(1)}, f32[128,112]{1,0:T(8,128)}, u32[]{:S(2)}) copy-start(f32[128,112]{1,0:T(8,128)} %copy-done.17) | copy-start | bytes 172036
  165.0 19.6 %copy-start.20 = (f32[128,112]{1,0:T(8,128)S(1)}, f32[128,112]{1,0:T(8,128)}, u32[]{:S(2)}) copy-start(f32[128,112]{1,0:T(8,128)} %copy-done.19) | copy-start | bytes 172036
  165.0 19.6 %copy-start.22 = (f32[128,112]{1,0:T(8,128)S(1)}, f32[128,112]{1,0:T(8,128)}, u32[]{:S(2)}) copy-start(f32[128,112]{1,0:T(8,128)} %copy-done.21) | copy-start | bytes 172036
  166.7 68.4 %slice-start.2 = ((s8[7340032]{0:T(1024)(128)(4,1)}), s8[4194304]{0:T(1024)(128)(4,1)S(1)}, s32[]{:S(2)}) async-start(s8[7340032]{0:T(1024)(128)(4,1)} %bitcast.26), calls=%async_computation.9 | async-start | bytes 8388608
  184.5 50.6 %slice-start.3 = ((s8[7340032]{0:T(1024)(128)(4,1)}), s8[3145728]{0:T(1024)(128)(4,1)S(1)}, s32[]{:S(2)}) async-start(s8[7340032]{0:T(1024)(128)(4,1)} %bitcast.26), calls=%async_computation.10 | async-start | bytes 6291456
  206.6 28.5 %copy-start.9 = (bf16[256,1024]{1,0:T(8,128)(2,1)S(1)}, bf16[256,1024]{1,0:T(8,128)(2,1)}, u32[]{:S(2)}) copy-start(bf16[256,1024]{1,0:T(8,128)(2,1)} %copy-done.8) | copy-start | bytes 1572868
  238.0 14.9 %collective-permute-start.9 = (bf16[256,1024]{1,0:T(8,128)(2,1)S(1)}, bf16[256,1024]{1,0:T(8,128)(2,1)S(1)}, u32[]{:S(2)}, u32[]{:S(2)}) collective-permute-start(bf16[256,1024]{1,0:T(8,128)(2,1)S(1)} %shard_map.129.refs_4_), channel_id=1, source_target_pairs={{0,64},{64,0},{1,65},{65,1},{2,66},{66,2},{3,67},{67,3},{4,68},{68... | collective-permute-start | bytes 1572872 | tf_op jit(solution)/shard_map/ppermute | solution.py:31
  238.3 20.2 %collective-permute-start.13 = (bf16[256,896]{1,0:T(8,128)(2,1)S(1)}, bf16[256,896]{1,0:T(8,128)(2,1)S(1)}, u32[]{:S(2)}, u32[]{:S(2)}) collective-permute-start(bf16[256,896]{1,0:T(8,128)(2,1)S(1)} %get-tuple-element.48), channel_id=1, source_target_pairs={{0,96},{32,64},{64,32},{96,0},{1,97},{33,65},{65,33},{97,1},{2,98}... | collective-permute-start | bytes 1376264 | tf_op jit(solution)/shard_map/ppermute | solution.py:31
  238.4 28.3 %collective-permute-start.12 = (bf16[256,896]{1,0:T(8,128)(2,1)S(1)}, bf16[256,896]{1,0:T(8,128)(2,1)S(1)}, u32[]{:S(2)}, u32[]{:S(2)}) collective-permute-start(bf16[256,896]{1,0:T(8,128)(2,1)S(1)} %get-tuple-element.49), channel_id=1, source_target_pairs={{0,64},{64,0},{1,65},{65,1},{2,66},{66,2},{3,67},{67,3},{4,68},{68... | collective-permute-start | bytes 1376264 | tf_op jit(solution)/shard_map/ppermute | solution.py:31
  240.4 26.2 %collective-permute-start.11 = (bf16[256,896]{1,0:T(8,128)(2,1)S(1)}, bf16[256,896]{1,0:T(8,128)(2,1)S(1)}, u32[]{:S(2)}, u32[]{:S(2)}) collective-permute-start(bf16[256,896]{1,0:T(8,128)(2,1)S(1)} %get-tuple-element.50), channel_id=1, source_target_pairs={{0,32},{32,0},{1,33},{33,1},{2,34},{34,2},{3,35},{35,3},{4,36},{36... | collective-permute-start | bytes 1376264 | tf_op jit(solution)/shard_map/ppermute | solution.py:31
  240.5 34.0 %collective-permute-start.8 = (bf16[256,1024]{1,0:T(8,128)(2,1)S(1)}, bf16[256,1024]{1,0:T(8,128)(2,1)S(1)}, u32[]{:S(2)}, u32[]{:S(2)}) collective-permute-start(bf16[256,1024]{1,0:T(8,128)(2,1)S(1)} %shard_map.129.refs_4_), channel_id=1, source_target_pairs={{0,32},{32,0},{1,33},{33,1},{2,34},{34,2},{3,35},{35,3},{4,36},{36... | collective-permute-start | bytes 1572872 | tf_op jit(solution)/shard_map/ppermute | solution.py:31
  252.9 21.6 %collective-permute-start.10 = (bf16[256,1024]{1,0:T(8,128)(2,1)S(1)}, bf16[256,1024]{1,0:T(8,128)(2,1)S(1)}, u32[]{:S(2)}, u32[]{:S(2)}) collective-permute-start(bf16[256,1024]{1,0:T(8,128)(2,1)S(1)} %collective-permute-done.9.refs_6_), channel_id=1, source_target_pairs={{0,32},{32,0},{1,33},{33,1},{2,34},{34,2},{3,35},{35,3},{4,36},{36... | collective-permute-start | bytes 1572872 | tf_op jit(solution)/shard_map/ppermute | solution.py:31
  266.6 7.8 %copy-start.12 = (bf16[896,256]{1,0:T(8,128)(2,1)S(1)}, bf16[896,256]{1,0:T(8,128)(2,1)}, u32[]{:S(2)}) copy-start(bf16[896,256]{1,0:T(8,128)(2,1)} %get-tuple-element.26.refs_0_) | copy-start | bytes 1376260
  266.6 7.8 %copy-start.25 = (bf16[896,256]{1,0:T(8,128)(2,1)S(1)}, bf16[896,256]{1,0:T(8,128)(2,1)}, u32[]{:S(2)}) copy-start(bf16[896,256]{1,0:T(8,128)(2,1)} %copy-done.24) | copy-start | bytes 1376260
  266.6 7.8 %copy-start.27 = (bf16[896,256]{1,0:T(8,128)(2,1)S(1)}, bf16[896,256]{1,0:T(8,128)(2,1)}, u32[]{:S(2)}) copy-start(bf16[896,256]{1,0:T(8,128)(2,1)} %copy-done.26) | copy-start | bytes 1376260
  266.6 7.9 %copy-start.29 = (bf16[896,256]{1,0:T(8,128)(2,1)S(1)}, bf16[896,256]{1,0:T(8,128)(2,1)}, u32[]{:S(2)}) copy-start(bf16[896,256]{1,0:T(8,128)(2,1)} %copy-done.28) | copy-start | bytes 1376260
  (8 other events, 5.5 us)

commit v4 on v3

--- a/solution.py
+++ b/solution.py
@@ -19,7 +19,7 @@
 bf16 = jnp.bfloat16
 LAST = (((1,), (1,)), ((), ()))
 WHOLE = pl.BlockSpec(memory_space=pltpu.VMEM)
-LIMIT = 40 * 1024 * 1024
+LIMIT = 12 * 1024 * 1024
 
 
 def exchange(pieces, axes):
@@ -67,18 +67,23 @@
     return lax.dot_general(left, right, LAST, preferred_element_type=f32)
 
 
-def encode_kernel(centered_ref, weight_ref, bias_ref, latents_ref, turned_ref, rows_ref):
-    width = centered_ref.shape[0]
-
-    @pl.when(pl.program_id(0) == 0)
+def encode_kernel(centered_ref, weight_ref, bias_ref, latents_ref, turned_ref, total_ref):
+    step = pl.program_id(0)
+    term = product(centered_ref[...].T, weight_ref[...])
+
+    @pl.when(step == 0)
     def _():
-        for at in range(0, width, 256):
-            rows_ref[:, at : at + 256] = centered_ref[at : at + 256, :].T
-
-    preact = product(rows_ref[...], weight_ref[...]) + bias_ref[...].astype(f32)
-    latents = jnp.maximum(preact, 0.0).astype(bf16)
-    latents_ref[...] = latents
-    turned_ref[...] = latents.T
+        total_ref[...] = term + bias_ref[...].astype(f32)
+
+    @pl.when(step > 0)
+    def _():
+        total_ref[...] += term
+
+    @pl.when(step == pl.num_programs(0) - 1)
+    def _():
+        latents = jnp.maximum(total_ref[...], 0.0).astype(bf16)
+        latents_ref[...] = latents
+        turned_ref[...] = latents.T
 
 
 def encode(centered, weight, bias, tile):
@@ -88,18 +93,15 @@
         encode_kernel,
         [array((tokens, count)), array((count, tokens))],
         2 * tokens * width * count,
-        [centered, weight, bias.reshape(1, count)],
-        grid=(count // tile,),
+        [centered, pltpu.with_memory_space_constraint(weight, pltpu.HBM), bias.reshape(1, count)],
+        grid=(width // tile,),
         in_specs=[
+            pl.BlockSpec((tile, tokens), lambda j: (j, 0)),
+            pl.BlockSpec((tile, count), lambda j: (j, 0)),
             WHOLE,
-            pl.BlockSpec((width, tile), lambda j: (0, j)),
-            pl.BlockSpec((1, tile), lambda j: (0, j)),
         ],
-        out_specs=[
-            pl.BlockSpec((tokens, tile), lambda j: (0, j)),
-            pl.BlockSpec((tile, tokens), lambda j: (j, 0)),
-        ],
-        scratch_shapes=[pltpu.VMEM((tokens, width), bf16)],
+        out_specs=[WHOLE, WHOLE],
+        scratch_shapes=[pltpu.VMEM((tokens, count), f32)],
     )
 
 
@@ -155,7 +157,7 @@
     send_to_all(out_ref, (recon * scale_in * gain_ref[...].astype(f32)).astype(bf16))
 
 
-def output_kernel(token_count, pieces_ref, recon_ref, target_ref, gain_ref, out_ref, grad_ref):
+def output_kernel(token_count, pieces_ref, gain_ref, recon_ref, target_ref, out_ref, grad_ref):
     gain = gain_ref[...].astype(f32)
     output = total_of(pieces_ref, recon_ref.shape[1])
     scale_out = lax.rsqrt(mean_of(output * output) + epsilon)
@@ -168,7 +170,7 @@
     send_to_all(out_ref, (scale_out * (grad_normed - normed_out * inner)).astype(bf16))
 
 
-def input_kernel(pieces_ref, recon_ref, grad_ref, gain_ref, out_ref):
+def input_kernel(pieces_ref, gain_ref, recon_ref, grad_ref, out_ref):
     recon = recon_ref[...]
     scale_in = lax.rsqrt(mean_of(recon * recon) + epsilon)
     unit = recon * scale_in
@@ -177,19 +179,20 @@
     send_to_all(out_ref, (grad_ref[...] + scale_in * (grad_unit - unit * inner)).astype(bf16))
 
 
-def local(body, outs, args):
-    return call(body, outs, 0, args, in_specs=[WHOLE] * len(args), out_specs=[WHOLE] * len(outs))
-
-
-def parts_of(own, near, far):
-    return [own, [near.at[k] for k in range(3)], [far.at[k] for k in range(3)]]
-
-
-def forward_kernel(rows_ref, gate_ref, up_ref, down_ref, near_ref, far_ref, out_ref, *saved):
+def local(body, outs, args, kept=0):
+    stay = len(args) - kept
+    return call(body, outs, 0, args, in_specs=[WHOLE] * stay + [pl.BlockSpec()] * kept)
+
+
+def parts_of(own, other):
+    return [own, [other.at[k] for k in range(3)]]
+
+
+def forward_kernel(rows_ref, gate_ref, up_ref, down_ref, other_ref, out_ref, *saved):
     root = 0.7978845608028654
     cube = 0.044715
     rows = rows_ref[...]
-    parts = parts_of([gate_ref, up_ref, down_ref], near_ref, far_ref)
+    parts = parts_of([gate_ref, up_ref, down_ref], other_ref)
     hidden = []
     for (gate, up, _), gelu_ref, slope_ref in zip(parts, saved[0::2], saved[1::2]):
         gate_value = product_t(rows, gate[...])
@@ -208,10 +211,10 @@
         out_ref[:, span] = sum(terms[1:], terms[0]).astype(bf16)
 
 
-def backward_kernel(rows_ref, gate_ref, up_ref, down_ref, near_ref, far_ref, *refs):
+def backward_kernel(rows_ref, gate_ref, up_ref, down_ref, other_ref, *refs):
     saved, out_ref = refs[:-1], refs[-1]
     rows = rows_ref[...]
-    parts = parts_of([gate_ref, up_ref, down_ref], near_ref, far_ref)
+    parts = parts_of([gate_ref, up_ref, down_ref], other_ref)
     grads = []
     for (_, _, down), gelu_ref, slope_ref in zip(parts, saved[0::2], saved[1::2]):
         grad_hidden = product_t(rows, down[...])
@@ -248,25 +251,27 @@
     )
 
 
-def products_kernel(*refs):
+def products_kernel(spans, *refs):
     count = len(refs) // 2
     out_ref = refs[-1]
-    total = product(refs[0][...], refs[count][...])
-    for k in range(1, count):
-        total += product(refs[k][...], refs[count + k][...])
-    out_ref[...] = total.astype(bf16)
+    for span in spans:
+        total = product(refs[0][...], refs[count][:, span])
+        for k in range(1, count):
+            total += product(refs[k][...], refs[count + k][:, span])
+        out_ref[:, span] = total.astype(bf16)
 
 
 def sum_of_products(left, right, tile):
     rows, depth = left[0].shape
     columns = right[0].shape[1]
+    spans = [slice(at, min(at + 256, tile)) for at in range(0, tile, 256)]
     return call(
-        products_kernel,
+        functools.partial(products_kernel, spans),
         array((rows, columns)),
         2 * rows * depth * columns * len(left),
         [*left, *right],
         grid=(columns // tile,),
-        in_specs=[pl.BlockSpec((rows, depth), lambda j: (0, 0))] * len(left)
+        in_specs=[WHOLE] * len(left)
         + [pl.BlockSpec((depth, tile), lambda j: (0, j))] * len(right),
         out_specs=pl.BlockSpec((rows, tile), lambda j: (0, j)),
     )
@@ -306,54 +311,61 @@
     def all_tokens(pieces, axes):
         return exchange(pieces, axes).reshape(-1, width)
 
-    units = gate.shape[0] // 2
-    at = lax.axis_index(BATCH[1]) * units
+    hidden = gate.shape[0]
+    units = hidden // copies
+    at = (lax.axis_index(BATCH) ^ (copies // 2)) * units
     weights = [gate, up, down_weight]
     sent = jnp.stack([lax.dynamic_slice_in_dim(w, at, units, axis=0) for w in weights])
-    near = swap(sent, OTHER_HALF)
-    far = swap(near, BATCH[1])
-
+    quarter = swap(sent, OTHER_HALF)
     bias_share = lax.dynamic_slice_in_dim(decoder_bias.astype(f32), offset, share_width)
     centered_share = (residual.astype(f32) - bias_share).astype(bf16).T
     pieces = jnp.broadcast_to(centered_share, (shards, share_width, tokens))
     centered = exchange(pieces, SHARDS).reshape(width, tokens)
 
-    centered_blocks = blocks_of_all(
-        lambda b: lax.dynamic_slice_in_dim(centered, b * block, block, axis=0)
-    )
     latents, turned_latents = encode(centered, encoder_weight, encoder_bias, 256)
     partial_recon = decode(latents, decoder_weight, target.T, 128)
-    partial_recon, *centered_blocks = lax.optimization_barrier((partial_recon, *centered_blocks))
+
+    _, quarter = lax.optimization_barrier((partial_recon, quarter))
+    other = jnp.concatenate(copies_of_all(quarter), axis=1)
 
     pieces = to_owners(partial_recon, SHARDS)
     own_target = pieces[:, :, width : width + share_width]
     own_target = jnp.moveaxis(own_target, 0, 1).reshape(own_tokens, width)
     pieces, recon = local(recon_kernel, [half_of_them, own_rows], [pieces, bias, gain_in])
 
+    pieces, centered, turned_latents = lax.optimization_barrier((pieces, centered, turned_latents))
     normed_input = all_tokens(pieces, HALF)
     latent_blocks = copies_of_all(turned_latents)
+    centered_blocks = blocks_of_all(
+        lambda b: lax.dynamic_slice_in_dim(centered, b * block, block, axis=0)
+    )
     rows = half * own_tokens
-    saved = [array((rows, n), f32) for n in (2 * units, 2 * units, units, units, units, units)]
     partial_out, *saved = local(
         forward_kernel,
-        [array((rows, width)), *saved],
-        [normed_input, *weights, near, far],
-    )
-    partial_out, *latent_blocks = lax.optimization_barrier((partial_out, *latent_blocks))
+        [array((rows, width))] + [array((rows, hidden), f32)] * 4,
+        [normed_input, *weights, other],
+    )
+    partial_out, latent_blocks = lax.optimization_barrier((partial_out, latent_blocks))
 
     pieces, grad_result = local(
         functools.partial(output_kernel, token_count),
         [half_of_them, own_rows],
-        [to_owners(partial_out, HALF), recon, own_target, gain_out],
+        [to_owners(partial_out, HALF), gain_out, recon, own_target],
+        kept=2,
     )
     grad_output = all_tokens(pieces, HALF)
     (partial_input,) = local(
         backward_kernel,
         [array((rows, width))],
-        [grad_output, *weights, near, far, *saved],
-    )
+        [grad_output, *weights, other, *saved],
+        kept=4,
+    )
+    partial_input, centered_blocks = lax.optimization_barrier((partial_input, centered_blocks))
     (pieces,) = local(
-        input_kernel, [everyone], [to_owners(partial_input, HALF), recon, grad_result, gain_in]
+        input_kernel,
+        [everyone],
+        [to_owners(partial_input, HALF), gain_in, recon, grad_result],
+        kept=2,
     )
     grad_recon = all_tokens(pieces, SHARDS)
 
@@ -361,8 +373,9 @@
         lambda b: lax.dynamic_slice_in_dim(grad_recon, b * block, block, axis=1)
     )
     grad_preact = grad_of_preact(grad_recon, decoder_weight, latents, 256)
-    decoder_grad = sum_of_products(latent_blocks, recon_blocks, 128)
     encoder_grad = sum_of_products(centered_blocks, copies_of_all(grad_preact), 256)
+    encoder_grad, recon_blocks = lax.optimization_barrier((encoder_grad, recon_blocks))
+    decoder_grad = sum_of_products(latent_blocks, recon_blocks, block)
     return encoder_grad, decoder_grad
 
 

time: 281 us -> 301 us (1.071)
  blocking collectives: 62.5 us -> 51.7 us
  starting transfers between devices: 39.2 us -> 48.5 us
  local copies, waits for them, and re-layouts: 20.9 us -> 29.4 us
  waiting for transfers between devices: 111 us -> 119 us
  Pallas kernels: 39.8 us -> 43 us
    all_to_all x3 -> x2, blocking collectives: 62.5 us -> 51.7 us  [exchange(): return lax.all_to_all(pieces, axes, split_axis=0, concat_axis=0, tiled=True)]
    unnamed x76 -> x61, local copies, waits for them, and re-layouts: 13.3 us -> 19.2 us
    all_to_all x4 -> x5, starting transfers between devices: 31.1 us -> 37 us  [exchange(): return lax.all_to_all(pieces, axes, split_axis=0, concat_axis=0, tiled=True)]
    ppermute x14 -> x16, waiting for transfers between devices: 71.8 us -> 76.8 us  [swap(): lax.ppermute(block, axes, [(i, for_all - 1 - i) for i in range(for_all)])]
    ppermute x14 -> x16, starting transfers between devices: 8.08 us -> 11.6 us  [swap(): lax.ppermute(block, axes, [(i, for_all - 1 - i) for i in range(for_all)])]
    pallas_call x10, Pallas kernels: 39.8 us -> 43 us  [call(): pl.pallas_call(body, out_shape=outs, cost_estimate=cost, compiler_params=...]
    all_to_all x4 -> x5, waiting for transfers between devices: 39.6 us -> 42.1 us  [exchange(): return lax.all_to_all(pieces, axes, split_axis=0, concat_axis=0, tiled=True)]
  transfers between devices with their start and end apart: 18 -> 21, of which waited for: 9 -> 10; matrix products, arithmetic and copies ran while one was open for 3% -> 5% of each run, Pallas kernels for 9% -> 11%
where the time goes in v4:
time: 301 us; the launch traced here: 295 us
  waiting for transfers between devices  119 us (40%)
  blocking collectives  51.7 us (17%)
  starting transfers between devices  48.5 us (16%)
  Pallas kernels  43 us (14%)
  local copies, waits for them, and re-layouts  29.4 us (10%)
    ppermute x16, waiting for transfers between devices, swap(): lax.ppermute(block, axes, [(i, for_all - 1 - i) for i in range(for_all)])  76.8 us
    all_to_all x2, blocking collectives, exchange(): return lax.all_to_all(pieces, axes, split_axis=0, concat_axis=0, tiled=True)  51.7 us
    pallas_call x10, Pallas kernels, call(): pl.pallas_call(body, out_shape=outs, cost_estimate=cost, compiler_params=...  43 us
    all_to_all x5, waiting for transfers between devices, exchange(): return lax.all_to_all(pieces, axes, split_axis=0, concat_axis=0, tiled=True)  42.1 us
    all_to_all x5, starting transfers between devices, exchange(): return lax.all_to_all(pieces, axes, split_axis=0, concat_axis=0, tiled=True)  37 us
    unnamed x61, local copies, waits for them, and re-layouts  19.2 us
    ppermute x16, starting transfers between devices, swap(): lax.ppermute(block, axes, [(i, for_all - 1 - i) for i in range(for_all)])  11.6 us
  transfers between devices with their start and end apart: 21, of which 10 were waited for; matrix products, arithmetic and copies ran while one was open for 5% of the time, Pallas kernels for 11%

profile of v4, /device:TPU:14, one launch (start us, length us, event | category | flops | bytes accessed | tf_op | source)
XLA Modules:
  0.0 295.3 jit_solution(17461905787535709638)
XLA Ops:
  2.3 1.3 broadcast_in_dim.4
  3.7 10.2 %all-to-all-start = ((bf16[32,112,256]{2,1,0:T(8,128)(2,1)}), bf16[32,112,256]{2,1,0:T(8,128)(2,1)}, u32[]{:S(2)}, u32[]{:S(2)}) async-start(bf16[32,112,256]{2,1,0:T(8,128)(2,1)} %broadcast_in_dim.4), calls=%async_computation | async-start | bytes 3670016 | tf_op jit(solution)/shard_map/all_to_all | solution.py:26
  13.9 1.2 dynamic-slice_bitcast_fusion
  15.1 1.2 dynamic-slice_bitcast_fusion.1
  16.3 1.2 pad_maximum_fusion
  17.5 2.3 collective-permute-start
  19.7 18.7 %all-to-all-done = bf16[32,112,256]{2,1,0:T(8,128)(2,1)} async-done(((bf16[32,112,256]{2,1,0:T(8,128)(2,1)}), bf16[32,112,256]{2,1,0:T(8,128)(2,1)}, u32[]{:S(2)}, u32[]{:S(2)}) %all-to-all-start) | async-done | bytes 1835040 | tf_op jit(solution)/shard_map/all_to_all | solution.py:26
  38.4 12.5 %shard_map.122 = (bf16[256,1024]{1,0:T(8,128)(2,1)S(1)}, bf16[1024,256]{1,0:T(8,128)(2,1)}) custom-call(bf16[3584,256]{1,0:T(8,128)(2,1)} %bitcast.1.centered_ref, bf16[3584,1024]{1,0:T(8,128)(2,1)} %weight_ref.3, bf16[1,1024]{1,0:T(2,128)(2,1)S(1)} %reshape.42.bias_ref), custom_call_target="tpu_custom_call" | custom-call | flops 1879048192 | bytes 10225664 | tf_op jit(solution)/shard_map/pallas_call | solution.py:49
  50.9 3.8 %shard_map.123 = bf16[256,3712]{1,0:T(8,128)(2,1)S(1)} custom-call(bf16[256,1024]{1,0:T(8,128)(2,1)S(1)} %get-tuple-element.32.latents_ref, bf16[1024,3584]{1,0:T(8,128)(2,1)S(1)} %bitcast.25, bf16[112,256]{1,0:T(8,128)(2,1)S(1)} %bitcast.37), custom_call_target="tpu_custom_call" | custom-call | flops 1879048192 | bytes 9822208 | tf_op jit(solution)/shard_map/pallas_call | solution.py:49
  54.7 1.3 copy-done.7
  56.0 7.3 %all-to-all-start.1 = ((bf16[32,8,3712]{2,1,0:T(8,128)(2,1)}), bf16[32,8,3712]{2,1,0:T(8,128)(2,1)S(1)}, u32[]{:S(2)}, u32[]{:S(2)}) async-start(bf16[32,8,3712]{2,1,0:T(8,128)(2,1)} %bitcast.34), calls=%async_computation.1 | async-start | bytes 3801088 | tf_op jit(solution)/shard_map/all_to_all | solution.py:26
  63.3 1.6 collective-permute-start.2
  65.0 47.0 %collective-permute-done.2 = bf16[3,56,3584]{2,1,0:T(8,128)(2,1)} collective-permute-done((bf16[3,56,3584]{2,1,0:T(8,128)(2,1)}, bf16[3,56,3584]{2,1,0:T(8,128)(2,1)}, u32[]{:S(2)}, u32[]{:S(2)}) %collective-permute-start.2) | collective-permute-done | bytes 1204256 | tf_op jit(solution)/shard_map/ppermute | solution.py:31
  112.0 1.5 shard_map.124
  113.5 2.4 constant_dynamic-update-slice_fusion.3
  115.9 1.1 constant_dynamic-update-slice_fusion.2
  117.5 7.2 %all-to-all-start.2 = ((bf16[16,8,3584]{2,1,0:T(8,128)(2,1)}), bf16[16,8,3584]{2,1,0:T(8,128)(2,1)}, u32[]{:S(2)}, u32[]{:S(2)}) async-start(bf16[16,8,3584]{2,1,0:T(8,128)(2,1)} %get-tuple-element.35), calls=%async_computation.2 | async-start | bytes 1835008 | tf_op jit(solution)/shard_map/all_to_all | solution.py:26
  124.8 3.4 %collective-permute-done.5.refs_2_ = bf16[1024,256]{1,0:T(8,128)(2,1)} collective-permute-done((bf16[1024,256]{1,0:T(8,128)(2,1)}, bf16[1024,256]{1,0:T(8,128)(2,1)}, u32[]{:S(2)}, u32[]{:S(2)}) %collective-permute-start.5) | collective-permute-done | bytes 524320 | tf_op jit(solution)/shard_map/ppermute | solution.py:31
  128.2 2.4 constant_dynamic-update-slice_fusion.1
  130.6 2.4 constant_dynamic-update-slice_fusion.other_ref
  133.0 5.8 %all-to-all-done.2 = bf16[16,8,3584]{2,1,0:T(8,128)(2,1)} async-done(((bf16[16,8,3584]{2,1,0:T(8,128)(2,1)}), bf16[16,8,3584]{2,1,0:T(8,128)(2,1)}, u32[]{:S(2)}, u32[]{:S(2)}) %all-to-all-start.2) | async-done | bytes 917536 | tf_op jit(solution)/shard_map/all_to_all | solution.py:26
  138.8 1.4 copy-done.4
  140.2 5.5 %shard_map.125 = (bf16[128,3584]{1,0:T(8,128)(2,1)S(1)}, f32[128,224]{1,0:T(8,128)S(1)}, f32[128,224]{1,0:T(8,128)S(1)}, f32[128,224]{1,0:T(8,128)S(1)}, f32[128,224]{1,0:T(8,128)S(1)}) custom-call(bf16[128,3584]{1,0:T(8,128)(2,1)} %bitcast.4.rows_ref, bf16[224,3584]{1,0:T(8,128)(2,1)S(1)} %bitcast.30, bf16[224,3584]{1,0:T(8,128)(2,1)S(1)} %bitcast.32, ...), custom_call_target="tpu_custom_call" | custom-call | bytes 11927552 | tf_op jit(solution)/shard_map/pallas_call | solution.py:49
  145.7 0.9 copy-done.10
  148.6 6.0 %all-to-all-start.3 = ((bf16[16,8,3584]{2,1,0:T(8,128)(2,1)}), bf16[16,8,3584]{2,1,0:T(8,128)(2,1)S(1)}, u32[]{:S(2)}, u32[]{:S(2)}) async-start(bf16[16,8,3584]{2,1,0:T(8,128)(2,1)} %bitcast.36), calls=%async_computation.3 | async-start | bytes 1835008 | tf_op jit(solution)/shard_map/all_to_all | solution.py:26
  155.6 11.3 %all-to-all-done.3.pieces_ref = bf16[16,8,3584]{2,1,0:T(8,128)(2,1)S(1)} async-done(((bf16[16,8,3584]{2,1,0:T(8,128)(2,1)}), bf16[16,8,3584]{2,1,0:T(8,128)(2,1)S(1)}, u32[]{:S(2)}, u32[]{:S(2)}) %all-to-all-start.3) | async-done | bytes 917536 | tf_op jit(solution)/shard_map/all_to_all | solution.py:26
  166.9 1.4 shard_map.126
  168.9 6.2 %all-to-all-start.4 = ((bf16[16,8,3584]{2,1,0:T(8,128)(2,1)}), bf16[16,8,3584]{2,1,0:T(8,128)(2,1)}, u32[]{:S(2)}, u32[]{:S(2)}) async-start(bf16[16,8,3584]{2,1,0:T(8,128)(2,1)} %get-tuple-element.41), calls=%async_computation.4 | async-start | bytes 1835008 | tf_op jit(solution)/shard_map/all_to_all | solution.py:26
  175.1 2.9 constant_dynamic-slice_fusion.4
  178.0 2.6 collective-permute-start.8
  180.7 6.3 %all-to-all-done.4 = bf16[16,8,3584]{2,1,0:T(8,128)(2,1)} async-done(((bf16[16,8,3584]{2,1,0:T(8,128)(2,1)}), bf16[16,8,3584]{2,1,0:T(8,128)(2,1)}, u32[]{:S(2)}, u32[]{:S(2)}) %all-to-all-start.4) | async-done | bytes 917536 | tf_op jit(solution)/shard_map/all_to_all | solution.py:26
  187.1 1.4 copy-done.1
  188.5 1.4 copy-done.3
  189.9 1.4 copy-done.5
  192.2 0.9 copy-done.15
  193.1 0.9 copy-done.17
  194.0 5.0 %shard_map.127 = bf16[128,3584]{1,0:T(8,128)(2,1)S(1)} custom-call(bf16[128,3584]{1,0:T(8,128)(2,1)} %bitcast.14.rows_ref, bf16[224,3584]{1,0:T(8,128)(2,1)S(1)} %bitcast.31, bf16[224,3584]{1,0:T(8,128)(2,1)S(1)} %bitcast.33, bf16[224,3584]{1,0:T(8,128)(2,1)S(1)} %copy-done.5, bf16[3,224,3584]{2,1,0:T(8,128)(2,1)} %constant_dynamic-update-slice_fusion.other_ref, ...), custom_call_target="tpu_custom_call" | custom-call | bytes 11927552 | tf_op jit(solution)/shard_map/pallas_call | solution.py:49
  199.1 2.6 collective-permute-done.9.refs_3_
  201.7 20.9 %all_to_all.35.pieces_ref = bf16[16,8,3584]{2,1,0:T(8,128)(2,1)S(1)} all-to-all(bf16[16,8,3584]{2,1,0:T(8,128)(2,1)S(1)} %bitcast.35), channel_id=1, replica_groups=mesh['batch_0'=2,'batch_1'=2,'tensor_0'=4,'tensor_1'=2,'latent'=4] {'ten..., dimensions={0} | all-to-all | bytes 1835008 | tf_op jit(solution)/shard_map/all_to_all | solution.py:26
  223.0 30.8 %all_to_all.36 = bf16[32,8,3584]{2,1,0:T(8,128)(2,1)S(1)} all-to-all(bf16[32,8,3584]{2,1,0:T(8,128)(2,1)S(1)} %shard_map.128), channel_id=1, replica_groups=mesh['batch_0'=2,'batch_1'=2,'tensor_0'=4,'tensor_1'=2,'latent'=4] {'ten..., dimensions={0} | all-to-all | bytes 3670016 | tf_op jit(solution)/shard_map/all_to_all | solution.py:26
  253.9 2.9 shard_map.129.refs_4_
  256.8 2.1 collective-permute-start.11
  258.9 9.0 %collective-permute-done.11.refs_6_ = bf16[256,1024]{1,0:T(8,128)(2,1)S(1)} collective-permute-done((bf16[256,1024]{1,0:T(8,128)(2,1)S(1)}, bf16[256,1024]{1,0:T(8,128)(2,1)S(1)}, u32[]{:S(2)}, u32[]{:S(2)}) %collective-permute-start.11) | collective-permute-done | bytes 524320 | tf_op jit(solution)/shard_map/ppermute | solution.py:31
  268.6 1.7 collective-permute-start.14
  270.3 5.0 %shard_map.130 = bf16[896,1024]{1,0:T(8,128)(2,1)} custom-call(bf16[896,256]{1,0:T(8,128)(2,1)S(1)} %copy-done.11, bf16[896,256]{1,0:T(8,128)(2,1)} %collective-permute-done.7.refs_1_, bf16[896,256]{1,0:T(8,128)(2,1)} %collective-permute-done.8.refs_2_, bf16[896,256]{1,0:T(8,128)(2,1)} %collective-permute-done.9.refs_3_, ...), custom_call_target="tpu_custom_call" | custom-call | flops 1879048192 | bytes 5767168 | tf_op jit(solution)/shard_map/pallas_call | solution.py:49
  275.3 6.6 %collective-permute-done.14.refs_6_ = bf16[256,896]{1,0:T(8,128)(2,1)S(1)} collective-permute-done((bf16[256,896]{1,0:T(8,128)(2,1)S(1)}, bf16[256,896]{1,0:T(8,128)(2,1)S(1)}, u32[]{:S(2)}, u32[]{:S(2)}) %collective-permute-start.14) | collective-permute-done | bytes 458784 | tf_op jit(solution)/shard_map/ppermute | solution.py:31
  282.0 8.2 %collective-permute-done.15.refs_7_ = bf16[256,896]{1,0:T(8,128)(2,1)S(1)} collective-permute-done((bf16[256,896]{1,0:T(8,128)(2,1)S(1)}, bf16[256,896]{1,0:T(8,128)(2,1)S(1)}, u32[]{:S(2)}, u32[]{:S(2)}) %collective-permute-start.15) | collective-permute-done | bytes 458784 | tf_op jit(solution)/shard_map/ppermute | solution.py:31
  290.2 5.1 %shard_map.131 = bf16[1024,896]{1,0:T(8,128)(2,1)} custom-call(bf16[1024,256]{1,0:T(8,128)(2,1)} %get-tuple-element.54.refs_0_, bf16[1024,256]{1,0:T(8,128)(2,1)} %collective-permute-done.4.refs_1_, bf16[1024,256]{1,0:T(8,128)(2,1)} %collective-permute-done.5.refs_2_, bf16[1024,256]{1,0:T(8,128)(2,1)} %collective-permute-done.6.refs_3_, ...), custom_call_target="tpu_custom_call" | custom-call | flops 1879048192 | bytes 5767168 | tf_op jit(solution)/shard_map/pallas_call | solution.py:49
  (85 shorter events, 8.1 us)
Async XLA Ops:
  3.7 34.8 %all-to-all-start = ((bf16[32,112,256]{2,1,0:T(8,128)(2,1)}), bf16[32,112,256]{2,1,0:T(8,128)(2,1)}, u32[]{:S(2)}, u32[]{:S(2)}) async-start(bf16[32,112,256]{2,1,0:T(8,128)(2,1)} %broadcast_in_dim.4), calls=%async_computation | async-start | bytes 3670016 | tf_op jit(solution)/shard_map/all_to_all | solution.py:26
  13.9 37.0 %slice-start = ((s8[7340032]{0:T(1024)(128)(4,1)}), s8[3145728]{0:T(1024)(128)(4,1)S(1)}, s32[]{:S(2)}) async-start(s8[7340032]{0:T(1024)(128)(4,1)} %bitcast.24), calls=%async_computation.7 | async-start | bytes 6291456
  15.1 4.6 %copy-start.24 = (bf16[1024]{0:T(1024)(128)(2,1)S(1)}, bf16[1024]{0:T(1024)(128)(2,1)}, u32[]{:S(2)}) copy-start(bf16[1024]{0:T(1024)(128)(2,1)} %param.14) | copy-start | bytes 6148
  17.5 45.9 %collective-permute-start = (bf16[3,56,3584]{2,1,0:T(8,128)(2,1)}, bf16[3,56,3584]{2,1,0:T(8,128)(2,1)}, u32[]{:S(2)}, u32[]{:S(2)}) collective-permute-start(bf16[3,56,3584]{2,1,0:T(8,128)(2,1)} %pad_maximum_fusion), channel_id=1, source_target_pairs={{0,68},{4,64},{64,4},{68,0},{1,69},{5,65},{65,5},{69,1},{2,70},{6,... | collective-permute-start | bytes 3612680 | tf_op jit(solution)/shard_map/ppermute | solution.py:31
  38.4 12.5 %slice-start.1 = ((s8[7340032]{0:T(1024)(128)(4,1)}), s8[4194304]{0:T(1024)(128)(4,1)S(1)}, s32[]{:S(2)}) async-start(s8[7340032]{0:T(1024)(128)(4,1)} %bitcast.24), calls=%async_computation.8 | async-start | bytes 8388608
  38.4 12.5 %copy-start.20 = (bf16[256,112]{0,1:T(8,128)(2,1)S(1)}, bf16[256,112]{0,1:T(8,128)(2,1)}, u32[]{:S(2)}) copy-start(bf16[256,112]{0,1:T(8,128)(2,1)} %param.12) | copy-start | bytes 172036
  50.9 3.8 %copy-start.8 = (bf16[256,1024]{1,0:T(8,128)(2,1)}, bf16[256,1024]{1,0:T(8,128)(2,1)S(1)}, u32[]{:S(2)}) copy-start(bf16[256,1024]{1,0:T(8,128)(2,1)S(1)} %get-tuple-element.32.latents_ref) | copy-start | bytes 1572868
  54.7 1.3 copy-start.7
  56.0 8.9 %copy-start.21 = (bf16[3584]{0:T(1024)(128)(2,1)S(1)}, bf16[3584]{0:T(1024)(128)(2,1)}, u32[]{:S(2)}) copy-start(bf16[3584]{0:T(1024)(128)(2,1)} %param.16) | copy-start | bytes 21508
  56.0 9.0 %copy-start.22 = (bf16[3584]{0:T(1024)(128)(2,1)S(1)}, bf16[3584]{0:T(1024)(128)(2,1)}, u32[]{:S(2)}) copy-start(bf16[3584]{0:T(1024)(128)(2,1)} %param.17) | copy-start | bytes 21508
  56.0 55.9 %all-to-all-start.1 = ((bf16[32,8,3712]{2,1,0:T(8,128)(2,1)}), bf16[32,8,3712]{2,1,0:T(8,128)(2,1)S(1)}, u32[]{:S(2)}, u32[]{:S(2)}) async-start(bf16[32,8,3712]{2,1,0:T(8,128)(2,1)} %bitcast.34), calls=%async_computation.1 | async-start | bytes 3801088 | tf_op jit(solution)/shard_map/all_to_all | solution.py:26
  63.3 48.6 %collective-permute-start.2 = (bf16[3,56,3584]{2,1,0:T(8,128)(2,1)}, bf16[3,56,3584]{2,1,0:T(8,128)(2,1)}, u32[]{:S(2)}, u32[]{:S(2)}) collective-permute-start(bf16[3,56,3584]{2,1,0:T(8,128)(2,1)} %collective-permute-done), channel_id=1, source_target_pairs={{0,64},{64,0},{1,65},{65,1},{2,66},{66,2},{3,67},{67,3},{4,68},{68... | collective-permute-start | bytes 3612680 | tf_op jit(solution)/shard_map/ppermute | solution.py:31
  64.9 51.0 %collective-permute-start.1 = (bf16[3,56,3584]{2,1,0:T(8,128)(2,1)}, bf16[3,56,3584]{2,1,0:T(8,128)(2,1)S(1)}, u32[]{:S(2)}, u32[]{:S(2)}) collective-permute-start(bf16[3,56,3584]{2,1,0:T(8,128)(2,1)} %collective-permute-done), channel_id=1, source_target_pairs={{0,32},{32,0},{1,33},{33,1},{2,34},{34,2},{3,35},{35,3},{4,36},{36... | collective-permute-start | bytes 3612680 | tf_op jit(solution)/shard_map/ppermute | solution.py:31
  112.0 18.6 %collective-permute-start.3 = (bf16[3,56,3584]{2,1,0:T(8,128)(2,1)}, bf16[3,56,3584]{2,1,0:T(8,128)(2,1)}, u32[]{:S(2)}, u32[]{:S(2)}) collective-permute-start(bf16[3,56,3584]{2,1,0:T(8,128)(2,1)} %collective-permute-done.2), channel_id=1, source_target_pairs={{0,32},{32,0},{1,33},{33,1},{2,34},{34,2},{3,35},{35,3},{4,36},{36... | collective-permute-start | bytes 3612680 | tf_op jit(solution)/shard_map/ppermute | solution.py:31
  112.0 4.0 %copy-start.6 = (bf16[32,8,3712]{2,1,0:T(8,128)(2,1)}, bf16[32,8,3712]{2,1,0:T(8,128)(2,1)S(1)}, u32[]{:S(2)}) copy-start(bf16[32,8,3712]{2,1,0:T(8,128)(2,1)S(1)} %all-to-all-done.1.pieces_ref) | copy-start | bytes 5701636
  113.5 14.7 %collective-permute-start.5 = (bf16[1024,256]{1,0:T(8,128)(2,1)}, bf16[1024,256]{1,0:T(8,128)(2,1)}, u32[]{:S(2)}, u32[]{:S(2)}) collective-permute-start(bf16[1024,256]{1,0:T(8,128)(2,1)} %get-tuple-element.54.refs_0_), channel_id=1, source_target_pairs={{0,64},{64,0},{1,65},{65,1},{2,66},{66,2},{3,67},{67,3},{4,68},{68... | collective-permute-start | bytes 1572872 | tf_op jit(solution)/shard_map/ppermute | solution.py:31
  117.0 31.5 %collective-permute-start.4 = (bf16[1024,256]{1,0:T(8,128)(2,1)}, bf16[1024,256]{1,0:T(8,128)(2,1)}, u32[]{:S(2)}, u32[]{:S(2)}) collective-permute-start(bf16[1024,256]{1,0:T(8,128)(2,1)} %get-tuple-element.54.refs_0_), channel_id=1, source_target_pairs={{0,32},{32,0},{1,33},{33,1},{2,34},{34,2},{3,35},{35,3},{4,36},{36... | collective-permute-start | bytes 1572872 | tf_op jit(solution)/shard_map/ppermute | solution.py:31
  117.5 21.2 %all-to-all-start.2 = ((bf16[16,8,3584]{2,1,0:T(8,128)(2,1)}), bf16[16,8,3584]{2,1,0:T(8,128)(2,1)}, u32[]{:S(2)}, u32[]{:S(2)}) async-start(bf16[16,8,3584]{2,1,0:T(8,128)(2,1)} %get-tuple-element.35), calls=%async_computation.2 | async-start | bytes 1835008 | tf_op jit(solution)/shard_map/all_to_all | solution.py:26
  124.8 14.0 %copy-start = (bf16[3584,224]{0,1:T(8,128)(2,1)S(1)}, bf16[3584,224]{0,1:T(8,128)(2,1)}, u32[]{:S(2)}) copy-start(bf16[3584,224]{0,1:T(8,128)(2,1)} %param.19) | copy-start | bytes 4816900
  124.8 14.0 %copy-start.2 = (bf16[3584,224]{0,1:T(8,128)(2,1)S(1)}, bf16[3584,224]{0,1:T(8,128)(2,1)}, u32[]{:S(2)}) copy-start(bf16[3584,224]{0,1:T(8,128)(2,1)} %param.20) | copy-start | bytes 4816900
  128.2 20.4 %collective-permute-start.6 = (bf16[1024,256]{1,0:T(8,128)(2,1)}, bf16[1024,256]{1,0:T(8,128)(2,1)}, u32[]{:S(2)}, u32[]{:S(2)}) collective-permute-start(bf16[1024,256]{1,0:T(8,128)(2,1)} %collective-permute-done.5.refs_2_), channel_id=1, source_target_pairs={{0,32},{32,0},{1,33},{33,1},{2,34},{34,2},{3,35},{35,3},{4,36},{36... | collective-permute-start | bytes 1572872 | tf_op jit(solution)/shard_map/ppermute | solution.py:31
  138.8 1.4 copy-start.4
  145.7 0.9 copy-start.10
  146.6 0.7 copy-start.12
  148.6 6.0 %copy-start.23 = (bf16[3584]{0:T(1024)(128)(2,1)S(1)}, bf16[3584]{0:T(1024)(128)(2,1)}, u32[]{:S(2)}) copy-start(bf16[3584]{0:T(1024)(128)(2,1)} %param.18) | copy-start | bytes 21508
  148.6 18.3 %all-to-all-start.3 = ((bf16[16,8,3584]{2,1,0:T(8,128)(2,1)}), bf16[16,8,3584]{2,1,0:T(8,128)(2,1)S(1)}, u32[]{:S(2)}, u32[]{:S(2)}) async-start(bf16[16,8,3584]{2,1,0:T(8,128)(2,1)} %bitcast.36), calls=%async_computation.3 | async-start | bytes 1835008 | tf_op jit(solution)/shard_map/all_to_all | solution.py:26
  168.3 0.7 copy-start.18
  168.9 18.1 %all-to-all-start.4 = ((bf16[16,8,3584]{2,1,0:T(8,128)(2,1)}), bf16[16,8,3584]{2,1,0:T(8,128)(2,1)}, u32[]{:S(2)}, u32[]{:S(2)}) async-start(bf16[16,8,3584]{2,1,0:T(8,128)(2,1)} %get-tuple-element.41), calls=%async_computation.4 | async-start | bytes 1835008 | tf_op jit(solution)/shard_map/all_to_all | solution.py:26
  175.1 78.7 %slice-start.2 = ((s8[7340032]{0:T(1024)(128)(4,1)}), s8[3145728]{0:T(1024)(128)(4,1)S(1)}, s32[]{:S(2)}) async-start(s8[7340032]{0:T(1024)(128)(4,1)} %bitcast.26), calls=%async_computation.9 | async-start | bytes 6291456
  178.0 21.1 %collective-permute-start.7 = (bf16[896,256]{1,0:T(8,128)(2,1)}, bf16[896,256]{1,0:T(8,128)(2,1)}, u32[]{:S(2)}, u32[]{:S(2)}) collective-permute-start(bf16[896,256]{1,0:T(8,128)(2,1)} %get-tuple-element.68), channel_id=1, source_target_pairs={{0,32},{32,0},{1,33},{33,1},{2,34},{34,2},{3,35},{35,3},{4,36},{36... | collective-permute-start | bytes 1376264 | tf_op jit(solution)/shard_map/ppermute | solution.py:31
  178.0 21.1 %collective-permute-start.8 = (bf16[896,256]{1,0:T(8,128)(2,1)}, bf16[896,256]{1,0:T(8,128)(2,1)}, u32[]{:S(2)}, u32[]{:S(2)}) collective-permute-start(bf16[896,256]{1,0:T(8,128)(2,1)} %get-tuple-element.67), channel_id=1, source_target_pairs={{0,64},{64,0},{1,65},{65,1},{2,66},{66,2},{3,67},{67,3},{4,68},{68... | collective-permute-start | bytes 1376264 | tf_op jit(solution)/shard_map/ppermute | solution.py:31
  180.6 21.1 %collective-permute-start.9 = (bf16[896,256]{1,0:T(8,128)(2,1)}, bf16[896,256]{1,0:T(8,128)(2,1)}, u32[]{:S(2)}, u32[]{:S(2)}) collective-permute-start(bf16[896,256]{1,0:T(8,128)(2,1)} %get-tuple-element.66), channel_id=1, source_target_pairs={{0,96},{32,64},{64,32},{96,0},{1,97},{33,65},{65,33},{97,1},{2,98}... | collective-permute-start | bytes 1376264 | tf_op jit(solution)/shard_map/ppermute | solution.py:31
  187.1 1.4 copy-start.1
  188.5 1.4 copy-start.3
  189.9 1.4 copy-start.5
  191.3 0.9 copy-start.13
  192.2 0.9 copy-start.15
  193.1 0.9 copy-start.17
  194.0 59.8 %slice-start.3 = ((s8[7340032]{0:T(1024)(128)(4,1)}), s8[4194304]{0:T(1024)(128)(4,1)S(1)}, s32[]{:S(2)}) async-start(s8[7340032]{0:T(1024)(128)(4,1)} %bitcast.26), calls=%async_computation.10 | async-start | bytes 8388608
  199.1 23.5 %copy-start.19 = (f32[8,3584]{1,0:T(8,128)S(1)}, f32[8,3584]{1,0:T(8,128)}, u32[]{:S(2)}) copy-start(f32[8,3584]{1,0:T(8,128)} %copy-done.18) | copy-start | bytes 344068
  223.0 30.8 %copy-start.9 = (bf16[256,1024]{1,0:T(8,128)(2,1)S(1)}, bf16[256,1024]{1,0:T(8,128)(2,1)}, u32[]{:S(2)}) copy-start(bf16[256,1024]{1,0:T(8,128)(2,1)} %copy-done.8) | copy-start | bytes 1572868
  256.8 13.6 %copy-start.11 = (bf16[896,256]{1,0:T(8,128)(2,1)S(1)}, bf16[896,256]{1,0:T(8,128)(2,1)}, u32[]{:S(2)}) copy-start(bf16[896,256]{1,0:T(8,128)(2,1)} %get-tuple-element.47.refs_0_) | copy-start | bytes 1376260
  256.8 11.1 %collective-permute-start.11 = (bf16[256,1024]{1,0:T(8,128)(2,1)S(1)}, bf16[256,1024]{1,0:T(8,128)(2,1)S(1)}, u32[]{:S(2)}, u32[]{:S(2)}) collective-permute-start(bf16[256,1024]{1,0:T(8,128)(2,1)S(1)} %shard_map.129.refs_4_), channel_id=1, source_target_pairs={{0,64},{64,0},{1,65},{65,1},{2,66},{66,2},{3,67},{67,3},{4,68},{68... | collective-permute-start | bytes 1572872 | tf_op jit(solution)/shard_map/ppermute | solution.py:31
  258.9 11.5 %collective-permute-start.10 = (bf16[256,1024]{1,0:T(8,128)(2,1)S(1)}, bf16[256,1024]{1,0:T(8,128)(2,1)S(1)}, u32[]{:S(2)}, u32[]{:S(2)}) collective-permute-start(bf16[256,1024]{1,0:T(8,128)(2,1)S(1)} %shard_map.129.refs_4_), channel_id=1, source_target_pairs={{0,32},{32,0},{1,33},{33,1},{2,34},{34,2},{3,35},{35,3},{4,36},{36... | collective-permute-start | bytes 1572872 | tf_op jit(solution)/shard_map/ppermute | solution.py:31
  267.8 2.5 collective-permute-start.12
  268.0 7.3 %collective-permute-start.13 = (bf16[256,896]{1,0:T(8,128)(2,1)S(1)}, bf16[256,896]{1,0:T(8,128)(2,1)S(1)}, u32[]{:S(2)}, u32[]{:S(2)}) collective-permute-start(bf16[256,896]{1,0:T(8,128)(2,1)S(1)} %get-tuple-element.64), channel_id=1, source_target_pairs={{0,32},{32,0},{1,33},{33,1},{2,34},{34,2},{3,35},{35,3},{4,36},{36... | collective-permute-start | bytes 1376264 | tf_op jit(solution)/shard_map/ppermute | solution.py:31
  268.6 13.4 %collective-permute-start.14 = (bf16[256,896]{1,0:T(8,128)(2,1)S(1)}, bf16[256,896]{1,0:T(8,128)(2,1)S(1)}, u32[]{:S(2)}, u32[]{:S(2)}) collective-permute-start(bf16[256,896]{1,0:T(8,128)(2,1)S(1)} %get-tuple-element.63), channel_id=1, source_target_pairs={{0,64},{64,0},{1,65},{65,1},{2,66},{66,2},{3,67},{67,3},{4,68},{68... | collective-permute-start | bytes 1376264 | tf_op jit(solution)/shard_map/ppermute | solution.py:31
  270.3 19.9 %collective-permute-start.15 = (bf16[256,896]{1,0:T(8,128)(2,1)S(1)}, bf16[256,896]{1,0:T(8,128)(2,1)S(1)}, u32[]{:S(2)}, u32[]{:S(2)}) collective-permute-start(bf16[256,896]{1,0:T(8,128)(2,1)S(1)} %get-tuple-element.62), channel_id=1, source_target_pairs={{0,96},{32,64},{64,32},{96,0},{1,97},{33,65},{65,33},{97,1},{2,98}... | collective-permute-start | bytes 1376264 | tf_op jit(solution)/shard_map/ppermute | solution.py:31
  (2 other events, 1.3 us)

commit v5 on v3

--- a/solution.py
+++ b/solution.py
@@ -1,4 +1,5 @@
 import functools
+import math
 
 import jax
 import jax.numpy as jnp
@@ -19,7 +20,7 @@
 bf16 = jnp.bfloat16
 LAST = (((1,), (1,)), ((), ()))
 WHOLE = pl.BlockSpec(memory_space=pltpu.VMEM)
-LIMIT = 40 * 1024 * 1024
+LIMIT = 24 * 1024 * 1024
 
 
 def exchange(pieces, axes):
@@ -44,7 +45,8 @@
 
 
 def call(body, outs, flops, args, **more):
-    moved = sum(a.size * a.dtype.itemsize for a in [*args, *jax.tree.leaves(outs)])
+    arrays = [*args, *jax.tree.leaves(outs)]
+    moved = sum(math.prod(a.shape) * jnp.dtype(a.dtype).itemsize for a in arrays)
     cost = pl.CostEstimate(flops=flops, bytes_accessed=moved, transcendentals=0)
     return pl.pallas_call(
         body,
@@ -59,6 +61,14 @@
     return jax.ShapeDtypeStruct(shape, dtype)
 
 
+def hbm_array(shape, dtype=bf16):
+    return pltpu.HBM(shape, dtype)
+
+
+def in_hbm(value):
+    return pltpu.with_memory_space_constraint(value, pltpu.HBM)
+
+
 def product(left, right):
     return jnp.dot(left, right, preferred_element_type=f32)
 
@@ -67,13 +77,21 @@
     return lax.dot_general(left, right, LAST, preferred_element_type=f32)
 
 
-def encode_kernel(centered_ref, weight_ref, bias_ref, latents_ref, turned_ref, rows_ref):
-    width = centered_ref.shape[0]
+def encode_kernel(share, centered_ref, weight_ref, bias_ref, latents_ref, turned_ref, rows_ref):
+    width = rows_ref.shape[1]
 
     @pl.when(pl.program_id(0) == 0)
     def _():
         for at in range(0, width, 256):
-            rows_ref[:, at : at + 256] = centered_ref[at : at + 256, :].T
+            runs, f = [], at
+            while f < at + 256:
+                shard, inside = divmod(f, share)
+                far, half, near = shard // 8, shard // 4 % 2, shard % 4
+                run = min(share - inside, at + 256 - f)
+                start = (far * 8 + near * 2 + half) * share + inside
+                runs.append(centered_ref[start : start + run, :])
+                f += run
+            rows_ref[:, at : at + 256] = jnp.concatenate(runs, axis=0).T
 
     preact = product(rows_ref[...], weight_ref[...]) + bias_ref[...].astype(f32)
     latents = jnp.maximum(preact, 0.0).astype(bf16)
@@ -81,17 +99,17 @@
     turned_ref[...] = latents.T
 
 
-def encode(centered, weight, bias, tile):
+def encode(centered, weight, bias, share, tile):
     width, tokens = centered.shape
     count = weight.shape[1]
     return call(
-        encode_kernel,
-        [array((tokens, count)), array((count, tokens))],
+        functools.partial(encode_kernel, share),
+        [array((tokens, count)), hbm_array((count, tokens))],
         2 * tokens * width * count,
-        [centered, weight, bias.reshape(1, count)],
+        [centered, in_hbm(weight), bias.reshape(1, count)],
         grid=(count // tile,),
         in_specs=[
-            WHOLE,
+            pl.BlockSpec((width, tokens), lambda j: (0, 0)),
             pl.BlockSpec((width, tile), lambda j: (0, j)),
             pl.BlockSpec((1, tile), lambda j: (0, j)),
         ],
@@ -103,6 +121,33 @@
     )
 
 
+def gather_kernel(at_ref, *refs):
+    *weights, out_ref, sems = refs
+    count = out_ref.shape[1]
+    at = pl.multiple_of(at_ref[0], count)
+    copies = [
+        pltpu.make_async_copy(w.at[pl.ds(at, count)], out_ref.at[k], sems.at[k])
+        for k, w in enumerate(weights)
+    ]
+    for copy in copies:
+        copy.start()
+    for copy in copies:
+        copy.wait()
+
+
+def rows_of_each(weights, at, count):
+    anywhere = pl.BlockSpec(memory_space=pl.ANY)
+    return call(
+        gather_kernel,
+        hbm_array((len(weights), count, weights[0].shape[1])),
+        0,
+        [at.reshape(1), *(in_hbm(w) for w in weights)],
+        in_specs=[pl.BlockSpec(memory_space=pltpu.SMEM)] + [anywhere] * len(weights),
+        out_specs=anywhere,
+        scratch_shapes=[pltpu.SemaphoreType.DMA((len(weights),))],
+    )
+
+
 def decode_kernel(latents_ref, weight_ref, target_ref, out_ref):
     tile = weight_ref.shape[1]
     step = pl.program_id(0)
@@ -125,7 +170,7 @@
         decode_kernel,
         array((tokens, width + room)),
         2 * tokens * width * count,
-        [latents, weight, turned_target],
+        [latents, in_hbm(weight), turned_target],
         grid=(7,),
         in_specs=[WHOLE, pl.BlockSpec((count, tile), lambda j: (0, j)), WHOLE],
         out_specs=WHOLE,
@@ -177,8 +222,10 @@
     send_to_all(out_ref, (grad_ref[...] + scale_in * (grad_unit - unit * inner)).astype(bf16))
 
 
-def local(body, outs, args):
-    return call(body, outs, 0, args, in_specs=[WHOLE] * len(args), out_specs=[WHOLE] * len(outs))
+def local(body, outs, args, kept=0):
+    stay = len(args) - kept
+    args = [*args[:stay], *(in_hbm(a) for a in args[stay:])]
+    return call(body, outs, 0, args, in_specs=[WHOLE] * stay + [pl.BlockSpec()] * kept)
 
 
 def parts_of(own, near, far):
@@ -248,20 +295,22 @@
     )
 
 
-def products_kernel(*refs):
+def products_kernel(spans, *refs):
     count = len(refs) // 2
     out_ref = refs[-1]
-    total = product(refs[0][...], refs[count][...])
-    for k in range(1, count):
-        total += product(refs[k][...], refs[count + k][...])
-    out_ref[...] = total.astype(bf16)
+    for span in spans:
+        total = product(refs[0][...], refs[count][:, span])
+        for k in range(1, count):
+            total += product(refs[k][...], refs[count + k][:, span])
+        out_ref[:, span] = total.astype(bf16)
 
 
 def sum_of_products(left, right, tile):
     rows, depth = left[0].shape
     columns = right[0].shape[1]
+    spans = [slice(at, min(at + 256, tile)) for at in range(0, tile, 256)]
     return call(
-        products_kernel,
+        functools.partial(products_kernel, spans),
         array((rows, columns)),
         2 * rows * depth * columns * len(left),
         [*left, *right],
@@ -297,7 +346,7 @@
     gate, up = gate_weight.T, up_weight.T
     everyone = array((shards, own_tokens, width))
     half = lax.axis_size(HALF)
-    half_of_them = array((half, own_tokens, width))
+    half_of_them = hbm_array((half, own_tokens, width))
     own_rows = array((own_tokens, width), f32)
 
     def to_owners(partial, axes):
@@ -309,48 +358,63 @@
     units = gate.shape[0] // 2
     at = lax.axis_index(BATCH[1]) * units
     weights = [gate, up, down_weight]
-    sent = jnp.stack([lax.dynamic_slice_in_dim(w, at, units, axis=0) for w in weights])
+
+    bias_share = lax.dynamic_slice_in_dim(decoder_bias.astype(f32), offset, share_width)
+    centered_share = (residual.astype(f32) - bias_share).astype(bf16).T
+    partner = swap(centered_share, SHARDS[1])
+    first = lax.axis_index(SHARDS[1]) == 0
+    pair = jnp.stack(
+        [jnp.where(first, centered_share, partner), jnp.where(first, partner, centered_share)]
+    )
+    pieces = jnp.broadcast_to(pair, (lax.axis_size(HALF), *pair.shape))
+    pieces, weights_then = lax.optimization_barrier((pieces, weights))
+    sent = rows_of_each(weights_then, at, units)
     near = swap(sent, OTHER_HALF)
     far = swap(near, BATCH[1])
-
-    bias_share = lax.dynamic_slice_in_dim(decoder_bias.astype(f32), offset, share_width)
-    centered_share = (residual.astype(f32) - bias_share).astype(bf16).T
-    pieces = jnp.broadcast_to(centered_share, (shards, share_width, tokens))
-    centered = exchange(pieces, SHARDS).reshape(width, tokens)
-
-    centered_blocks = blocks_of_all(
-        lambda b: lax.dynamic_slice_in_dim(centered, b * block, block, axis=0)
-    )
-    latents, turned_latents = encode(centered, encoder_weight, encoder_bias, 256)
+    centered = exchange(pieces, HALF).reshape(width, tokens)
+
+    latents, turned_latents = encode(
+        centered, encoder_weight, encoder_bias, share_width, 256
+    )
     partial_recon = decode(latents, decoder_weight, target.T, 128)
-    partial_recon, *centered_blocks = lax.optimization_barrier((partial_recon, *centered_blocks))
 
     pieces = to_owners(partial_recon, SHARDS)
     own_target = pieces[:, :, width : width + share_width]
     own_target = jnp.moveaxis(own_target, 0, 1).reshape(own_tokens, width)
     pieces, recon = local(recon_kernel, [half_of_them, own_rows], [pieces, bias, gain_in])
 
+    pieces, centered, turned_latents = lax.optimization_barrier((pieces, centered, turned_latents))
     normed_input = all_tokens(pieces, HALF)
     latent_blocks = copies_of_all(turned_latents)
+
+    def feature_block(b):
+        part = lax.dynamic_slice_in_dim(centered, b * block, block, axis=0)
+        part = part.reshape(lax.axis_size(SHARDS[2]), lax.axis_size(SHARDS[1]), share_width, tokens)
+        return jnp.swapaxes(part, 0, 1).reshape(block, tokens)
+
+    centered_blocks = blocks_of_all(feature_block)
     rows = half * own_tokens
-    saved = [array((rows, n), f32) for n in (2 * units, 2 * units, units, units, units, units)]
+    saved = [hbm_array((rows, n), f32) for n in (2 * units, 2 * units, units, units, units, units)]
     partial_out, *saved = local(
         forward_kernel,
-        [array((rows, width)), *saved],
+        [hbm_array((rows, width)), *saved],
         [normed_input, *weights, near, far],
     )
-    partial_out, *latent_blocks = lax.optimization_barrier((partial_out, *latent_blocks))
 
     pieces, grad_result = local(
         functools.partial(output_kernel, token_count),
         [half_of_them, own_rows],
         [to_owners(partial_out, HALF), recon, own_target, gain_out],
+    )
+    pieces, latent_blocks, centered_blocks = lax.optimization_barrier(
+        (pieces, latent_blocks, centered_blocks)
     )
     grad_output = all_tokens(pieces, HALF)
     (partial_input,) = local(
         backward_kernel,
         [array((rows, width))],
         [grad_output, *weights, near, far, *saved],
+        kept=6,
     )
     (pieces,) = local(
         input_kernel, [everyone], [to_owners(partial_input, HALF), recon, grad_result, gain_in]
@@ -361,8 +425,8 @@
         lambda b: lax.dynamic_slice_in_dim(grad_recon, b * block, block, axis=1)
     )
     grad_preact = grad_of_preact(grad_recon, decoder_weight, latents, 256)
-    decoder_grad = sum_of_products(latent_blocks, recon_blocks, 128)
     encoder_grad = sum_of_products(centered_blocks, copies_of_all(grad_preact), 256)
+    decoder_grad = sum_of_products(latent_blocks, recon_blocks, block)
     return encoder_grad, decoder_grad
 
 

time: 281 us -> 353 us (1.26)
  Pallas kernels: 39.8 us -> 118 us
  blocking collectives: 62.5 us -> 73.3 us
  waiting for transfers between devices: 111 us -> 104 us
  local copies, waits for them, and re-layouts: 20.9 us -> 14.7 us
    pallas_call x10 -> x11, Pallas kernels: 39.8 us -> 118 us  [call(): pl.pallas_call(body, out_shape=outs, cost_estimate=cost, compiler_params=...]
    ppermute x14 -> x15, waiting for transfers between devices: 71.8 us -> 41.4 us  [swap(): lax.ppermute(block, axes, [(i, for_all - 1 - i) for i in range(for_all)])]
    all_to_all x4, waiting for transfers between devices: 39.6 us -> 62.7 us  [exchange(): return lax.all_to_all(pieces, axes, split_axis=0, concat_axis=0, tiled=True)]
    all_to_all x3, blocking collectives: 62.5 us -> 73.3 us  [exchange(): return lax.all_to_all(pieces, axes, split_axis=0, concat_axis=0, tiled=True)]
    unnamed x76 -> x40, local copies, waits for them, and re-layouts: 13.3 us -> 5.63 us
    all_to_all x4, starting transfers between devices: 31.1 us -> 26.5 us  [exchange(): return lax.all_to_all(pieces, axes, split_axis=0, concat_axis=0, tiled=True)]
    transpose x0 -> x4, local copies, waits for them, and re-layouts: none -> 4.35 us  [feature_block(): return jnp.swapaxes(part, 0, 1).reshape(block, tokens)]
    ppermute x14 -> x15, starting transfers between devices: 8.08 us -> 9.42 us  [swap(): lax.ppermute(block, axes, [(i, for_all - 1 - i) for i in range(for_all)])]
  transfers between devices with their start and end apart: 18 -> 19, of which waited for: 9 -> 10; matrix products, arithmetic and copies ran while one was open for 3% -> 2% of each run, Pallas kernels for 9% -> 9%
where the time goes in v5:
time: 353 us; the launch traced here: 350 us
  Pallas kernels  118 us (33%)
  waiting for transfers between devices  104 us (29%)
  blocking collectives  73.3 us (21%)
  starting transfers between devices  35.9 us (10%)
  local copies, waits for them, and re-layouts  14.7 us (4%)
    pallas_call x11, Pallas kernels, call(): pl.pallas_call(body, out_shape=outs, cost_estimate=cost, compiler_params=...  118 us
    all_to_all x3, blocking collectives, exchange(): return lax.all_to_all(pieces, axes, split_axis=0, concat_axis=0, tiled=True)  73.3 us
    all_to_all x4, waiting for transfers between devices, exchange(): return lax.all_to_all(pieces, axes, split_axis=0, concat_axis=0, tiled=True)  62.7 us
    ppermute x15, waiting for transfers between devices, swap(): lax.ppermute(block, axes, [(i, for_all - 1 - i) for i in range(for_all)])  41.4 us
    all_to_all x4, starting transfers between devices, exchange(): return lax.all_to_all(pieces, axes, split_axis=0, concat_axis=0, tiled=True)  26.5 us
    ppermute x15, starting transfers between devices, swap(): lax.ppermute(block, axes, [(i, for_all - 1 - i) for i in range(for_all)])  9.42 us
  transfers between devices with their start and end apart: 19, of which 10 were waited for; matrix products, arithmetic and copies ran while one was open for 2% of the time, Pallas kernels for 9%

profile of v5, /device:TPU:14, one launch (start us, length us, event | category | flops | bytes accessed | tf_op | source)
XLA Modules:
  0.0 349.7 jit_solution(5157586628590398824)
XLA Ops:
  0.6 0.8 dynamic-slice_convert_fusion
  1.4 0.9 fusion
  2.3 2.4 collective-permute-start
  4.7 3.4 collective-permute-done
  8.1 0.9 select_bitcast_fusion.1
  9.0 1.4 broadcast_in_dim.4
  10.4 74.1 %shard_map.125 = bf16[3,112,3584]{2,1,0:T(8,128)(2,1)} custom-call(s32[1]{0:T(128)} %bitcast.9.at_ref, bf16[224,3584]{1,0:T(8,128)(2,1)} %bitcast.43, bf16[224,3584]{1,0:T(8,128)(2,1)} %bitcast.46, bf16[224,3584]{1,0:T(8,128)(2,1)} %down_ref.3), custom_call_target="tpu_custom_call" | custom-call | bytes 7225348 | tf_op jit(solution)/shard_map/pallas_call | solution.py:51
  84.5 1.7 collective-permute-start.1
  86.2 8.3 %all-to-all-start = ((bf16[16,2,112,256]{3,2,1,0:T(8,128)(2,1)}), bf16[16,2,112,256]{3,2,1,0:T(8,128)(2,1)S(1)}, u32[]{:S(2)}, u32[]{:S(2)}) async-start(bf16[16,2,112,256]{3,2,1,0:T(8,128)(2,1)} %broadcast_in_dim.4), calls=%async_computation | async-start | bytes 3670016 | tf_op jit(solution)/shard_map/all_to_all | solution.py:27
  94.5 22.8 %all-to-all-done = bf16[16,2,112,256]{3,2,1,0:T(8,128)(2,1)S(1)} async-done(((bf16[16,2,112,256]{3,2,1,0:T(8,128)(2,1)}), bf16[16,2,112,256]{3,2,1,0:T(8,128)(2,1)S(1)}, u32[]{:S(2)}, u32[]{:S(2)}) %all-to-all-start) | async-done | bytes 1835040 | tf_op jit(solution)/shard_map/all_to_all | solution.py:27
  117.3 6.5 %shard_map.122 = (bf16[256,1024]{1,0:T(8,128)(2,1)S(1)}, bf16[1024,256]{1,0:T(8,128)(2,1)}) custom-call(bf16[3584,256]{1,0:T(8,128)(2,1)S(1)} %bitcast.41, bf16[3584,1024]{1,0:T(8,128)(2,1)} %weight_ref.3, bf16[1,1024]{1,0:T(2,128)(2,1)S(1)} %reshape.69.bias_ref), custom_call_target="tpu_custom_call" | custom-call | flops 1879048192 | bytes 10225664 | tf_op jit(solution)/shard_map/pallas_call | solution.py:51
  123.8 7.0 %shard_map.123 = bf16[256,3712]{1,0:T(8,128)(2,1)S(1)} custom-call(bf16[256,1024]{1,0:T(8,128)(2,1)S(1)} %get-tuple-element.32.latents_ref, bf16[1024,3584]{1,0:T(8,128)(2,1)} %weight_ref.5, bf16[112,256]{1,0:T(8,128)(2,1)S(1)} %bitcast.53), custom_call_target="tpu_custom_call" | custom-call | flops 1879048192 | bytes 9822208 | tf_op jit(solution)/shard_map/pallas_call | solution.py:51
  130.8 1.3 copy-done.5
  132.1 7.2 %all-to-all-start.1 = ((bf16[32,8,3712]{2,1,0:T(8,128)(2,1)}), bf16[32,8,3712]{2,1,0:T(8,128)(2,1)}, u32[]{:S(2)}, u32[]{:S(2)}) async-start(bf16[32,8,3712]{2,1,0:T(8,128)(2,1)} %bitcast.49), calls=%async_computation.1 | async-start | bytes 3801088 | tf_op jit(solution)/shard_map/all_to_all | solution.py:27
  139.4 0.6 reshape.71.bias_ref
  140.0 0.6 reshape.72.gain_ref
  140.7 23.9 %all-to-all-done.1.pieces_ref = bf16[32,8,3712]{2,1,0:T(8,128)(2,1)} async-done(((bf16[32,8,3712]{2,1,0:T(8,128)(2,1)}), bf16[32,8,3712]{2,1,0:T(8,128)(2,1)}, u32[]{:S(2)}, u32[]{:S(2)}) %all-to-all-start.1) | async-done | bytes 1900576 | tf_op jit(solution)/shard_map/all_to_all | solution.py:27
  164.6 0.7 copy-done.9
  165.3 0.7 copy-done.11
  166.0 2.9 shard_map.124
  168.9 4.8 %all-to-all-start.2 = ((bf16[16,8,3584]{2,1,0:T(8,128)(2,1)}), bf16[16,8,3584]{2,1,0:T(8,128)(2,1)}, u32[]{:S(2)}, u32[]{:S(2)}) async-start(bf16[16,8,3584]{2,1,0:T(8,128)(2,1)} %get-tuple-element.35), calls=%async_computation.2 | async-start | bytes 1835008 | tf_op jit(solution)/shard_map/all_to_all | solution.py:27
  173.8 12.6 %all-to-all-done.2 = bf16[16,8,3584]{2,1,0:T(8,128)(2,1)} async-done(((bf16[16,8,3584]{2,1,0:T(8,128)(2,1)}), bf16[16,8,3584]{2,1,0:T(8,128)(2,1)}, u32[]{:S(2)}, u32[]{:S(2)}) %all-to-all-start.2) | async-done | bytes 917536 | tf_op jit(solution)/shard_map/all_to_all | solution.py:27
  186.4 1.4 copy-done.1
  187.8 1.4 copy-done.3
  189.2 6.6 %shard_map.126 = (bf16[128,3584]{1,0:T(8,128)(2,1)}, f32[128,224]{1,0:T(8,128)}, f32[128,224]{1,0:T(8,128)}, f32[128,112]{1,0:T(8,128)}, f32[128,112]{1,0:T(8,12...) custom-call(bf16[128,3584]{1,0:T(8,128)(2,1)} %bitcast.8.rows_ref, bf16[224,3584]{1,0:T(8,128)(2,1)S(1)} %bitcast.44, ...), custom_call_target="tpu_custom_call" | custom-call | bytes 11927552 | tf_op jit(solution)/shard_map/pallas_call | solution.py:51
  195.8 6.2 %all-to-all-start.3 = ((bf16[16,8,3584]{2,1,0:T(8,128)(2,1)}), bf16[16,8,3584]{2,1,0:T(8,128)(2,1)}, u32[]{:S(2)}, u32[]{:S(2)}) async-start(bf16[16,8,3584]{2,1,0:T(8,128)(2,1)} %bitcast.58), calls=%async_computation.3 | async-start | bytes 1835008 | tf_op jit(solution)/shard_map/all_to_all | solution.py:27
  202.5 0.9 constant_dynamic-slice_fusion.4
  203.4 0.8 copy.18
  204.2 0.8 copy.17
  205.0 0.8 copy.16
  205.9 1.6 collective-permute-start.7
  207.7 0.8 slice_bitcast_fusion
  208.8 1.9 copy.15
  210.7 3.2 all-to-all-done.3.pieces_ref
  213.9 2.7 shard_map.127
  216.6 3.0 collective-permute-done.7.refs_2_
  219.6 8.9 %collective-permute-done.8.refs_3_ = bf16[896,256]{1,0:T(8,128)(2,1)} collective-permute-done((bf16[896,256]{1,0:T(8,128)(2,1)}, bf16[896,256]{1,0:T(8,128)(2,1)}, u32[]{:S(2)}, u32[]{:S(2)}) %collective-permute-start.8) | collective-permute-done | bytes 458784 | tf_op jit(solution)/shard_map/ppermute | solution.py:32
  228.5 21.5 %all_to_all.35 = bf16[16,8,3584]{2,1,0:T(8,128)(2,1)S(1)} all-to-all(bf16[16,8,3584]{2,1,0:T(8,128)(2,1)} %get-tuple-element.48), channel_id=1, replica_groups=mesh['batch_0'=2,'batch_1'=2,'tensor_0'=4,'tensor_1'=2,'latent'=4] {'ten..., dimensions={0} | all-to-all | bytes 1835008 | tf_op jit(solution)/shard_map/all_to_all | solution.py:27
  250.0 5.4 %shard_map.128 = bf16[128,3584]{1,0:T(8,128)(2,1)S(1)} custom-call(bf16[128,3584]{1,0:T(8,128)(2,1)S(1)} %bitcast.50, bf16[224,3584]{1,0:T(8,128)(2,1)S(1)} %bitcast.45, bf16[224,3584]{1,0:T(8,128)(2,1)S(1)} %bitcast.48, bf16[224,3584]{1,0:T(8,128)(2,1)S(1)} %copy-done.4, bf16[3,112,3584]{2,1,0:T(8,128)(2,1)} %collective-permute-done.1.near_ref, ...), custom_call_target="tpu_custom_call" | custom-call | bytes 11927552 | tf_op jit(solution)/shard_map/pallas_call | solution.py:51
  255.4 18.3 %all_to_all.36.pieces_ref = bf16[16,8,3584]{2,1,0:T(8,128)(2,1)S(1)} all-to-all(bf16[16,8,3584]{2,1,0:T(8,128)(2,1)S(1)} %bitcast.51), channel_id=1, replica_groups=mesh['batch_0'=2,'batch_1'=2,'tensor_0'=4,'tensor_1'=2,'latent'=4] {'ten..., dimensions={0} | all-to-all | bytes 1835008 | tf_op jit(solution)/shard_map/all_to_all | solution.py:27
  274.1 33.4 %all_to_all.37 = bf16[32,8,3584]{2,1,0:T(8,128)(2,1)S(1)} all-to-all(bf16[32,8,3584]{2,1,0:T(8,128)(2,1)S(1)} %shard_map.129), channel_id=1, replica_groups=mesh['batch_0'=2,'batch_1'=2,'tensor_0'=4,'tensor_1'=2,'latent'=4] {'ten..., dimensions={0} | all-to-all | bytes 3670016 | tf_op jit(solution)/shard_map/all_to_all | solution.py:27
  307.6 2.9 shard_map.130.refs_4_
  311.0 2.1 collective-permute-start.13
  313.6 12.0 %collective-permute-done.10.refs_6_ = bf16[256,1024]{1,0:T(8,128)(2,1)S(1)} collective-permute-done((bf16[256,1024]{1,0:T(8,128)(2,1)S(1)}, bf16[256,1024]{1,0:T(8,128)(2,1)S(1)}, u32[]{:S(2)}, u32[]{:S(2)}) %collective-permute-start.10) | collective-permute-done | bytes 524320 | tf_op jit(solution)/shard_map/ppermute | solution.py:32
  325.6 7.3 %collective-permute-done.14.refs_7_ = bf16[256,896]{1,0:T(8,128)(2,1)S(1)} collective-permute-done((bf16[256,896]{1,0:T(8,128)(2,1)S(1)}, bf16[256,896]{1,0:T(8,128)(2,1)S(1)}, u32[]{:S(2)}, u32[]{:S(2)}) %collective-permute-start.14) | collective-permute-done | bytes 458784 | tf_op jit(solution)/shard_map/ppermute | solution.py:32
  332.9 6.9 %collective-permute-done.13.refs_6_ = bf16[256,896]{1,0:T(8,128)(2,1)S(1)} collective-permute-done((bf16[256,896]{1,0:T(8,128)(2,1)S(1)}, bf16[256,896]{1,0:T(8,128)(2,1)S(1)}, u32[]{:S(2)}, u32[]{:S(2)}) %collective-permute-start.13) | collective-permute-done | bytes 458784 | tf_op jit(solution)/shard_map/ppermute | solution.py:32
  339.8 5.0 %shard_map.132 = bf16[1024,896]{1,0:T(8,128)(2,1)} custom-call(bf16[1024,256]{1,0:T(8,128)(2,1)S(1)} %copy-done.13, bf16[1024,256]{1,0:T(8,128)(2,1)} %collective-permute-done.3.refs_1_, bf16[1024,256]{1,0:T(8,128)(2,1)} %collective-permute-done.4.refs_2_, bf16[1024,256]{1,0:T(8,128)(2,1)} %collective-permute-done.5.refs_3_, ...), custom_call_target="tpu_custom_call" | custom-call | flops 1879048192 | bytes 5767168 | tf_op jit(solution)/shard_map/pallas_call | solution.py:51
  344.7 5.0 %shard_map.131 = bf16[896,1024]{1,0:T(8,128)(2,1)} custom-call(bf16[896,256]{1,0:T(8,128)(2,1)S(1)} %bitcast.52, bf16[896,256]{1,0:T(8,128)(2,1)} %collective-permute-done.6.refs_1_, bf16[896,256]{1,0:T(8,128)(2,1)} %collective-permute-done.7.refs_2_, bf16[896,256]{1,0:T(8,128)(2,1)} %collective-permute-done.8.refs_3_, ...), custom_call_target="tpu_custom_call" | custom-call | flops 1879048192 | bytes 5767168 | tf_op jit(solution)/shard_map/pallas_call | solution.py:51
  (63 shorter events, 2.5 us)
Async XLA Ops:
  2.3 5.8 %collective-permute-start = (bf16[112,256]{1,0:T(8,128)(2,1)S(1)}, bf16[112,256]{1,0:T(8,128)(2,1)S(1)}, u32[]{:S(2)}, u32[]{:S(2)}) collective-permute-start(bf16[112,256]{1,0:T(8,128)(2,1)S(1)} %fusion), channel_id=1, source_target_pairs={{0,4},{4,0},{1,5},{5,1},{2,6},{6,2},{3,7},{7,3},{8,12},{12,8},{9,1... | collective-permute-start | bytes 172040 | tf_op jit(solution)/shard_map/ppermute | solution.py:32
  84.5 9.9 %copy-start.17 = (bf16[1024]{0:T(1024)(128)(2,1)S(1)}, bf16[1024]{0:T(1024)(128)(2,1)}, u32[]{:S(2)}) copy-start(bf16[1024]{0:T(1024)(128)(2,1)} %param.14) | copy-start | bytes 6148
  84.5 54.8 %collective-permute-start.1 = (bf16[3,112,3584]{2,1,0:T(8,128)(2,1)}, bf16[3,112,3584]{2,1,0:T(8,128)(2,1)}, u32[]{:S(2)}, u32[]{:S(2)}) collective-permute-start(bf16[3,112,3584]{2,1,0:T(8,128)(2,1)} %shard_map.125), channel_id=1, source_target_pairs={{0,68},{4,64},{64,4},{68,0},{1,69},{5,65},{65,5},{69,1},{2,70},{6,... | collective-permute-start | bytes 7225352 | tf_op jit(solution)/shard_map/ppermute | solution.py:32
  86.2 31.1 %all-to-all-start = ((bf16[16,2,112,256]{3,2,1,0:T(8,128)(2,1)}), bf16[16,2,112,256]{3,2,1,0:T(8,128)(2,1)S(1)}, u32[]{:S(2)}, u32[]{:S(2)}) async-start(bf16[16,2,112,256]{3,2,1,0:T(8,128)(2,1)} %broadcast_in_dim.4), calls=%async_computation | async-start | bytes 3670016 | tf_op jit(solution)/shard_map/all_to_all | solution.py:27
  117.3 6.5 %copy-start.12 = (bf16[256,112]{0,1:T(8,128)(2,1)S(1)}, bf16[256,112]{0,1:T(8,128)(2,1)}, u32[]{:S(2)}) copy-start(bf16[256,112]{0,1:T(8,128)(2,1)} %param.12) | copy-start | bytes 172036
  123.8 7.0 %copy-start.6 = (bf16[256,1024]{1,0:T(8,128)(2,1)}, bf16[256,1024]{1,0:T(8,128)(2,1)S(1)}, u32[]{:S(2)}) copy-start(bf16[256,1024]{1,0:T(8,128)(2,1)S(1)} %get-tuple-element.32.latents_ref) | copy-start | bytes 1572868
  130.8 1.3 copy-start.5
  132.1 7.3 %copy-start.14 = (bf16[3584]{0:T(1024)(128)(2,1)S(1)}, bf16[3584]{0:T(1024)(128)(2,1)}, u32[]{:S(2)}) copy-start(bf16[3584]{0:T(1024)(128)(2,1)} %param.16) | copy-start | bytes 21508
  132.1 7.9 %copy-start.15 = (bf16[3584]{0:T(1024)(128)(2,1)S(1)}, bf16[3584]{0:T(1024)(128)(2,1)}, u32[]{:S(2)}) copy-start(bf16[3584]{0:T(1024)(128)(2,1)} %param.17) | copy-start | bytes 21508
  132.1 32.5 %all-to-all-start.1 = ((bf16[32,8,3712]{2,1,0:T(8,128)(2,1)}), bf16[32,8,3712]{2,1,0:T(8,128)(2,1)}, u32[]{:S(2)}, u32[]{:S(2)}) async-start(bf16[32,8,3712]{2,1,0:T(8,128)(2,1)} %bitcast.49), calls=%async_computation.1 | async-start | bytes 3801088 | tf_op jit(solution)/shard_map/all_to_all | solution.py:27
  139.3 47.1 %collective-permute-start.2 = (bf16[3,112,3584]{2,1,0:T(8,128)(2,1)}, bf16[3,112,3584]{2,1,0:T(8,128)(2,1)}, u32[]{:S(2)}, u32[]{:S(2)}) collective-permute-start(bf16[3,112,3584]{2,1,0:T(8,128)(2,1)} %collective-permute-done.1.near_ref), channel_id=1, source_target_pairs={{0,32},{32,0},{1,33},{33,1},{2,34},{34,2},{3,35},{35,3},{4,36},{36... | collective-permute-start | bytes 7225352 | tf_op jit(solution)/shard_map/ppermute | solution.py:32
  140.7 45.8 %copy-start = (bf16[3584,224]{0,1:T(8,128)(2,1)S(1)}, bf16[3584,224]{0,1:T(8,128)(2,1)}, u32[]{:S(2)}) copy-start(bf16[3584,224]{0,1:T(8,128)(2,1)} %param.19) | copy-start | bytes 4816900
  164.6 0.7 copy-start.9
  165.3 0.7 copy-start.11
  168.9 17.5 %all-to-all-start.2 = ((bf16[16,8,3584]{2,1,0:T(8,128)(2,1)}), bf16[16,8,3584]{2,1,0:T(8,128)(2,1)}, u32[]{:S(2)}, u32[]{:S(2)}) async-start(bf16[16,8,3584]{2,1,0:T(8,128)(2,1)} %get-tuple-element.35), calls=%async_computation.2 | async-start | bytes 1835008 | tf_op jit(solution)/shard_map/all_to_all | solution.py:27
  173.7 28.3 %collective-permute-start.4 = (bf16[1024,256]{1,0:T(8,128)(2,1)}, bf16[1024,256]{1,0:T(8,128)(2,1)}, u32[]{:S(2)}, u32[]{:S(2)}) collective-permute-start(bf16[1024,256]{1,0:T(8,128)(2,1)} %get-tuple-element.56.refs_0_), channel_id=1, source_target_pairs={{0,64},{64,0},{1,65},{65,1},{2,66},{66,2},{3,67},{67,3},{4,68},{68... | collective-permute-start | bytes 1572872 | tf_op jit(solution)/shard_map/ppermute | solution.py:32
  186.4 1.4 copy-start.1
  187.8 1.4 copy-start.3
  195.8 18.1 %all-to-all-start.3 = ((bf16[16,8,3584]{2,1,0:T(8,128)(2,1)}), bf16[16,8,3584]{2,1,0:T(8,128)(2,1)}, u32[]{:S(2)}, u32[]{:S(2)}) async-start(bf16[16,8,3584]{2,1,0:T(8,128)(2,1)} %bitcast.58), calls=%async_computation.3 | async-start | bytes 1835008 | tf_op jit(solution)/shard_map/all_to_all | solution.py:27
  202.0 26.5 %collective-permute-start.3 = (bf16[1024,256]{1,0:T(8,128)(2,1)}, bf16[1024,256]{1,0:T(8,128)(2,1)}, u32[]{:S(2)}, u32[]{:S(2)}) collective-permute-start(bf16[1024,256]{1,0:T(8,128)(2,1)} %get-tuple-element.56.refs_0_), channel_id=1, source_target_pairs={{0,32},{32,0},{1,33},{33,1},{2,34},{34,2},{3,35},{35,3},{4,36},{36... | collective-permute-start | bytes 1572872 | tf_op jit(solution)/shard_map/ppermute | solution.py:32
  202.0 26.4 %collective-permute-start.5 = (bf16[1024,256]{1,0:T(8,128)(2,1)}, bf16[1024,256]{1,0:T(8,128)(2,1)}, u32[]{:S(2)}, u32[]{:S(2)}) collective-permute-start(bf16[1024,256]{1,0:T(8,128)(2,1)} %collective-permute-done.4.refs_2_), channel_id=1, source_target_pairs={{0,32},{32,0},{1,33},{33,1},{2,34},{34,2},{3,35},{35,3},{4,36},{36... | collective-permute-start | bytes 1572872 | tf_op jit(solution)/shard_map/ppermute | solution.py:32
  203.4 4.3 %copy-start.16 = (bf16[3584]{0:T(1024)(128)(2,1)S(1)}, bf16[3584]{0:T(1024)(128)(2,1)}, u32[]{:S(2)}) copy-start(bf16[3584]{0:T(1024)(128)(2,1)} %param.18) | copy-start | bytes 21508
  205.8 10.8 %collective-permute-start.6 = (bf16[896,256]{1,0:T(8,128)(2,1)}, bf16[896,256]{1,0:T(8,128)(2,1)}, u32[]{:S(2)}, u32[]{:S(2)}) collective-permute-start(bf16[896,256]{1,0:T(8,128)(2,1)} %bitcast.17), channel_id=1, source_target_pairs={{0,32},{32,0},{1,33},{33,1},{2,34},{34,2},{3,35},{35,3},{4,36},{36... | collective-permute-start | bytes 1376264 | tf_op jit(solution)/shard_map/ppermute | solution.py:32
  205.9 13.6 %collective-permute-start.7 = (bf16[896,256]{1,0:T(8,128)(2,1)}, bf16[896,256]{1,0:T(8,128)(2,1)}, u32[]{:S(2)}, u32[]{:S(2)}) collective-permute-start(bf16[896,256]{1,0:T(8,128)(2,1)} %bitcast.20), channel_id=1, source_target_pairs={{0,64},{64,0},{1,65},{65,1},{2,66},{66,2},{3,67},{67,3},{4,68},{68... | collective-permute-start | bytes 1376264 | tf_op jit(solution)/shard_map/ppermute | solution.py:32
  207.6 20.9 %collective-permute-start.8 = (bf16[896,256]{1,0:T(8,128)(2,1)}, bf16[896,256]{1,0:T(8,128)(2,1)}, u32[]{:S(2)}, u32[]{:S(2)}) collective-permute-start(bf16[896,256]{1,0:T(8,128)(2,1)} %bitcast.23), channel_id=1, source_target_pairs={{0,96},{32,64},{64,32},{96,0},{1,97},{33,65},{65,33},{97,1},{2,98}... | collective-permute-start | bytes 1376264 | tf_op jit(solution)/shard_map/ppermute | solution.py:32
  208.7 41.3 %copy-start.2 = (bf16[3584,224]{0,1:T(8,128)(2,1)S(1)}, bf16[3584,224]{0,1:T(8,128)(2,1)}, u32[]{:S(2)}) copy-start(bf16[3584,224]{0,1:T(8,128)(2,1)} %param.20) | copy-start | bytes 4816900
  213.9 36.1 %copy-start.4 = (bf16[224,3584]{1,0:T(8,128)(2,1)S(1)}, bf16[224,3584]{1,0:T(8,128)(2,1)}, u32[]{:S(2)}) copy-start(bf16[224,3584]{1,0:T(8,128)(2,1)} %down_ref.3) | copy-start | bytes 4816900
  228.5 79.1 %slice-start = ((s8[7340032]{0:T(1024)(128)(4,1)}), s8[4194304]{0:T(1024)(128)(4,1)S(1)}, s32[]{:S(2)}) async-start(s8[7340032]{0:T(1024)(128)(4,1)} %bitcast.37), calls=%async_computation.7 | async-start | bytes 8388608
  250.0 57.5 %slice-start.1 = ((s8[7340032]{0:T(1024)(128)(4,1)}), s8[3145728]{0:T(1024)(128)(4,1)S(1)}, s32[]{:S(2)}) async-start(s8[7340032]{0:T(1024)(128)(4,1)} %bitcast.37), calls=%async_computation.8 | async-start | bytes 6291456
  255.4 18.3 %copy-start.10 = (bf16[1,3584]{1,0:T(2,128)(2,1)S(1)}, bf16[1,3584]{1,0:T(2,128)(2,1)}, u32[]{:S(2)}) copy-start(bf16[1,3584]{1,0:T(2,128)(2,1)} %reshape.72.gain_ref) | copy-start | bytes 21508
  274.1 33.4 %copy-start.7 = (bf16[256,1024]{1,0:T(8,128)(2,1)S(1)}, bf16[256,1024]{1,0:T(8,128)(2,1)}, u32[]{:S(2)}) copy-start(bf16[256,1024]{1,0:T(8,128)(2,1)} %copy-done.6) | copy-start | bytes 1572868
  310.5 29.3 %copy-start.13 = (bf16[1024,256]{1,0:T(8,128)(2,1)S(1)}, bf16[1024,256]{1,0:T(8,128)(2,1)}, u32[]{:S(2)}) copy-start(bf16[1024,256]{1,0:T(8,128)(2,1)} %get-tuple-element.56.refs_0_) | copy-start | bytes 1572868
  310.5 15.1 %collective-permute-start.10 = (bf16[256,1024]{1,0:T(8,128)(2,1)S(1)}, bf16[256,1024]{1,0:T(8,128)(2,1)S(1)}, u32[]{:S(2)}, u32[]{:S(2)}) collective-permute-start(bf16[256,1024]{1,0:T(8,128)(2,1)S(1)} %shard_map.130.refs_4_), channel_id=1, source_target_pairs={{0,64},{64,0},{1,65},{65,1},{2,66},{66,2},{3,67},{67,3},{4,68},{68... | collective-permute-start | bytes 1572872 | tf_op jit(solution)/shard_map/ppermute | solution.py:32
  310.9 22.0 %collective-permute-start.14 = (bf16[256,896]{1,0:T(8,128)(2,1)S(1)}, bf16[256,896]{1,0:T(8,128)(2,1)S(1)}, u32[]{:S(2)}, u32[]{:S(2)}) collective-permute-start(bf16[256,896]{1,0:T(8,128)(2,1)S(1)} %get-tuple-element.60), channel_id=1, source_target_pairs={{0,96},{32,64},{64,32},{96,0},{1,97},{33,65},{65,33},{97,1},{2,98}... | collective-permute-start | bytes 1376264 | tf_op jit(solution)/shard_map/ppermute | solution.py:32
  311.0 28.7 %collective-permute-start.13 = (bf16[256,896]{1,0:T(8,128)(2,1)S(1)}, bf16[256,896]{1,0:T(8,128)(2,1)S(1)}, u32[]{:S(2)}, u32[]{:S(2)}) collective-permute-start(bf16[256,896]{1,0:T(8,128)(2,1)S(1)} %get-tuple-element.61), channel_id=1, source_target_pairs={{0,64},{64,0},{1,65},{65,1},{2,66},{66,2},{3,67},{67,3},{4,68},{68... | collective-permute-start | bytes 1376264 | tf_op jit(solution)/shard_map/ppermute | solution.py:32
  313.1 26.7 %collective-permute-start.12 = (bf16[256,896]{1,0:T(8,128)(2,1)S(1)}, bf16[256,896]{1,0:T(8,128)(2,1)S(1)}, u32[]{:S(2)}, u32[]{:S(2)}) collective-permute-start(bf16[256,896]{1,0:T(8,128)(2,1)S(1)} %get-tuple-element.62), channel_id=1, source_target_pairs={{0,32},{32,0},{1,33},{33,1},{2,34},{34,2},{3,35},{35,3},{4,36},{36... | collective-permute-start | bytes 1376264 | tf_op jit(solution)/shard_map/ppermute | solution.py:32
  313.1 31.6 %collective-permute-start.9 = (bf16[256,1024]{1,0:T(8,128)(2,1)S(1)}, bf16[256,1024]{1,0:T(8,128)(2,1)S(1)}, u32[]{:S(2)}, u32[]{:S(2)}) collective-permute-start(bf16[256,1024]{1,0:T(8,128)(2,1)S(1)} %shard_map.130.refs_4_), channel_id=1, source_target_pairs={{0,32},{32,0},{1,33},{33,1},{2,34},{34,2},{3,35},{35,3},{4,36},{36... | collective-permute-start | bytes 1572872 | tf_op jit(solution)/shard_map/ppermute | solution.py:32
  325.6 19.1 %collective-permute-start.11 = (bf16[256,1024]{1,0:T(8,128)(2,1)S(1)}, bf16[256,1024]{1,0:T(8,128)(2,1)S(1)}, u32[]{:S(2)}, u32[]{:S(2)}) collective-permute-start(bf16[256,1024]{1,0:T(8,128)(2,1)S(1)} %collective-permute-done.10.refs_6_), channel_id=1, source_target_pairs={{0,32},{32,0},{1,33},{33,1},{2,34},{34,2},{3,35},{35,3},{4,36},{36... | collective-permute-start | bytes 1572872 | tf_op jit(solution)/shard_map/ppermute | solution.py:32
  339.8 5.0 %copy-start.8 = (bf16[2,4,112,256]{3,2,1,0:T(8,128)(2,1)S(1)}, bf16[2,4,112,256]{3,2,1,0:T(8,128)(2,1)}, u32[]{:S(2)}) copy-start(bf16[2,4,112,256]{3,2,1,0:T(8,128)(2,1)} %copy.15) | copy-start | bytes 1376260

commit v6 on v5

--- a/solution.py
+++ b/solution.py
@@ -20,6 +20,7 @@
 bf16 = jnp.bfloat16
 LAST = (((1,), (1,)), ((), ()))
 WHOLE = pl.BlockSpec(memory_space=pltpu.VMEM)
+EFFORT = 8
 LIMIT = 24 * 1024 * 1024
 
 
@@ -105,7 +106,7 @@
     return call(
         functools.partial(encode_kernel, share),
         [array((tokens, count)), hbm_array((count, tokens))],
-        2 * tokens * width * count,
+        EFFORT * 2 * tokens * width * count,
         [centered, in_hbm(weight), bias.reshape(1, count)],
         grid=(count // tile,),
         in_specs=[
@@ -121,33 +122,6 @@
     )
 
 
-def gather_kernel(at_ref, *refs):
-    *weights, out_ref, sems = refs
-    count = out_ref.shape[1]
-    at = pl.multiple_of(at_ref[0], count)
-    copies = [
-        pltpu.make_async_copy(w.at[pl.ds(at, count)], out_ref.at[k], sems.at[k])
-        for k, w in enumerate(weights)
-    ]
-    for copy in copies:
-        copy.start()
-    for copy in copies:
-        copy.wait()
-
-
-def rows_of_each(weights, at, count):
-    anywhere = pl.BlockSpec(memory_space=pl.ANY)
-    return call(
-        gather_kernel,
-        hbm_array((len(weights), count, weights[0].shape[1])),
-        0,
-        [at.reshape(1), *(in_hbm(w) for w in weights)],
-        in_specs=[pl.BlockSpec(memory_space=pltpu.SMEM)] + [anywhere] * len(weights),
-        out_specs=anywhere,
-        scratch_shapes=[pltpu.SemaphoreType.DMA((len(weights),))],
-    )
-
-
 def decode_kernel(latents_ref, weight_ref, target_ref, out_ref):
     tile = weight_ref.shape[1]
     step = pl.program_id(0)
@@ -170,7 +144,7 @@
         decode_kernel,
         array((tokens, width + room)),
         2 * tokens * width * count,
-        [latents, in_hbm(weight), turned_target],
+        [latents, weight, turned_target],
         grid=(7,),
         in_specs=[WHOLE, pl.BlockSpec((count, tile), lambda j: (0, j)), WHOLE],
         out_specs=WHOLE,
@@ -284,7 +258,7 @@
         latent_kernel,
         array((tokens, count)),
         2 * tokens * width * count,
-        [rows, weight, latents],
+        [rows, in_hbm(weight), latents],
         grid=(count // tile,),
         in_specs=[
             WHOLE,
@@ -368,7 +342,7 @@
     )
     pieces = jnp.broadcast_to(pair, (lax.axis_size(HALF), *pair.shape))
     pieces, weights_then = lax.optimization_barrier((pieces, weights))
-    sent = rows_of_each(weights_then, at, units)
+    sent = jnp.stack([lax.dynamic_slice_in_dim(w, at, units, axis=0) for w in weights_then])
     near = swap(sent, OTHER_HALF)
     far = swap(near, BATCH[1])
     centered = exchange(pieces, HALF).reshape(width, tokens)
@@ -406,9 +380,7 @@
         [half_of_them, own_rows],
         [to_owners(partial_out, HALF), recon, own_target, gain_out],
     )
-    pieces, latent_blocks, centered_blocks = lax.optimization_barrier(
-        (pieces, latent_blocks, centered_blocks)
-    )
+    pieces, latent_blocks = lax.optimization_barrier((pieces, latent_blocks))
     grad_output = all_tokens(pieces, HALF)
     (partial_input,) = local(
         backward_kernel,
@@ -416,6 +388,7 @@
         [grad_output, *weights, near, far, *saved],
         kept=6,
     )
+    partial_input, centered_blocks = lax.optimization_barrier((partial_input, centered_blocks))
     (pieces,) = local(
         input_kernel, [everyone], [to_owners(partial_input, HALF), recon, grad_result, gain_in]
     )

time: 353 us -> 286 us (0.81)
  Pallas kernels: 118 us -> 44.3 us
  blocking collectives: 73.3 us -> 53.7 us
  waiting for transfers between devices: 104 us -> 118 us
  starting transfers between devices: 35.9 us -> 47.1 us
    pallas_call x11 -> x10, Pallas kernels: 118 us -> 44.3 us  [call(): pl.pallas_call(body, out_shape=outs, cost_estimate=cost, compiler_params=...]
    ppermute x15, waiting for transfers between devices: 41.4 us -> 71.5 us  [swap(): lax.ppermute(block, axes, [(i, for_all - 1 - i) for i in range(for_all)])]
    all_to_all x3 -> x2, blocking collectives: 73.3 us -> 53.7 us  [exchange(): return lax.all_to_all(pieces, axes, split_axis=0, concat_axis=0, tiled=True)]
    all_to_all x4 -> x5, waiting for transfers between devices: 62.7 us -> 46.4 us  [exchange(): return lax.all_to_all(pieces, axes, split_axis=0, concat_axis=0, tiled=True)]
    all_to_all x4 -> x5, starting transfers between devices: 26.5 us -> 36.2 us  [exchange(): return lax.all_to_all(pieces, axes, split_axis=0, concat_axis=0, tiled=True)]
  transfers between devices with their start and end apart: 19 -> 20, of which waited for: 10 -> 10; matrix products, arithmetic and copies ran while one was open for 2% -> 3% of each run, Pallas kernels for 9% -> 12%
where the time goes in v6:
time: 286 us; the launch traced here: 283 us
  waiting for transfers between devices  118 us (41%)
  blocking collectives  53.7 us (19%)
  starting transfers between devices  47.1 us (16%)
  Pallas kernels  44.3 us (15%)
  local copies, waits for them, and re-layouts  14.6 us (5%)
  other arithmetic  4.35 us (2%)
    ppermute x15, waiting for transfers between devices, swap(): lax.ppermute(block, axes, [(i, for_all - 1 - i) for i in range(for_all)])  71.5 us
    all_to_all x2, blocking collectives, exchange(): return lax.all_to_all(pieces, axes, split_axis=0, concat_axis=0, tiled=True)  53.7 us
    all_to_all x5, waiting for transfers between devices, exchange(): return lax.all_to_all(pieces, axes, split_axis=0, concat_axis=0, tiled=True)  46.4 us
    pallas_call x10, Pallas kernels, call(): pl.pallas_call(body, out_shape=outs, cost_estimate=cost, compiler_params=...  44.3 us
    all_to_all x5, starting transfers between devices, exchange(): return lax.all_to_all(pieces, axes, split_axis=0, concat_axis=0, tiled=True)  36.2 us
    ppermute x15, starting transfers between devices, swap(): lax.ppermute(block, axes, [(i, for_all - 1 - i) for i in range(for_all)])  10.8 us
  transfers between devices with their start and end apart: 20, of which 10 were waited for; matrix products, arithmetic and copies ran while one was open for 3% of the time, Pallas kernels for 12%

profile of v6, /device:TPU:14, one launch (start us, length us, event | category | flops | bytes accessed | tf_op | source)
XLA Modules:
  0.0 282.9 jit_solution(11198057100418638202)
XLA Ops:
  0.6 0.8 dynamic-slice_convert_fusion
  1.4 0.9 fusion
  2.3 2.4 collective-permute-start
  4.7 3.4 %collective-permute-done = bf16[112,256]{1,0:T(8,128)(2,1)S(1)} collective-permute-done((bf16[112,256]{1,0:T(8,128)(2,1)S(1)}, bf16[112,256]{1,0:T(8,128)(2,1)S(1)}, u32[]{:S(2)}, u32[]{:S(2)}) %collective-permute-start) | collective-permute-done | bytes 57376 | tf_op jit(solution)/shard_map/ppermute | solution.py:33
  8.1 0.9 select_bitcast_fusion.1
  9.0 1.4 broadcast_in_dim.4
  10.4 8.5 %all-to-all-start = ((bf16[16,2,112,256]{3,2,1,0:T(8,128)(2,1)}), bf16[16,2,112,256]{3,2,1,0:T(8,128)(2,1)}, u32[]{:S(2)}, u32[]{:S(2)}) async-start(bf16[16,2,112,256]{3,2,1,0:T(8,128)(2,1)} %broadcast_in_dim.4), calls=%async_computation | async-start | bytes 3670016 | tf_op jit(solution)/shard_map/all_to_all | solution.py:28
  19.1 1.3 copy-done.2
  20.5 1.8 pad_maximum_fusion
  22.3 1.6 collective-permute-start.1
  23.8 18.4 %all-to-all-done = bf16[16,2,112,256]{3,2,1,0:T(8,128)(2,1)} async-done(((bf16[16,2,112,256]{3,2,1,0:T(8,128)(2,1)}), bf16[16,2,112,256]{3,2,1,0:T(8,128)(2,1)}, u32[]{:S(2)}, u32[]{:S(2)}) %all-to-all-start) | async-done | bytes 1835040 | tf_op jit(solution)/shard_map/all_to_all | solution.py:28
  42.3 7.5 %shard_map.122 = (bf16[256,1024]{1,0:T(8,128)(2,1)S(1)}, bf16[1024,256]{1,0:T(8,128)(2,1)}) custom-call(bf16[3584,256]{1,0:T(8,128)(2,1)} %bitcast.5.centered_ref, bf16[3584,1024]{1,0:T(8,128)(2,1)} %weight_ref.3, bf16[1,1024]{1,0:T(2,128)(2,1)S(1)} %reshape.66.bias_ref), custom_call_target="tpu_custom_call" | custom-call | flops 15032385536 | bytes 10225664 | tf_op jit(solution)/shard_map/pallas_call | solution.py:52
  49.8 3.7 %shard_map.123 = bf16[256,3712]{1,0:T(8,128)(2,1)S(1)} custom-call(bf16[256,1024]{1,0:T(8,128)(2,1)S(1)} %get-tuple-element.33.latents_ref, bf16[1024,3584]{1,0:T(8,128)(2,1)S(1)} %bitcast.43, bf16[112,256]{1,0:T(8,128)(2,1)S(1)} %bitcast.55), custom_call_target="tpu_custom_call" | custom-call | flops 1879048192 | bytes 9822208 | tf_op jit(solution)/shard_map/pallas_call | solution.py:52
  53.5 1.3 copy-done.5
  54.8 7.7 %all-to-all-start.1 = ((bf16[32,8,3712]{2,1,0:T(8,128)(2,1)}), bf16[32,8,3712]{2,1,0:T(8,128)(2,1)}, u32[]{:S(2)}, u32[]{:S(2)}) async-start(bf16[32,8,3712]{2,1,0:T(8,128)(2,1)} %bitcast.52), calls=%async_computation.1 | async-start | bytes 3801088 | tf_op jit(solution)/shard_map/all_to_all | solution.py:28
  62.5 32.7 %collective-permute-done.1.near_ref = bf16[3,112,3584]{2,1,0:T(8,128)(2,1)} collective-permute-done((bf16[3,112,3584]{2,1,0:T(8,128)(2,1)}, bf16[3,112,3584]{2,1,0:T(8,128)(2,1)}, u32[]{:S(2)}, u32[]{:S(2)}) %collective-permute-start.1) | collective-permute-done | bytes 2408480 | tf_op jit(solution)/shard_map/ppermute | solution.py:33
  95.3 2.9 %shard_map.124 = (bf16[16,8,3584]{2,1,0:T(8,128)(2,1)}, f32[8,3584]{1,0:T(8,128)S(1)}) custom-call(bf16[32,8,3712]{2,1,0:T(8,128)(2,1)} %all-to-all-done.1.pieces_ref, bf16[1,3584]{1,0:T(2,128)(2,1)S(1)} %reshape.68.bias_ref, bf16[1,3584]{1,0:T(2,128)(2,1)S(1)} %reshape.69.gain_ref), custom_call_target="tpu_custom_call" | custom-call | bytes 2947072 | tf_op jit(solution)/shard_map/pallas_call | solution.py:52
  98.3 7.2 %all-to-all-start.2 = ((bf16[16,8,3584]{2,1,0:T(8,128)(2,1)}), bf16[16,8,3584]{2,1,0:T(8,128)(2,1)}, u32[]{:S(2)}, u32[]{:S(2)}) async-start(bf16[16,8,3584]{2,1,0:T(8,128)(2,1)} %get-tuple-element.36), calls=%async_computation.2 | async-start | bytes 1835008 | tf_op jit(solution)/shard_map/all_to_all | solution.py:28
  105.5 1.7 collective-permute-start.4
  107.2 13.1 %all-to-all-done.2 = bf16[16,8,3584]{2,1,0:T(8,128)(2,1)} async-done(((bf16[16,8,3584]{2,1,0:T(8,128)(2,1)}), bf16[16,8,3584]{2,1,0:T(8,128)(2,1)}, u32[]{:S(2)}, u32[]{:S(2)}) %all-to-all-start.2) | async-done | bytes 917536 | tf_op jit(solution)/shard_map/all_to_all | solution.py:28
  120.3 1.4 copy-done.3
  121.7 6.6 %shard_map.125 = (bf16[128,3584]{1,0:T(8,128)(2,1)}, f32[128,224]{1,0:T(8,128)}, f32[128,224]{1,0:T(8,128)}, f32[128,112]{1,0:T(8,128)}, f32[128,112]{1,0:T(8,12...) custom-call(bf16[128,3584]{1,0:T(8,128)(2,1)} %bitcast.8.rows_ref, bf16[224,3584]{1,0:T(8,128)(2,1)S(1)} %bitcast.47, ...), custom_call_target="tpu_custom_call" | custom-call | bytes 11927552 | tf_op jit(solution)/shard_map/pallas_call | solution.py:52
  128.3 6.6 %all-to-all-start.3 = ((bf16[16,8,3584]{2,1,0:T(8,128)(2,1)}), bf16[16,8,3584]{2,1,0:T(8,128)(2,1)}, u32[]{:S(2)}, u32[]{:S(2)}) async-start(bf16[16,8,3584]{2,1,0:T(8,128)(2,1)} %bitcast.60), calls=%async_computation.3 | async-start | bytes 1835008 | tf_op jit(solution)/shard_map/all_to_all | solution.py:28
  135.3 0.8 slice_bitcast_fusion
  136.8 1.0 reshape.72.target_ref
  137.8 9.8 %all-to-all-done.3.pieces_ref = bf16[16,8,3584]{2,1,0:T(8,128)(2,1)} async-done(((bf16[16,8,3584]{2,1,0:T(8,128)(2,1)}), bf16[16,8,3584]{2,1,0:T(8,128)(2,1)}, u32[]{:S(2)}, u32[]{:S(2)}) %all-to-all-start.3) | async-done | bytes 917536 | tf_op jit(solution)/shard_map/all_to_all | solution.py:28
  147.6 2.5 shard_map.126
  150.1 6.3 %all-to-all-start.4 = ((bf16[16,8,3584]{2,1,0:T(8,128)(2,1)}), bf16[16,8,3584]{2,1,0:T(8,128)(2,1)}, u32[]{:S(2)}, u32[]{:S(2)}) async-start(bf16[16,8,3584]{2,1,0:T(8,128)(2,1)} %get-tuple-element.44), calls=%async_computation.4 | async-start | bytes 1835008 | tf_op jit(solution)/shard_map/all_to_all | solution.py:28
  156.4 1.6 constant_dynamic-slice_fusion.4
  158.0 0.8 copy.18
  158.8 0.8 copy.17
  159.6 0.8 copy.16
  160.4 1.7 collective-permute-start.7
  162.3 0.8 copy.15
  163.1 5.1 %all-to-all-done.4 = bf16[16,8,3584]{2,1,0:T(8,128)(2,1)} async-done(((bf16[16,8,3584]{2,1,0:T(8,128)(2,1)}), bf16[16,8,3584]{2,1,0:T(8,128)(2,1)}, u32[]{:S(2)}, u32[]{:S(2)}) %all-to-all-start.4) | async-done | bytes 917536 | tf_op jit(solution)/shard_map/all_to_all | solution.py:28
  168.2 1.4 copy-done.4
  169.7 5.5 %shard_map.127 = bf16[128,3584]{1,0:T(8,128)(2,1)S(1)} custom-call(bf16[128,3584]{1,0:T(8,128)(2,1)} %bitcast.14.rows_ref, bf16[224,3584]{1,0:T(8,128)(2,1)S(1)} %bitcast.48, bf16[224,3584]{1,0:T(8,128)(2,1)S(1)} %bitcast.51, bf16[224,3584]{1,0:T(8,128)(2,1)S(1)} %copy-done.4, bf16[3,112,3584]{2,1,0:T(8,128)(2,1)} %collective-permute-done.1.near_ref, ...), custom_call_target="tpu_custom_call" | custom-call | bytes 11927552 | tf_op jit(solution)/shard_map/pallas_call | solution.py:52
  175.2 7.9 %collective-permute-done.8.refs_3_ = bf16[896,256]{1,0:T(8,128)(2,1)} collective-permute-done((bf16[896,256]{1,0:T(8,128)(2,1)}, bf16[896,256]{1,0:T(8,128)(2,1)}, u32[]{:S(2)}, u32[]{:S(2)}) %collective-permute-start.8) | collective-permute-done | bytes 458784 | tf_op jit(solution)/shard_map/ppermute | solution.py:33
  183.1 21.0 %all_to_all.35.pieces_ref = bf16[16,8,3584]{2,1,0:T(8,128)(2,1)S(1)} all-to-all(bf16[16,8,3584]{2,1,0:T(8,128)(2,1)S(1)} %bitcast.53), channel_id=1, replica_groups=mesh['batch_0'=2,'batch_1'=2,'tensor_0'=4,'tensor_1'=2,'latent'=4] {'ten..., dimensions={0} | all-to-all | bytes 1835008 | tf_op jit(solution)/shard_map/all_to_all | solution.py:28
  204.5 32.8 %all_to_all.36 = bf16[32,8,3584]{2,1,0:T(8,128)(2,1)S(1)} all-to-all(bf16[32,8,3584]{2,1,0:T(8,128)(2,1)S(1)} %shard_map.128), channel_id=1, replica_groups=mesh['batch_0'=2,'batch_1'=2,'tensor_0'=4,'tensor_1'=2,'latent'=4] {'ten..., dimensions={0} | all-to-all | bytes 3670016 | tf_op jit(solution)/shard_map/all_to_all | solution.py:28
  237.2 5.2 %shard_map.129.refs_4_ = bf16[256,1024]{1,0:T(8,128)(2,1)S(1)} custom-call(bf16[256,3584]{1,0:T(8,128)(2,1)S(1)} %bitcast.44, bf16[1024,3584]{1,0:T(8,128)(2,1)} %weight_ref.5, bf16[256,1024]{1,0:T(8,128)(2,1)S(1)} %copy-done.7), custom_call_target="tpu_custom_call" | custom-call | flops 1879048192 | bytes 10223616 | tf_op jit(solution)/shard_map/pallas_call | solution.py:52
  242.5 0.9 collective-permute-start.10
  243.6 1.3 collective-permute-start.13
  245.4 12.0 %collective-permute-done.10.refs_6_ = bf16[256,1024]{1,0:T(8,128)(2,1)S(1)} collective-permute-done((bf16[256,1024]{1,0:T(8,128)(2,1)S(1)}, bf16[256,1024]{1,0:T(8,128)(2,1)S(1)}, u32[]{:S(2)}, u32[]{:S(2)}) %collective-permute-start.10) | collective-permute-done | bytes 524320 | tf_op jit(solution)/shard_map/ppermute | solution.py:33
  257.4 8.1 %collective-permute-done.14.refs_7_ = bf16[256,896]{1,0:T(8,128)(2,1)S(1)} collective-permute-done((bf16[256,896]{1,0:T(8,128)(2,1)S(1)}, bf16[256,896]{1,0:T(8,128)(2,1)S(1)}, u32[]{:S(2)}, u32[]{:S(2)}) %collective-permute-start.14) | collective-permute-done | bytes 458784 | tf_op jit(solution)/shard_map/ppermute | solution.py:33
  265.5 7.4 %collective-permute-done.13.refs_6_ = bf16[256,896]{1,0:T(8,128)(2,1)S(1)} collective-permute-done((bf16[256,896]{1,0:T(8,128)(2,1)S(1)}, bf16[256,896]{1,0:T(8,128)(2,1)S(1)}, u32[]{:S(2)}, u32[]{:S(2)}) %collective-permute-start.13) | collective-permute-done | bytes 458784 | tf_op jit(solution)/shard_map/ppermute | solution.py:33
  272.9 5.0 %shard_map.131 = bf16[1024,896]{1,0:T(8,128)(2,1)} custom-call(bf16[1024,256]{1,0:T(8,128)(2,1)S(1)} %copy-done.10, bf16[1024,256]{1,0:T(8,128)(2,1)} %collective-permute-done.3.refs_1_, bf16[1024,256]{1,0:T(8,128)(2,1)} %collective-permute-done.4.refs_2_, bf16[1024,256]{1,0:T(8,128)(2,1)} %collective-permute-done.5.refs_3_, ...), custom_call_target="tpu_custom_call" | custom-call | flops 1879048192 | bytes 5767168 | tf_op jit(solution)/shard_map/pallas_call | solution.py:52
  277.9 5.0 %shard_map.130 = bf16[896,1024]{1,0:T(8,128)(2,1)} custom-call(bf16[896,256]{1,0:T(8,128)(2,1)S(1)} %bitcast.54, bf16[896,256]{1,0:T(8,128)(2,1)} %collective-permute-done.6.refs_1_, bf16[896,256]{1,0:T(8,128)(2,1)} %collective-permute-done.7.refs_2_, bf16[896,256]{1,0:T(8,128)(2,1)} %collective-permute-done.8.refs_3_, ...), custom_call_target="tpu_custom_call" | custom-call | flops 1879048192 | bytes 5767168 | tf_op jit(solution)/shard_map/pallas_call | solution.py:52
  (60 shorter events, 2.7 us)
Async XLA Ops:
  2.3 5.8 %collective-permute-start = (bf16[112,256]{1,0:T(8,128)(2,1)S(1)}, bf16[112,256]{1,0:T(8,128)(2,1)S(1)}, u32[]{:S(2)}, u32[]{:S(2)}) collective-permute-start(bf16[112,256]{1,0:T(8,128)(2,1)S(1)} %fusion), channel_id=1, source_target_pairs={{0,4},{4,0},{1,5},{5,1},{2,6},{6,2},{3,7},{7,3},{8,12},{12,8},{9,1... | collective-permute-start | bytes 172040 | tf_op jit(solution)/shard_map/ppermute | solution.py:33
  10.4 8.5 %copy-start = (bf16[3584,224]{0,1:T(8,128)(2,1)S(1)}, bf16[3584,224]{0,1:T(8,128)(2,1)}, u32[]{:S(2)}) copy-start(bf16[3584,224]{0,1:T(8,128)(2,1)} %param.19) | copy-start | bytes 4816900
  10.4 8.6 %copy-start.1 = (bf16[3584,224]{0,1:T(8,128)(2,1)S(1)}, bf16[3584,224]{0,1:T(8,128)(2,1)}, u32[]{:S(2)}) copy-start(bf16[3584,224]{0,1:T(8,128)(2,1)} %param.20) | copy-start | bytes 4816900
  10.4 31.9 %all-to-all-start = ((bf16[16,2,112,256]{3,2,1,0:T(8,128)(2,1)}), bf16[16,2,112,256]{3,2,1,0:T(8,128)(2,1)}, u32[]{:S(2)}, u32[]{:S(2)}) async-start(bf16[16,2,112,256]{3,2,1,0:T(8,128)(2,1)} %broadcast_in_dim.4), calls=%async_computation | async-start | bytes 3670016 | tf_op jit(solution)/shard_map/all_to_all | solution.py:28
  19.0 1.4 copy-start.2
  20.5 3.4 %copy-start.14 = (bf16[1024]{0:T(1024)(128)(2,1)S(1)}, bf16[1024]{0:T(1024)(128)(2,1)}, u32[]{:S(2)}) copy-start(bf16[1024]{0:T(1024)(128)(2,1)} %param.14) | copy-start | bytes 6148
  22.3 73.0 %collective-permute-start.1 = (bf16[3,112,3584]{2,1,0:T(8,128)(2,1)}, bf16[3,112,3584]{2,1,0:T(8,128)(2,1)}, u32[]{:S(2)}, u32[]{:S(2)}) collective-permute-start(bf16[3,112,3584]{2,1,0:T(8,128)(2,1)} %pad_maximum_fusion), channel_id=1, source_target_pairs={{0,68},{4,64},{64,4},{68,0},{1,69},{5,65},{65,5},{69,1},{2,70},{6,... | collective-permute-start | bytes 7225352 | tf_op jit(solution)/shard_map/ppermute | solution.py:33
  42.3 7.5 %slice-start = ((s8[7340032]{0:T(1024)(128)(4,1)}), s8[4194304]{0:T(1024)(128)(4,1)S(1)}, s32[]{:S(2)}) async-start(s8[7340032]{0:T(1024)(128)(4,1)} %bitcast.42), calls=%async_computation.7 | async-start | bytes 8388608
  42.3 7.5 %slice-start.1 = ((s8[7340032]{0:T(1024)(128)(4,1)}), s8[3145728]{0:T(1024)(128)(4,1)S(1)}, s32[]{:S(2)}) async-start(s8[7340032]{0:T(1024)(128)(4,1)} %bitcast.42), calls=%async_computation.8 | async-start | bytes 6291456
  42.3 7.5 %copy-start.9 = (bf16[256,112]{0,1:T(8,128)(2,1)S(1)}, bf16[256,112]{0,1:T(8,128)(2,1)}, u32[]{:S(2)}) copy-start(bf16[256,112]{0,1:T(8,128)(2,1)} %param.12) | copy-start | bytes 172036
  49.8 3.7 %copy-start.6 = (bf16[256,1024]{1,0:T(8,128)(2,1)}, bf16[256,1024]{1,0:T(8,128)(2,1)S(1)}, u32[]{:S(2)}) copy-start(bf16[256,1024]{1,0:T(8,128)(2,1)S(1)} %get-tuple-element.33.latents_ref) | copy-start | bytes 1572868
  53.5 1.3 copy-start.5
  54.8 40.4 %copy-start.11 = (bf16[3584]{0:T(1024)(128)(2,1)S(1)}, bf16[3584]{0:T(1024)(128)(2,1)}, u32[]{:S(2)}) copy-start(bf16[3584]{0:T(1024)(128)(2,1)} %param.16) | copy-start | bytes 21508
  54.8 40.5 %copy-start.12 = (bf16[3584]{0:T(1024)(128)(2,1)S(1)}, bf16[3584]{0:T(1024)(128)(2,1)}, u32[]{:S(2)}) copy-start(bf16[3584]{0:T(1024)(128)(2,1)} %param.17) | copy-start | bytes 21508
  54.8 40.5 %all-to-all-start.1 = ((bf16[32,8,3712]{2,1,0:T(8,128)(2,1)}), bf16[32,8,3712]{2,1,0:T(8,128)(2,1)}, u32[]{:S(2)}, u32[]{:S(2)}) async-start(bf16[32,8,3712]{2,1,0:T(8,128)(2,1)} %bitcast.52), calls=%async_computation.1 | async-start | bytes 3801088 | tf_op jit(solution)/shard_map/all_to_all | solution.py:28
  95.3 25.0 %collective-permute-start.2 = (bf16[3,112,3584]{2,1,0:T(8,128)(2,1)}, bf16[3,112,3584]{2,1,0:T(8,128)(2,1)}, u32[]{:S(2)}, u32[]{:S(2)}) collective-permute-start(bf16[3,112,3584]{2,1,0:T(8,128)(2,1)} %collective-permute-done.1.near_ref), channel_id=1, source_target_pairs={{0,32},{32,0},{1,33},{33,1},{2,34},{34,2},{3,35},{35,3},{4,36},{36... | collective-permute-start | bytes 7225352 | tf_op jit(solution)/shard_map/ppermute | solution.py:33
  98.3 22.0 %all-to-all-start.2 = ((bf16[16,8,3584]{2,1,0:T(8,128)(2,1)}), bf16[16,8,3584]{2,1,0:T(8,128)(2,1)}, u32[]{:S(2)}, u32[]{:S(2)}) async-start(bf16[16,8,3584]{2,1,0:T(8,128)(2,1)} %get-tuple-element.36), calls=%async_computation.2 | async-start | bytes 1835008 | tf_op jit(solution)/shard_map/all_to_all | solution.py:28
  105.5 29.4 %collective-permute-start.4 = (bf16[1024,256]{1,0:T(8,128)(2,1)}, bf16[1024,256]{1,0:T(8,128)(2,1)}, u32[]{:S(2)}, u32[]{:S(2)}) collective-permute-start(bf16[1024,256]{1,0:T(8,128)(2,1)} %get-tuple-element.58.refs_0_), channel_id=1, source_target_pairs={{0,64},{64,0},{1,65},{65,1},{2,66},{66,2},{3,67},{67,3},{4,68},{68... | collective-permute-start | bytes 1572872 | tf_op jit(solution)/shard_map/ppermute | solution.py:33
  120.3 1.4 copy-start.3
  128.3 7.1 %copy-start.13 = (bf16[3584]{0:T(1024)(128)(2,1)S(1)}, bf16[3584]{0:T(1024)(128)(2,1)}, u32[]{:S(2)}) copy-start(bf16[3584]{0:T(1024)(128)(2,1)} %param.18) | copy-start | bytes 21508
  128.3 19.3 %all-to-all-start.3 = ((bf16[16,8,3584]{2,1,0:T(8,128)(2,1)}), bf16[16,8,3584]{2,1,0:T(8,128)(2,1)}, u32[]{:S(2)}, u32[]{:S(2)}) async-start(bf16[16,8,3584]{2,1,0:T(8,128)(2,1)} %bitcast.60), calls=%async_computation.3 | async-start | bytes 1835008 | tf_op jit(solution)/shard_map/all_to_all | solution.py:28
  134.8 15.3 %collective-permute-start.3 = (bf16[1024,256]{1,0:T(8,128)(2,1)}, bf16[1024,256]{1,0:T(8,128)(2,1)}, u32[]{:S(2)}, u32[]{:S(2)}) collective-permute-start(bf16[1024,256]{1,0:T(8,128)(2,1)} %get-tuple-element.58.refs_0_), channel_id=1, source_target_pairs={{0,32},{32,0},{1,33},{33,1},{2,34},{34,2},{3,35},{35,3},{4,36},{36... | collective-permute-start | bytes 1572872 | tf_op jit(solution)/shard_map/ppermute | solution.py:33
  134.8 15.3 %collective-permute-start.5 = (bf16[1024,256]{1,0:T(8,128)(2,1)}, bf16[1024,256]{1,0:T(8,128)(2,1)}, u32[]{:S(2)}, u32[]{:S(2)}) collective-permute-start(bf16[1024,256]{1,0:T(8,128)(2,1)} %collective-permute-done.4.refs_2_), channel_id=1, source_target_pairs={{0,32},{32,0},{1,33},{33,1},{2,34},{34,2},{3,35},{35,3},{4,36},{36... | collective-permute-start | bytes 1572872 | tf_op jit(solution)/shard_map/ppermute | solution.py:33
  150.1 18.1 %all-to-all-start.4 = ((bf16[16,8,3584]{2,1,0:T(8,128)(2,1)}), bf16[16,8,3584]{2,1,0:T(8,128)(2,1)}, u32[]{:S(2)}, u32[]{:S(2)}) async-start(bf16[16,8,3584]{2,1,0:T(8,128)(2,1)} %get-tuple-element.44), calls=%async_computation.4 | async-start | bytes 1835008 | tf_op jit(solution)/shard_map/all_to_all | solution.py:28
  160.4 14.8 %collective-permute-start.6 = (bf16[896,256]{1,0:T(8,128)(2,1)}, bf16[896,256]{1,0:T(8,128)(2,1)}, u32[]{:S(2)}, u32[]{:S(2)}) collective-permute-start(bf16[896,256]{1,0:T(8,128)(2,1)} %bitcast.20), channel_id=1, source_target_pairs={{0,32},{32,0},{1,33},{33,1},{2,34},{34,2},{3,35},{35,3},{4,36},{36... | collective-permute-start | bytes 1376264 | tf_op jit(solution)/shard_map/ppermute | solution.py:33
  160.4 14.8 %collective-permute-start.7 = (bf16[896,256]{1,0:T(8,128)(2,1)}, bf16[896,256]{1,0:T(8,128)(2,1)}, u32[]{:S(2)}, u32[]{:S(2)}) collective-permute-start(bf16[896,256]{1,0:T(8,128)(2,1)} %bitcast.23), channel_id=1, source_target_pairs={{0,64},{64,0},{1,65},{65,1},{2,66},{66,2},{3,67},{67,3},{4,68},{68... | collective-permute-start | bytes 1376264 | tf_op jit(solution)/shard_map/ppermute | solution.py:33
  162.1 21.0 %collective-permute-start.8 = (bf16[896,256]{1,0:T(8,128)(2,1)}, bf16[896,256]{1,0:T(8,128)(2,1)}, u32[]{:S(2)}, u32[]{:S(2)}) collective-permute-start(bf16[896,256]{1,0:T(8,128)(2,1)} %bitcast.26), channel_id=1, source_target_pairs={{0,96},{32,64},{64,32},{96,0},{1,97},{33,65},{65,33},{97,1},{2,98}... | collective-permute-start | bytes 1376264 | tf_op jit(solution)/shard_map/ppermute | solution.py:33
  168.2 1.4 copy-start.4
  204.5 32.8 %copy-start.7 = (bf16[256,1024]{1,0:T(8,128)(2,1)S(1)}, bf16[256,1024]{1,0:T(8,128)(2,1)}, u32[]{:S(2)}) copy-start(bf16[256,1024]{1,0:T(8,128)(2,1)} %copy-done.6) | copy-start | bytes 1572868
  242.5 30.5 %copy-start.10 = (bf16[1024,256]{1,0:T(8,128)(2,1)S(1)}, bf16[1024,256]{1,0:T(8,128)(2,1)}, u32[]{:S(2)}) copy-start(bf16[1024,256]{1,0:T(8,128)(2,1)} %get-tuple-element.58.refs_0_) | copy-start | bytes 1572868
  242.5 14.9 %collective-permute-start.10 = (bf16[256,1024]{1,0:T(8,128)(2,1)S(1)}, bf16[256,1024]{1,0:T(8,128)(2,1)S(1)}, u32[]{:S(2)}, u32[]{:S(2)}) collective-permute-start(bf16[256,1024]{1,0:T(8,128)(2,1)S(1)} %shard_map.129.refs_4_), channel_id=1, source_target_pairs={{0,64},{64,0},{1,65},{65,1},{2,66},{66,2},{3,67},{67,3},{4,68},{68... | collective-permute-start | bytes 1572872 | tf_op jit(solution)/shard_map/ppermute | solution.py:33
  243.5 22.1 %collective-permute-start.14 = (bf16[256,896]{1,0:T(8,128)(2,1)S(1)}, bf16[256,896]{1,0:T(8,128)(2,1)S(1)}, u32[]{:S(2)}, u32[]{:S(2)}) collective-permute-start(bf16[256,896]{1,0:T(8,128)(2,1)S(1)} %get-tuple-element.62), channel_id=1, source_target_pairs={{0,96},{32,64},{64,32},{96,0},{1,97},{33,65},{65,33},{97,1},{2,98}... | collective-permute-start | bytes 1376264 | tf_op jit(solution)/shard_map/ppermute | solution.py:33
  243.6 29.3 %collective-permute-start.13 = (bf16[256,896]{1,0:T(8,128)(2,1)S(1)}, bf16[256,896]{1,0:T(8,128)(2,1)S(1)}, u32[]{:S(2)}, u32[]{:S(2)}) collective-permute-start(bf16[256,896]{1,0:T(8,128)(2,1)S(1)} %get-tuple-element.63), channel_id=1, source_target_pairs={{0,64},{64,0},{1,65},{65,1},{2,66},{66,2},{3,67},{67,3},{4,68},{68... | collective-permute-start | bytes 1376264 | tf_op jit(solution)/shard_map/ppermute | solution.py:33
  244.9 28.0 %collective-permute-start.12 = (bf16[256,896]{1,0:T(8,128)(2,1)S(1)}, bf16[256,896]{1,0:T(8,128)(2,1)S(1)}, u32[]{:S(2)}, u32[]{:S(2)}) collective-permute-start(bf16[256,896]{1,0:T(8,128)(2,1)S(1)} %get-tuple-element.64), channel_id=1, source_target_pairs={{0,32},{32,0},{1,33},{33,1},{2,34},{34,2},{3,35},{35,3},{4,36},{36... | collective-permute-start | bytes 1376264 | tf_op jit(solution)/shard_map/ppermute | solution.py:33
  245.4 32.5 %collective-permute-start.9 = (bf16[256,1024]{1,0:T(8,128)(2,1)S(1)}, bf16[256,1024]{1,0:T(8,128)(2,1)S(1)}, u32[]{:S(2)}, u32[]{:S(2)}) collective-permute-start(bf16[256,1024]{1,0:T(8,128)(2,1)S(1)} %shard_map.129.refs_4_), channel_id=1, source_target_pairs={{0,32},{32,0},{1,33},{33,1},{2,34},{34,2},{3,35},{35,3},{4,36},{36... | collective-permute-start | bytes 1572872 | tf_op jit(solution)/shard_map/ppermute | solution.py:33
  257.4 20.5 %collective-permute-start.11 = (bf16[256,1024]{1,0:T(8,128)(2,1)S(1)}, bf16[256,1024]{1,0:T(8,128)(2,1)S(1)}, u32[]{:S(2)}, u32[]{:S(2)}) collective-permute-start(bf16[256,1024]{1,0:T(8,128)(2,1)S(1)} %collective-permute-done.10.refs_6_), channel_id=1, source_target_pairs={{0,32},{32,0},{1,33},{33,1},{2,34},{34,2},{3,35},{35,3},{4,36},{36... | collective-permute-start | bytes 1572872 | tf_op jit(solution)/shard_map/ppermute | solution.py:33
  272.9 5.0 %copy-start.8 = (bf16[2,4,112,256]{3,2,1,0:T(8,128)(2,1)S(1)}, bf16[2,4,112,256]{3,2,1,0:T(8,128)(2,1)}, u32[]{:S(2)}) copy-start(bf16[2,4,112,256]{3,2,1,0:T(8,128)(2,1)} %copy.15) | copy-start | bytes 1376260

commit v7 on v6

--- a/solution.py
+++ b/solution.py
@@ -12,6 +12,7 @@
 SHARDS = ("tensor_0", "tensor_1", "latent")
 BATCH = ("batch_0", "batch_1")
 HALF = ("tensor_0", "latent")
+OWNERS = ("tensor_0", "latent", "tensor_1")
 OTHER_HALF = ("batch_0", "tensor_1")
 
 epsilon = 1e-06
@@ -78,21 +79,13 @@
     return lax.dot_general(left, right, LAST, preferred_element_type=f32)
 
 
-def encode_kernel(share, centered_ref, weight_ref, bias_ref, latents_ref, turned_ref, rows_ref):
-    width = rows_ref.shape[1]
+def encode_kernel(centered_ref, weight_ref, bias_ref, latents_ref, turned_ref, rows_ref):
+    width = centered_ref.shape[0]
 
     @pl.when(pl.program_id(0) == 0)
     def _():
         for at in range(0, width, 256):
-            runs, f = [], at
-            while f < at + 256:
-                shard, inside = divmod(f, share)
-                far, half, near = shard // 8, shard // 4 % 2, shard % 4
-                run = min(share - inside, at + 256 - f)
-                start = (far * 8 + near * 2 + half) * share + inside
-                runs.append(centered_ref[start : start + run, :])
-                f += run
-            rows_ref[:, at : at + 256] = jnp.concatenate(runs, axis=0).T
+            rows_ref[:, at : at + 256] = centered_ref[at : at + 256, :].T
 
     preact = product(rows_ref[...], weight_ref[...]) + bias_ref[...].astype(f32)
     latents = jnp.maximum(preact, 0.0).astype(bf16)
@@ -100,11 +93,11 @@
     turned_ref[...] = latents.T
 
 
-def encode(centered, weight, bias, share, tile):
+def encode(centered, weight, bias, tile):
     width, tokens = centered.shape
     count = weight.shape[1]
     return call(
-        functools.partial(encode_kernel, share),
+        encode_kernel,
         [array((tokens, count)), hbm_array((count, tokens))],
         EFFORT * 2 * tokens * width * count,
         [centered, in_hbm(weight), bias.reshape(1, count)],
@@ -167,8 +160,23 @@
     return jnp.sum(values, axis=1, keepdims=True) / values.shape[1]
 
 
-def recon_kernel(pieces_ref, bias_ref, gain_ref, out_ref, recon_ref):
-    recon = total_of(pieces_ref, recon_ref.shape[1]) + bias_ref[...].astype(f32)
+def halves_kernel(side_ref, pieces_ref, sum_ref, target_ref, sent_ref):
+    rows, width = sum_ref.shape
+    count = pieces_ref.shape[0]
+    first = side_ref[0] == 0
+    total = total_of(pieces_ref, width)
+    sum_ref[...] = jnp.where(first, total[:rows], total[rows:])
+    sent_ref[:, :width] = jnp.where(first, total[rows:], total[:rows]).astype(bf16)
+    for k in range(count):
+        piece = pieces_ref[k, :, width:].astype(f32)
+        target_ref[k] = jnp.where(first, piece[:rows], piece[rows:]).astype(bf16)
+        other = jnp.where(first, piece[rows:], piece[:rows]).astype(bf16)
+        sent_ref[:, width + 128 * k : width + 128 * (k + 1)] = other
+
+
+def recon_kernel(sum_ref, partner_ref, bias_ref, gain_ref, out_ref, recon_ref):
+    partner = partner_ref[:, : recon_ref.shape[1]].astype(f32)
+    recon = sum_ref[...] + partner + bias_ref[...].astype(f32)
     recon_ref[...] = recon
     scale_in = lax.rsqrt(mean_of(recon * recon) + epsilon)
     send_to_all(out_ref, (recon * scale_in * gain_ref[...].astype(f32)).astype(bf16))
@@ -258,7 +266,7 @@
         latent_kernel,
         array((tokens, count)),
         2 * tokens * width * count,
-        [rows, in_hbm(weight), latents],
+        [rows, weight, latents],
         grid=(count // tile,),
         in_specs=[
             WHOLE,
@@ -269,29 +277,33 @@
     )
 
 
-def products_kernel(spans, *refs):
-    count = len(refs) // 2
+def products_kernel(spans, count, *refs):
     out_ref = refs[-1]
     for span in spans:
-        total = product(refs[0][...], refs[count][:, span])
-        for k in range(1, count):
-            total += product(refs[k][...], refs[count + k][:, span])
-        out_ref[:, span] = total.astype(bf16)
-
-
-def sum_of_products(left, right, tile):
+        total = refs[2 * count][:, span] if len(refs) > 2 * count + 1 else None
+        for k in range(count):
+            term = product(refs[k][...], refs[count + k][:, span])
+            total = term if total is None else total + term
+        out_ref[:, span] = total.astype(out_ref.dtype)
+
+
+def sum_of_products(left, right, tile, rows_tile=None, start=None, kind=bf16):
     rows, depth = left[0].shape
     columns = right[0].shape[1]
+    rows_tile = rows_tile or rows
     spans = [slice(at, min(at + 256, tile)) for at in range(0, tile, 256)]
+    count = len(left)
+    out_spec = pl.BlockSpec((rows_tile, tile), lambda i, j: (i, j))
     return call(
-        functools.partial(products_kernel, spans),
-        array((rows, columns)),
-        2 * rows * depth * columns * len(left),
-        [*left, *right],
-        grid=(columns // tile,),
-        in_specs=[pl.BlockSpec((rows, depth), lambda j: (0, 0))] * len(left)
-        + [pl.BlockSpec((depth, tile), lambda j: (0, j))] * len(right),
-        out_specs=pl.BlockSpec((rows, tile), lambda j: (0, j)),
+        functools.partial(products_kernel, spans, count),
+        array((rows, columns), kind),
+        2 * rows * depth * columns * count,
+        [*map(in_hbm, left), *right, *([] if start is None else [start])],
+        grid=(rows // rows_tile, columns // tile),
+        in_specs=[pl.BlockSpec((rows_tile, depth), lambda i, j: (i, 0))] * count
+        + [pl.BlockSpec((depth, tile), lambda i, j: (0, j))] * count
+        + ([] if start is None else [out_spec]),
+        out_specs=out_spec,
     )
 
 
@@ -335,38 +347,46 @@
 
     bias_share = lax.dynamic_slice_in_dim(decoder_bias.astype(f32), offset, share_width)
     centered_share = (residual.astype(f32) - bias_share).astype(bf16).T
-    partner = swap(centered_share, SHARDS[1])
-    first = lax.axis_index(SHARDS[1]) == 0
-    pair = jnp.stack(
-        [jnp.where(first, centered_share, partner), jnp.where(first, partner, centered_share)]
-    )
-    pieces = jnp.broadcast_to(pair, (lax.axis_size(HALF), *pair.shape))
+    pieces = jnp.broadcast_to(centered_share, (shards, share_width, tokens))
     pieces, weights_then = lax.optimization_barrier((pieces, weights))
     sent = jnp.stack([lax.dynamic_slice_in_dim(w, at, units, axis=0) for w in weights_then])
     near = swap(sent, OTHER_HALF)
     far = swap(near, BATCH[1])
-    centered = exchange(pieces, HALF).reshape(width, tokens)
-
-    latents, turned_latents = encode(
-        centered, encoder_weight, encoder_bias, share_width, 256
-    )
+    centered = exchange(pieces, SHARDS).reshape(width, tokens)
+
+    latents, turned_latents = encode(centered, encoder_weight, encoder_bias, 256)
     partial_recon = decode(latents, decoder_weight, target.T, 128)
 
-    pieces = to_owners(partial_recon, SHARDS)
-    own_target = pieces[:, :, width : width + share_width]
-    own_target = jnp.moveaxis(own_target, 0, 1).reshape(own_tokens, width)
-    pieces, recon = local(recon_kernel, [half_of_them, own_rows], [pieces, bias, gain_in])
+    pieces = exchange(partial_recon.reshape(half, 2 * own_tokens, -1), HALF)
+    side = lax.axis_index(SHARDS[1]).reshape(1)
+    own_sum, own_targets, sent = call(
+        halves_kernel,
+        [
+            array((own_tokens, width), f32),
+            hbm_array((half, own_tokens, 128)),
+            array((own_tokens, width + half * 128)),
+        ],
+        0,
+        [side, pieces],
+        in_specs=[pl.BlockSpec(memory_space=pltpu.SMEM), WHOLE],
+    )
+    partner = swap(sent, SHARDS[1])
+    pieces, recon = local(
+        recon_kernel, [half_of_them, own_rows], [own_sum, partner, bias, gain_in]
+    )
+    partner_targets = partner[:, width:].reshape(own_tokens, half, 128)
+    targets = jnp.stack([jnp.moveaxis(own_targets, 0, 1), partner_targets], axis=2)
+    targets = jnp.where(side[0] == 0, targets, jnp.flip(targets, 2))[..., :share_width]
+    targets = targets.reshape(own_tokens, *(lax.axis_size(a) for a in OWNERS), share_width)
+    own_target = jnp.swapaxes(targets, 2, 3).reshape(own_tokens, width)
 
     pieces, centered, turned_latents = lax.optimization_barrier((pieces, centered, turned_latents))
     normed_input = all_tokens(pieces, HALF)
     latent_blocks = copies_of_all(turned_latents)
 
-    def feature_block(b):
-        part = lax.dynamic_slice_in_dim(centered, b * block, block, axis=0)
-        part = part.reshape(lax.axis_size(SHARDS[2]), lax.axis_size(SHARDS[1]), share_width, tokens)
-        return jnp.swapaxes(part, 0, 1).reshape(block, tokens)
-
-    centered_blocks = blocks_of_all(feature_block)
+    centered_blocks = blocks_of_all(
+        lambda b: lax.dynamic_slice_in_dim(centered, b * block, block, axis=0)
+    )
     rows = half * own_tokens
     saved = [hbm_array((rows, n), f32) for n in (2 * units, 2 * units, units, units, units, units)]
     partial_out, *saved = local(
@@ -380,26 +400,32 @@
         [half_of_them, own_rows],
         [to_owners(partial_out, HALF), recon, own_target, gain_out],
     )
-    pieces, latent_blocks = lax.optimization_barrier((pieces, latent_blocks))
+    pieces, latent_blocks, centered_blocks[:3] = lax.optimization_barrier(
+        (pieces, latent_blocks, centered_blocks[:3])
+    )
     grad_output = all_tokens(pieces, HALF)
     (partial_input,) = local(
         backward_kernel,
         [array((rows, width))],
         [grad_output, *weights, near, far, *saved],
-        kept=6,
-    )
-    partial_input, centered_blocks = lax.optimization_barrier((partial_input, centered_blocks))
+        kept=11,
+    )
+    partial_input, centered_blocks[3] = lax.optimization_barrier(
+        (partial_input, centered_blocks[3])
+    )
     (pieces,) = local(
         input_kernel, [everyone], [to_owners(partial_input, HALF), recon, grad_result, gain_in]
     )
-    grad_recon = all_tokens(pieces, SHARDS)
+    grad_recon = all_tokens(pieces, OWNERS)
 
     recon_blocks = blocks_of_all(
         lambda b: lax.dynamic_slice_in_dim(grad_recon, b * block, block, axis=1)
     )
     grad_preact = grad_of_preact(grad_recon, decoder_weight, latents, 256)
+    part = sum_of_products(latent_blocks[:3], recon_blocks[:3], block, kind=f32)
     encoder_grad = sum_of_products(centered_blocks, copies_of_all(grad_preact), 256)
-    decoder_grad = sum_of_products(latent_blocks, recon_blocks, block)
+    part, encoder_grad = lax.optimization_barrier((part, encoder_grad))
+    decoder_grad = sum_of_products(latent_blocks[3:], recon_blocks[3:], block, 256, part)
     return encoder_grad, decoder_grad
 
 

time: 286 us -> 267 us (0.934)
  blocking collectives: 53.7 us -> 47.7 us
  local copies, waits for them, and re-layouts: 14.6 us -> 9.6 us
  waiting for transfers between devices: 118 us -> 114 us
    ppermute x15, waiting for transfers between devices: 71.5 us -> 61.9 us  [swap(): lax.ppermute(block, axes, [(i, for_all - 1 - i) for i in range(for_all)])]
    all_to_all x2, blocking collectives: 53.7 us -> 47.7 us  [exchange(): return lax.all_to_all(pieces, axes, split_axis=0, concat_axis=0, tiled=True)]
    all_to_all x5, waiting for transfers between devices: 46.4 us -> 51.9 us  [exchange(): return lax.all_to_all(pieces, axes, split_axis=0, concat_axis=0, tiled=True)]
    transpose x6 -> x0, local copies, waits for them, and re-layouts: 4.74 us -> none  [the longest x4 3.26 us: feature_block(): return jnp.swapaxes(part, 0, 1).reshape(block, tokens)]
    pallas_call x10 -> x12, Pallas kernels: 44.3 us -> 44.9 us  [call(): pl.pallas_call(body, out_shape=outs, cost_estimate=cost, compiler_params=...]
  transfers between devices with their start and end apart: 20 -> 20, of which waited for: 10 -> 9; matrix products, arithmetic and copies ran while one was open for 3% -> 2% of each run, Pallas kernels for 12% -> 14%
where the time goes in v7:
time: 267 us; the launch traced here: 266 us
  waiting for transfers between devices  114 us (43%)
  blocking collectives  47.7 us (18%)
  starting transfers between devices  45.5 us (17%)
  Pallas kernels  44.9 us (17%)
  local copies, waits for them, and re-layouts  9.6 us (4%)
  other arithmetic  3.42 us (1%)
    ppermute x15, waiting for transfers between devices, swap(): lax.ppermute(block, axes, [(i, for_all - 1 - i) for i in range(for_all)])  61.9 us
    all_to_all x5, waiting for transfers between devices, exchange(): return lax.all_to_all(pieces, axes, split_axis=0, concat_axis=0, tiled=True)  51.9 us
    all_to_all x2, blocking collectives, exchange(): return lax.all_to_all(pieces, axes, split_axis=0, concat_axis=0, tiled=True)  47.7 us
    pallas_call x12, Pallas kernels, call(): pl.pallas_call(body, out_shape=outs, cost_estimate=cost, compiler_params=...  44.9 us
    all_to_all x5, starting transfers between devices, exchange(): return lax.all_to_all(pieces, axes, split_axis=0, concat_axis=0, tiled=True)  37.3 us
    ppermute x15, starting transfers between devices, swap(): lax.ppermute(block, axes, [(i, for_all - 1 - i) for i in range(for_all)])  8.24 us
  transfers between devices with their start and end apart: 20, of which 9 were waited for; matrix products, arithmetic and copies ran while one was open for 2% of the time, Pallas kernels for 14%

profile of v7, /device:TPU:14, one launch (start us, length us, event | category | flops | bytes accessed | tf_op | source)
XLA Modules:
  0.0 266.0 jit_solution(13541910088872453096)
XLA Ops:
  0.6 0.8 dynamic-slice_convert_fusion
  1.4 0.9 fusion.2
  2.3 1.3 broadcast_in_dim.4
  3.7 10.5 %all-to-all-start = ((bf16[32,112,256]{2,1,0:T(8,128)(2,1)}), bf16[32,112,256]{2,1,0:T(8,128)(2,1)}, u32[]{:S(2)}, u32[]{:S(2)}) async-start(bf16[32,112,256]{2,1,0:T(8,128)(2,1)} %broadcast_in_dim.4), calls=%async_computation | async-start | bytes 3670016 | tf_op jit(solution)/shard_map/all_to_all | solution.py:29
  14.3 1.3 copy-done.2
  15.6 0.1 dynamic-slice_bitcast_fusion
  15.7 1.7 pad_maximum_fusion
  17.5 2.3 collective-permute-start.1
  19.7 18.9 %all-to-all-done = bf16[32,112,256]{2,1,0:T(8,128)(2,1)} async-done(((bf16[32,112,256]{2,1,0:T(8,128)(2,1)}), bf16[32,112,256]{2,1,0:T(8,128)(2,1)}, u32[]{:S(2)}, u32[]{:S(2)}) %all-to-all-start) | async-done | bytes 1835040 | tf_op jit(solution)/shard_map/all_to_all | solution.py:29
  38.7 7.5 %shard_map.122 = (bf16[256,1024]{1,0:T(8,128)(2,1)S(1)}, bf16[1024,256]{1,0:T(8,128)(2,1)}) custom-call(bf16[3584,256]{1,0:T(8,128)(2,1)} %bitcast.4.centered_ref, bf16[3584,1024]{1,0:T(8,128)(2,1)} %weight_ref.3, bf16[1,1024]{1,0:T(2,128)(2,1)S(1)} %reshape.49.bias_ref), custom_call_target="tpu_custom_call" | custom-call | flops 15032385536 | bytes 10225664 | tf_op jit(solution)/shard_map/pallas_call | solution.py:53
  46.2 3.7 %shard_map.123 = bf16[256,3712]{1,0:T(8,128)(2,1)S(1)} custom-call(bf16[256,1024]{1,0:T(8,128)(2,1)S(1)} %get-tuple-element.38.latents_ref, bf16[1024,3584]{1,0:T(8,128)(2,1)S(1)} %bitcast.29, bf16[112,256]{1,0:T(8,128)(2,1)S(1)} %bitcast.42), custom_call_target="tpu_custom_call" | custom-call | flops 1879048192 | bytes 9822208 | tf_op jit(solution)/shard_map/pallas_call | solution.py:53
  49.9 1.3 copy-done.4
  51.3 6.8 %all-to-all-start.1 = ((bf16[16,16,3712]{2,1,0:T(8,128)(2,1)}), bf16[16,16,3712]{2,1,0:T(8,128)(2,1)}, u32[]{:S(2)}, u32[]{:S(2)}) async-start(bf16[16,16,3712]{2,1,0:T(8,128)(2,1)} %bitcast.40), calls=%async_computation.1 | async-start | bytes 3801088 | tf_op jit(solution)/shard_map/all_to_all | solution.py:29
  58.1 31.3 %collective-permute-done.1.near_ref = bf16[3,112,3584]{2,1,0:T(8,128)(2,1)} collective-permute-done((bf16[3,112,3584]{2,1,0:T(8,128)(2,1)}, bf16[3,112,3584]{2,1,0:T(8,128)(2,1)}, u32[]{:S(2)}, u32[]{:S(2)}) %collective-permute-start.1) | collective-permute-done | bytes 2408480 | tf_op jit(solution)/shard_map/ppermute | solution.py:34
  89.3 2.1 shard_map.124
  91.5 6.5 %collective-permute-done.partner_ref = bf16[8,5632]{1,0:T(8,128)(2,1)S(1)} collective-permute-done((bf16[8,5632]{1,0:T(8,128)(2,1)S(1)}, bf16[8,5632]{1,0:T(8,128)(2,1)S(1)}, u32[]{:S(2)}, u32[]{:S(2)}) %collective-permute-start) | collective-permute-done | bytes 90144 | tf_op jit(solution)/shard_map/ppermute | solution.py:34
  98.0 1.1 shard_map.125
  99.1 6.6 %all-to-all-start.2 = ((bf16[16,8,3584]{2,1,0:T(8,128)(2,1)}), bf16[16,8,3584]{2,1,0:T(8,128)(2,1)}, u32[]{:S(2)}, u32[]{:S(2)}) async-start(bf16[16,8,3584]{2,1,0:T(8,128)(2,1)} %get-tuple-element.43), calls=%async_computation.2 | async-start | bytes 1835008 | tf_op jit(solution)/shard_map/all_to_all | solution.py:29
  105.7 1.3 collective-permute-start.4
  107.0 12.4 %all-to-all-done.2 = bf16[16,8,3584]{2,1,0:T(8,128)(2,1)} async-done(((bf16[16,8,3584]{2,1,0:T(8,128)(2,1)}), bf16[16,8,3584]{2,1,0:T(8,128)(2,1)}, u32[]{:S(2)}, u32[]{:S(2)}) %all-to-all-start.2) | async-done | bytes 917536 | tf_op jit(solution)/shard_map/all_to_all | solution.py:29
  119.5 1.4 copy-done.3
  120.9 6.6 %shard_map.126 = (bf16[128,3584]{1,0:T(8,128)(2,1)}, f32[128,224]{1,0:T(8,128)}, f32[128,224]{1,0:T(8,128)}, f32[128,112]{1,0:T(8,128)}, f32[128,112]{1,0:T(8,12...) custom-call(bf16[128,3584]{1,0:T(8,128)(2,1)} %bitcast.7.rows_ref, bf16[224,3584]{1,0:T(8,128)(2,1)S(1)} %bitcast.36, ...), custom_call_target="tpu_custom_call" | custom-call | bytes 11927552 | tf_op jit(solution)/shard_map/pallas_call | solution.py:53
  127.5 6.0 %all-to-all-start.3 = ((bf16[16,8,3584]{2,1,0:T(8,128)(2,1)}), bf16[16,8,3584]{2,1,0:T(8,128)(2,1)S(1)}, u32[]{:S(2)}, u32[]{:S(2)}) async-start(bf16[16,8,3584]{2,1,0:T(8,128)(2,1)} %bitcast.43), calls=%async_computation.3 | async-start | bytes 1835008 | tf_op jit(solution)/shard_map/all_to_all | solution.py:29
  133.6 2.6 constant_dynamic-slice_fusion.4
  136.2 0.5 collective-permute-start.6
  136.7 1.3 collective-permute-start.7
  138.1 0.1 reshape.56.target_ref
  138.2 7.3 %all-to-all-done.3.pieces_ref = bf16[16,8,3584]{2,1,0:T(8,128)(2,1)S(1)} async-done(((bf16[16,8,3584]{2,1,0:T(8,128)(2,1)}), bf16[16,8,3584]{2,1,0:T(8,128)(2,1)S(1)}, u32[]{:S(2)}, u32[]{:S(2)}) %all-to-all-start.3) | async-done | bytes 917536 | tf_op jit(solution)/shard_map/all_to_all | solution.py:29
  145.5 1.4 shard_map.127
  146.9 2.3 collective-permute-done.7.refs_2_
  149.3 0.8 copy-done.10
  150.0 0.2 copy-done.9
  150.2 7.5 %all-to-all-start.4 = ((bf16[16,8,3584]{2,1,0:T(8,128)(2,1)}), bf16[16,8,3584]{2,1,0:T(8,128)(2,1)}, u32[]{:S(2)}, u32[]{:S(2)}) async-start(bf16[16,8,3584]{2,1,0:T(8,128)(2,1)} %get-tuple-element.56), calls=%async_computation.4 | async-start | bytes 1835008 | tf_op jit(solution)/shard_map/all_to_all | solution.py:29
  157.7 13.2 %all-to-all-done.4 = bf16[16,8,3584]{2,1,0:T(8,128)(2,1)} async-done(((bf16[16,8,3584]{2,1,0:T(8,128)(2,1)}), bf16[16,8,3584]{2,1,0:T(8,128)(2,1)}, u32[]{:S(2)}, u32[]{:S(2)}) %all-to-all-start.4) | async-done | bytes 917536 | tf_op jit(solution)/shard_map/all_to_all | solution.py:29
  170.9 7.0 %shard_map.128 = bf16[128,3584]{1,0:T(8,128)(2,1)S(1)} custom-call(bf16[128,3584]{1,0:T(8,128)(2,1)} %bitcast.17.rows_ref, bf16[224,3584]{1,0:T(8,128)(2,1)} %bitcast.34, bf16[224,3584]{1,0:T(8,128)(2,1)} %bitcast.37, bf16[224,3584]{1,0:T(8,128)(2,1)} %down_ref.3, bf16[3,112,3584]{2,1,0:T(8,128)(2,1)} %collective-permute-done.1.near_ref, ...), custom_call_target="tpu_custom_call" | custom-call | bytes 11927552 | tf_op jit(solution)/shard_map/pallas_call | solution.py:53
  177.9 17.3 %all_to_all.35.pieces_ref = bf16[16,8,3584]{2,1,0:T(8,128)(2,1)S(1)} all-to-all(bf16[16,8,3584]{2,1,0:T(8,128)(2,1)S(1)} %bitcast.41), channel_id=1, replica_groups=mesh['batch_0'=2,'batch_1'=2,'tensor_0'=4,'tensor_1'=2,'latent'=4] {'ten..., dimensions={0} | all-to-all | bytes 1835008 | tf_op jit(solution)/shard_map/all_to_all | solution.py:29
  195.3 0.4 shard_map.129
  195.7 30.4 %all_to_all.36 = bf16[32,8,3584]{2,1,0:T(8,128)(2,1)S(1)} all-to-all(bf16[32,8,3584]{2,1,0:T(8,128)(2,1)S(1)} %shard_map.129), channel_id=1, replica_groups=mesh['batch_0'=2,'batch_1'=2,'tensor_0'=4,'tensor_1'=2,'latent'=4] {'ten..., dimensions={0} | all-to-all | bytes 3670016 | tf_op jit(solution)/shard_map/all_to_all | solution.py:29
  226.1 2.9 %shard_map.131.refs_4_ = bf16[256,1024]{1,0:T(8,128)(2,1)S(1)} custom-call(bf16[256,3584]{1,0:T(8,128)(2,1)S(1)} %bitcast.32, bf16[1024,3584]{1,0:T(8,128)(2,1)S(1)} %bitcast.31, bf16[256,1024]{1,0:T(8,128)(2,1)S(1)} %copy-done.6), custom_call_target="tpu_custom_call" | custom-call | flops 1879048192 | bytes 10223616 | tf_op jit(solution)/shard_map/pallas_call | solution.py:53
  229.1 0.2 constant_dynamic-slice_fusion
  229.3 2.1 collective-permute-start.10
  231.3 0.5 collective-permute-start.11
  231.8 12.1 %collective-permute-done.12.refs_6_ = bf16[256,1024]{1,0:T(8,128)(2,1)S(1)} collective-permute-done((bf16[256,1024]{1,0:T(8,128)(2,1)S(1)}, bf16[256,1024]{1,0:T(8,128)(2,1)S(1)}, u32[]{:S(2)}, u32[]{:S(2)}) %collective-permute-start.12) | collective-permute-done | bytes 524320 | tf_op jit(solution)/shard_map/ppermute | solution.py:34
  243.9 0.1 collective-permute-start.14
  244.1 9.7 %collective-permute-done.10.refs_5_ = bf16[256,896]{1,0:T(8,128)(2,1)S(1)} collective-permute-done((bf16[256,896]{1,0:T(8,128)(2,1)S(1)}, bf16[256,896]{1,0:T(8,128)(2,1)S(1)}, u32[]{:S(2)}, u32[]{:S(2)}) %collective-permute-start.10) | collective-permute-done | bytes 458784 | tf_op jit(solution)/shard_map/ppermute | solution.py:34
  253.8 3.1 %shard_map.130.refs_2_ = f32[1024,896]{1,0:T(8,128)S(1)} custom-call(bf16[1024,256]{1,0:T(8,128)(2,1)} %get-tuple-element.53.refs_0_, bf16[1024,256]{1,0:T(8,128)(2,1)} %copy-done.10, bf16[1024,256]{1,0:T(8,128)(2,1)} %collective-permute-done.4.refs_2_, bf16[256,896]{1,0:T(8,128)(2,1)S(1)} %get-tuple-element.75.refs_3_, ...), custom_call_target="tpu_custom_call" | custom-call | flops 1409286144 | bytes 6619136 | tf_op jit(solution)/shard_map/pallas_call | solution.py:53
  256.9 5.1 %shard_map.132 = bf16[896,1024]{1,0:T(8,128)(2,1)} custom-call(bf16[896,256]{1,0:T(8,128)(2,1)} %get-tuple-element.65.refs_0_, bf16[896,256]{1,0:T(8,128)(2,1)} %collective-permute-done.6.refs_1_, bf16[896,256]{1,0:T(8,128)(2,1)} %collective-permute-done.7.refs_2_, bf16[896,256]{1,0:T(8,128)(2,1)} %collective-permute-done.8.refs_3_, ...), custom_call_target="tpu_custom_call" | custom-call | flops 1879048192 | bytes 5767168 | tf_op jit(solution)/shard_map/pallas_call | solution.py:53
  262.1 4.0 %shard_map.133 = bf16[1024,896]{1,0:T(8,128)(2,1)} custom-call(bf16[1024,256]{1,0:T(8,128)(2,1)} %copy-done.9, bf16[256,896]{1,0:T(8,128)(2,1)S(1)} %collective-permute-done.14.refs_1_, f32[1024,896]{1,0:T(8,128)S(1)} %shard_map.130.refs_2_), custom_call_target="tpu_custom_call" | custom-call | flops 469762048 | bytes 6488064 | tf_op jit(solution)/shard_map/pallas_call | solution.py:53
  (66 shorter events, 0.4 us)
Async XLA Ops:
  3.7 10.5 %copy-start = (bf16[3584,224]{0,1:T(8,128)(2,1)S(1)}, bf16[3584,224]{0,1:T(8,128)(2,1)}, u32[]{:S(2)}) copy-start(bf16[3584,224]{0,1:T(8,128)(2,1)} %param.19) | copy-start | bytes 4816900
  3.7 10.6 %copy-start.1 = (bf16[3584,224]{0,1:T(8,128)(2,1)S(1)}, bf16[3584,224]{0,1:T(8,128)(2,1)}, u32[]{:S(2)}) copy-start(bf16[3584,224]{0,1:T(8,128)(2,1)} %param.20) | copy-start | bytes 4816900
  3.7 35.0 %all-to-all-start = ((bf16[32,112,256]{2,1,0:T(8,128)(2,1)}), bf16[32,112,256]{2,1,0:T(8,128)(2,1)}, u32[]{:S(2)}, u32[]{:S(2)}) async-start(bf16[32,112,256]{2,1,0:T(8,128)(2,1)} %broadcast_in_dim.4), calls=%async_computation | async-start | bytes 3670016 | tf_op jit(solution)/shard_map/all_to_all | solution.py:29
  14.2 1.4 copy-start.2
  15.7 4.0 %copy-start.15 = (bf16[1024]{0:T(1024)(128)(2,1)S(1)}, bf16[1024]{0:T(1024)(128)(2,1)}, u32[]{:S(2)}) copy-start(bf16[1024]{0:T(1024)(128)(2,1)} %param.14) | copy-start | bytes 6148
  17.5 71.9 %collective-permute-start.1 = (bf16[3,112,3584]{2,1,0:T(8,128)(2,1)}, bf16[3,112,3584]{2,1,0:T(8,128)(2,1)}, u32[]{:S(2)}, u32[]{:S(2)}) collective-permute-start(bf16[3,112,3584]{2,1,0:T(8,128)(2,1)} %pad_maximum_fusion), channel_id=1, source_target_pairs={{0,68},{4,64},{64,4},{68,0},{1,69},{5,65},{65,5},{69,1},{2,70},{6,... | collective-permute-start | bytes 7225352 | tf_op jit(solution)/shard_map/ppermute | solution.py:34
  38.7 7.5 %slice-start = ((s8[7340032]{0:T(1024)(128)(4,1)}), s8[4194304]{0:T(1024)(128)(4,1)S(1)}, s32[]{:S(2)}) async-start(s8[7340032]{0:T(1024)(128)(4,1)} %bitcast.28), calls=%async_computation.7 | async-start | bytes 8388608
  38.7 7.5 %slice-start.1 = ((s8[7340032]{0:T(1024)(128)(4,1)}), s8[3145728]{0:T(1024)(128)(4,1)S(1)}, s32[]{:S(2)}) async-start(s8[7340032]{0:T(1024)(128)(4,1)} %bitcast.28), calls=%async_computation.8 | async-start | bytes 6291456
  38.7 7.5 %copy-start.7 = (bf16[256,112]{0,1:T(8,128)(2,1)S(1)}, bf16[256,112]{0,1:T(8,128)(2,1)}, u32[]{:S(2)}) copy-start(bf16[256,112]{0,1:T(8,128)(2,1)} %param.12) | copy-start | bytes 172036
  46.2 3.7 %copy-start.5 = (bf16[256,1024]{1,0:T(8,128)(2,1)}, bf16[256,1024]{1,0:T(8,128)(2,1)S(1)}, u32[]{:S(2)}) copy-start(bf16[256,1024]{1,0:T(8,128)(2,1)S(1)} %get-tuple-element.38.latents_ref) | copy-start | bytes 1572868
  49.9 1.3 copy-start.4
  51.3 38.1 %all-to-all-start.1 = ((bf16[16,16,3712]{2,1,0:T(8,128)(2,1)}), bf16[16,16,3712]{2,1,0:T(8,128)(2,1)}, u32[]{:S(2)}, u32[]{:S(2)}) async-start(bf16[16,16,3712]{2,1,0:T(8,128)(2,1)} %bitcast.40), calls=%async_computation.1 | async-start | bytes 3801088 | tf_op jit(solution)/shard_map/all_to_all | solution.py:29
  58.0 33.4 %copy-start.12 = (bf16[3584]{0:T(1024)(128)(2,1)S(1)}, bf16[3584]{0:T(1024)(128)(2,1)}, u32[]{:S(2)}) copy-start(bf16[3584]{0:T(1024)(128)(2,1)} %param.16) | copy-start | bytes 21508
  58.1 33.4 %copy-start.13 = (bf16[3584]{0:T(1024)(128)(2,1)S(1)}, bf16[3584]{0:T(1024)(128)(2,1)}, u32[]{:S(2)}) copy-start(bf16[3584]{0:T(1024)(128)(2,1)} %param.17) | copy-start | bytes 21508
  89.3 30.1 %collective-permute-start.2 = (bf16[3,112,3584]{2,1,0:T(8,128)(2,1)}, bf16[3,112,3584]{2,1,0:T(8,128)(2,1)}, u32[]{:S(2)}, u32[]{:S(2)}) collective-permute-start(bf16[3,112,3584]{2,1,0:T(8,128)(2,1)} %collective-permute-done.1.near_ref), channel_id=1, source_target_pairs={{0,32},{32,0},{1,33},{33,1},{2,34},{34,2},{3,35},{35,3},{4,36},{36... | collective-permute-start | bytes 7225352 | tf_op jit(solution)/shard_map/ppermute | solution.py:34
  91.5 6.5 %collective-permute-start = (bf16[8,5632]{1,0:T(8,128)(2,1)S(1)}, bf16[8,5632]{1,0:T(8,128)(2,1)S(1)}, u32[]{:S(2)}, u32[]{:S(2)}) collective-permute-start(bf16[8,5632]{1,0:T(8,128)(2,1)S(1)} %get-tuple-element.40), channel_id=1, source_target_pairs={{0,4},{4,0},{1,5},{5,1},{2,6},{6,2},{3,7},{7,3},{8,12},{12,8},{9,1... | collective-permute-start | bytes 270344 | tf_op jit(solution)/shard_map/ppermute | solution.py:34
  99.1 20.3 %all-to-all-start.2 = ((bf16[16,8,3584]{2,1,0:T(8,128)(2,1)}), bf16[16,8,3584]{2,1,0:T(8,128)(2,1)}, u32[]{:S(2)}, u32[]{:S(2)}) async-start(bf16[16,8,3584]{2,1,0:T(8,128)(2,1)} %get-tuple-element.43), calls=%async_computation.2 | async-start | bytes 1835008 | tf_op jit(solution)/shard_map/all_to_all | solution.py:29
  105.7 32.2 %collective-permute-start.4 = (bf16[1024,256]{1,0:T(8,128)(2,1)}, bf16[1024,256]{1,0:T(8,128)(2,1)}, u32[]{:S(2)}, u32[]{:S(2)}) collective-permute-start(bf16[1024,256]{1,0:T(8,128)(2,1)} %get-tuple-element.53.refs_0_), channel_id=1, source_target_pairs={{0,64},{64,0},{1,65},{65,1},{2,66},{66,2},{3,67},{67,3},{4,68},{68... | collective-permute-start | bytes 1572872 | tf_op jit(solution)/shard_map/ppermute | solution.py:34
  119.5 1.4 copy-start.3
  127.4 6.0 %copy-start.14 = (bf16[3584]{0:T(1024)(128)(2,1)S(1)}, bf16[3584]{0:T(1024)(128)(2,1)}, u32[]{:S(2)}) copy-start(bf16[3584]{0:T(1024)(128)(2,1)} %param.18) | copy-start | bytes 21508
  127.4 6.0 %copy-start.8 = (bf16[1024,256]{1,0:T(8,128)(2,1)S(1)}, bf16[1024,256]{1,0:T(8,128)(2,1)}, u32[]{:S(2)}) copy-start(bf16[1024,256]{1,0:T(8,128)(2,1)} %get-tuple-element.53.refs_0_) | copy-start | bytes 1572868
  127.5 18.1 %all-to-all-start.3 = ((bf16[16,8,3584]{2,1,0:T(8,128)(2,1)}), bf16[16,8,3584]{2,1,0:T(8,128)(2,1)S(1)}, u32[]{:S(2)}, u32[]{:S(2)}) async-start(bf16[16,8,3584]{2,1,0:T(8,128)(2,1)} %bitcast.43), calls=%async_computation.3 | async-start | bytes 1835008 | tf_op jit(solution)/shard_map/all_to_all | solution.py:29
  133.5 4.5 %copy-start.11 = (bf16[16,8,128]{2,1,0:T(8,128)(2,1)S(1)}, bf16[16,8,128]{2,1,0:T(8,128)(2,1)}, u32[]{:S(2)}) copy-start(bf16[16,8,128]{2,1,0:T(8,128)(2,1)} %get-tuple-element.49) | copy-start | bytes 98308
  133.5 15.8 %collective-permute-start.3 = (bf16[1024,256]{1,0:T(8,128)(2,1)S(1)}, bf16[1024,256]{1,0:T(8,128)(2,1)S(1)}, u32[]{:S(2)}, u32[]{:S(2)}) collective-permute-start(bf16[1024,256]{1,0:T(8,128)(2,1)S(1)} %copy-done.8), channel_id=1, source_target_pairs={{0,32},{32,0},{1,33},{33,1},{2,34},{34,2},{3,35},{35,3},{4,36},{36... | collective-permute-start | bytes 1572872 | tf_op jit(solution)/shard_map/ppermute | solution.py:34
  136.2 10.7 %collective-permute-start.6 = (bf16[896,256]{1,0:T(8,128)(2,1)}, bf16[896,256]{1,0:T(8,128)(2,1)}, u32[]{:S(2)}, u32[]{:S(2)}) collective-permute-start(bf16[896,256]{1,0:T(8,128)(2,1)} %get-tuple-element.78), channel_id=1, source_target_pairs={{0,32},{32,0},{1,33},{33,1},{2,34},{34,2},{3,35},{35,3},{4,36},{36... | collective-permute-start | bytes 1376264 | tf_op jit(solution)/shard_map/ppermute | solution.py:34
  136.7 12.6 %collective-permute-start.7 = (bf16[896,256]{1,0:T(8,128)(2,1)S(1)}, bf16[896,256]{1,0:T(8,128)(2,1)}, u32[]{:S(2)}, u32[]{:S(2)}) collective-permute-start(bf16[896,256]{1,0:T(8,128)(2,1)S(1)} %get-tuple-element.77), channel_id=1, source_target_pairs={{0,64},{64,0},{1,65},{65,1},{2,66},{66,2},{3,67},{67,3},{4,68},{68... | collective-permute-start | bytes 1376264 | tf_op jit(solution)/shard_map/ppermute | solution.py:34
  138.0 11.3 %collective-permute-start.5 = (bf16[1024,256]{1,0:T(8,128)(2,1)}, bf16[1024,256]{1,0:T(8,128)(2,1)S(1)}, u32[]{:S(2)}, u32[]{:S(2)}) collective-permute-start(bf16[1024,256]{1,0:T(8,128)(2,1)} %collective-permute-done.4.refs_2_), channel_id=1, source_target_pairs={{0,32},{32,0},{1,33},{33,1},{2,34},{34,2},{3,35},{35,3},{4,36},{36... | collective-permute-start | bytes 1572872 | tf_op jit(solution)/shard_map/ppermute | solution.py:34
  149.2 0.8 copy-start.10
  149.2 1.0 copy-start.9
  150.2 75.9 %slice-start.2 = ((s8[7340032]{0:T(1024)(128)(4,1)}), s8[3145728]{0:T(1024)(128)(4,1)S(1)}, s32[]{:S(2)}) async-start(s8[7340032]{0:T(1024)(128)(4,1)} %bitcast.30), calls=%async_computation.9 | async-start | bytes 6291456
  150.2 20.7 %all-to-all-start.4 = ((bf16[16,8,3584]{2,1,0:T(8,128)(2,1)}), bf16[16,8,3584]{2,1,0:T(8,128)(2,1)}, u32[]{:S(2)}, u32[]{:S(2)}) async-start(bf16[16,8,3584]{2,1,0:T(8,128)(2,1)} %get-tuple-element.56), calls=%async_computation.4 | async-start | bytes 1835008 | tf_op jit(solution)/shard_map/all_to_all | solution.py:29
  157.7 20.2 %collective-permute-start.8 = (bf16[896,256]{1,0:T(8,128)(2,1)}, bf16[896,256]{1,0:T(8,128)(2,1)}, u32[]{:S(2)}, u32[]{:S(2)}) collective-permute-start(bf16[896,256]{1,0:T(8,128)(2,1)} %get-tuple-element.76), channel_id=1, source_target_pairs={{0,96},{32,64},{64,32},{96,0},{1,97},{33,65},{65,33},{97,1},{2,98}... | collective-permute-start | bytes 1376264 | tf_op jit(solution)/shard_map/ppermute | solution.py:34
  170.9 55.2 %slice-start.3 = ((s8[7340032]{0:T(1024)(128)(4,1)}), s8[4194304]{0:T(1024)(128)(4,1)S(1)}, s32[]{:S(2)}) async-start(s8[7340032]{0:T(1024)(128)(4,1)} %bitcast.30), calls=%async_computation.10 | async-start | bytes 8388608
  195.7 30.4 %copy-start.6 = (bf16[256,1024]{1,0:T(8,128)(2,1)S(1)}, bf16[256,1024]{1,0:T(8,128)(2,1)}, u32[]{:S(2)}) copy-start(bf16[256,1024]{1,0:T(8,128)(2,1)} %copy-done.5) | copy-start | bytes 1572868
  229.0 14.9 %collective-permute-start.12 = (bf16[256,1024]{1,0:T(8,128)(2,1)S(1)}, bf16[256,1024]{1,0:T(8,128)(2,1)S(1)}, u32[]{:S(2)}, u32[]{:S(2)}) collective-permute-start(bf16[256,1024]{1,0:T(8,128)(2,1)S(1)} %shard_map.131.refs_4_), channel_id=1, source_target_pairs={{0,64},{64,0},{1,65},{65,1},{2,66},{66,2},{3,67},{67,3},{4,68},{68... | collective-permute-start | bytes 1572872 | tf_op jit(solution)/shard_map/ppermute | solution.py:34
  229.3 24.5 %collective-permute-start.10 = (bf16[256,896]{1,0:T(8,128)(2,1)S(1)}, bf16[256,896]{1,0:T(8,128)(2,1)S(1)}, u32[]{:S(2)}, u32[]{:S(2)}) collective-permute-start(bf16[256,896]{1,0:T(8,128)(2,1)S(1)} %get-tuple-element.73), channel_id=1, source_target_pairs={{0,64},{64,0},{1,65},{65,1},{2,66},{66,2},{3,67},{67,3},{4,68},{68... | collective-permute-start | bytes 1376264 | tf_op jit(solution)/shard_map/ppermute | solution.py:34
  231.3 22.4 %collective-permute-start.9 = (bf16[256,896]{1,0:T(8,128)(2,1)S(1)}, bf16[256,896]{1,0:T(8,128)(2,1)S(1)}, u32[]{:S(2)}, u32[]{:S(2)}) collective-permute-start(bf16[256,896]{1,0:T(8,128)(2,1)S(1)} %get-tuple-element.74), channel_id=1, source_target_pairs={{0,32},{32,0},{1,33},{33,1},{2,34},{34,2},{3,35},{35,3},{4,36},{36... | collective-permute-start | bytes 1376264 | tf_op jit(solution)/shard_map/ppermute | solution.py:34
  231.3 25.6 %collective-permute-start.11 = (bf16[256,1024]{1,0:T(8,128)(2,1)S(1)}, bf16[256,1024]{1,0:T(8,128)(2,1)S(1)}, u32[]{:S(2)}, u32[]{:S(2)}) collective-permute-start(bf16[256,1024]{1,0:T(8,128)(2,1)S(1)} %shard_map.131.refs_4_), channel_id=1, source_target_pairs={{0,32},{32,0},{1,33},{33,1},{2,34},{34,2},{3,35},{35,3},{4,36},{36... | collective-permute-start | bytes 1572872 | tf_op jit(solution)/shard_map/ppermute | solution.py:34
  243.9 13.0 %collective-permute-start.13 = (bf16[256,1024]{1,0:T(8,128)(2,1)S(1)}, bf16[256,1024]{1,0:T(8,128)(2,1)S(1)}, u32[]{:S(2)}, u32[]{:S(2)}) collective-permute-start(bf16[256,1024]{1,0:T(8,128)(2,1)S(1)} %collective-permute-done.12.refs_6_), channel_id=1, source_target_pairs={{0,32},{32,0},{1,33},{33,1},{2,34},{34,2},{3,35},{35,3},{4,36},{36... | collective-permute-start | bytes 1572872 | tf_op jit(solution)/shard_map/ppermute | solution.py:34
  243.9 18.1 %collective-permute-start.14 = (bf16[256,896]{1,0:T(8,128)(2,1)S(1)}, bf16[256,896]{1,0:T(8,128)(2,1)S(1)}, u32[]{:S(2)}, u32[]{:S(2)}) collective-permute-start(bf16[256,896]{1,0:T(8,128)(2,1)S(1)} %get-tuple-element.72), channel_id=1, source_target_pairs={{0,96},{32,64},{64,32},{96,0},{1,97},{33,65},{65,33},{97,1},{2,98}... | collective-permute-start | bytes 1376264 | tf_op jit(solution)/shard_map/ppermute | solution.py:34

commit v8 on v7

--- a/solution.py
+++ b/solution.py
@@ -22,6 +22,7 @@
 LAST = (((1,), (1,)), ((), ()))
 WHOLE = pl.BlockSpec(memory_space=pltpu.VMEM)
 EFFORT = 8
+LIGHT = 1.0
 LIMIT = 24 * 1024 * 1024
 
 
@@ -46,10 +47,12 @@
     return [block_at(own)] + [swap(block_at(own ^ step), axes) for step, axes in steps]
 
 
-def call(body, outs, flops, args, **more):
+def call(body, outs, flops, args, effort=1.0, **more):
     arrays = [*args, *jax.tree.leaves(outs)]
     moved = sum(math.prod(a.shape) * jnp.dtype(a.dtype).itemsize for a in arrays)
-    cost = pl.CostEstimate(flops=flops, bytes_accessed=moved, transcendentals=0)
+    cost = pl.CostEstimate(
+        flops=int(effort * flops), bytes_accessed=int(effort * moved), transcendentals=0
+    )
     return pl.pallas_call(
         body,
         out_shape=outs,
@@ -99,8 +102,9 @@
     return call(
         encode_kernel,
         [array((tokens, count)), hbm_array((count, tokens))],
-        EFFORT * 2 * tokens * width * count,
+        2 * tokens * width * count,
         [centered, in_hbm(weight), bias.reshape(1, count)],
+        EFFORT,
         grid=(count // tile,),
         in_specs=[
             pl.BlockSpec((width, tokens), lambda j: (0, 0)),
@@ -238,20 +242,46 @@
 
 
 def backward_kernel(rows_ref, gate_ref, up_ref, down_ref, near_ref, far_ref, *refs):
-    saved, out_ref = refs[:-1], refs[-1]
+    saved, out_ref, (own, near, far, sems) = refs[:6], refs[6], refs[7:]
+    pairs = [(down_ref, own.at[2]), (near_ref.at[2], near.at[2]), (far_ref.at[2], far.at[2])]
+    pairs += [(gate_ref, own.at[0]), (near_ref.at[0], near.at[0]), (far_ref.at[0], far.at[0])]
+    pairs += [(up_ref, own.at[1]), (near_ref.at[1], near.at[1]), (far_ref.at[1], far.at[1])]
+    copies = [pltpu.make_async_copy(*pair, sems.at[k]) for k, pair in enumerate(pairs)]
+    for copy in copies:
+        copy.start()
     rows = rows_ref[...]
-    parts = parts_of([gate_ref, up_ref, down_ref], near_ref, far_ref)
     grads = []
-    for (_, _, down), gelu_ref, slope_ref in zip(parts, saved[0::2], saved[1::2]):
-        grad_hidden = product_t(rows, down[...])
+    for k, (part, gelu_ref, slope_ref) in enumerate(
+        zip((own, near, far), saved[0::2], saved[1::2])
+    ):
+        copies[k].wait()
+        grad_hidden = product_t(rows, part[2])
         grad_gate = (grad_hidden * slope_ref[...]).astype(bf16)
         grads.append((grad_gate, (grad_hidden * gelu_ref[...]).astype(bf16)))
+    for copy in copies[3:]:
+        copy.wait()
     for at in range(0, out_ref.shape[1], 512):
         span = slice(at, at + 512)
         terms = []
-        for (grad_gate, grad_up), (gate, up, _) in zip(grads, parts):
-            terms += [product(grad_gate, gate[:, span]), product(grad_up, up[:, span])]
+        for (grad_gate, grad_up), part in zip(grads, (own, near, far)):
+            terms += [product(grad_gate, part[0, :, span]), product(grad_up, part[1, :, span])]
         out_ref[:, span] = sum(terms[1:], terms[0]).astype(bf16)
+
+
+def backward(rows, weights, near, far, saved):
+    anywhere = pl.BlockSpec(memory_space=pl.ANY)
+    units, width = weights[0].shape
+    tokens = rows.shape[0]
+    return call(
+        backward_kernel,
+        array((tokens, width)),
+        12 * tokens * width * units,
+        [rows, *(in_hbm(a) for a in (*weights, near, far, *saved))],
+        in_specs=[WHOLE] + [anywhere] * 5 + [pl.BlockSpec()] * len(saved),
+        scratch_shapes=[pltpu.VMEM((3, units, width), bf16)]
+        + [pltpu.VMEM(near.shape, bf16)] * 2
+        + [pltpu.SemaphoreType.DMA((9,))],
+    )
 
 
 def latent_kernel(rows_ref, weight_ref, latents_ref, out_ref):
@@ -280,14 +310,18 @@
 def products_kernel(spans, count, *refs):
     out_ref = refs[-1]
     for span in spans:
-        total = refs[2 * count][:, span] if len(refs) > 2 * count + 1 else None
+        total = None
+        if len(refs) > 2 * count + 1:
+            rows = out_ref.shape[0]
+            at = pl.multiple_of(pl.program_id(0) * rows, rows)
+            total = refs[2 * count][pl.ds(at, rows), span]
         for k in range(count):
             term = product(refs[k][...], refs[count + k][:, span])
             total = term if total is None else total + term
         out_ref[:, span] = total.astype(out_ref.dtype)
 
 
-def sum_of_products(left, right, tile, rows_tile=None, start=None, kind=bf16):
+def sum_of_products(left, right, tile, rows_tile=None, start=None, kind=bf16, effort=LIGHT):
     rows, depth = left[0].shape
     columns = right[0].shape[1]
     rows_tile = rows_tile or rows
@@ -299,10 +333,11 @@
         array((rows, columns), kind),
         2 * rows * depth * columns * count,
         [*map(in_hbm, left), *right, *([] if start is None else [start])],
+        effort,
         grid=(rows // rows_tile, columns // tile),
         in_specs=[pl.BlockSpec((rows_tile, depth), lambda i, j: (i, 0))] * count
         + [pl.BlockSpec((depth, tile), lambda i, j: (0, j))] * count
-        + ([] if start is None else [out_spec]),
+        + ([] if start is None else [WHOLE]),
         out_specs=out_spec,
     )
 
@@ -351,12 +386,18 @@
     pieces, weights_then = lax.optimization_barrier((pieces, weights))
     sent = jnp.stack([lax.dynamic_slice_in_dim(w, at, units, axis=0) for w in weights_then])
     near = swap(sent, OTHER_HALF)
-    far = swap(near, BATCH[1])
     centered = exchange(pieces, SHARDS).reshape(width, tokens)
 
     latents, turned_latents = encode(centered, encoder_weight, encoder_bias, 256)
     partial_recon = decode(latents, decoder_weight, target.T, 128)
 
+    partial_recon, centered, turned_latents = lax.optimization_barrier(
+        (partial_recon, centered, turned_latents)
+    )
+    far_latents = swap(turned_latents, BATCH[0])
+    centered_blocks = blocks_of_all(
+        lambda b: lax.dynamic_slice_in_dim(centered, b * block, block, axis=0)
+    )
     pieces = exchange(partial_recon.reshape(half, 2 * own_tokens, -1), HALF)
     side = lax.axis_index(SHARDS[1]).reshape(1)
     own_sum, own_targets, sent = call(
@@ -370,6 +411,9 @@
         [side, pieces],
         in_specs=[pl.BlockSpec(memory_space=pltpu.SMEM), WHOLE],
     )
+    sent, far_latents, centered_blocks[3] = lax.optimization_barrier(
+        (sent, far_latents, centered_blocks[3])
+    )
     partner = swap(sent, SHARDS[1])
     pieces, recon = local(
         recon_kernel, [half_of_them, own_rows], [own_sum, partner, bias, gain_in]
@@ -380,13 +424,9 @@
     targets = targets.reshape(own_tokens, *(lax.axis_size(a) for a in OWNERS), share_width)
     own_target = jnp.swapaxes(targets, 2, 3).reshape(own_tokens, width)
 
-    pieces, centered, turned_latents = lax.optimization_barrier((pieces, centered, turned_latents))
+    pieces, near = lax.optimization_barrier((pieces, near))
+    far = swap(near, BATCH[1])
     normed_input = all_tokens(pieces, HALF)
-    latent_blocks = copies_of_all(turned_latents)
-
-    centered_blocks = blocks_of_all(
-        lambda b: lax.dynamic_slice_in_dim(centered, b * block, block, axis=0)
-    )
     rows = half * own_tokens
     saved = [hbm_array((rows, n), f32) for n in (2 * units, 2 * units, units, units, units, units)]
     partial_out, *saved = local(
@@ -395,35 +435,39 @@
         [normed_input, *weights, near, far],
     )
 
+    partial_out, centered_blocks[2] = lax.optimization_barrier((partial_out, centered_blocks[2]))
+
     pieces, grad_result = local(
         functools.partial(output_kernel, token_count),
         [half_of_them, own_rows],
         [to_owners(partial_out, HALF), recon, own_target, gain_out],
     )
-    pieces, latent_blocks, centered_blocks[:3] = lax.optimization_barrier(
-        (pieces, latent_blocks, centered_blocks[:3])
+    latent_blocks = [turned_latents, swap(turned_latents, BATCH[1])]
+    latent_blocks += [far_latents, swap(far_latents, BATCH[1])]
+    pieces, latent_blocks, centered_blocks[1] = lax.optimization_barrier(
+        (pieces, latent_blocks, centered_blocks[1])
     )
     grad_output = all_tokens(pieces, HALF)
-    (partial_input,) = local(
-        backward_kernel,
-        [array((rows, width))],
-        [grad_output, *weights, near, far, *saved],
-        kept=11,
-    )
-    partial_input, centered_blocks[3] = lax.optimization_barrier(
-        (partial_input, centered_blocks[3])
-    )
+    partial_input = backward(grad_output, weights, near, far, saved)
     (pieces,) = local(
         input_kernel, [everyone], [to_owners(partial_input, HALF), recon, grad_result, gain_in]
     )
     grad_recon = all_tokens(pieces, OWNERS)
 
-    recon_blocks = blocks_of_all(
-        lambda b: lax.dynamic_slice_in_dim(grad_recon, b * block, block, axis=1)
-    )
+    own = lax.axis_index(BATCH)
+    recon_blocks = [
+        lax.dynamic_slice_in_dim(grad_recon, (own ^ step) * block, block, axis=1)
+        for step in range(copies)
+    ]
+    recon_blocks[2] = swap(recon_blocks[2], BATCH[0])
+    recon_blocks[3] = swap(recon_blocks[3], BATCH)
     grad_preact = grad_of_preact(grad_recon, decoder_weight, latents, 256)
+    far = swap(grad_preact, BATCH[0])
+    far, near, recon_blocks[1] = lax.optimization_barrier((far, grad_preact, recon_blocks[1]))
+    recon_blocks[1] = swap(recon_blocks[1], BATCH[1])
+    preact_blocks = [grad_preact, swap(near, BATCH[1]), far, swap(far, BATCH[1])]
     part = sum_of_products(latent_blocks[:3], recon_blocks[:3], block, kind=f32)
-    encoder_grad = sum_of_products(centered_blocks, copies_of_all(grad_preact), 256)
+    encoder_grad = sum_of_products(centered_blocks, preact_blocks, 256)
     part, encoder_grad = lax.optimization_barrier((part, encoder_grad))
     decoder_grad = sum_of_products(latent_blocks[3:], recon_blocks[3:], block, 256, part)
     return encoder_grad, decoder_grad

time: 267 us -> 255 us (0.955)
  waiting for transfers between devices: 114 us -> 93.1 us
  blocking collectives: 47.7 us -> 63.2 us
  starting transfers between devices: 45.5 us -> 38.6 us
    ppermute x15, waiting for transfers between devices: 61.9 us -> 26.4 us  [swap(): lax.ppermute(block, axes, [(i, for_all - 1 - i) for i in range(for_all)])]
    all_to_all x2 -> x3, blocking collectives: 47.7 us -> 63.2 us  [exchange(): return lax.all_to_all(pieces, axes, split_axis=0, concat_axis=0, tiled=True)]
    all_to_all x5 -> x4, waiting for transfers between devices: 51.9 us -> 66.6 us  [exchange(): return lax.all_to_all(pieces, axes, split_axis=0, concat_axis=0, tiled=True)]
    all_to_all x5 -> x4, starting transfers between devices: 37.3 us -> 29.6 us  [exchange(): return lax.all_to_all(pieces, axes, split_axis=0, concat_axis=0, tiled=True)]
  transfers between devices with their start and end apart: 20 -> 19, of which waited for: 9 -> 7; matrix products, arithmetic and copies ran while one was open for 2% -> 2% of each run, Pallas kernels for 14% -> 12%
where the time goes in v8:
time: 255 us; the launch traced here: 253 us
  waiting for transfers between devices  93.1 us (37%)
  blocking collectives  63.2 us (25%)
  Pallas kernels  44.7 us (18%)
  starting transfers between devices  38.6 us (15%)
  local copies, waits for them, and re-layouts  9.51 us (4%)
  other arithmetic  3.43 us (1%)
    all_to_all x4, waiting for transfers between devices, exchange(): return lax.all_to_all(pieces, axes, split_axis=0, concat_axis=0, tiled=True)  66.6 us
    all_to_all x3, blocking collectives, exchange(): return lax.all_to_all(pieces, axes, split_axis=0, concat_axis=0, tiled=True)  63.2 us
    pallas_call x12, Pallas kernels, call(): pl.pallas_call(body, out_shape=outs, cost_estimate=cost, compiler_params=...  44.7 us
    all_to_all x4, starting transfers between devices, exchange(): return lax.all_to_all(pieces, axes, split_axis=0, concat_axis=0, tiled=True)  29.6 us
    ppermute x15, waiting for transfers between devices, swap(): lax.ppermute(block, axes, [(i, for_all - 1 - i) for i in range(for_all)])  26.4 us
    ppermute x15, starting transfers between devices, swap(): lax.ppermute(block, axes, [(i, for_all - 1 - i) for i in range(for_all)])  8.97 us
  transfers between devices with their start and end apart: 19, of which 7 were waited for; matrix products, arithmetic and copies ran while one was open for 2% of the time, Pallas kernels for 12%

profile of v8, /device:TPU:14, one launch (start us, length us, event | category | flops | bytes accessed | tf_op | source)
XLA Modules:
  0.0 253.4 jit_solution(9894084520631640352)
XLA Ops:
  0.6 0.8 dynamic-slice_convert_fusion
  1.4 0.9 fusion.2
  2.3 1.3 broadcast_in_dim.4
  3.7 10.5 %all-to-all-start = ((bf16[32,112,256]{2,1,0:T(8,128)(2,1)}), bf16[32,112,256]{2,1,0:T(8,128)(2,1)}, u32[]{:S(2)}, u32[]{:S(2)}) async-start(bf16[32,112,256]{2,1,0:T(8,128)(2,1)} %broadcast_in_dim.4), calls=%async_computation | async-start | bytes 3670016 | tf_op jit(solution)/shard_map/all_to_all | solution.py:30
  14.3 1.3 copy-done.2
  15.6 0.1 dynamic-slice_bitcast_fusion
  15.7 1.7 pad_maximum_fusion
  17.5 2.3 collective-permute-start.3
  19.7 18.9 %all-to-all-done = bf16[32,112,256]{2,1,0:T(8,128)(2,1)} async-done(((bf16[32,112,256]{2,1,0:T(8,128)(2,1)}), bf16[32,112,256]{2,1,0:T(8,128)(2,1)}, u32[]{:S(2)}, u32[]{:S(2)}) %all-to-all-start) | async-done | bytes 1835040 | tf_op jit(solution)/shard_map/all_to_all | solution.py:30
  38.7 7.5 %shard_map.122 = (bf16[256,1024]{1,0:T(8,128)(2,1)S(1)}, bf16[1024,256]{1,0:T(8,128)(2,1)}) custom-call(bf16[3584,256]{1,0:T(8,128)(2,1)} %bitcast.4.centered_ref, bf16[3584,1024]{1,0:T(8,128)(2,1)} %weight_ref.3, bf16[1,1024]{1,0:T(2,128)(2,1)S(1)} %reshape.49.bias_ref), custom_call_target="tpu_custom_call" | custom-call | flops 15032385536 | bytes 81805312 | tf_op jit(solution)/shard_map/pallas_call | solution.py:56
  46.2 3.7 %shard_map.123 = bf16[256,3712]{1,0:T(8,128)(2,1)S(1)} custom-call(bf16[256,1024]{1,0:T(8,128)(2,1)S(1)} %get-tuple-element.44.latents_ref, bf16[1024,3584]{1,0:T(8,128)(2,1)S(1)} %bitcast.29, bf16[112,256]{1,0:T(8,128)(2,1)S(1)} %bitcast.43), custom_call_target="tpu_custom_call" | custom-call | flops 1879048192 | bytes 9822208 | tf_op jit(solution)/shard_map/pallas_call | solution.py:56
  49.9 1.3 copy-done.4
  51.3 6.8 %all-to-all-start.1 = ((bf16[16,16,3712]{2,1,0:T(8,128)(2,1)}), bf16[16,16,3712]{2,1,0:T(8,128)(2,1)}, u32[]{:S(2)}, u32[]{:S(2)}) async-start(bf16[16,16,3712]{2,1,0:T(8,128)(2,1)} %bitcast.40), calls=%async_computation.1 | async-start | bytes 3801088 | tf_op jit(solution)/shard_map/all_to_all | solution.py:30
  58.0 0.6 collective-permute-start
  58.6 2.7 %constant_dynamic-slice_fusion.1 = (bf16[896,256]{1,0:T(8,128)(2,1)}, bf16[896,256]{1,0:T(8,128)(2,1)}, bf16[896,256]{1,0:T(8,128)(2,1)}, bf16[896,256]{1,0:T(8,128)(2,1)}) fusion(bf16[3584,256]{1,0:T(8,128)(2,1)} %bitcast.4.centered_ref, s32[]{:T(128)S(6)} %select_n.39, s32[]{:T(128)S(6)} %select_n.38, s32[]{:T(128)S(6)} %select_n.35, s32[]{:T(128)S(6)} %select_n.33), kind=kLoop, calls=%fused_computation.14 | loop fusion | bytes 3670032 | tf_op jit(solution)/shard_map/dynamic_slice | solution.py:399
  61.4 20.9 %all-to-all-done.1.pieces_ref = bf16[16,16,3712]{2,1,0:T(8,128)(2,1)} async-done(((bf16[16,16,3712]{2,1,0:T(8,128)(2,1)}), bf16[16,16,3712]{2,1,0:T(8,128)(2,1)}, u32[]{:S(2)}, u32[]{:S(2)}) %all-to-all-start.1) | async-done | bytes 1900576 | tf_op jit(solution)/shard_map/all_to_all | solution.py:30
  82.4 2.1 shard_map.124
  84.5 0.7 collective-permute-start.2
  85.2 5.4 %collective-permute-done.2.partner_ref = bf16[8,5632]{1,0:T(8,128)(2,1)S(1)} collective-permute-done((bf16[8,5632]{1,0:T(8,128)(2,1)S(1)}, bf16[8,5632]{1,0:T(8,128)(2,1)S(1)}, u32[]{:S(2)}, u32[]{:S(2)}) %collective-permute-start.2) | collective-permute-done | bytes 90144 | tf_op jit(solution)/shard_map/ppermute | solution.py:35
  90.6 1.1 shard_map.125
  91.8 6.4 %all-to-all-start.2 = ((bf16[16,8,3584]{2,1,0:T(8,128)(2,1)}), bf16[16,8,3584]{2,1,0:T(8,128)(2,1)}, u32[]{:S(2)}, u32[]{:S(2)}) async-start(bf16[16,8,3584]{2,1,0:T(8,128)(2,1)} %get-tuple-element.56), calls=%async_computation.2 | async-start | bytes 1835008 | tf_op jit(solution)/shard_map/all_to_all | solution.py:30
  98.1 1.0 collective-permute-start.5
  99.2 14.2 %all-to-all-done.2 = bf16[16,8,3584]{2,1,0:T(8,128)(2,1)} async-done(((bf16[16,8,3584]{2,1,0:T(8,128)(2,1)}), bf16[16,8,3584]{2,1,0:T(8,128)(2,1)}, u32[]{:S(2)}, u32[]{:S(2)}) %all-to-all-start.2) | async-done | bytes 917536 | tf_op jit(solution)/shard_map/all_to_all | solution.py:30
  113.3 1.4 copy-done.3
  114.8 6.6 %shard_map.126 = (bf16[128,3584]{1,0:T(8,128)(2,1)}, f32[128,224]{1,0:T(8,128)}, f32[128,224]{1,0:T(8,128)}, f32[128,112]{1,0:T(8,128)}, f32[128,112]{1,0:T(8,12...) custom-call(bf16[128,3584]{1,0:T(8,128)(2,1)} %bitcast.10.rows_ref, bf16[224,3584]{1,0:T(8,128)(2,1)S(1)} %bitcast.36, ...), custom_call_target="tpu_custom_call" | custom-call | bytes 11927552 | tf_op jit(solution)/shard_map/pallas_call | solution.py:56
  121.4 6.0 %all-to-all-start.3 = ((bf16[16,8,3584]{2,1,0:T(8,128)(2,1)}), bf16[16,8,3584]{2,1,0:T(8,128)(2,1)S(1)}, u32[]{:S(2)}, u32[]{:S(2)}) async-start(bf16[16,8,3584]{2,1,0:T(8,128)(2,1)} %bitcast.44), calls=%async_computation.3 | async-start | bytes 1835008 | tf_op jit(solution)/shard_map/all_to_all | solution.py:30
  127.5 0.5 collective-permute-start.8
  128.0 0.1 collective-permute-start.7
  128.2 0.1 reshape.56.target_ref
  128.3 12.6 %all-to-all-done.3.pieces_ref = bf16[16,8,3584]{2,1,0:T(8,128)(2,1)S(1)} async-done(((bf16[16,8,3584]{2,1,0:T(8,128)(2,1)}), bf16[16,8,3584]{2,1,0:T(8,128)(2,1)S(1)}, u32[]{:S(2)}, u32[]{:S(2)}) %all-to-all-start.3) | async-done | bytes 917536 | tf_op jit(solution)/shard_map/all_to_all | solution.py:30
  140.9 1.4 shard_map.127
  142.3 0.8 copy-done.9
  143.1 18.1 %all_to_all.35 = bf16[16,8,3584]{2,1,0:T(8,128)(2,1)S(1)} all-to-all(bf16[16,8,3584]{2,1,0:T(8,128)(2,1)} %get-tuple-element.67), channel_id=1, replica_groups=mesh['batch_0'=2,'batch_1'=2,'tensor_0'=4,'tensor_1'=2,'latent'=4] {'ten..., dimensions={0} | all-to-all | bytes 1835008 | tf_op jit(solution)/shard_map/all_to_all | solution.py:30
  161.2 6.8 %shard_map.128 = bf16[128,3584]{1,0:T(8,128)(2,1)S(1)} custom-call(bf16[128,3584]{1,0:T(8,128)(2,1)S(1)} %bitcast.41, bf16[224,3584]{1,0:T(8,128)(2,1)} %bitcast.34, bf16[224,3584]{1,0:T(8,128)(2,1)} %bitcast.37, bf16[224,3584]{1,0:T(8,128)(2,1)} %down_ref.3, bf16[3,112,3584]{2,1,0:T(8,128)(2,1)} %collective-permute-done.3.near_ref, ...), custom_call_target="tpu_custom_call" | custom-call | flops 1233125376 | bytes 11927552 | tf_op jit(solution)/shard_map/pallas_call | solution.py:56
  168.0 16.1 %all_to_all.36.pieces_ref = bf16[16,8,3584]{2,1,0:T(8,128)(2,1)S(1)} all-to-all(bf16[16,8,3584]{2,1,0:T(8,128)(2,1)S(1)} %bitcast.42), channel_id=1, replica_groups=mesh['batch_0'=2,'batch_1'=2,'tensor_0'=4,'tensor_1'=2,'latent'=4] {'ten..., dimensions={0} | all-to-all | bytes 1835008 | tf_op jit(solution)/shard_map/all_to_all | solution.py:30
  184.2 0.4 shard_map.129
  184.6 28.9 %all_to_all.37 = bf16[32,8,3584]{2,1,0:T(8,128)(2,1)S(1)} all-to-all(bf16[32,8,3584]{2,1,0:T(8,128)(2,1)S(1)} %shard_map.129), channel_id=1, replica_groups=mesh['batch_0'=2,'batch_1'=2,'tensor_0'=4,'tensor_1'=2,'latent'=4] {'ten..., dimensions={0} | all-to-all | bytes 3670016 | tf_op jit(solution)/shard_map/all_to_all | solution.py:30
  213.5 2.9 %shard_map.130.refs_4_ = bf16[256,1024]{1,0:T(8,128)(2,1)S(1)} custom-call(bf16[256,3584]{1,0:T(8,128)(2,1)S(1)} %bitcast.32, bf16[1024,3584]{1,0:T(8,128)(2,1)S(1)} %bitcast.31, bf16[256,1024]{1,0:T(8,128)(2,1)S(1)} %copy-done.6), custom_call_target="tpu_custom_call" | custom-call | flops 1879048192 | bytes 10223616 | tf_op jit(solution)/shard_map/pallas_call | solution.py:56
  216.4 0.9 collective-permute-start.9
  217.3 0.1 constant_dynamic-slice_fusion
  217.5 1.3 collective-permute-start.11
  218.8 12.6 %collective-permute-done.9.refs_6_ = bf16[256,1024]{1,0:T(8,128)(2,1)S(1)} collective-permute-done((bf16[256,1024]{1,0:T(8,128)(2,1)S(1)}, bf16[256,1024]{1,0:T(8,128)(2,1)S(1)}, u32[]{:S(2)}, u32[]{:S(2)}) %collective-permute-start.9) | collective-permute-done | bytes 524320 | tf_op jit(solution)/shard_map/ppermute | solution.py:35
  231.4 0.5 collective-permute-start.12
  231.9 0.9 collective-permute-start.14
  232.8 8.4 %collective-permute-done.11.refs_5_ = bf16[256,896]{1,0:T(8,128)(2,1)S(1)} collective-permute-done((bf16[256,896]{1,0:T(8,128)(2,1)S(1)}, bf16[256,896]{1,0:T(8,128)(2,1)S(1)}, u32[]{:S(2)}, u32[]{:S(2)}) %collective-permute-start.11) | collective-permute-done | bytes 458784 | tf_op jit(solution)/shard_map/ppermute | solution.py:35
  241.2 3.1 %shard_map.131.refs_2_ = f32[1024,896]{1,0:T(8,128)S(1)} custom-call(bf16[1024,256]{1,0:T(8,128)(2,1)} %get-tuple-element.64.refs_0_, bf16[1024,256]{1,0:T(8,128)(2,1)} %copy-done.10, bf16[1024,256]{1,0:T(8,128)(2,1)} %collective-permute-done.refs_2_, bf16[256,896]{1,0:T(8,128)(2,1)S(1)} %get-tuple-element.87.refs_3_, ...), custom_call_target="tpu_custom_call" | custom-call | flops 1409286144 | bytes 6619136 | tf_op jit(solution)/shard_map/pallas_call | solution.py:56
  244.4 5.1 %shard_map.132 = bf16[896,1024]{1,0:T(8,128)(2,1)} custom-call(bf16[896,256]{1,0:T(8,128)(2,1)} %get-tuple-element.88.refs_0_, bf16[896,256]{1,0:T(8,128)(2,1)} %collective-permute-done.8.refs_1_, bf16[896,256]{1,0:T(8,128)(2,1)} %collective-permute-done.5.refs_2_, bf16[896,256]{1,0:T(8,128)(2,1)} %collective-permute-done.1.refs_3_, ...), custom_call_target="tpu_custom_call" | custom-call | flops 1879048192 | bytes 5767168 | tf_op jit(solution)/shard_map/pallas_call | solution.py:56
  249.5 4.0 %shard_map.133 = bf16[1024,896]{1,0:T(8,128)(2,1)} custom-call(bf16[1024,256]{1,0:T(8,128)(2,1)} %copy-done.9, bf16[256,896]{1,0:T(8,128)(2,1)S(1)} %collective-permute-done.14.refs_1_, f32[1024,896]{1,0:T(8,128)S(1)} %shard_map.131.refs_2_), custom_call_target="tpu_custom_call" | custom-call | flops 469762048 | bytes 6488064 | tf_op jit(solution)/shard_map/pallas_call | solution.py:56
  (67 shorter events, 0.4 us)
Async XLA Ops:
  3.7 10.5 %copy-start = (bf16[3584,224]{0,1:T(8,128)(2,1)S(1)}, bf16[3584,224]{0,1:T(8,128)(2,1)}, u32[]{:S(2)}) copy-start(bf16[3584,224]{0,1:T(8,128)(2,1)} %param.19) | copy-start | bytes 4816900
  3.7 10.6 %copy-start.1 = (bf16[3584,224]{0,1:T(8,128)(2,1)S(1)}, bf16[3584,224]{0,1:T(8,128)(2,1)}, u32[]{:S(2)}) copy-start(bf16[3584,224]{0,1:T(8,128)(2,1)} %param.20) | copy-start | bytes 4816900
  3.7 35.0 %all-to-all-start = ((bf16[32,112,256]{2,1,0:T(8,128)(2,1)}), bf16[32,112,256]{2,1,0:T(8,128)(2,1)}, u32[]{:S(2)}, u32[]{:S(2)}) async-start(bf16[32,112,256]{2,1,0:T(8,128)(2,1)} %broadcast_in_dim.4), calls=%async_computation | async-start | bytes 3670016 | tf_op jit(solution)/shard_map/all_to_all | solution.py:30
  14.2 1.4 copy-start.2
  15.7 4.0 %copy-start.16 = (bf16[1024]{0:T(1024)(128)(2,1)S(1)}, bf16[1024]{0:T(1024)(128)(2,1)}, u32[]{:S(2)}) copy-start(bf16[1024]{0:T(1024)(128)(2,1)} %param.14) | copy-start | bytes 6148
  17.5 74.3 %collective-permute-start.3 = (bf16[3,112,3584]{2,1,0:T(8,128)(2,1)}, bf16[3,112,3584]{2,1,0:T(8,128)(2,1)}, u32[]{:S(2)}, u32[]{:S(2)}) collective-permute-start(bf16[3,112,3584]{2,1,0:T(8,128)(2,1)} %pad_maximum_fusion), channel_id=1, source_target_pairs={{0,68},{4,64},{64,4},{68,0},{1,69},{5,65},{65,5},{69,1},{2,70},{6,... | collective-permute-start | bytes 7225352 | tf_op jit(solution)/shard_map/ppermute | solution.py:35
  38.7 7.5 %slice-start = ((s8[7340032]{0:T(1024)(128)(4,1)}), s8[4194304]{0:T(1024)(128)(4,1)S(1)}, s32[]{:S(2)}) async-start(s8[7340032]{0:T(1024)(128)(4,1)} %bitcast.28), calls=%async_computation.7 | async-start | bytes 8388608
  38.7 7.5 %slice-start.1 = ((s8[7340032]{0:T(1024)(128)(4,1)}), s8[3145728]{0:T(1024)(128)(4,1)S(1)}, s32[]{:S(2)}) async-start(s8[7340032]{0:T(1024)(128)(4,1)} %bitcast.28), calls=%async_computation.8 | async-start | bytes 6291456
  38.7 7.5 %copy-start.7 = (bf16[256,112]{0,1:T(8,128)(2,1)S(1)}, bf16[256,112]{0,1:T(8,128)(2,1)}, u32[]{:S(2)}) copy-start(bf16[256,112]{0,1:T(8,128)(2,1)} %param.12) | copy-start | bytes 172036
  46.2 3.7 %copy-start.5 = (bf16[256,1024]{1,0:T(8,128)(2,1)}, bf16[256,1024]{1,0:T(8,128)(2,1)S(1)}, u32[]{:S(2)}) copy-start(bf16[256,1024]{1,0:T(8,128)(2,1)S(1)} %get-tuple-element.44.latents_ref) | copy-start | bytes 1572868
  49.9 1.3 copy-start.4
  51.3 31.1 %all-to-all-start.1 = ((bf16[16,16,3712]{2,1,0:T(8,128)(2,1)}), bf16[16,16,3712]{2,1,0:T(8,128)(2,1)}, u32[]{:S(2)}, u32[]{:S(2)}) async-start(bf16[16,16,3712]{2,1,0:T(8,128)(2,1)} %bitcast.40), calls=%async_computation.1 | async-start | bytes 3801088 | tf_op jit(solution)/shard_map/all_to_all | solution.py:30
  58.0 26.5 %collective-permute-start = (bf16[1024,256]{1,0:T(8,128)(2,1)}, bf16[1024,256]{1,0:T(8,128)(2,1)}, u32[]{:S(2)}, u32[]{:S(2)}) collective-permute-start(bf16[1024,256]{1,0:T(8,128)(2,1)} %get-tuple-element.64.refs_0_), channel_id=1, source_target_pairs={{0,64},{64,0},{1,65},{65,1},{2,66},{66,2},{3,67},{67,3},{4,68},{68... | collective-permute-start | bytes 1572872 | tf_op jit(solution)/shard_map/ppermute | solution.py:35
  61.3 23.8 %copy-start.13 = (bf16[3584]{0:T(1024)(128)(2,1)S(1)}, bf16[3584]{0:T(1024)(128)(2,1)}, u32[]{:S(2)}) copy-start(bf16[3584]{0:T(1024)(128)(2,1)} %param.16) | copy-start | bytes 21508
  61.3 23.9 %copy-start.14 = (bf16[3584]{0:T(1024)(128)(2,1)S(1)}, bf16[3584]{0:T(1024)(128)(2,1)}, u32[]{:S(2)}) copy-start(bf16[3584]{0:T(1024)(128)(2,1)} %param.17) | copy-start | bytes 21508
  61.3 23.2 %collective-permute-start.1 = (bf16[896,256]{1,0:T(8,128)(2,1)}, bf16[896,256]{1,0:T(8,128)(2,1)}, u32[]{:S(2)}, u32[]{:S(2)}) collective-permute-start(bf16[896,256]{1,0:T(8,128)(2,1)} %get-tuple-element.91), channel_id=1, source_target_pairs={{0,96},{32,64},{64,32},{96,0},{1,97},{33,65},{65,33},{97,1},{2,98}... | collective-permute-start | bytes 1376264 | tf_op jit(solution)/shard_map/ppermute | solution.py:35
  84.5 6.1 %collective-permute-start.2 = (bf16[8,5632]{1,0:T(8,128)(2,1)S(1)}, bf16[8,5632]{1,0:T(8,128)(2,1)S(1)}, u32[]{:S(2)}, u32[]{:S(2)}) collective-permute-start(bf16[8,5632]{1,0:T(8,128)(2,1)S(1)} %get-tuple-element.51), channel_id=1, source_target_pairs={{0,4},{4,0},{1,5},{5,1},{2,6},{6,2},{3,7},{7,3},{8,12},{12,8},{9,1... | collective-permute-start | bytes 270344 | tf_op jit(solution)/shard_map/ppermute | solution.py:35
  91.8 21.6 %collective-permute-start.4 = (bf16[3,112,3584]{2,1,0:T(8,128)(2,1)}, bf16[3,112,3584]{2,1,0:T(8,128)(2,1)}, u32[]{:S(2)}, u32[]{:S(2)}) collective-permute-start(bf16[3,112,3584]{2,1,0:T(8,128)(2,1)} %collective-permute-done.3.near_ref), channel_id=1, source_target_pairs={{0,32},{32,0},{1,33},{33,1},{2,34},{34,2},{3,35},{35,3},{4,36},{36... | collective-permute-start | bytes 7225352 | tf_op jit(solution)/shard_map/ppermute | solution.py:35
  91.8 21.6 %all-to-all-start.2 = ((bf16[16,8,3584]{2,1,0:T(8,128)(2,1)}), bf16[16,8,3584]{2,1,0:T(8,128)(2,1)}, u32[]{:S(2)}, u32[]{:S(2)}) async-start(bf16[16,8,3584]{2,1,0:T(8,128)(2,1)} %get-tuple-element.56), calls=%async_computation.2 | async-start | bytes 1835008 | tf_op jit(solution)/shard_map/all_to_all | solution.py:30
  98.1 23.2 %collective-permute-start.5 = (bf16[896,256]{1,0:T(8,128)(2,1)}, bf16[896,256]{1,0:T(8,128)(2,1)}, u32[]{:S(2)}, u32[]{:S(2)}) collective-permute-start(bf16[896,256]{1,0:T(8,128)(2,1)} %get-tuple-element.90), channel_id=1, source_target_pairs={{0,64},{64,0},{1,65},{65,1},{2,66},{66,2},{3,67},{67,3},{4,68},{68... | collective-permute-start | bytes 1376264 | tf_op jit(solution)/shard_map/ppermute | solution.py:35
  113.3 1.4 copy-start.3
  121.3 6.0 %copy-start.15 = (bf16[3584]{0:T(1024)(128)(2,1)S(1)}, bf16[3584]{0:T(1024)(128)(2,1)}, u32[]{:S(2)}) copy-start(bf16[3584]{0:T(1024)(128)(2,1)} %param.18) | copy-start | bytes 21508
  121.3 6.0 %copy-start.8 = (bf16[1024,256]{1,0:T(8,128)(2,1)S(1)}, bf16[1024,256]{1,0:T(8,128)(2,1)}, u32[]{:S(2)}) copy-start(bf16[1024,256]{1,0:T(8,128)(2,1)} %get-tuple-element.64.refs_0_) | copy-start | bytes 1572868
  121.3 6.1 %copy-start.11 = (bf16[896,256]{1,0:T(8,128)(2,1)S(1)}, bf16[896,256]{1,0:T(8,128)(2,1)}, u32[]{:S(2)}) copy-start(bf16[896,256]{1,0:T(8,128)(2,1)} %get-tuple-element.89) | copy-start | bytes 1376260
  121.3 6.7 %copy-start.12 = (bf16[16,8,128]{2,1,0:T(8,128)(2,1)S(1)}, bf16[16,8,128]{2,1,0:T(8,128)(2,1)}, u32[]{:S(2)}) copy-start(bf16[16,8,128]{2,1,0:T(8,128)(2,1)} %get-tuple-element.61) | copy-start | bytes 98308
  121.4 19.5 %all-to-all-start.3 = ((bf16[16,8,3584]{2,1,0:T(8,128)(2,1)}), bf16[16,8,3584]{2,1,0:T(8,128)(2,1)S(1)}, u32[]{:S(2)}, u32[]{:S(2)}) async-start(bf16[16,8,3584]{2,1,0:T(8,128)(2,1)} %bitcast.44), calls=%async_computation.3 | async-start | bytes 1835008 | tf_op jit(solution)/shard_map/all_to_all | solution.py:30
  127.4 14.9 %collective-permute-start.6 = (bf16[1024,256]{1,0:T(8,128)(2,1)S(1)}, bf16[1024,256]{1,0:T(8,128)(2,1)S(1)}, u32[]{:S(2)}, u32[]{:S(2)}) collective-permute-start(bf16[1024,256]{1,0:T(8,128)(2,1)S(1)} %copy-done.8), channel_id=1, source_target_pairs={{0,32},{32,0},{1,33},{33,1},{2,34},{34,2},{3,35},{35,3},{4,36},{36... | collective-permute-start | bytes 1572872 | tf_op jit(solution)/shard_map/ppermute | solution.py:35
  127.5 14.8 %collective-permute-start.8 = (bf16[896,256]{1,0:T(8,128)(2,1)S(1)}, bf16[896,256]{1,0:T(8,128)(2,1)}, u32[]{:S(2)}, u32[]{:S(2)}) collective-permute-start(bf16[896,256]{1,0:T(8,128)(2,1)S(1)} %copy-done.11), channel_id=1, source_target_pairs={{0,32},{32,0},{1,33},{33,1},{2,34},{34,2},{3,35},{35,3},{4,36},{36... | collective-permute-start | bytes 1376264 | tf_op jit(solution)/shard_map/ppermute | solution.py:35
  128.0 14.3 %collective-permute-start.7 = (bf16[1024,256]{1,0:T(8,128)(2,1)}, bf16[1024,256]{1,0:T(8,128)(2,1)S(1)}, u32[]{:S(2)}, u32[]{:S(2)}) collective-permute-start(bf16[1024,256]{1,0:T(8,128)(2,1)} %collective-permute-done.refs_2_), channel_id=1, source_target_pairs={{0,32},{32,0},{1,33},{33,1},{2,34},{34,2},{3,35},{35,3},{4,36},{36... | collective-permute-start | bytes 1572872 | tf_op jit(solution)/shard_map/ppermute | solution.py:35
  142.2 19.0 %copy-start.10 = (bf16[1024,256]{1,0:T(8,128)(2,1)}, bf16[1024,256]{1,0:T(8,128)(2,1)S(1)}, u32[]{:S(2)}) copy-start(bf16[1024,256]{1,0:T(8,128)(2,1)S(1)} %collective-permute-done.6.refs_1_) | copy-start | bytes 1572868
  142.3 0.8 copy-start.9
  143.1 70.4 %slice-start.2 = ((s8[7340032]{0:T(1024)(128)(4,1)}), s8[4194304]{0:T(1024)(128)(4,1)S(1)}, s32[]{:S(2)}) async-start(s8[7340032]{0:T(1024)(128)(4,1)} %bitcast.30), calls=%async_computation.9 | async-start | bytes 8388608
  161.2 52.3 %slice-start.3 = ((s8[7340032]{0:T(1024)(128)(4,1)}), s8[3145728]{0:T(1024)(128)(4,1)S(1)}, s32[]{:S(2)}) async-start(s8[7340032]{0:T(1024)(128)(4,1)} %bitcast.30), calls=%async_computation.10 | async-start | bytes 6291456
  184.6 29.0 %copy-start.6 = (bf16[256,1024]{1,0:T(8,128)(2,1)S(1)}, bf16[256,1024]{1,0:T(8,128)(2,1)}, u32[]{:S(2)}) copy-start(bf16[256,1024]{1,0:T(8,128)(2,1)} %copy-done.5) | copy-start | bytes 1572868
  216.4 14.9 %collective-permute-start.9 = (bf16[256,1024]{1,0:T(8,128)(2,1)S(1)}, bf16[256,1024]{1,0:T(8,128)(2,1)S(1)}, u32[]{:S(2)}, u32[]{:S(2)}) collective-permute-start(bf16[256,1024]{1,0:T(8,128)(2,1)S(1)} %shard_map.130.refs_4_), channel_id=1, source_target_pairs={{0,64},{64,0},{1,65},{65,1},{2,66},{66,2},{3,67},{67,3},{4,68},{68... | collective-permute-start | bytes 1572872 | tf_op jit(solution)/shard_map/ppermute | solution.py:35
  217.5 23.7 %collective-permute-start.11 = (bf16[256,896]{1,0:T(8,128)(2,1)S(1)}, bf16[256,896]{1,0:T(8,128)(2,1)S(1)}, u32[]{:S(2)}, u32[]{:S(2)}) collective-permute-start(bf16[256,896]{1,0:T(8,128)(2,1)S(1)} %get-tuple-element.85), channel_id=1, source_target_pairs={{0,64},{64,0},{1,65},{65,1},{2,66},{66,2},{3,67},{67,3},{4,68},{68... | collective-permute-start | bytes 1376264 | tf_op jit(solution)/shard_map/ppermute | solution.py:35
  231.4 9.8 %collective-permute-start.10 = (bf16[256,896]{1,0:T(8,128)(2,1)S(1)}, bf16[256,896]{1,0:T(8,128)(2,1)S(1)}, u32[]{:S(2)}, u32[]{:S(2)}) collective-permute-start(bf16[256,896]{1,0:T(8,128)(2,1)S(1)} %get-tuple-element.75), channel_id=1, source_target_pairs={{0,32},{32,0},{1,33},{33,1},{2,34},{34,2},{3,35},{35,3},{4,36},{36... | collective-permute-start | bytes 1376264 | tf_op jit(solution)/shard_map/ppermute | solution.py:35
  231.4 13.0 %collective-permute-start.12 = (bf16[256,1024]{1,0:T(8,128)(2,1)S(1)}, bf16[256,1024]{1,0:T(8,128)(2,1)S(1)}, u32[]{:S(2)}, u32[]{:S(2)}) collective-permute-start(bf16[256,1024]{1,0:T(8,128)(2,1)S(1)} %shard_map.130.refs_4_), channel_id=1, source_target_pairs={{0,32},{32,0},{1,33},{33,1},{2,34},{34,2},{3,35},{35,3},{4,36},{36... | collective-permute-start | bytes 1572872 | tf_op jit(solution)/shard_map/ppermute | solution.py:35
  231.9 12.5 %collective-permute-start.13 = (bf16[256,1024]{1,0:T(8,128)(2,1)S(1)}, bf16[256,1024]{1,0:T(8,128)(2,1)S(1)}, u32[]{:S(2)}, u32[]{:S(2)}) collective-permute-start(bf16[256,1024]{1,0:T(8,128)(2,1)S(1)} %collective-permute-done.9.refs_6_), channel_id=1, source_target_pairs={{0,32},{32,0},{1,33},{33,1},{2,34},{34,2},{3,35},{35,3},{4,36},{36... | collective-permute-start | bytes 1572872 | tf_op jit(solution)/shard_map/ppermute | solution.py:35
  231.9 17.6 %collective-permute-start.14 = (bf16[256,896]{1,0:T(8,128)(2,1)S(1)}, bf16[256,896]{1,0:T(8,128)(2,1)S(1)}, u32[]{:S(2)}, u32[]{:S(2)}) collective-permute-start(bf16[256,896]{1,0:T(8,128)(2,1)S(1)} %get-tuple-element.84), channel_id=1, source_target_pairs={{0,96},{32,64},{64,32},{96,0},{1,97},{33,65},{65,33},{97,1},{2,98}... | collective-permute-start | bytes 1376264 | tf_op jit(solution)/shard_map/ppermute | solution.py:35

commit v9 on v8

--- a/solution.py
+++ b/solution.py
@@ -85,15 +85,24 @@
 def encode_kernel(centered_ref, weight_ref, bias_ref, latents_ref, turned_ref, rows_ref):
     width = centered_ref.shape[0]
 
+    def finish(total):
+        latents = jnp.maximum(total + bias_ref[...].astype(f32), 0.0).astype(bf16)
+        latents_ref[...] = latents
+        turned_ref[...] = latents.T
+
     @pl.when(pl.program_id(0) == 0)
     def _():
+        total = None
         for at in range(0, width, 256):
-            rows_ref[:, at : at + 256] = centered_ref[at : at + 256, :].T
-
-    preact = product(rows_ref[...], weight_ref[...]) + bias_ref[...].astype(f32)
-    latents = jnp.maximum(preact, 0.0).astype(bf16)
-    latents_ref[...] = latents
-    turned_ref[...] = latents.T
+            chunk = centered_ref[at : at + 256, :].T
+            rows_ref[:, at : at + 256] = chunk
+            term = product(chunk, weight_ref[at : at + 256, :])
+            total = term if total is None else total + term
+        finish(total)
+
+    @pl.when(pl.program_id(0) > 0)
+    def _():
+        finish(product(rows_ref[...], weight_ref[...]))
 
 
 def encode(centered, weight, bias, tile):
@@ -119,18 +128,33 @@
     )
 
 
-def decode_kernel(latents_ref, weight_ref, target_ref, out_ref):
+def decode_kernel(latents_ref, weight_ref, target_ref, out_ref, held_ref, sems):
     tile = weight_ref.shape[1]
     step = pl.program_id(0)
-    at = pl.multiple_of(step * tile, tile)
-    out_ref[:, pl.ds(at, tile)] = product(latents_ref[...], weight_ref[...]).astype(bf16)
+    last = pl.num_programs(0) - 1
+    rows, tokens = target_ref.shape
+    spare = -rows % 128
+    width = out_ref.shape[1] - rows - spare
+
+    def to_out(at, size, k):
+        span = pl.ds(at, size)
+        return pltpu.make_async_copy(held_ref.at[:, span], out_ref.at[:, span], sems.at[k])
 
     @pl.when(step == 0)
     def _():
-        rows, tokens = target_ref.shape
-        spare = -rows % 128
         padded = jnp.concatenate([target_ref[...], jnp.zeros((spare, tokens), bf16)], axis=0)
-        out_ref[:, out_ref.shape[1] - rows - spare :] = padded.T
+        held_ref[:, width:] = padded.T
+        to_out(width, rows + spare, width // tile).start()
+
+    at = pl.multiple_of(step * tile, tile)
+    held_ref[:, pl.ds(at, tile)] = product(latents_ref[...], weight_ref[...]).astype(bf16)
+    to_out(at, tile, step).start()
+
+    @pl.when(step == last)
+    def _():
+        for k in range(width // tile):
+            to_out(k * tile, tile, k).wait()
+        to_out(width, rows + spare, width // tile).wait()
 
 
 def decode(latents, weight, turned_target, room):
@@ -139,12 +163,16 @@
     tile = width // 7
     return call(
         decode_kernel,
-        array((tokens, width + room)),
+        hbm_array((tokens, width + room)),
         2 * tokens * width * count,
         [latents, weight, turned_target],
         grid=(7,),
         in_specs=[WHOLE, pl.BlockSpec((count, tile), lambda j: (0, j)), WHOLE],
-        out_specs=WHOLE,
+        out_specs=pl.BlockSpec(memory_space=pl.ANY),
+        scratch_shapes=[
+            pltpu.VMEM((tokens, width + room), bf16),
+            pltpu.SemaphoreType.DMA((8,)),
+        ],
     )
 
 
@@ -214,73 +242,77 @@
     return call(body, outs, 0, args, in_specs=[WHOLE] * stay + [pl.BlockSpec()] * kept)
 
 
-def parts_of(own, near, far):
-    return [own, [near.at[k] for k in range(3)], [far.at[k] for k in range(3)]]
-
-
-def forward_kernel(rows_ref, gate_ref, up_ref, down_ref, near_ref, far_ref, out_ref, *saved):
+def fetches(refs, weights_ref, sems, order):
+    *own, near, far = refs
+    units, more = own[0].shape[0], near.shape[1]
+    copies = []
+    for k in order:
+        rows = weights_ref.at[k]
+        pairs = [(own[k], rows.at[pl.ds(0, units)])]
+        pairs += [(near.at[k], rows.at[pl.ds(units, more)])]
+        pairs += [(far.at[k], rows.at[pl.ds(units + more, more)])]
+        copies.append([pltpu.make_async_copy(*p, sems.at[k, i]) for i, p in enumerate(pairs)])
+    for copy in sum(copies, []):
+        copy.start()
+    return copies
+
+
+def arrive(copies):
+    for copy in copies:
+        copy.wait()
+
+
+def forward_kernel(rows_ref, *refs):
+    out_ref, gelu_ref, slope_ref, weights_ref, sems = refs[5:]
     root = 0.7978845608028654
     cube = 0.044715
+    gate, up, down = fetches(refs[:5], weights_ref, sems, (0, 1, 2))
     rows = rows_ref[...]
-    parts = parts_of([gate_ref, up_ref, down_ref], near_ref, far_ref)
-    hidden = []
-    for (gate, up, _), gelu_ref, slope_ref in zip(parts, saved[0::2], saved[1::2]):
-        gate_value = product_t(rows, gate[...])
-        up_value = product_t(rows, up[...])
-        square = gate_value * gate_value
-        curve = jnp.tanh(root * gate_value * (1.0 + cube * square))
-        half = 0.5 * (1.0 + curve)
-        gelu_value = gate_value * half
-        rise = 0.5 * gate_value * (1.0 - curve * curve) * root * (1.0 + 3.0 * cube * square)
-        gelu_ref[...] = gelu_value
-        slope_ref[...] = up_value * (half + rise)
-        hidden.append((gelu_value * up_value).astype(bf16))
+    arrive(gate)
+    gate_value = product_t(rows, weights_ref[0])
+    arrive(up)
+    up_value = product_t(rows, weights_ref[1])
+    square = gate_value * gate_value
+    curve = jnp.tanh(root * gate_value * (1.0 + cube * square))
+    half = 0.5 * (1.0 + curve)
+    gelu_value = gate_value * half
+    rise = 0.5 * gate_value * (1.0 - curve * curve) * root * (1.0 + 3.0 * cube * square)
+    gelu_ref[...] = gelu_value
+    slope_ref[...] = up_value * (half + rise)
+    hidden = (gelu_value * up_value).astype(bf16)
+    arrive(down)
     for at in range(0, out_ref.shape[1], 512):
         span = slice(at, at + 512)
-        terms = [product(h, down[:, span]) for h, (_, _, down) in zip(hidden, parts)]
-        out_ref[:, span] = sum(terms[1:], terms[0]).astype(bf16)
-
-
-def backward_kernel(rows_ref, gate_ref, up_ref, down_ref, near_ref, far_ref, *refs):
-    saved, out_ref, (own, near, far, sems) = refs[:6], refs[6], refs[7:]
-    pairs = [(down_ref, own.at[2]), (near_ref.at[2], near.at[2]), (far_ref.at[2], far.at[2])]
-    pairs += [(gate_ref, own.at[0]), (near_ref.at[0], near.at[0]), (far_ref.at[0], far.at[0])]
-    pairs += [(up_ref, own.at[1]), (near_ref.at[1], near.at[1]), (far_ref.at[1], far.at[1])]
-    copies = [pltpu.make_async_copy(*pair, sems.at[k]) for k, pair in enumerate(pairs)]
-    for copy in copies:
-        copy.start()
-    rows = rows_ref[...]
-    grads = []
-    for k, (part, gelu_ref, slope_ref) in enumerate(
-        zip((own, near, far), saved[0::2], saved[1::2])
-    ):
-        copies[k].wait()
-        grad_hidden = product_t(rows, part[2])
-        grad_gate = (grad_hidden * slope_ref[...]).astype(bf16)
-        grads.append((grad_gate, (grad_hidden * gelu_ref[...]).astype(bf16)))
-    for copy in copies[3:]:
-        copy.wait()
+        out_ref[:, span] = product(hidden, weights_ref[2, :, span]).astype(bf16)
+
+
+def backward_kernel(rows_ref, *refs):
+    gelu_ref, slope_ref, out_ref, weights_ref, sems = refs[5:]
+    down, gate, up = fetches(refs[:5], weights_ref, sems, (2, 0, 1))
+    arrive(down)
+    grad_hidden = product_t(rows_ref[...], weights_ref[2])
+    grad_gate = (grad_hidden * slope_ref[...]).astype(bf16)
+    grad_up = (grad_hidden * gelu_ref[...]).astype(bf16)
+    arrive(gate)
+    arrive(up)
     for at in range(0, out_ref.shape[1], 512):
         span = slice(at, at + 512)
-        terms = []
-        for (grad_gate, grad_up), part in zip(grads, (own, near, far)):
-            terms += [product(grad_gate, part[0, :, span]), product(grad_up, part[1, :, span])]
-        out_ref[:, span] = sum(terms[1:], terms[0]).astype(bf16)
-
-
-def backward(rows, weights, near, far, saved):
+        part = product(grad_gate, weights_ref[0, :, span])
+        part += product(grad_up, weights_ref[1, :, span])
+        out_ref[:, span] = part.astype(bf16)
+
+
+def with_weights(body, outs, rows, weights, near, far, saved=()):
     anywhere = pl.BlockSpec(memory_space=pl.ANY)
     units, width = weights[0].shape
-    tokens = rows.shape[0]
+    units += 2 * near.shape[1]
     return call(
-        backward_kernel,
-        array((tokens, width)),
-        12 * tokens * width * units,
+        body,
+        outs,
+        6 * rows.shape[0] * width * units,
         [rows, *(in_hbm(a) for a in (*weights, near, far, *saved))],
         in_specs=[WHOLE] + [anywhere] * 5 + [pl.BlockSpec()] * len(saved),
-        scratch_shapes=[pltpu.VMEM((3, units, width), bf16)]
-        + [pltpu.VMEM(near.shape, bf16)] * 2
-        + [pltpu.SemaphoreType.DMA((9,))],
+        scratch_shapes=[pltpu.VMEM((3, units, width), bf16), pltpu.SemaphoreType.DMA((3, 3))],
     )
 
 
@@ -428,13 +460,15 @@
     far = swap(near, BATCH[1])
     normed_input = all_tokens(pieces, HALF)
     rows = half * own_tokens
-    saved = [hbm_array((rows, n), f32) for n in (2 * units, 2 * units, units, units, units, units)]
-    partial_out, *saved = local(
+    hidden = gate.shape[0] + 2 * units
+    partial_out, *saved = with_weights(
         forward_kernel,
-        [hbm_array((rows, width)), *saved],
-        [normed_input, *weights, near, far],
-    )
-
+        [hbm_array((rows, width))] + [hbm_array((rows, hidden), f32)] * 2,
+        normed_input,
+        weights,
+        near,
+        far,
+    )
     partial_out, centered_blocks[2] = lax.optimization_barrier((partial_out, centered_blocks[2]))
 
     pieces, grad_result = local(
@@ -448,7 +482,9 @@
         (pieces, latent_blocks, centered_blocks[1])
     )
     grad_output = all_tokens(pieces, HALF)
-    partial_input = backward(grad_output, weights, near, far, saved)
+    partial_input = with_weights(
+        backward_kernel, array((rows, width)), grad_output, weights, near, far, saved
+    )
     (pieces,) = local(
         input_kernel, [everyone], [to_owners(partial_input, HALF), recon, grad_result, gain_in]
     )

time: 255 us -> 249 us (0.976)
    unnamed x42 -> x34, local copies, waits for them, and re-layouts: 4.95 us -> 1.42 us
  transfers between devices with their start and end apart: 19 -> 19, of which waited for: 7 -> 8; matrix products, arithmetic and copies ran while one was open for 2% -> 3% of each run, Pallas kernels for 12% -> 12%
where the time goes in v9:
time: 249 us; the launch traced here: 248 us
  waiting for transfers between devices  94.5 us (38%)
  blocking collectives  62.6 us (25%)
  Pallas kernels  42.8 us (17%)
  starting transfers between devices  36.5 us (15%)
  local copies, waits for them, and re-layouts  7.19 us (3%)
  other arithmetic  3.45 us (1%)
    all_to_all x4, waiting for transfers between devices, exchange(): return lax.all_to_all(pieces, axes, split_axis=0, concat_axis=0, tiled=True)  65.6 us
    all_to_all x3, blocking collectives, exchange(): return lax.all_to_all(pieces, axes, split_axis=0, concat_axis=0, tiled=True)  62.6 us
    pallas_call x12, Pallas kernels, call(): pl.pallas_call(body, out_shape=outs, cost_estimate=cost, compiler_params=...  42.8 us
    ppermute x15, waiting for transfers between devices, swap(): lax.ppermute(block, axes, [(i, for_all - 1 - i) for i in range(for_all)])  28.9 us
    all_to_all x4, starting transfers between devices, exchange(): return lax.all_to_all(pieces, axes, split_axis=0, concat_axis=0, tiled=True)  28.2 us
    ppermute x15, starting transfers between devices, swap(): lax.ppermute(block, axes, [(i, for_all - 1 - i) for i in range(for_all)])  8.28 us
  transfers between devices with their start and end apart: 19, of which 8 were waited for; matrix products, arithmetic and copies ran while one was open for 3% of the time, Pallas kernels for 12%

profile of v9, /device:TPU:14, one launch (start us, length us, event | category | flops | bytes accessed | tf_op | source)
XLA Modules:
  0.0 248.0 jit_solution(8308194894681615333)
XLA Ops:
  0.6 0.8 dynamic-slice_convert_fusion
  1.4 0.9 fusion.2
  2.3 1.3 broadcast_in_dim.4
  3.7 10.3 %all-to-all-start = ((bf16[32,112,256]{2,1,0:T(8,128)(2,1)}), bf16[32,112,256]{2,1,0:T(8,128)(2,1)S(1)}, u32[]{:S(2)}, u32[]{:S(2)}) async-start(bf16[32,112,256]{2,1,0:T(8,128)(2,1)} %broadcast_in_dim.4), calls=%async_computation | async-start | bytes 3670016 | tf_op jit(solution)/shard_map/all_to_all | solution.py:30
  14.0 0.1 dynamic-slice_bitcast_fusion.2
  14.1 1.3 copy-done.3
  15.4 1.2 dynamic-slice_bitcast_fusion
  16.7 1.8 pad_maximum_fusion
  18.4 2.3 collective-permute-start.3
  20.7 19.1 %all-to-all-done = bf16[32,112,256]{2,1,0:T(8,128)(2,1)S(1)} async-done(((bf16[32,112,256]{2,1,0:T(8,128)(2,1)}), bf16[32,112,256]{2,1,0:T(8,128)(2,1)S(1)}, u32[]{:S(2)}, u32[]{:S(2)}) %all-to-all-start) | async-done | bytes 1835040 | tf_op jit(solution)/shard_map/all_to_all | solution.py:30
  39.9 7.5 %shard_map.122 = (bf16[256,1024]{1,0:T(8,128)(2,1)S(1)}, bf16[1024,256]{1,0:T(8,128)(2,1)}) custom-call(bf16[3584,256]{1,0:T(8,128)(2,1)S(1)} %bitcast.34, bf16[3584,1024]{1,0:T(8,128)(2,1)} %weight_ref.3, bf16[1,1024]{1,0:T(2,128)(2,1)S(1)} %reshape.49.bias_ref), custom_call_target="tpu_custom_call" | custom-call | flops 15032385536 | bytes 81805312 | tf_op jit(solution)/shard_map/pallas_call | solution.py:56
  47.3 4.6 %shard_map.123 = bf16[256,3712]{1,0:T(8,128)(2,1)} custom-call(bf16[256,1024]{1,0:T(8,128)(2,1)S(1)} %get-tuple-element.40.latents_ref, bf16[1024,3584]{1,0:T(8,128)(2,1)S(1)} %bitcast.29, bf16[112,256]{1,0:T(8,128)(2,1)S(1)} %bitcast.39), custom_call_target="tpu_custom_call" | custom-call | flops 1879048192 | bytes 9822208 | tf_op jit(solution)/shard_map/pallas_call | solution.py:56
  51.9 5.5 %all-to-all-start.1 = ((bf16[16,16,3712]{2,1,0:T(8,128)(2,1)}), bf16[16,16,3712]{2,1,0:T(8,128)(2,1)S(1)}, u32[]{:S(2)}, u32[]{:S(2)}) async-start(bf16[16,16,3712]{2,1,0:T(8,128)(2,1)} %bitcast.46), calls=%async_computation.1 | async-start | bytes 3801088 | tf_op jit(solution)/shard_map/all_to_all | solution.py:30
  57.5 0.5 collective-permute-start
  58.0 2.8 %constant_dynamic-slice_fusion.1 = (bf16[896,256]{1,0:T(8,128)(2,1)}, bf16[896,256]{1,0:T(8,128)(2,1)}, bf16[896,256]{1,0:T(8,128)(2,1)}, bf16[896,256]{1,0:T(8,128)(2,1)}) fusion(bf16[3584,256]{1,0:T(8,128)(2,1)} %bitcast.35, s32[]{:T(128)S(6)} %select_n.39, s32[]{:T(128)S(6)} %select_n.38, s32[]{:T(128)S(6)} %select_n.35, s32[]{:T(128)S(6)} %select_n.33), kind=kLoop, calls=%fused_computation.14 | loop fusion | bytes 3670032 | tf_op jit(solution)/shard_map/dynamic_slice | solution.py:431
  60.8 20.9 %all-to-all-done.1.pieces_ref = bf16[16,16,3712]{2,1,0:T(8,128)(2,1)S(1)} async-done(((bf16[16,16,3712]{2,1,0:T(8,128)(2,1)}), bf16[16,16,3712]{2,1,0:T(8,128)(2,1)S(1)}, u32[]{:S(2)}, u32[]{:S(2)}) %all-to-all-start.1) | async-done | bytes 1900576 | tf_op jit(solution)/shard_map/all_to_all | solution.py:30
  81.7 0.6 shard_map.124
  82.3 0.8 collective-permute-start.2
  83.2 5.4 %collective-permute-done.2.partner_ref = bf16[8,5632]{1,0:T(8,128)(2,1)S(1)} collective-permute-done((bf16[8,5632]{1,0:T(8,128)(2,1)S(1)}, bf16[8,5632]{1,0:T(8,128)(2,1)S(1)}, u32[]{:S(2)}, u32[]{:S(2)}) %collective-permute-start.2) | collective-permute-done | bytes 90144 | tf_op jit(solution)/shard_map/ppermute | solution.py:35
  88.5 1.1 shard_map.125
  89.7 1.7 collective-permute-done.3.refs_3_
  91.4 6.6 %all-to-all-start.2 = ((bf16[16,8,3584]{2,1,0:T(8,128)(2,1)}), bf16[16,8,3584]{2,1,0:T(8,128)(2,1)S(1)}, u32[]{:S(2)}, u32[]{:S(2)}) async-start(bf16[16,8,3584]{2,1,0:T(8,128)(2,1)} %get-tuple-element.52), calls=%async_computation.2 | async-start | bytes 1835008 | tf_op jit(solution)/shard_map/all_to_all | solution.py:30
  97.9 1.2 collective-permute-start.5
  99.1 13.5 %all-to-all-done.2 = bf16[16,8,3584]{2,1,0:T(8,128)(2,1)S(1)} async-done(((bf16[16,8,3584]{2,1,0:T(8,128)(2,1)}), bf16[16,8,3584]{2,1,0:T(8,128)(2,1)S(1)}, u32[]{:S(2)}, u32[]{:S(2)}) %all-to-all-start.2) | async-done | bytes 917536 | tf_op jit(solution)/shard_map/all_to_all | solution.py:30
  112.6 5.9 %shard_map.126 = (bf16[128,3584]{1,0:T(8,128)(2,1)}, f32[128,448]{1,0:T(8,128)}, f32[128,448]{1,0:T(8,128)}) custom-call(bf16[128,3584]{1,0:T(8,128)(2,1)S(1)} %bitcast.36, bf16[224,3584]{1,0:T(8,128)(2,1)} %bitcast.40, bf16[224,3584]{1,0:T(8,128)(2,1)} %bitcast.43, bf16[224,3584]{1,0:T(8,128)(2,1)} %refs_2_.3, ...), custom_call_target="tpu_custom_call" | custom-call | flops 1233125376 | bytes 11927552 | tf_op jit(solution)/shard_map/pallas_call | solution.py:56
  118.5 5.8 %all-to-all-start.3 = ((bf16[16,8,3584]{2,1,0:T(8,128)(2,1)}), bf16[16,8,3584]{2,1,0:T(8,128)(2,1)S(1)}, u32[]{:S(2)}, u32[]{:S(2)}) async-start(bf16[16,8,3584]{2,1,0:T(8,128)(2,1)} %bitcast.47), calls=%async_computation.3 | async-start | bytes 1835008 | tf_op jit(solution)/shard_map/all_to_all | solution.py:30
  124.4 0.1 collective-permute-start.6
  124.5 0.5 collective-permute-start.8
  125.0 0.1 collective-permute-start.7
  125.1 0.1 reshape.56.target_ref
  125.3 12.1 %all-to-all-done.3.pieces_ref = bf16[16,8,3584]{2,1,0:T(8,128)(2,1)S(1)} async-done(((bf16[16,8,3584]{2,1,0:T(8,128)(2,1)}), bf16[16,8,3584]{2,1,0:T(8,128)(2,1)S(1)}, u32[]{:S(2)}, u32[]{:S(2)}) %all-to-all-start.3) | async-done | bytes 917536 | tf_op jit(solution)/shard_map/all_to_all | solution.py:30
  137.4 1.4 shard_map.127
  138.8 17.8 %all_to_all.35 = bf16[16,8,3584]{2,1,0:T(8,128)(2,1)S(1)} all-to-all(bf16[16,8,3584]{2,1,0:T(8,128)(2,1)} %get-tuple-element.63), channel_id=1, replica_groups=mesh['batch_0'=2,'batch_1'=2,'tensor_0'=4,'tensor_1'=2,'latent'=4] {'ten..., dimensions={0} | all-to-all | bytes 1835008 | tf_op jit(solution)/shard_map/all_to_all | solution.py:30
  156.6 6.2 %shard_map.128 = bf16[128,3584]{1,0:T(8,128)(2,1)S(1)} custom-call(bf16[128,3584]{1,0:T(8,128)(2,1)S(1)} %bitcast.37, bf16[224,3584]{1,0:T(8,128)(2,1)} %bitcast.41, bf16[224,3584]{1,0:T(8,128)(2,1)} %bitcast.44, bf16[224,3584]{1,0:T(8,128)(2,1)} %refs_2_.3, bf16[3,112,3584]{2,1,0:T(8,128)(2,1)} %collective-permute-done.3.refs_3_, ...), custom_call_target="tpu_custom_call" | custom-call | flops 1233125376 | bytes 11927552 | tf_op jit(solution)/shard_map/pallas_call | solution.py:56
  162.9 16.1 %all_to_all.36.pieces_ref = bf16[16,8,3584]{2,1,0:T(8,128)(2,1)S(1)} all-to-all(bf16[16,8,3584]{2,1,0:T(8,128)(2,1)S(1)} %bitcast.38), channel_id=1, replica_groups=mesh['batch_0'=2,'batch_1'=2,'tensor_0'=4,'tensor_1'=2,'latent'=4] {'ten..., dimensions={0} | all-to-all | bytes 1835008 | tf_op jit(solution)/shard_map/all_to_all | solution.py:30
  179.0 0.4 shard_map.129
  179.4 28.6 %all_to_all.37 = bf16[32,8,3584]{2,1,0:T(8,128)(2,1)S(1)} all-to-all(bf16[32,8,3584]{2,1,0:T(8,128)(2,1)S(1)} %shard_map.129), channel_id=1, replica_groups=mesh['batch_0'=2,'batch_1'=2,'tensor_0'=4,'tensor_1'=2,'latent'=4] {'ten..., dimensions={0} | all-to-all | bytes 3670016 | tf_op jit(solution)/shard_map/all_to_all | solution.py:30
  208.0 2.9 %shard_map.130.refs_4_ = bf16[256,1024]{1,0:T(8,128)(2,1)S(1)} custom-call(bf16[256,3584]{1,0:T(8,128)(2,1)S(1)} %bitcast.32, bf16[1024,3584]{1,0:T(8,128)(2,1)S(1)} %bitcast.31, bf16[256,1024]{1,0:T(8,128)(2,1)S(1)} %get-tuple-element.40.latents_ref), custom_call_target="tpu_custom_call" | custom-call | flops 1879048192 | bytes 10223616 | tf_op jit(solution)/shard_map/pallas_call | solution.py:56
  210.9 0.1 collective-permute-start.9
  211.0 0.2 constant_dynamic-slice_fusion
  211.2 2.1 collective-permute-start.11
  213.3 12.6 %collective-permute-done.9.refs_6_ = bf16[256,1024]{1,0:T(8,128)(2,1)S(1)} collective-permute-done((bf16[256,1024]{1,0:T(8,128)(2,1)S(1)}, bf16[256,1024]{1,0:T(8,128)(2,1)S(1)}, u32[]{:S(2)}, u32[]{:S(2)}) %collective-permute-start.9) | collective-permute-done | bytes 524320 | tf_op jit(solution)/shard_map/ppermute | solution.py:35
  225.9 0.5 collective-permute-start.12
  226.4 0.1 collective-permute-start.14
  226.5 9.2 %collective-permute-done.11.refs_5_ = bf16[256,896]{1,0:T(8,128)(2,1)S(1)} collective-permute-done((bf16[256,896]{1,0:T(8,128)(2,1)S(1)}, bf16[256,896]{1,0:T(8,128)(2,1)S(1)}, u32[]{:S(2)}, u32[]{:S(2)}) %collective-permute-start.11) | collective-permute-done | bytes 458784 | tf_op jit(solution)/shard_map/ppermute | solution.py:35
  235.7 3.1 %shard_map.131.refs_2_ = f32[1024,896]{1,0:T(8,128)S(1)} custom-call(bf16[1024,256]{1,0:T(8,128)(2,1)} %get-tuple-element.60.refs_0_, bf16[1024,256]{1,0:T(8,128)(2,1)} %collective-permute-done.6.refs_1_, bf16[1024,256]{1,0:T(8,128)(2,1)} %copy-done.5, bf16[256,896]{1,0:T(8,128)(2,1)S(1)} %get-tuple-element.79.refs_3_, ...), custom_call_target="tpu_custom_call" | custom-call | flops 1409286144 | bytes 6619136 | tf_op jit(solution)/shard_map/pallas_call | solution.py:56
  238.9 5.1 %shard_map.132 = bf16[896,1024]{1,0:T(8,128)(2,1)} custom-call(bf16[896,256]{1,0:T(8,128)(2,1)} %get-tuple-element.80.refs_0_, bf16[896,256]{1,0:T(8,128)(2,1)} %collective-permute-done.8.refs_1_, bf16[896,256]{1,0:T(8,128)(2,1)} %collective-permute-done.5.refs_2_, bf16[896,256]{1,0:T(8,128)(2,1)} %collective-permute-done.1.refs_3_, ...), custom_call_target="tpu_custom_call" | custom-call | flops 1879048192 | bytes 5767168 | tf_op jit(solution)/shard_map/pallas_call | solution.py:56
  244.0 4.0 %shard_map.133 = bf16[1024,896]{1,0:T(8,128)(2,1)} custom-call(bf16[1024,256]{1,0:T(8,128)(2,1)} %copy-done.6, bf16[256,896]{1,0:T(8,128)(2,1)S(1)} %collective-permute-done.14.refs_1_, f32[1024,896]{1,0:T(8,128)S(1)} %shard_map.131.refs_2_), custom_call_target="tpu_custom_call" | custom-call | flops 469762048 | bytes 6488064 | tf_op jit(solution)/shard_map/pallas_call | solution.py:56
  (59 shorter events, 0.2 us)
Async XLA Ops:
  3.7 10.3 %copy-start.2 = (bf16[3584,224]{0,1:T(8,128)(2,1)S(1)}, bf16[3584,224]{0,1:T(8,128)(2,1)}, u32[]{:S(2)}) copy-start(bf16[3584,224]{0,1:T(8,128)(2,1)} %param.19) | copy-start | bytes 4816900
  3.7 36.2 %all-to-all-start = ((bf16[32,112,256]{2,1,0:T(8,128)(2,1)}), bf16[32,112,256]{2,1,0:T(8,128)(2,1)S(1)}, u32[]{:S(2)}, u32[]{:S(2)}) async-start(bf16[32,112,256]{2,1,0:T(8,128)(2,1)} %broadcast_in_dim.4), calls=%async_computation | async-start | bytes 3670016 | tf_op jit(solution)/shard_map/all_to_all | solution.py:30
  14.0 1.4 copy-start.3
  16.7 4.1 %copy-start.12 = (bf16[1024]{0:T(1024)(128)(2,1)S(1)}, bf16[1024]{0:T(1024)(128)(2,1)}, u32[]{:S(2)}) copy-start(bf16[1024]{0:T(1024)(128)(2,1)} %param.14) | copy-start | bytes 6148
  18.4 72.9 %collective-permute-start.3 = (bf16[3,112,3584]{2,1,0:T(8,128)(2,1)}, bf16[3,112,3584]{2,1,0:T(8,128)(2,1)}, u32[]{:S(2)}, u32[]{:S(2)}) collective-permute-start(bf16[3,112,3584]{2,1,0:T(8,128)(2,1)} %pad_maximum_fusion), channel_id=1, source_target_pairs={{0,68},{4,64},{64,4},{68,0},{1,69},{5,65},{65,5},{69,1},{2,70},{6,... | collective-permute-start | bytes 7225352 | tf_op jit(solution)/shard_map/ppermute | solution.py:35
  39.8 7.5 %copy-start = (bf16[32,112,256]{2,1,0:T(8,128)(2,1)}, bf16[32,112,256]{2,1,0:T(8,128)(2,1)S(1)}, u32[]{:S(2)}) copy-start(bf16[32,112,256]{2,1,0:T(8,128)(2,1)S(1)} %all-to-all-done) | copy-start | bytes 5505028
  39.8 7.5 %slice-start = ((s8[7340032]{0:T(1024)(128)(4,1)}), s8[4194304]{0:T(1024)(128)(4,1)S(1)}, s32[]{:S(2)}) async-start(s8[7340032]{0:T(1024)(128)(4,1)} %bitcast.28), calls=%async_computation.7 | async-start | bytes 8388608
  39.8 7.5 %slice-start.1 = ((s8[7340032]{0:T(1024)(128)(4,1)}), s8[3145728]{0:T(1024)(128)(4,1)S(1)}, s32[]{:S(2)}) async-start(s8[7340032]{0:T(1024)(128)(4,1)} %bitcast.28), calls=%async_computation.8 | async-start | bytes 6291456
  39.8 7.5 %copy-start.1 = (bf16[256,112]{0,1:T(8,128)(2,1)S(1)}, bf16[256,112]{0,1:T(8,128)(2,1)}, u32[]{:S(2)}) copy-start(bf16[256,112]{0,1:T(8,128)(2,1)} %param.12) | copy-start | bytes 172036
  51.9 5.5 %copy-start.4 = (bf16[1024,256]{1,0:T(8,128)(2,1)S(1)}, bf16[1024,256]{1,0:T(8,128)(2,1)}, u32[]{:S(2)}) copy-start(bf16[1024,256]{1,0:T(8,128)(2,1)} %get-tuple-element.60.refs_0_) | copy-start | bytes 1572868
  51.9 29.7 %all-to-all-start.1 = ((bf16[16,16,3712]{2,1,0:T(8,128)(2,1)}), bf16[16,16,3712]{2,1,0:T(8,128)(2,1)S(1)}, u32[]{:S(2)}, u32[]{:S(2)}) async-start(bf16[16,16,3712]{2,1,0:T(8,128)(2,1)} %bitcast.46), calls=%async_computation.1 | async-start | bytes 3801088 | tf_op jit(solution)/shard_map/all_to_all | solution.py:30
  57.5 24.9 %collective-permute-start = (bf16[1024,256]{1,0:T(8,128)(2,1)S(1)}, bf16[1024,256]{1,0:T(8,128)(2,1)S(1)}, u32[]{:S(2)}, u32[]{:S(2)}) collective-permute-start(bf16[1024,256]{1,0:T(8,128)(2,1)S(1)} %copy-done.4), channel_id=1, source_target_pairs={{0,64},{64,0},{1,65},{65,1},{2,66},{66,2},{3,67},{67,3},{4,68},{68... | collective-permute-start | bytes 1572872 | tf_op jit(solution)/shard_map/ppermute | solution.py:35
  60.7 22.4 %copy-start.9 = (bf16[3584]{0:T(1024)(128)(2,1)S(1)}, bf16[3584]{0:T(1024)(128)(2,1)}, u32[]{:S(2)}) copy-start(bf16[3584]{0:T(1024)(128)(2,1)} %param.16) | copy-start | bytes 21508
  60.7 22.4 %copy-start.10 = (bf16[3584]{0:T(1024)(128)(2,1)S(1)}, bf16[3584]{0:T(1024)(128)(2,1)}, u32[]{:S(2)}) copy-start(bf16[3584]{0:T(1024)(128)(2,1)} %param.17) | copy-start | bytes 21508
  60.8 21.6 %collective-permute-start.1 = (bf16[896,256]{1,0:T(8,128)(2,1)}, bf16[896,256]{1,0:T(8,128)(2,1)}, u32[]{:S(2)}, u32[]{:S(2)}) collective-permute-start(bf16[896,256]{1,0:T(8,128)(2,1)} %get-tuple-element.83), channel_id=1, source_target_pairs={{0,96},{32,64},{64,32},{96,0},{1,97},{33,65},{65,33},{97,1},{2,98}... | collective-permute-start | bytes 1376264 | tf_op jit(solution)/shard_map/ppermute | solution.py:35
  82.3 15.6 %copy-start.7 = (bf16[896,256]{1,0:T(8,128)(2,1)S(1)}, bf16[896,256]{1,0:T(8,128)(2,1)}, u32[]{:S(2)}) copy-start(bf16[896,256]{1,0:T(8,128)(2,1)} %get-tuple-element.82) | copy-start | bytes 1376260
  82.3 42.6 %copy-start.5 = (bf16[1024,256]{1,0:T(8,128)(2,1)}, bf16[1024,256]{1,0:T(8,128)(2,1)S(1)}, u32[]{:S(2)}) copy-start(bf16[1024,256]{1,0:T(8,128)(2,1)S(1)} %collective-permute-done.refs_2_) | copy-start | bytes 1572868
  82.3 6.2 %collective-permute-start.2 = (bf16[8,5632]{1,0:T(8,128)(2,1)S(1)}, bf16[8,5632]{1,0:T(8,128)(2,1)S(1)}, u32[]{:S(2)}, u32[]{:S(2)}) collective-permute-start(bf16[8,5632]{1,0:T(8,128)(2,1)S(1)} %get-tuple-element.47), channel_id=1, source_target_pairs={{0,4},{4,0},{1,5},{5,1},{2,6},{6,2},{3,7},{7,3},{8,12},{12,8},{9,1... | collective-permute-start | bytes 270344 | tf_op jit(solution)/shard_map/ppermute | solution.py:35
  91.4 21.2 %collective-permute-start.4 = (bf16[3,112,3584]{2,1,0:T(8,128)(2,1)}, bf16[3,112,3584]{2,1,0:T(8,128)(2,1)}, u32[]{:S(2)}, u32[]{:S(2)}) collective-permute-start(bf16[3,112,3584]{2,1,0:T(8,128)(2,1)} %collective-permute-done.3.refs_3_), channel_id=1, source_target_pairs={{0,32},{32,0},{1,33},{33,1},{2,34},{34,2},{3,35},{35,3},{4,36},{36... | collective-permute-start | bytes 7225352 | tf_op jit(solution)/shard_map/ppermute | solution.py:35
  91.4 21.2 %all-to-all-start.2 = ((bf16[16,8,3584]{2,1,0:T(8,128)(2,1)}), bf16[16,8,3584]{2,1,0:T(8,128)(2,1)S(1)}, u32[]{:S(2)}, u32[]{:S(2)}) async-start(bf16[16,8,3584]{2,1,0:T(8,128)(2,1)} %get-tuple-element.52), calls=%async_computation.2 | async-start | bytes 1835008 | tf_op jit(solution)/shard_map/all_to_all | solution.py:30
  97.9 20.6 %collective-permute-start.5 = (bf16[896,256]{1,0:T(8,128)(2,1)S(1)}, bf16[896,256]{1,0:T(8,128)(2,1)}, u32[]{:S(2)}, u32[]{:S(2)}) collective-permute-start(bf16[896,256]{1,0:T(8,128)(2,1)S(1)} %copy-done.7), channel_id=1, source_target_pairs={{0,64},{64,0},{1,65},{65,1},{2,66},{66,2},{3,67},{67,3},{4,68},{68... | collective-permute-start | bytes 1376264 | tf_op jit(solution)/shard_map/ppermute | solution.py:35
  118.5 5.8 %copy-start.11 = (bf16[3584]{0:T(1024)(128)(2,1)S(1)}, bf16[3584]{0:T(1024)(128)(2,1)}, u32[]{:S(2)}) copy-start(bf16[3584]{0:T(1024)(128)(2,1)} %param.18) | copy-start | bytes 21508
  118.5 6.6 %copy-start.8 = (bf16[16,8,128]{2,1,0:T(8,128)(2,1)S(1)}, bf16[16,8,128]{2,1,0:T(8,128)(2,1)}, u32[]{:S(2)}) copy-start(bf16[16,8,128]{2,1,0:T(8,128)(2,1)} %get-tuple-element.57) | copy-start | bytes 98308
  118.5 18.9 %all-to-all-start.3 = ((bf16[16,8,3584]{2,1,0:T(8,128)(2,1)}), bf16[16,8,3584]{2,1,0:T(8,128)(2,1)S(1)}, u32[]{:S(2)}, u32[]{:S(2)}) async-start(bf16[16,8,3584]{2,1,0:T(8,128)(2,1)} %bitcast.47), calls=%async_computation.3 | async-start | bytes 1835008 | tf_op jit(solution)/shard_map/all_to_all | solution.py:30
  124.4 14.4 %collective-permute-start.6 = (bf16[1024,256]{1,0:T(8,128)(2,1)S(1)}, bf16[1024,256]{1,0:T(8,128)(2,1)}, u32[]{:S(2)}, u32[]{:S(2)}) collective-permute-start(bf16[1024,256]{1,0:T(8,128)(2,1)S(1)} %copy-done.4), channel_id=1, source_target_pairs={{0,32},{32,0},{1,33},{33,1},{2,34},{34,2},{3,35},{35,3},{4,36},{36... | collective-permute-start | bytes 1572872 | tf_op jit(solution)/shard_map/ppermute | solution.py:35
  124.5 14.3 %collective-permute-start.8 = (bf16[896,256]{1,0:T(8,128)(2,1)}, bf16[896,256]{1,0:T(8,128)(2,1)}, u32[]{:S(2)}, u32[]{:S(2)}) collective-permute-start(bf16[896,256]{1,0:T(8,128)(2,1)} %get-tuple-element.81), channel_id=1, source_target_pairs={{0,32},{32,0},{1,33},{33,1},{2,34},{34,2},{3,35},{35,3},{4,36},{36... | collective-permute-start | bytes 1376264 | tf_op jit(solution)/shard_map/ppermute | solution.py:35
  125.0 13.8 %collective-permute-start.7 = (bf16[1024,256]{1,0:T(8,128)(2,1)S(1)}, bf16[1024,256]{1,0:T(8,128)(2,1)S(1)}, u32[]{:S(2)}, u32[]{:S(2)}) collective-permute-start(bf16[1024,256]{1,0:T(8,128)(2,1)S(1)} %collective-permute-done.refs_2_), channel_id=1, source_target_pairs={{0,32},{32,0},{1,33},{33,1},{2,34},{34,2},{3,35},{35,3},{4,36},{36... | collective-permute-start | bytes 1572872 | tf_op jit(solution)/shard_map/ppermute | solution.py:35
  138.8 24.1 %copy-start.6 = (bf16[1024,256]{1,0:T(8,128)(2,1)}, bf16[1024,256]{1,0:T(8,128)(2,1)S(1)}, u32[]{:S(2)}) copy-start(bf16[1024,256]{1,0:T(8,128)(2,1)S(1)} %collective-permute-done.7.refs_0_) | copy-start | bytes 1572868
  138.8 69.3 %slice-start.2 = ((s8[7340032]{0:T(1024)(128)(4,1)}), s8[4194304]{0:T(1024)(128)(4,1)S(1)}, s32[]{:S(2)}) async-start(s8[7340032]{0:T(1024)(128)(4,1)} %bitcast.30), calls=%async_computation.9 | async-start | bytes 8388608
  156.6 51.4 %slice-start.3 = ((s8[7340032]{0:T(1024)(128)(4,1)}), s8[3145728]{0:T(1024)(128)(4,1)S(1)}, s32[]{:S(2)}) async-start(s8[7340032]{0:T(1024)(128)(4,1)} %bitcast.30), calls=%async_computation.10 | async-start | bytes 6291456
  210.9 14.9 %collective-permute-start.9 = (bf16[256,1024]{1,0:T(8,128)(2,1)S(1)}, bf16[256,1024]{1,0:T(8,128)(2,1)S(1)}, u32[]{:S(2)}, u32[]{:S(2)}) collective-permute-start(bf16[256,1024]{1,0:T(8,128)(2,1)S(1)} %shard_map.130.refs_4_), channel_id=1, source_target_pairs={{0,64},{64,0},{1,65},{65,1},{2,66},{66,2},{3,67},{67,3},{4,68},{68... | collective-permute-start | bytes 1572872 | tf_op jit(solution)/shard_map/ppermute | solution.py:35
  211.2 24.5 %collective-permute-start.11 = (bf16[256,896]{1,0:T(8,128)(2,1)S(1)}, bf16[256,896]{1,0:T(8,128)(2,1)S(1)}, u32[]{:S(2)}, u32[]{:S(2)}) collective-permute-start(bf16[256,896]{1,0:T(8,128)(2,1)S(1)} %get-tuple-element.77), channel_id=1, source_target_pairs={{0,64},{64,0},{1,65},{65,1},{2,66},{66,2},{3,67},{67,3},{4,68},{68... | collective-permute-start | bytes 1376264 | tf_op jit(solution)/shard_map/ppermute | solution.py:35
  225.9 9.8 %collective-permute-start.10 = (bf16[256,896]{1,0:T(8,128)(2,1)S(1)}, bf16[256,896]{1,0:T(8,128)(2,1)S(1)}, u32[]{:S(2)}, u32[]{:S(2)}) collective-permute-start(bf16[256,896]{1,0:T(8,128)(2,1)S(1)} %get-tuple-element.67), channel_id=1, source_target_pairs={{0,32},{32,0},{1,33},{33,1},{2,34},{34,2},{3,35},{35,3},{4,36},{36... | collective-permute-start | bytes 1376264 | tf_op jit(solution)/shard_map/ppermute | solution.py:35
  225.9 13.0 %collective-permute-start.12 = (bf16[256,1024]{1,0:T(8,128)(2,1)S(1)}, bf16[256,1024]{1,0:T(8,128)(2,1)S(1)}, u32[]{:S(2)}, u32[]{:S(2)}) collective-permute-start(bf16[256,1024]{1,0:T(8,128)(2,1)S(1)} %shard_map.130.refs_4_), channel_id=1, source_target_pairs={{0,32},{32,0},{1,33},{33,1},{2,34},{34,2},{3,35},{35,3},{4,36},{36... | collective-permute-start | bytes 1572872 | tf_op jit(solution)/shard_map/ppermute | solution.py:35
  226.4 12.5 %collective-permute-start.13 = (bf16[256,1024]{1,0:T(8,128)(2,1)S(1)}, bf16[256,1024]{1,0:T(8,128)(2,1)S(1)}, u32[]{:S(2)}, u32[]{:S(2)}) collective-permute-start(bf16[256,1024]{1,0:T(8,128)(2,1)S(1)} %collective-permute-done.9.refs_6_), channel_id=1, source_target_pairs={{0,32},{32,0},{1,33},{33,1},{2,34},{34,2},{3,35},{35,3},{4,36},{36... | collective-permute-start | bytes 1572872 | tf_op jit(solution)/shard_map/ppermute | solution.py:35
  226.4 17.6 %collective-permute-start.14 = (bf16[256,896]{1,0:T(8,128)(2,1)S(1)}, bf16[256,896]{1,0:T(8,128)(2,1)S(1)}, u32[]{:S(2)}, u32[]{:S(2)}) collective-permute-start(bf16[256,896]{1,0:T(8,128)(2,1)S(1)} %get-tuple-element.76), channel_id=1, source_target_pairs={{0,96},{32,64},{64,32},{96,0},{1,97},{33,65},{65,33},{97,1},{2,98}... | collective-permute-start | bytes 1376264 | tf_op jit(solution)/shard_map/ppermute | solution.py:35

commit v10 on v9

--- a/solution.py
+++ b/solution.py
@@ -21,8 +21,6 @@
 bf16 = jnp.bfloat16
 LAST = (((1,), (1,)), ((), ()))
 WHOLE = pl.BlockSpec(memory_space=pltpu.VMEM)
-EFFORT = 8
-LIGHT = 1.0
 LIMIT = 24 * 1024 * 1024
 
 
@@ -47,12 +45,10 @@
     return [block_at(own)] + [swap(block_at(own ^ step), axes) for step, axes in steps]
 
 
-def call(body, outs, flops, args, effort=1.0, **more):
+def call(body, outs, flops, args, **more):
     arrays = [*args, *jax.tree.leaves(outs)]
     moved = sum(math.prod(a.shape) * jnp.dtype(a.dtype).itemsize for a in arrays)
-    cost = pl.CostEstimate(
-        flops=int(effort * flops), bytes_accessed=int(effort * moved), transcendentals=0
-    )
+    cost = pl.CostEstimate(flops=flops, bytes_accessed=moved, transcendentals=0)
     return pl.pallas_call(
         body,
         out_shape=outs,
@@ -113,7 +109,6 @@
         [array((tokens, count)), hbm_array((count, tokens))],
         2 * tokens * width * count,
         [centered, in_hbm(weight), bias.reshape(1, count)],
-        EFFORT,
         grid=(count // tile,),
         in_specs=[
             pl.BlockSpec((width, tokens), lambda j: (0, 0)),
@@ -293,13 +288,13 @@
     grad_hidden = product_t(rows_ref[...], weights_ref[2])
     grad_gate = (grad_hidden * slope_ref[...]).astype(bf16)
     grad_up = (grad_hidden * gelu_ref[...]).astype(bf16)
+    grads = jnp.concatenate([grad_gate, grad_up], axis=1)
     arrive(gate)
     arrive(up)
     for at in range(0, out_ref.shape[1], 512):
         span = slice(at, at + 512)
-        part = product(grad_gate, weights_ref[0, :, span])
-        part += product(grad_up, weights_ref[1, :, span])
-        out_ref[:, span] = part.astype(bf16)
+        part = jnp.concatenate([weights_ref[0, :, span], weights_ref[1, :, span]], axis=0)
+        out_ref[:, span] = product(grads, part).astype(bf16)
 
 
 def with_weights(body, outs, rows, weights, near, far, saved=()):
@@ -341,19 +336,18 @@
 
 def products_kernel(spans, count, *refs):
     out_ref = refs[-1]
+    left = jnp.concatenate([ref[...] for ref in refs[:count]], axis=1)
     for span in spans:
-        total = None
+        right = jnp.concatenate([ref[:, span] for ref in refs[count : 2 * count]], axis=0)
+        total = product(left, right)
         if len(refs) > 2 * count + 1:
             rows = out_ref.shape[0]
             at = pl.multiple_of(pl.program_id(0) * rows, rows)
-            total = refs[2 * count][pl.ds(at, rows), span]
-        for k in range(count):
-            term = product(refs[k][...], refs[count + k][:, span])
-            total = term if total is None else total + term
+            total += refs[2 * count][pl.ds(at, rows), span]
         out_ref[:, span] = total.astype(out_ref.dtype)
 
 
-def sum_of_products(left, right, tile, rows_tile=None, start=None, kind=bf16, effort=LIGHT):
+def sum_of_products(left, right, tile, rows_tile=None, start=None, kind=bf16):
     rows, depth = left[0].shape
     columns = right[0].shape[1]
     rows_tile = rows_tile or rows
@@ -365,7 +359,6 @@
         array((rows, columns), kind),
         2 * rows * depth * columns * count,
         [*map(in_hbm, left), *right, *([] if start is None else [start])],
-        effort,
         grid=(rows // rows_tile, columns // tile),
         in_specs=[pl.BlockSpec((rows_tile, depth), lambda i, j: (i, 0))] * count
         + [pl.BlockSpec((depth, tile), lambda i, j: (0, j))] * count

time: 249 us -> 250 us (level)
  transfers between devices with their start and end apart: 19 -> 19, of which waited for: 8 -> 8; matrix products, arithmetic and copies ran while one was open for 3% -> 2% of each run, Pallas kernels for 12% -> 11%
where the time goes in v10:
time: 250 us; the launch traced here: 249 us
  waiting for transfers between devices  94.8 us (38%)
  blocking collectives  62.5 us (25%)
  Pallas kernels  42.1 us (17%)
  starting transfers between devices  38.3 us (15%)
  local copies, waits for them, and re-layouts  7.36 us (3%)
  other arithmetic  3.42 us (1%)
    all_to_all x4, waiting for transfers between devices, exchange(): return lax.all_to_all(pieces, axes, split_axis=0, concat_axis=0, tiled=True)  65.5 us
    all_to_all x3, blocking collectives, exchange(): return lax.all_to_all(pieces, axes, split_axis=0, concat_axis=0, tiled=True)  62.5 us
    pallas_call x12, Pallas kernels, call(): pl.pallas_call(body, out_shape=outs, cost_estimate=cost, compiler_params=...  42.1 us
    all_to_all x4, starting transfers between devices, exchange(): return lax.all_to_all(pieces, axes, split_axis=0, concat_axis=0, tiled=True)  29.9 us
    ppermute x15, waiting for transfers between devices, swap(): lax.ppermute(block, axes, [(i, for_all - 1 - i) for i in range(for_all)])  29.3 us
    ppermute x15, starting transfers between devices, swap(): lax.ppermute(block, axes, [(i, for_all - 1 - i) for i in range(for_all)])  8.34 us
  transfers between devices with their start and end apart: 19, of which 8 were waited for; matrix products, arithmetic and copies ran while one was open for 2% of the time, Pallas kernels for 11%

profile of v10, /device:TPU:14, one launch (start us, length us, event | category | flops | bytes accessed | tf_op | source)
XLA Modules:
  0.0 249.4 jit_solution(2480380237095160473)
XLA Ops:
  0.6 0.8 dynamic-slice_convert_fusion
  1.4 0.9 fusion.2
  2.3 1.3 broadcast_in_dim.4
  3.7 10.5 %all-to-all-start = ((bf16[32,112,256]{2,1,0:T(8,128)(2,1)}), bf16[32,112,256]{2,1,0:T(8,128)(2,1)}, u32[]{:S(2)}, u32[]{:S(2)}) async-start(bf16[32,112,256]{2,1,0:T(8,128)(2,1)} %broadcast_in_dim.4), calls=%async_computation | async-start | bytes 3670016 | tf_op jit(solution)/shard_map/all_to_all | solution.py:28
  14.3 1.3 copy-done.5
  15.6 0.1 dynamic-slice_bitcast_fusion
  15.7 1.7 pad_maximum_fusion
  17.5 2.3 collective-permute-start.3
  19.8 18.9 %all-to-all-done = bf16[32,112,256]{2,1,0:T(8,128)(2,1)} async-done(((bf16[32,112,256]{2,1,0:T(8,128)(2,1)}), bf16[32,112,256]{2,1,0:T(8,128)(2,1)}, u32[]{:S(2)}, u32[]{:S(2)}) %all-to-all-start) | async-done | bytes 1835040 | tf_op jit(solution)/shard_map/all_to_all | solution.py:28
  38.7 6.8 %shard_map.122 = (bf16[256,1024]{1,0:T(8,128)(2,1)S(1)}, bf16[1024,256]{1,0:T(8,128)(2,1)}) custom-call(bf16[3584,256]{1,0:T(8,128)(2,1)} %bitcast.4.centered_ref, bf16[3584,1024]{1,0:T(8,128)(2,1)} %weight_ref.3, bf16[1,1024]{1,0:T(2,128)(2,1)S(1)} %reshape.49.bias_ref), custom_call_target="tpu_custom_call" | custom-call | flops 1879048192 | bytes 10225664 | tf_op jit(solution)/shard_map/pallas_call | solution.py:52
  45.5 4.5 %shard_map.123 = bf16[256,3712]{1,0:T(8,128)(2,1)} custom-call(bf16[256,1024]{1,0:T(8,128)(2,1)S(1)} %get-tuple-element.40.latents_ref, bf16[1024,3584]{1,0:T(8,128)(2,1)S(1)} %bitcast.29, bf16[112,256]{1,0:T(8,128)(2,1)S(1)} %bitcast.37), custom_call_target="tpu_custom_call" | custom-call | flops 1879048192 | bytes 9822208 | tf_op jit(solution)/shard_map/pallas_call | solution.py:52
  50.1 6.9 %all-to-all-start.1 = ((bf16[16,16,3712]{2,1,0:T(8,128)(2,1)}), bf16[16,16,3712]{2,1,0:T(8,128)(2,1)S(1)}, u32[]{:S(2)}, u32[]{:S(2)}) async-start(bf16[16,16,3712]{2,1,0:T(8,128)(2,1)} %bitcast.44), calls=%async_computation.1 | async-start | bytes 3801088 | tf_op jit(solution)/shard_map/all_to_all | solution.py:28
  57.0 0.5 collective-permute-start
  57.5 2.6 %constant_dynamic-slice_fusion.1 = (bf16[896,256]{1,0:T(8,128)(2,1)}, bf16[896,256]{1,0:T(8,128)(2,1)}, bf16[896,256]{1,0:T(8,128)(2,1)}, bf16[896,256]{1,0:T(8,128)(2,1)S(1)}) fusion(bf16[3584,256]{1,0:T(8,128)(2,1)} %bitcast.4.centered_ref, s32[]{:T(128)S(6)} %select_n.39, s32[]{:T(128)S(6)} %select_n.38, s32[]{:T(128)S(6)} %select_n.35, s32[]{:T(128)S(6)} %select_n.33), kind=kLoop, calls=%fused_computation.14 | loop fusion | bytes 3670032 | tf_op jit(solution)/shard_map/dynamic_slice | solution.py:424
  60.1 21.1 %all-to-all-done.1.pieces_ref = bf16[16,16,3712]{2,1,0:T(8,128)(2,1)S(1)} async-done(((bf16[16,16,3712]{2,1,0:T(8,128)(2,1)}), bf16[16,16,3712]{2,1,0:T(8,128)(2,1)S(1)}, u32[]{:S(2)}, u32[]{:S(2)}) %all-to-all-start.1) | async-done | bytes 1900576 | tf_op jit(solution)/shard_map/all_to_all | solution.py:28
  81.2 0.7 shard_map.124
  81.9 0.8 collective-permute-start.2
  82.7 5.4 %collective-permute-done.2.partner_ref = bf16[8,5632]{1,0:T(8,128)(2,1)S(1)} collective-permute-done((bf16[8,5632]{1,0:T(8,128)(2,1)S(1)}, bf16[8,5632]{1,0:T(8,128)(2,1)S(1)}, u32[]{:S(2)}, u32[]{:S(2)}) %collective-permute-start.2) | collective-permute-done | bytes 90144 | tf_op jit(solution)/shard_map/ppermute | solution.py:33
  88.1 1.1 shard_map.125
  89.2 2.1 collective-permute-done.3.refs_3_
  91.3 6.6 %all-to-all-start.2 = ((bf16[16,8,3584]{2,1,0:T(8,128)(2,1)}), bf16[16,8,3584]{2,1,0:T(8,128)(2,1)S(1)}, u32[]{:S(2)}, u32[]{:S(2)}) async-start(bf16[16,8,3584]{2,1,0:T(8,128)(2,1)} %get-tuple-element.52), calls=%async_computation.2 | async-start | bytes 1835008 | tf_op jit(solution)/shard_map/all_to_all | solution.py:28
  97.9 1.3 collective-permute-start.5
  99.2 13.4 %all-to-all-done.2 = bf16[16,8,3584]{2,1,0:T(8,128)(2,1)S(1)} async-done(((bf16[16,8,3584]{2,1,0:T(8,128)(2,1)}), bf16[16,8,3584]{2,1,0:T(8,128)(2,1)S(1)}, u32[]{:S(2)}, u32[]{:S(2)}) %all-to-all-start.2) | async-done | bytes 917536 | tf_op jit(solution)/shard_map/all_to_all | solution.py:28
  112.5 1.5 copy-done.6
  114.0 5.9 %shard_map.126 = (bf16[128,3584]{1,0:T(8,128)(2,1)}, f32[128,448]{1,0:T(8,128)}, f32[128,448]{1,0:T(8,128)}) custom-call(bf16[128,3584]{1,0:T(8,128)(2,1)S(1)} %bitcast.34, bf16[224,3584]{1,0:T(8,128)(2,1)} %bitcast.38, bf16[224,3584]{1,0:T(8,128)(2,1)} %bitcast.41, bf16[224,3584]{1,0:T(8,128)(2,1)} %refs_2_.3, ...), custom_call_target="tpu_custom_call" | custom-call | flops 1233125376 | bytes 11927552 | tf_op jit(solution)/shard_map/pallas_call | solution.py:52
  120.0 5.9 %all-to-all-start.3 = ((bf16[16,8,3584]{2,1,0:T(8,128)(2,1)}), bf16[16,8,3584]{2,1,0:T(8,128)(2,1)S(1)}, u32[]{:S(2)}, u32[]{:S(2)}) async-start(bf16[16,8,3584]{2,1,0:T(8,128)(2,1)} %bitcast.45), calls=%async_computation.3 | async-start | bytes 1835008 | tf_op jit(solution)/shard_map/all_to_all | solution.py:28
  126.0 0.1 collective-permute-start.6
  126.0 0.5 collective-permute-start.8
  126.5 0.1 collective-permute-start.7
  126.7 0.1 reshape.56.target_ref
  126.9 12.1 %all-to-all-done.3.pieces_ref = bf16[16,8,3584]{2,1,0:T(8,128)(2,1)S(1)} async-done(((bf16[16,8,3584]{2,1,0:T(8,128)(2,1)}), bf16[16,8,3584]{2,1,0:T(8,128)(2,1)S(1)}, u32[]{:S(2)}, u32[]{:S(2)}) %all-to-all-start.3) | async-done | bytes 917536 | tf_op jit(solution)/shard_map/all_to_all | solution.py:28
  139.0 1.4 shard_map.127
  140.4 17.8 %all_to_all.35 = bf16[16,8,3584]{2,1,0:T(8,128)(2,1)S(1)} all-to-all(bf16[16,8,3584]{2,1,0:T(8,128)(2,1)} %get-tuple-element.63), channel_id=1, replica_groups=mesh['batch_0'=2,'batch_1'=2,'tensor_0'=4,'tensor_1'=2,'latent'=4] {'ten..., dimensions={0} | all-to-all | bytes 1835008 | tf_op jit(solution)/shard_map/all_to_all | solution.py:28
  158.2 6.2 %shard_map.128 = bf16[128,3584]{1,0:T(8,128)(2,1)S(1)} custom-call(bf16[128,3584]{1,0:T(8,128)(2,1)S(1)} %bitcast.35, bf16[224,3584]{1,0:T(8,128)(2,1)} %bitcast.39, bf16[224,3584]{1,0:T(8,128)(2,1)} %bitcast.42, bf16[224,3584]{1,0:T(8,128)(2,1)} %refs_2_.3, bf16[3,112,3584]{2,1,0:T(8,128)(2,1)} %collective-permute-done.3.refs_3_, ...), custom_call_target="tpu_custom_call" | custom-call | flops 1233125376 | bytes 11927552 | tf_op jit(solution)/shard_map/pallas_call | solution.py:52
  164.5 16.0 %all_to_all.36.pieces_ref = bf16[16,8,3584]{2,1,0:T(8,128)(2,1)S(1)} all-to-all(bf16[16,8,3584]{2,1,0:T(8,128)(2,1)S(1)} %bitcast.36), channel_id=1, replica_groups=mesh['batch_0'=2,'batch_1'=2,'tensor_0'=4,'tensor_1'=2,'latent'=4] {'ten..., dimensions={0} | all-to-all | bytes 1835008 | tf_op jit(solution)/shard_map/all_to_all | solution.py:28
  180.5 0.4 shard_map.129
  180.9 28.6 %all_to_all.37 = bf16[32,8,3584]{2,1,0:T(8,128)(2,1)S(1)} all-to-all(bf16[32,8,3584]{2,1,0:T(8,128)(2,1)S(1)} %shard_map.129), channel_id=1, replica_groups=mesh['batch_0'=2,'batch_1'=2,'tensor_0'=4,'tensor_1'=2,'latent'=4] {'ten..., dimensions={0} | all-to-all | bytes 3670016 | tf_op jit(solution)/shard_map/all_to_all | solution.py:28
  209.5 2.9 %shard_map.130.refs_4_ = bf16[256,1024]{1,0:T(8,128)(2,1)S(1)} custom-call(bf16[256,3584]{1,0:T(8,128)(2,1)S(1)} %bitcast.32, bf16[1024,3584]{1,0:T(8,128)(2,1)S(1)} %bitcast.31, bf16[256,1024]{1,0:T(8,128)(2,1)S(1)} %copy-done.1), custom_call_target="tpu_custom_call" | custom-call | flops 1879048192 | bytes 10223616 | tf_op jit(solution)/shard_map/pallas_call | solution.py:52
  212.4 0.1 collective-permute-start.9
  212.5 0.2 constant_dynamic-slice_fusion
  212.7 2.1 collective-permute-start.11
  214.8 12.6 %collective-permute-done.9.refs_6_ = bf16[256,1024]{1,0:T(8,128)(2,1)S(1)} collective-permute-done((bf16[256,1024]{1,0:T(8,128)(2,1)S(1)}, bf16[256,1024]{1,0:T(8,128)(2,1)S(1)}, u32[]{:S(2)}, u32[]{:S(2)}) %collective-permute-start.9) | collective-permute-done | bytes 524320 | tf_op jit(solution)/shard_map/ppermute | solution.py:33
  227.4 0.5 collective-permute-start.12
  227.9 0.1 collective-permute-start.14
  228.0 9.2 %collective-permute-done.11.refs_5_ = bf16[256,896]{1,0:T(8,128)(2,1)S(1)} collective-permute-done((bf16[256,896]{1,0:T(8,128)(2,1)S(1)}, bf16[256,896]{1,0:T(8,128)(2,1)S(1)}, u32[]{:S(2)}, u32[]{:S(2)}) %collective-permute-start.11) | collective-permute-done | bytes 458784 | tf_op jit(solution)/shard_map/ppermute | solution.py:33
  237.2 3.1 %shard_map.131.refs_2_ = f32[1024,896]{1,0:T(8,128)S(1)} custom-call(bf16[1024,256]{1,0:T(8,128)(2,1)} %get-tuple-element.60.refs_0_, bf16[1024,256]{1,0:T(8,128)(2,1)} %copy-done.12, bf16[1024,256]{1,0:T(8,128)(2,1)} %copy-done.9, bf16[256,896]{1,0:T(8,128)(2,1)S(1)} %get-tuple-element.79.refs_3_, bf16[256,896]{1,0:T(8,128)(2,1)S(1)} %collective-permute-done.10.refs_4_, ...), custom_call_target="tpu_custom_call" | custom-call | flops 1409286144 | bytes 6619136 | tf_op jit(solution)/shard_map/pallas_call | solution.py:52
  240.3 5.1 %shard_map.132 = bf16[896,1024]{1,0:T(8,128)(2,1)} custom-call(bf16[896,256]{1,0:T(8,128)(2,1)} %get-tuple-element.80.refs_0_, bf16[896,256]{1,0:T(8,128)(2,1)} %collective-permute-done.8.refs_1_, bf16[896,256]{1,0:T(8,128)(2,1)} %collective-permute-done.5.refs_2_, bf16[896,256]{1,0:T(8,128)(2,1)} %collective-permute-done.1.refs_3_, ...), custom_call_target="tpu_custom_call" | custom-call | flops 1879048192 | bytes 5767168 | tf_op jit(solution)/shard_map/pallas_call | solution.py:52
  245.5 4.0 %shard_map.133 = bf16[1024,896]{1,0:T(8,128)(2,1)} custom-call(bf16[1024,256]{1,0:T(8,128)(2,1)} %copy-done.11, bf16[256,896]{1,0:T(8,128)(2,1)S(1)} %collective-permute-done.14.refs_1_, f32[1024,896]{1,0:T(8,128)S(1)} %shard_map.131.refs_2_), custom_call_target="tpu_custom_call" | custom-call | flops 469762048 | bytes 6488064 | tf_op jit(solution)/shard_map/pallas_call | solution.py:52
  (69 shorter events, 0.3 us)
Async XLA Ops:
  3.7 10.5 %copy-start.3 = (bf16[3584,224]{0,1:T(8,128)(2,1)S(1)}, bf16[3584,224]{0,1:T(8,128)(2,1)}, u32[]{:S(2)}) copy-start(bf16[3584,224]{0,1:T(8,128)(2,1)} %param.19) | copy-start | bytes 4816900
  3.7 10.6 %copy-start.4 = (bf16[3584,224]{0,1:T(8,128)(2,1)S(1)}, bf16[3584,224]{0,1:T(8,128)(2,1)}, u32[]{:S(2)}) copy-start(bf16[3584,224]{0,1:T(8,128)(2,1)} %param.20) | copy-start | bytes 4816900
  3.7 35.0 %all-to-all-start = ((bf16[32,112,256]{2,1,0:T(8,128)(2,1)}), bf16[32,112,256]{2,1,0:T(8,128)(2,1)}, u32[]{:S(2)}, u32[]{:S(2)}) async-start(bf16[32,112,256]{2,1,0:T(8,128)(2,1)} %broadcast_in_dim.4), calls=%async_computation | async-start | bytes 3670016 | tf_op jit(solution)/shard_map/all_to_all | solution.py:28
  14.2 1.4 copy-start.5
  15.7 4.0 %copy-start.17 = (bf16[1024]{0:T(1024)(128)(2,1)S(1)}, bf16[1024]{0:T(1024)(128)(2,1)}, u32[]{:S(2)}) copy-start(bf16[1024]{0:T(1024)(128)(2,1)} %param.14) | copy-start | bytes 6148
  15.7 29.8 %slice-start = ((s8[7340032]{0:T(1024)(128)(4,1)}), s8[3145728]{0:T(1024)(128)(4,1)S(1)}, s32[]{:S(2)}) async-start(s8[7340032]{0:T(1024)(128)(4,1)} %bitcast.28), calls=%async_computation.7 | async-start | bytes 6291456
  17.5 73.8 %collective-permute-start.3 = (bf16[3,112,3584]{2,1,0:T(8,128)(2,1)}, bf16[3,112,3584]{2,1,0:T(8,128)(2,1)}, u32[]{:S(2)}, u32[]{:S(2)}) collective-permute-start(bf16[3,112,3584]{2,1,0:T(8,128)(2,1)} %pad_maximum_fusion), channel_id=1, source_target_pairs={{0,68},{4,64},{64,4},{68,0},{1,69},{5,65},{65,5},{69,1},{2,70},{6,... | collective-permute-start | bytes 7225352 | tf_op jit(solution)/shard_map/ppermute | solution.py:33
  38.7 6.8 %slice-start.1 = ((s8[7340032]{0:T(1024)(128)(4,1)}), s8[4194304]{0:T(1024)(128)(4,1)S(1)}, s32[]{:S(2)}) async-start(s8[7340032]{0:T(1024)(128)(4,1)} %bitcast.28), calls=%async_computation.8 | async-start | bytes 8388608
  38.7 6.8 %copy-start.2 = (bf16[256,112]{0,1:T(8,128)(2,1)S(1)}, bf16[256,112]{0,1:T(8,128)(2,1)}, u32[]{:S(2)}) copy-start(bf16[256,112]{0,1:T(8,128)(2,1)} %param.12) | copy-start | bytes 172036
  45.5 4.6 %copy-start = (bf16[256,1024]{1,0:T(8,128)(2,1)}, bf16[256,1024]{1,0:T(8,128)(2,1)S(1)}, u32[]{:S(2)}) copy-start(bf16[256,1024]{1,0:T(8,128)(2,1)S(1)} %get-tuple-element.40.latents_ref) | copy-start | bytes 1572868
  50.0 6.9 %copy-start.7 = (bf16[1024,256]{1,0:T(8,128)(2,1)S(1)}, bf16[1024,256]{1,0:T(8,128)(2,1)}, u32[]{:S(2)}) copy-start(bf16[1024,256]{1,0:T(8,128)(2,1)} %get-tuple-element.60.refs_0_) | copy-start | bytes 1572868
  50.1 31.1 %all-to-all-start.1 = ((bf16[16,16,3712]{2,1,0:T(8,128)(2,1)}), bf16[16,16,3712]{2,1,0:T(8,128)(2,1)S(1)}, u32[]{:S(2)}, u32[]{:S(2)}) async-start(bf16[16,16,3712]{2,1,0:T(8,128)(2,1)} %bitcast.44), calls=%async_computation.1 | async-start | bytes 3801088 | tf_op jit(solution)/shard_map/all_to_all | solution.py:28
  57.0 24.9 %collective-permute-start = (bf16[1024,256]{1,0:T(8,128)(2,1)S(1)}, bf16[1024,256]{1,0:T(8,128)(2,1)S(1)}, u32[]{:S(2)}, u32[]{:S(2)}) collective-permute-start(bf16[1024,256]{1,0:T(8,128)(2,1)S(1)} %copy-done.7), channel_id=1, source_target_pairs={{0,64},{64,0},{1,65},{65,1},{2,66},{66,2},{3,67},{67,3},{4,68},{68... | collective-permute-start | bytes 1572872 | tf_op jit(solution)/shard_map/ppermute | solution.py:33
  60.1 22.5 %copy-start.14 = (bf16[3584]{0:T(1024)(128)(2,1)S(1)}, bf16[3584]{0:T(1024)(128)(2,1)}, u32[]{:S(2)}) copy-start(bf16[3584]{0:T(1024)(128)(2,1)} %param.16) | copy-start | bytes 21508
  60.1 22.6 %copy-start.15 = (bf16[3584]{0:T(1024)(128)(2,1)S(1)}, bf16[3584]{0:T(1024)(128)(2,1)}, u32[]{:S(2)}) copy-start(bf16[3584]{0:T(1024)(128)(2,1)} %param.17) | copy-start | bytes 21508
  60.1 21.8 %collective-permute-start.1 = (bf16[896,256]{1,0:T(8,128)(2,1)S(1)}, bf16[896,256]{1,0:T(8,128)(2,1)}, u32[]{:S(2)}, u32[]{:S(2)}) collective-permute-start(bf16[896,256]{1,0:T(8,128)(2,1)S(1)} %get-tuple-element.83), channel_id=1, source_target_pairs={{0,96},{32,64},{64,32},{96,0},{1,97},{33,65},{65,33},{97,1},{2,98}... | collective-permute-start | bytes 1376264 | tf_op jit(solution)/shard_map/ppermute | solution.py:33
  81.9 9.4 %copy-start.9 = (bf16[1024,256]{1,0:T(8,128)(2,1)}, bf16[1024,256]{1,0:T(8,128)(2,1)S(1)}, u32[]{:S(2)}) copy-start(bf16[1024,256]{1,0:T(8,128)(2,1)S(1)} %collective-permute-done.refs_2_) | copy-start | bytes 1572868
  81.9 6.2 %collective-permute-start.2 = (bf16[8,5632]{1,0:T(8,128)(2,1)S(1)}, bf16[8,5632]{1,0:T(8,128)(2,1)S(1)}, u32[]{:S(2)}, u32[]{:S(2)}) collective-permute-start(bf16[8,5632]{1,0:T(8,128)(2,1)S(1)} %get-tuple-element.47), channel_id=1, source_target_pairs={{0,4},{4,0},{1,5},{5,1},{2,6},{6,2},{3,7},{7,3},{8,12},{12,8},{9,1... | collective-permute-start | bytes 270344 | tf_op jit(solution)/shard_map/ppermute | solution.py:33
  91.3 21.3 %collective-permute-start.4 = (bf16[3,112,3584]{2,1,0:T(8,128)(2,1)}, bf16[3,112,3584]{2,1,0:T(8,128)(2,1)S(1)}, u32[]{:S(2)}, u32[]{:S(2)}) collective-permute-start(bf16[3,112,3584]{2,1,0:T(8,128)(2,1)} %collective-permute-done.3.refs_3_), channel_id=1, source_target_pairs={{0,32},{32,0},{1,33},{33,1},{2,34},{34,2},{3,35},{35,3},{4,36},{36... | collective-permute-start | bytes 7225352 | tf_op jit(solution)/shard_map/ppermute | solution.py:33
  91.3 21.3 %all-to-all-start.2 = ((bf16[16,8,3584]{2,1,0:T(8,128)(2,1)}), bf16[16,8,3584]{2,1,0:T(8,128)(2,1)S(1)}, u32[]{:S(2)}, u32[]{:S(2)}) async-start(bf16[16,8,3584]{2,1,0:T(8,128)(2,1)} %get-tuple-element.52), calls=%async_computation.2 | async-start | bytes 1835008 | tf_op jit(solution)/shard_map/all_to_all | solution.py:28
  97.9 22.1 %collective-permute-start.5 = (bf16[896,256]{1,0:T(8,128)(2,1)}, bf16[896,256]{1,0:T(8,128)(2,1)}, u32[]{:S(2)}, u32[]{:S(2)}) collective-permute-start(bf16[896,256]{1,0:T(8,128)(2,1)} %get-tuple-element.82), channel_id=1, source_target_pairs={{0,64},{64,0},{1,65},{65,1},{2,66},{66,2},{3,67},{67,3},{4,68},{68... | collective-permute-start | bytes 1376264 | tf_op jit(solution)/shard_map/ppermute | solution.py:33
  112.5 1.5 copy-start.6
  119.9 6.0 %copy-start.16 = (bf16[3584]{0:T(1024)(128)(2,1)S(1)}, bf16[3584]{0:T(1024)(128)(2,1)}, u32[]{:S(2)}) copy-start(bf16[3584]{0:T(1024)(128)(2,1)} %param.18) | copy-start | bytes 21508
  119.9 6.0 %copy-start.8 = (bf16[1024,256]{1,0:T(8,128)(2,1)S(1)}, bf16[1024,256]{1,0:T(8,128)(2,1)}, u32[]{:S(2)}) copy-start(bf16[1024,256]{1,0:T(8,128)(2,1)} %get-tuple-element.60.refs_0_) | copy-start | bytes 1572868
  119.9 6.6 %copy-start.10 = (bf16[1024,256]{1,0:T(8,128)(2,1)S(1)}, bf16[1024,256]{1,0:T(8,128)(2,1)}, u32[]{:S(2)}) copy-start(bf16[1024,256]{1,0:T(8,128)(2,1)} %copy-done.9) | copy-start | bytes 1572868
  120.0 6.7 %copy-start.13 = (bf16[16,8,128]{2,1,0:T(8,128)(2,1)S(1)}, bf16[16,8,128]{2,1,0:T(8,128)(2,1)}, u32[]{:S(2)}) copy-start(bf16[16,8,128]{2,1,0:T(8,128)(2,1)} %get-tuple-element.57) | copy-start | bytes 98308
  120.0 19.0 %all-to-all-start.3 = ((bf16[16,8,3584]{2,1,0:T(8,128)(2,1)}), bf16[16,8,3584]{2,1,0:T(8,128)(2,1)S(1)}, u32[]{:S(2)}, u32[]{:S(2)}) async-start(bf16[16,8,3584]{2,1,0:T(8,128)(2,1)} %bitcast.45), calls=%async_computation.3 | async-start | bytes 1835008 | tf_op jit(solution)/shard_map/all_to_all | solution.py:28
  126.0 14.4 %collective-permute-start.6 = (bf16[1024,256]{1,0:T(8,128)(2,1)S(1)}, bf16[1024,256]{1,0:T(8,128)(2,1)S(1)}, u32[]{:S(2)}, u32[]{:S(2)}) collective-permute-start(bf16[1024,256]{1,0:T(8,128)(2,1)S(1)} %copy-done.8), channel_id=1, source_target_pairs={{0,32},{32,0},{1,33},{33,1},{2,34},{34,2},{3,35},{35,3},{4,36},{36... | collective-permute-start | bytes 1572872 | tf_op jit(solution)/shard_map/ppermute | solution.py:33
  126.0 14.3 %collective-permute-start.8 = (bf16[896,256]{1,0:T(8,128)(2,1)}, bf16[896,256]{1,0:T(8,128)(2,1)}, u32[]{:S(2)}, u32[]{:S(2)}) collective-permute-start(bf16[896,256]{1,0:T(8,128)(2,1)} %get-tuple-element.81), channel_id=1, source_target_pairs={{0,32},{32,0},{1,33},{33,1},{2,34},{34,2},{3,35},{35,3},{4,36},{36... | collective-permute-start | bytes 1376264 | tf_op jit(solution)/shard_map/ppermute | solution.py:33
  126.5 13.8 %collective-permute-start.7 = (bf16[1024,256]{1,0:T(8,128)(2,1)S(1)}, bf16[1024,256]{1,0:T(8,128)(2,1)S(1)}, u32[]{:S(2)}, u32[]{:S(2)}) collective-permute-start(bf16[1024,256]{1,0:T(8,128)(2,1)S(1)} %copy-done.10), channel_id=1, source_target_pairs={{0,32},{32,0},{1,33},{33,1},{2,34},{34,2},{3,35},{35,3},{4,36},{36... | collective-permute-start | bytes 1572872 | tf_op jit(solution)/shard_map/ppermute | solution.py:33
  140.3 24.1 %copy-start.12 = (bf16[1024,256]{1,0:T(8,128)(2,1)}, bf16[1024,256]{1,0:T(8,128)(2,1)S(1)}, u32[]{:S(2)}) copy-start(bf16[1024,256]{1,0:T(8,128)(2,1)S(1)} %collective-permute-done.6.refs_1_) | copy-start | bytes 1572868
  140.4 24.1 %copy-start.11 = (bf16[1024,256]{1,0:T(8,128)(2,1)}, bf16[1024,256]{1,0:T(8,128)(2,1)S(1)}, u32[]{:S(2)}) copy-start(bf16[1024,256]{1,0:T(8,128)(2,1)S(1)} %collective-permute-done.7.refs_0_) | copy-start | bytes 1572868
  140.4 69.1 %slice-start.2 = ((s8[7340032]{0:T(1024)(128)(4,1)}), s8[4194304]{0:T(1024)(128)(4,1)S(1)}, s32[]{:S(2)}) async-start(s8[7340032]{0:T(1024)(128)(4,1)} %bitcast.30), calls=%async_computation.9 | async-start | bytes 8388608
  158.2 51.3 %slice-start.3 = ((s8[7340032]{0:T(1024)(128)(4,1)}), s8[3145728]{0:T(1024)(128)(4,1)S(1)}, s32[]{:S(2)}) async-start(s8[7340032]{0:T(1024)(128)(4,1)} %bitcast.30), calls=%async_computation.10 | async-start | bytes 6291456
  180.9 28.6 %copy-start.1 = (bf16[256,1024]{1,0:T(8,128)(2,1)S(1)}, bf16[256,1024]{1,0:T(8,128)(2,1)}, u32[]{:S(2)}) copy-start(bf16[256,1024]{1,0:T(8,128)(2,1)} %copy-done) | copy-start | bytes 1572868
  212.4 14.9 %collective-permute-start.9 = (bf16[256,1024]{1,0:T(8,128)(2,1)S(1)}, bf16[256,1024]{1,0:T(8,128)(2,1)S(1)}, u32[]{:S(2)}, u32[]{:S(2)}) collective-permute-start(bf16[256,1024]{1,0:T(8,128)(2,1)S(1)} %shard_map.130.refs_4_), channel_id=1, source_target_pairs={{0,64},{64,0},{1,65},{65,1},{2,66},{66,2},{3,67},{67,3},{4,68},{68... | collective-permute-start | bytes 1572872 | tf_op jit(solution)/shard_map/ppermute | solution.py:33
  212.7 24.5 %collective-permute-start.11 = (bf16[256,896]{1,0:T(8,128)(2,1)S(1)}, bf16[256,896]{1,0:T(8,128)(2,1)S(1)}, u32[]{:S(2)}, u32[]{:S(2)}) collective-permute-start(bf16[256,896]{1,0:T(8,128)(2,1)S(1)} %get-tuple-element.77), channel_id=1, source_target_pairs={{0,64},{64,0},{1,65},{65,1},{2,66},{66,2},{3,67},{67,3},{4,68},{68... | collective-permute-start | bytes 1376264 | tf_op jit(solution)/shard_map/ppermute | solution.py:33
  227.4 9.8 %collective-permute-start.10 = (bf16[256,896]{1,0:T(8,128)(2,1)S(1)}, bf16[256,896]{1,0:T(8,128)(2,1)S(1)}, u32[]{:S(2)}, u32[]{:S(2)}) collective-permute-start(bf16[256,896]{1,0:T(8,128)(2,1)S(1)} %get-tuple-element.67), channel_id=1, source_target_pairs={{0,32},{32,0},{1,33},{33,1},{2,34},{34,2},{3,35},{35,3},{4,36},{36... | collective-permute-start | bytes 1376264 | tf_op jit(solution)/shard_map/ppermute | solution.py:33
  227.4 13.0 %collective-permute-start.12 = (bf16[256,1024]{1,0:T(8,128)(2,1)S(1)}, bf16[256,1024]{1,0:T(8,128)(2,1)S(1)}, u32[]{:S(2)}, u32[]{:S(2)}) collective-permute-start(bf16[256,1024]{1,0:T(8,128)(2,1)S(1)} %shard_map.130.refs_4_), channel_id=1, source_target_pairs={{0,32},{32,0},{1,33},{33,1},{2,34},{34,2},{3,35},{35,3},{4,36},{36... | collective-permute-start | bytes 1572872 | tf_op jit(solution)/shard_map/ppermute | solution.py:33
  227.9 12.5 %collective-permute-start.13 = (bf16[256,1024]{1,0:T(8,128)(2,1)S(1)}, bf16[256,1024]{1,0:T(8,128)(2,1)S(1)}, u32[]{:S(2)}, u32[]{:S(2)}) collective-permute-start(bf16[256,1024]{1,0:T(8,128)(2,1)S(1)} %collective-permute-done.9.refs_6_), channel_id=1, source_target_pairs={{0,32},{32,0},{1,33},{33,1},{2,34},{34,2},{3,35},{35,3},{4,36},{36... | collective-permute-start | bytes 1572872 | tf_op jit(solution)/shard_map/ppermute | solution.py:33
  227.9 17.6 %collective-permute-start.14 = (bf16[256,896]{1,0:T(8,128)(2,1)S(1)}, bf16[256,896]{1,0:T(8,128)(2,1)S(1)}, u32[]{:S(2)}, u32[]{:S(2)}) collective-permute-start(bf16[256,896]{1,0:T(8,128)(2,1)S(1)} %get-tuple-element.76), channel_id=1, source_target_pairs={{0,96},{32,64},{64,32},{96,0},{1,97},{33,65},{65,33},{97,1},{2,98}... | collective-permute-start | bytes 1376264 | tf_op jit(solution)/shard_map/ppermute | solution.py:33

commit v11 on v10

--- a/solution.py
+++ b/solution.py
@@ -155,18 +155,18 @@
 def decode(latents, weight, turned_target, room):
     tokens, count = latents.shape
     width = weight.shape[1]
-    tile = width // 7
+    tile = width // 4
     return call(
         decode_kernel,
         hbm_array((tokens, width + room)),
         2 * tokens * width * count,
         [latents, weight, turned_target],
-        grid=(7,),
+        grid=(width // tile,),
         in_specs=[WHOLE, pl.BlockSpec((count, tile), lambda j: (0, j)), WHOLE],
         out_specs=pl.BlockSpec(memory_space=pl.ANY),
         scratch_shapes=[
             pltpu.VMEM((tokens, width + room), bf16),
-            pltpu.SemaphoreType.DMA((8,)),
+            pltpu.SemaphoreType.DMA((width // tile + 1,)),
         ],
     )
 
@@ -305,7 +305,7 @@
         body,
         outs,
         6 * rows.shape[0] * width * units,
-        [rows, *(in_hbm(a) for a in (*weights, near, far, *saved))],
+        [rows, *map(in_hbm, weights), in_hbm(near), far, *map(in_hbm, saved)],
         in_specs=[WHOLE] + [anywhere] * 5 + [pl.BlockSpec()] * len(saved),
         scratch_shapes=[pltpu.VMEM((3, units, width), bf16), pltpu.SemaphoreType.DMA((3, 3))],
     )
@@ -334,16 +334,20 @@
     )
 
 
-def products_kernel(spans, count, *refs):
+def products_kernel(tile, count, *refs):
     out_ref = refs[-1]
     left = jnp.concatenate([ref[...] for ref in refs[:count]], axis=1)
-    for span in spans:
-        right = jnp.concatenate([ref[:, span] for ref in refs[count : 2 * count]], axis=0)
+    first = pl.program_id(1) * tile
+    for at in range(0, tile, 256):
+        size = min(256, tile - at)
+        columns = pl.ds(pl.multiple_of(first + at, 128), size)
+        span = slice(at, at + size)
+        right = jnp.concatenate([ref[:, columns] for ref in refs[count : 2 * count]], axis=0)
         total = product(left, right)
         if len(refs) > 2 * count + 1:
             rows = out_ref.shape[0]
-            at = pl.multiple_of(pl.program_id(0) * rows, rows)
-            total += refs[2 * count][pl.ds(at, rows), span]
+            start = pl.multiple_of(pl.program_id(0) * rows, rows)
+            total += refs[2 * count][pl.ds(start, rows), span]
         out_ref[:, span] = total.astype(out_ref.dtype)
 
 
@@ -351,17 +355,16 @@
     rows, depth = left[0].shape
     columns = right[0].shape[1]
     rows_tile = rows_tile or rows
-    spans = [slice(at, min(at + 256, tile)) for at in range(0, tile, 256)]
     count = len(left)
     out_spec = pl.BlockSpec((rows_tile, tile), lambda i, j: (i, j))
     return call(
-        functools.partial(products_kernel, spans, count),
+        functools.partial(products_kernel, tile, count),
         array((rows, columns), kind),
         2 * rows * depth * columns * count,
         [*map(in_hbm, left), *right, *([] if start is None else [start])],
         grid=(rows // rows_tile, columns // tile),
         in_specs=[pl.BlockSpec((rows_tile, depth), lambda i, j: (i, 0))] * count
-        + [pl.BlockSpec((depth, tile), lambda i, j: (0, j))] * count
+        + [WHOLE] * count
         + ([] if start is None else [WHOLE]),
         out_specs=out_spec,
     )
@@ -413,7 +416,7 @@
     near = swap(sent, OTHER_HALF)
     centered = exchange(pieces, SHARDS).reshape(width, tokens)
 
-    latents, turned_latents = encode(centered, encoder_weight, encoder_bias, 256)
+    latents, turned_latents = encode(centered, encoder_weight, encoder_bias, 512)
     partial_recon = decode(latents, decoder_weight, target.T, 128)
 
     partial_recon, centered, turned_latents = lax.optimization_barrier(
@@ -476,7 +479,7 @@
     )
     grad_output = all_tokens(pieces, HALF)
     partial_input = with_weights(
-        backward_kernel, array((rows, width)), grad_output, weights, near, far, saved
+        backward_kernel, array((rows, width)), grad_output, weights, near, in_hbm(far), saved
     )
     (pieces,) = local(
         input_kernel, [everyone], [to_owners(partial_input, HALF), recon, grad_result, gain_in]
@@ -490,15 +493,15 @@
     ]
     recon_blocks[2] = swap(recon_blocks[2], BATCH[0])
     recon_blocks[3] = swap(recon_blocks[3], BATCH)
-    grad_preact = grad_of_preact(grad_recon, decoder_weight, latents, 256)
+    grad_preact = grad_of_preact(grad_recon, decoder_weight, latents, 512)
     far = swap(grad_preact, BATCH[0])
     far, near, recon_blocks[1] = lax.optimization_barrier((far, grad_preact, recon_blocks[1]))
     recon_blocks[1] = swap(recon_blocks[1], BATCH[1])
     preact_blocks = [grad_preact, swap(near, BATCH[1]), far, swap(far, BATCH[1])]
     part = sum_of_products(latent_blocks[:3], recon_blocks[:3], block, kind=f32)
-    encoder_grad = sum_of_products(centered_blocks, preact_blocks, 256)
+    encoder_grad = sum_of_products(centered_blocks, preact_blocks, 512)
     part, encoder_grad = lax.optimization_barrier((part, encoder_grad))
-    decoder_grad = sum_of_products(latent_blocks[3:], recon_blocks[3:], block, 256, part)
+    decoder_grad = sum_of_products(latent_blocks[3:], recon_blocks[3:], block, 512, part)
     return encoder_grad, decoder_grad
 
 

time: 250 us -> 247 us (0.988)
  Pallas kernels: 42.1 us -> 39.6 us
where the time goes in v11:
time: 247 us
  waiting for transfers between devices  95.8 us (39%)
  blocking collectives  62.7 us (25%)
  Pallas kernels  39.6 us (16%)
  starting transfers between devices  38.3 us (16%)
  local copies, waits for them, and re-layouts  5.87 us (2%)
  other arithmetic  3.43 us (1%)
    all_to_all x4, waiting for transfers between devices, exchange(): return lax.all_to_all(pieces, axes, split_axis=0, concat_axis=0, tiled=True)  65.5 us
    all_to_all x3, blocking collectives, exchange(): return lax.all_to_all(pieces, axes, split_axis=0, concat_axis=0, tiled=True)  62.7 us
    pallas_call x12, Pallas kernels, call(): pl.pallas_call(body, out_shape=outs, cost_estimate=cost, compiler_params=...  39.6 us
    ppermute x15, waiting for transfers between devices, swap(): lax.ppermute(block, axes, [(i, for_all - 1 - i) for i in range(for_all)])  30.3 us
    all_to_all x4, starting transfers between devices, exchange(): return lax.all_to_all(pieces, axes, split_axis=0, concat_axis=0, tiled=True)  29.9 us
    ppermute x15, starting transfers between devices, swap(): lax.ppermute(block, axes, [(i, for_all - 1 - i) for i in range(for_all)])  8.34 us
  transfers between devices with their start and end apart: 19, of which 8 were waited for; matrix products, arithmetic and copies ran while one was open for 2% of the time, Pallas kernels for 11%

profile of v11, /device:TPU:14, one launch (start us, length us, event | category | flops | bytes accessed | tf_op | source)
XLA Modules:
  0.0 246.7 jit_solution(7678417364174807559)
XLA Ops:
  0.6 0.8 dynamic-slice_convert_fusion
  1.4 0.9 fusion.2
  2.3 1.3 broadcast_in_dim.4
  3.7 10.5 %all-to-all-start = ((bf16[32,112,256]{2,1,0:T(8,128)(2,1)}), bf16[32,112,256]{2,1,0:T(8,128)(2,1)}, u32[]{:S(2)}, u32[]{:S(2)}) async-start(bf16[32,112,256]{2,1,0:T(8,128)(2,1)} %broadcast_in_dim.4), calls=%async_computation | async-start | bytes 3670016 | tf_op jit(solution)/shard_map/all_to_all | solution.py:28
  14.2 0.1 dynamic-slice_bitcast_fusion.2
  14.3 1.3 copy-done.6
  15.6 0.1 dynamic-slice_bitcast_fusion
  15.7 1.7 pad_maximum_fusion
  17.5 2.3 collective-permute-start.3
  19.8 18.9 %all-to-all-done = bf16[32,112,256]{2,1,0:T(8,128)(2,1)} async-done(((bf16[32,112,256]{2,1,0:T(8,128)(2,1)}), bf16[32,112,256]{2,1,0:T(8,128)(2,1)}, u32[]{:S(2)}, u32[]{:S(2)}) %all-to-all-start) | async-done | bytes 1835040 | tf_op jit(solution)/shard_map/all_to_all | solution.py:28
  38.7 5.9 %shard_map.122 = (bf16[256,1024]{1,0:T(8,128)(2,1)S(1)}, bf16[1024,256]{1,0:T(8,128)(2,1)}) custom-call(bf16[3584,256]{1,0:T(8,128)(2,1)} %bitcast.4.centered_ref, bf16[3584,1024]{1,0:T(8,128)(2,1)} %weight_ref.3, bf16[1,1024]{1,0:T(2,128)(2,1)S(1)} %reshape.49.bias_ref), custom_call_target="tpu_custom_call" | custom-call | flops 1879048192 | bytes 10225664 | tf_op jit(solution)/shard_map/pallas_call | solution.py:52
  44.7 4.4 %shard_map.123 = bf16[256,3712]{1,0:T(8,128)(2,1)} custom-call(bf16[256,1024]{1,0:T(8,128)(2,1)S(1)} %get-tuple-element.40.latents_ref, bf16[1024,3584]{1,0:T(8,128)(2,1)S(1)} %bitcast.29, bf16[112,256]{1,0:T(8,128)(2,1)S(1)} %bitcast.37), custom_call_target="tpu_custom_call" | custom-call | flops 1879048192 | bytes 9822208 | tf_op jit(solution)/shard_map/pallas_call | solution.py:52
  49.1 6.9 %all-to-all-start.1 = ((bf16[16,16,3712]{2,1,0:T(8,128)(2,1)}), bf16[16,16,3712]{2,1,0:T(8,128)(2,1)S(1)}, u32[]{:S(2)}, u32[]{:S(2)}) async-start(bf16[16,16,3712]{2,1,0:T(8,128)(2,1)} %bitcast.44), calls=%async_computation.1 | async-start | bytes 3801088 | tf_op jit(solution)/shard_map/all_to_all | solution.py:28
  56.0 0.5 collective-permute-start
  56.5 2.6 %constant_dynamic-slice_fusion.1 = (bf16[896,256]{1,0:T(8,128)(2,1)}, bf16[896,256]{1,0:T(8,128)(2,1)}, bf16[896,256]{1,0:T(8,128)(2,1)}, bf16[896,256]{1,0:T(8,128)(2,1)S(1)}) fusion(bf16[3584,256]{1,0:T(8,128)(2,1)} %bitcast.4.centered_ref, s32[]{:T(128)S(6)} %select_n.39, s32[]{:T(128)S(6)} %select_n.38, s32[]{:T(128)S(6)} %select_n.35, s32[]{:T(128)S(6)} %select_n.33), kind=kLoop, calls=%fused_computation.14 | loop fusion | bytes 3670032 | tf_op jit(solution)/shard_map/dynamic_slice | solution.py:427
  59.1 21.1 %all-to-all-done.1.pieces_ref = bf16[16,16,3712]{2,1,0:T(8,128)(2,1)S(1)} async-done(((bf16[16,16,3712]{2,1,0:T(8,128)(2,1)}), bf16[16,16,3712]{2,1,0:T(8,128)(2,1)S(1)}, u32[]{:S(2)}, u32[]{:S(2)}) %all-to-all-start.1) | async-done | bytes 1900576 | tf_op jit(solution)/shard_map/all_to_all | solution.py:28
  80.2 0.6 shard_map.124
  80.9 0.8 collective-permute-start.2
  81.7 5.4 %collective-permute-done.2.partner_ref = bf16[8,5632]{1,0:T(8,128)(2,1)S(1)} collective-permute-done((bf16[8,5632]{1,0:T(8,128)(2,1)S(1)}, bf16[8,5632]{1,0:T(8,128)(2,1)S(1)}, u32[]{:S(2)}, u32[]{:S(2)}) %collective-permute-start.2) | collective-permute-done | bytes 90144 | tf_op jit(solution)/shard_map/ppermute | solution.py:33
  87.1 1.1 shard_map.125
  88.2 3.0 %collective-permute-done.3.refs_3_ = bf16[3,112,3584]{2,1,0:T(8,128)(2,1)} collective-permute-done((bf16[3,112,3584]{2,1,0:T(8,128)(2,1)}, bf16[3,112,3584]{2,1,0:T(8,128)(2,1)}, u32[]{:S(2)}, u32[]{:S(2)}) %collective-permute-start.3) | collective-permute-done | bytes 2408480 | tf_op jit(solution)/shard_map/ppermute | solution.py:33
  91.3 6.6 %all-to-all-start.2 = ((bf16[16,8,3584]{2,1,0:T(8,128)(2,1)}), bf16[16,8,3584]{2,1,0:T(8,128)(2,1)S(1)}, u32[]{:S(2)}, u32[]{:S(2)}) async-start(bf16[16,8,3584]{2,1,0:T(8,128)(2,1)} %get-tuple-element.52), calls=%async_computation.2 | async-start | bytes 1835008 | tf_op jit(solution)/shard_map/all_to_all | solution.py:28
  97.9 1.3 collective-permute-start.5
  99.2 13.4 %all-to-all-done.2 = bf16[16,8,3584]{2,1,0:T(8,128)(2,1)S(1)} async-done(((bf16[16,8,3584]{2,1,0:T(8,128)(2,1)}), bf16[16,8,3584]{2,1,0:T(8,128)(2,1)S(1)}, u32[]{:S(2)}, u32[]{:S(2)}) %all-to-all-start.2) | async-done | bytes 917536 | tf_op jit(solution)/shard_map/all_to_all | solution.py:28
  112.5 6.5 %shard_map.126 = (bf16[128,3584]{1,0:T(8,128)(2,1)}, f32[128,448]{1,0:T(8,128)}, f32[128,448]{1,0:T(8,128)}) custom-call(bf16[128,3584]{1,0:T(8,128)(2,1)S(1)} %bitcast.34, bf16[224,3584]{1,0:T(8,128)(2,1)} %bitcast.38, bf16[224,3584]{1,0:T(8,128)(2,1)} %bitcast.41, bf16[224,3584]{1,0:T(8,128)(2,1)} %refs_2_.3, ...), custom_call_target="tpu_custom_call" | custom-call | flops 1233125376 | bytes 11927552 | tf_op jit(solution)/shard_map/pallas_call | solution.py:52
  119.1 5.9 %all-to-all-start.3 = ((bf16[16,8,3584]{2,1,0:T(8,128)(2,1)}), bf16[16,8,3584]{2,1,0:T(8,128)(2,1)S(1)}, u32[]{:S(2)}, u32[]{:S(2)}) async-start(bf16[16,8,3584]{2,1,0:T(8,128)(2,1)} %bitcast.45), calls=%async_computation.3 | async-start | bytes 1835008 | tf_op jit(solution)/shard_map/all_to_all | solution.py:28
  125.1 0.1 collective-permute-start.6
  125.2 0.5 collective-permute-start.8
  125.7 0.1 collective-permute-start.7
  125.9 0.1 reshape.56.target_ref
  126.0 12.1 %all-to-all-done.3.pieces_ref = bf16[16,8,3584]{2,1,0:T(8,128)(2,1)S(1)} async-done(((bf16[16,8,3584]{2,1,0:T(8,128)(2,1)}), bf16[16,8,3584]{2,1,0:T(8,128)(2,1)S(1)}, u32[]{:S(2)}, u32[]{:S(2)}) %all-to-all-start.3) | async-done | bytes 917536 | tf_op jit(solution)/shard_map/all_to_all | solution.py:28
  138.1 1.4 shard_map.127
  139.5 17.8 %all_to_all.35 = bf16[16,8,3584]{2,1,0:T(8,128)(2,1)S(1)} all-to-all(bf16[16,8,3584]{2,1,0:T(8,128)(2,1)} %get-tuple-element.63), channel_id=1, replica_groups=mesh['batch_0'=2,'batch_1'=2,'tensor_0'=4,'tensor_1'=2,'latent'=4] {'ten..., dimensions={0} | all-to-all | bytes 1835008 | tf_op jit(solution)/shard_map/all_to_all | solution.py:28
  157.4 6.2 %shard_map.128 = bf16[128,3584]{1,0:T(8,128)(2,1)S(1)} custom-call(bf16[128,3584]{1,0:T(8,128)(2,1)S(1)} %bitcast.35, bf16[224,3584]{1,0:T(8,128)(2,1)} %bitcast.39, bf16[224,3584]{1,0:T(8,128)(2,1)} %bitcast.42, bf16[224,3584]{1,0:T(8,128)(2,1)} %refs_2_.3, bf16[3,112,3584]{2,1,0:T(8,128)(2,1)} %collective-permute-done.3.refs_3_, ...), custom_call_target="tpu_custom_call" | custom-call | flops 1233125376 | bytes 11927552 | tf_op jit(solution)/shard_map/pallas_call | solution.py:52
  163.6 16.1 %all_to_all.36.pieces_ref = bf16[16,8,3584]{2,1,0:T(8,128)(2,1)S(1)} all-to-all(bf16[16,8,3584]{2,1,0:T(8,128)(2,1)S(1)} %bitcast.36), channel_id=1, replica_groups=mesh['batch_0'=2,'batch_1'=2,'tensor_0'=4,'tensor_1'=2,'latent'=4] {'ten..., dimensions={0} | all-to-all | bytes 1835008 | tf_op jit(solution)/shard_map/all_to_all | solution.py:28
  179.7 0.4 shard_map.129
  180.2 28.8 %all_to_all.37 = bf16[32,8,3584]{2,1,0:T(8,128)(2,1)S(1)} all-to-all(bf16[32,8,3584]{2,1,0:T(8,128)(2,1)S(1)} %shard_map.129), channel_id=1, replica_groups=mesh['batch_0'=2,'batch_1'=2,'tensor_0'=4,'tensor_1'=2,'latent'=4] {'ten..., dimensions={0} | all-to-all | bytes 3670016 | tf_op jit(solution)/shard_map/all_to_all | solution.py:28
  208.9 2.4 shard_map.130.refs_4_
  211.4 0.1 collective-permute-start.9
  211.4 0.2 constant_dynamic-slice_fusion
  211.6 2.1 collective-permute-start.11
  213.7 12.6 %collective-permute-done.9.refs_6_ = bf16[256,1024]{1,0:T(8,128)(2,1)S(1)} collective-permute-done((bf16[256,1024]{1,0:T(8,128)(2,1)S(1)}, bf16[256,1024]{1,0:T(8,128)(2,1)S(1)}, u32[]{:S(2)}, u32[]{:S(2)}) %collective-permute-start.9) | collective-permute-done | bytes 524320 | tf_op jit(solution)/shard_map/ppermute | solution.py:33
  226.3 0.5 collective-permute-start.12
  226.8 0.1 collective-permute-start.14
  226.9 9.2 %collective-permute-done.11.refs_5_ = bf16[256,896]{1,0:T(8,128)(2,1)S(1)} collective-permute-done((bf16[256,896]{1,0:T(8,128)(2,1)S(1)}, bf16[256,896]{1,0:T(8,128)(2,1)S(1)}, u32[]{:S(2)}, u32[]{:S(2)}) %collective-permute-start.11) | collective-permute-done | bytes 458784 | tf_op jit(solution)/shard_map/ppermute | solution.py:33
  236.1 3.1 %shard_map.131.refs_2_ = f32[1024,896]{1,0:T(8,128)S(1)} custom-call(bf16[1024,256]{1,0:T(8,128)(2,1)} %get-tuple-element.60.refs_0_, bf16[1024,256]{1,0:T(8,128)(2,1)} %collective-permute-done.6.refs_1_, bf16[1024,256]{1,0:T(8,128)(2,1)} %copy-done.9, bf16[256,896]{1,0:T(8,128)(2,1)S(1)} %get-tuple-element.79.refs_3_, ...), custom_call_target="tpu_custom_call" | custom-call | flops 1409286144 | bytes 6619136 | tf_op jit(solution)/shard_map/pallas_call | solution.py:52
  239.3 4.7 %shard_map.132 = bf16[896,1024]{1,0:T(8,128)(2,1)} custom-call(bf16[896,256]{1,0:T(8,128)(2,1)} %get-tuple-element.80.refs_0_, bf16[896,256]{1,0:T(8,128)(2,1)} %collective-permute-done.8.refs_1_, bf16[896,256]{1,0:T(8,128)(2,1)} %collective-permute-done.5.refs_2_, bf16[896,256]{1,0:T(8,128)(2,1)} %collective-permute-done.1.refs_3_, ...), custom_call_target="tpu_custom_call" | custom-call | flops 1879048192 | bytes 5767168 | tf_op jit(solution)/shard_map/pallas_call | solution.py:52
  244.0 2.8 %shard_map.133 = bf16[1024,896]{1,0:T(8,128)(2,1)} custom-call(bf16[1024,256]{1,0:T(8,128)(2,1)} %copy-done.11, bf16[256,896]{1,0:T(8,128)(2,1)S(1)} %collective-permute-done.14.refs_1_, f32[1024,896]{1,0:T(8,128)S(1)} %shard_map.131.refs_2_), custom_call_target="tpu_custom_call" | custom-call | flops 469762048 | bytes 6488064 | tf_op jit(solution)/shard_map/pallas_call | solution.py:52
  (67 shorter events, 0.2 us)
Async XLA Ops:
  3.7 10.5 %copy-start.4 = (bf16[3584,224]{0,1:T(8,128)(2,1)S(1)}, bf16[3584,224]{0,1:T(8,128)(2,1)}, u32[]{:S(2)}) copy-start(bf16[3584,224]{0,1:T(8,128)(2,1)} %param.19) | copy-start | bytes 4816900
  3.7 10.6 %copy-start.5 = (bf16[3584,224]{0,1:T(8,128)(2,1)S(1)}, bf16[3584,224]{0,1:T(8,128)(2,1)}, u32[]{:S(2)}) copy-start(bf16[3584,224]{0,1:T(8,128)(2,1)} %param.20) | copy-start | bytes 4816900
  3.7 35.0 %all-to-all-start = ((bf16[32,112,256]{2,1,0:T(8,128)(2,1)}), bf16[32,112,256]{2,1,0:T(8,128)(2,1)}, u32[]{:S(2)}, u32[]{:S(2)}) async-start(bf16[32,112,256]{2,1,0:T(8,128)(2,1)} %broadcast_in_dim.4), calls=%async_computation | async-start | bytes 3670016 | tf_op jit(solution)/shard_map/all_to_all | solution.py:28
  14.2 1.4 copy-start.6
  15.7 4.0 %copy-start.16 = (bf16[1024]{0:T(1024)(128)(2,1)S(1)}, bf16[1024]{0:T(1024)(128)(2,1)}, u32[]{:S(2)}) copy-start(bf16[1024]{0:T(1024)(128)(2,1)} %param.14) | copy-start | bytes 6148
  15.7 28.9 %slice-start = ((s8[7340032]{0:T(1024)(128)(4,1)}), s8[3145728]{0:T(1024)(128)(4,1)S(1)}, s32[]{:S(2)}) async-start(s8[7340032]{0:T(1024)(128)(4,1)} %bitcast.28), calls=%async_computation.7 | async-start | bytes 6291456
  17.5 73.8 %collective-permute-start.3 = (bf16[3,112,3584]{2,1,0:T(8,128)(2,1)}, bf16[3,112,3584]{2,1,0:T(8,128)(2,1)}, u32[]{:S(2)}, u32[]{:S(2)}) collective-permute-start(bf16[3,112,3584]{2,1,0:T(8,128)(2,1)} %pad_maximum_fusion), channel_id=1, source_target_pairs={{0,68},{4,64},{64,4},{68,0},{1,69},{5,65},{65,5},{69,1},{2,70},{6,... | collective-permute-start | bytes 7225352 | tf_op jit(solution)/shard_map/ppermute | solution.py:33
  38.7 6.0 %slice-start.1 = ((s8[7340032]{0:T(1024)(128)(4,1)}), s8[4194304]{0:T(1024)(128)(4,1)S(1)}, s32[]{:S(2)}) async-start(s8[7340032]{0:T(1024)(128)(4,1)} %bitcast.28), calls=%async_computation.8 | async-start | bytes 8388608
  38.7 6.0 %copy-start.3 = (bf16[256,112]{0,1:T(8,128)(2,1)S(1)}, bf16[256,112]{0,1:T(8,128)(2,1)}, u32[]{:S(2)}) copy-start(bf16[256,112]{0,1:T(8,128)(2,1)} %param.12) | copy-start | bytes 172036
  44.6 4.4 %copy-start.1 = (bf16[256,1024]{1,0:T(8,128)(2,1)}, bf16[256,1024]{1,0:T(8,128)(2,1)S(1)}, u32[]{:S(2)}) copy-start(bf16[256,1024]{1,0:T(8,128)(2,1)S(1)} %get-tuple-element.40.latents_ref) | copy-start | bytes 1572868
  49.1 6.9 %copy-start.7 = (bf16[1024,256]{1,0:T(8,128)(2,1)S(1)}, bf16[1024,256]{1,0:T(8,128)(2,1)}, u32[]{:S(2)}) copy-start(bf16[1024,256]{1,0:T(8,128)(2,1)} %get-tuple-element.60.refs_0_) | copy-start | bytes 1572868
  49.1 31.1 %all-to-all-start.1 = ((bf16[16,16,3712]{2,1,0:T(8,128)(2,1)}), bf16[16,16,3712]{2,1,0:T(8,128)(2,1)S(1)}, u32[]{:S(2)}, u32[]{:S(2)}) async-start(bf16[16,16,3712]{2,1,0:T(8,128)(2,1)} %bitcast.44), calls=%async_computation.1 | async-start | bytes 3801088 | tf_op jit(solution)/shard_map/all_to_all | solution.py:28
  56.0 24.9 %collective-permute-start = (bf16[1024,256]{1,0:T(8,128)(2,1)S(1)}, bf16[1024,256]{1,0:T(8,128)(2,1)S(1)}, u32[]{:S(2)}, u32[]{:S(2)}) collective-permute-start(bf16[1024,256]{1,0:T(8,128)(2,1)S(1)} %copy-done.7), channel_id=1, source_target_pairs={{0,64},{64,0},{1,65},{65,1},{2,66},{66,2},{3,67},{67,3},{4,68},{68... | collective-permute-start | bytes 1572872 | tf_op jit(solution)/shard_map/ppermute | solution.py:33
  59.1 22.6 %copy-start.13 = (bf16[3584]{0:T(1024)(128)(2,1)S(1)}, bf16[3584]{0:T(1024)(128)(2,1)}, u32[]{:S(2)}) copy-start(bf16[3584]{0:T(1024)(128)(2,1)} %param.16) | copy-start | bytes 21508
  59.1 22.6 %copy-start.14 = (bf16[3584]{0:T(1024)(128)(2,1)S(1)}, bf16[3584]{0:T(1024)(128)(2,1)}, u32[]{:S(2)}) copy-start(bf16[3584]{0:T(1024)(128)(2,1)} %param.17) | copy-start | bytes 21508
  59.1 21.8 %collective-permute-start.1 = (bf16[896,256]{1,0:T(8,128)(2,1)S(1)}, bf16[896,256]{1,0:T(8,128)(2,1)}, u32[]{:S(2)}, u32[]{:S(2)}) collective-permute-start(bf16[896,256]{1,0:T(8,128)(2,1)S(1)} %get-tuple-element.83), channel_id=1, source_target_pairs={{0,96},{32,64},{64,32},{96,0},{1,97},{33,65},{65,33},{97,1},{2,98}... | collective-permute-start | bytes 1376264 | tf_op jit(solution)/shard_map/ppermute | solution.py:33
  80.9 10.4 %copy-start.9 = (bf16[1024,256]{1,0:T(8,128)(2,1)}, bf16[1024,256]{1,0:T(8,128)(2,1)S(1)}, u32[]{:S(2)}) copy-start(bf16[1024,256]{1,0:T(8,128)(2,1)S(1)} %collective-permute-done.refs_2_) | copy-start | bytes 1572868
  80.9 6.2 %collective-permute-start.2 = (bf16[8,5632]{1,0:T(8,128)(2,1)S(1)}, bf16[8,5632]{1,0:T(8,128)(2,1)S(1)}, u32[]{:S(2)}, u32[]{:S(2)}) collective-permute-start(bf16[8,5632]{1,0:T(8,128)(2,1)S(1)} %get-tuple-element.47), channel_id=1, source_target_pairs={{0,4},{4,0},{1,5},{5,1},{2,6},{6,2},{3,7},{7,3},{8,12},{12,8},{9,1... | collective-permute-start | bytes 270344 | tf_op jit(solution)/shard_map/ppermute | solution.py:33
  91.3 21.3 %collective-permute-start.4 = (bf16[3,112,3584]{2,1,0:T(8,128)(2,1)}, bf16[3,112,3584]{2,1,0:T(8,128)(2,1)S(1)}, u32[]{:S(2)}, u32[]{:S(2)}) collective-permute-start(bf16[3,112,3584]{2,1,0:T(8,128)(2,1)} %collective-permute-done.3.refs_3_), channel_id=1, source_target_pairs={{0,32},{32,0},{1,33},{33,1},{2,34},{34,2},{3,35},{35,3},{4,36},{36... | collective-permute-start | bytes 7225352 | tf_op jit(solution)/shard_map/ppermute | solution.py:33
  91.3 21.3 %all-to-all-start.2 = ((bf16[16,8,3584]{2,1,0:T(8,128)(2,1)}), bf16[16,8,3584]{2,1,0:T(8,128)(2,1)S(1)}, u32[]{:S(2)}, u32[]{:S(2)}) async-start(bf16[16,8,3584]{2,1,0:T(8,128)(2,1)} %get-tuple-element.52), calls=%async_computation.2 | async-start | bytes 1835008 | tf_op jit(solution)/shard_map/all_to_all | solution.py:28
  97.9 21.3 %collective-permute-start.5 = (bf16[896,256]{1,0:T(8,128)(2,1)}, bf16[896,256]{1,0:T(8,128)(2,1)}, u32[]{:S(2)}, u32[]{:S(2)}) collective-permute-start(bf16[896,256]{1,0:T(8,128)(2,1)} %get-tuple-element.82), channel_id=1, source_target_pairs={{0,64},{64,0},{1,65},{65,1},{2,66},{66,2},{3,67},{67,3},{4,68},{68... | collective-permute-start | bytes 1376264 | tf_op jit(solution)/shard_map/ppermute | solution.py:33
  112.5 6.5 %copy-start = (bf16[3,112,3584]{2,1,0:T(8,128)(2,1)}, bf16[3,112,3584]{2,1,0:T(8,128)(2,1)S(1)}, u32[]{:S(2)}) copy-start(bf16[3,112,3584]{2,1,0:T(8,128)(2,1)S(1)} %collective-permute-done.4.refs_4_) | copy-start | bytes 7225348
  119.1 6.0 %copy-start.15 = (bf16[3584]{0:T(1024)(128)(2,1)S(1)}, bf16[3584]{0:T(1024)(128)(2,1)}, u32[]{:S(2)}) copy-start(bf16[3584]{0:T(1024)(128)(2,1)} %param.18) | copy-start | bytes 21508
  119.1 6.0 %copy-start.8 = (bf16[1024,256]{1,0:T(8,128)(2,1)S(1)}, bf16[1024,256]{1,0:T(8,128)(2,1)}, u32[]{:S(2)}) copy-start(bf16[1024,256]{1,0:T(8,128)(2,1)} %get-tuple-element.60.refs_0_) | copy-start | bytes 1572868
  119.1 6.7 %copy-start.12 = (bf16[16,8,128]{2,1,0:T(8,128)(2,1)S(1)}, bf16[16,8,128]{2,1,0:T(8,128)(2,1)}, u32[]{:S(2)}) copy-start(bf16[16,8,128]{2,1,0:T(8,128)(2,1)} %get-tuple-element.57) | copy-start | bytes 98308
  119.1 6.6 %copy-start.10 = (bf16[1024,256]{1,0:T(8,128)(2,1)S(1)}, bf16[1024,256]{1,0:T(8,128)(2,1)}, u32[]{:S(2)}) copy-start(bf16[1024,256]{1,0:T(8,128)(2,1)} %copy-done.9) | copy-start | bytes 1572868
  119.1 19.0 %all-to-all-start.3 = ((bf16[16,8,3584]{2,1,0:T(8,128)(2,1)}), bf16[16,8,3584]{2,1,0:T(8,128)(2,1)S(1)}, u32[]{:S(2)}, u32[]{:S(2)}) async-start(bf16[16,8,3584]{2,1,0:T(8,128)(2,1)} %bitcast.45), calls=%async_computation.3 | async-start | bytes 1835008 | tf_op jit(solution)/shard_map/all_to_all | solution.py:28
  125.1 14.4 %collective-permute-start.6 = (bf16[1024,256]{1,0:T(8,128)(2,1)S(1)}, bf16[1024,256]{1,0:T(8,128)(2,1)}, u32[]{:S(2)}, u32[]{:S(2)}) collective-permute-start(bf16[1024,256]{1,0:T(8,128)(2,1)S(1)} %copy-done.8), channel_id=1, source_target_pairs={{0,32},{32,0},{1,33},{33,1},{2,34},{34,2},{3,35},{35,3},{4,36},{36... | collective-permute-start | bytes 1572872 | tf_op jit(solution)/shard_map/ppermute | solution.py:33
  125.2 14.3 %collective-permute-start.8 = (bf16[896,256]{1,0:T(8,128)(2,1)}, bf16[896,256]{1,0:T(8,128)(2,1)}, u32[]{:S(2)}, u32[]{:S(2)}) collective-permute-start(bf16[896,256]{1,0:T(8,128)(2,1)} %get-tuple-element.81), channel_id=1, source_target_pairs={{0,32},{32,0},{1,33},{33,1},{2,34},{34,2},{3,35},{35,3},{4,36},{36... | collective-permute-start | bytes 1376264 | tf_op jit(solution)/shard_map/ppermute | solution.py:33
  125.7 13.8 %collective-permute-start.7 = (bf16[1024,256]{1,0:T(8,128)(2,1)S(1)}, bf16[1024,256]{1,0:T(8,128)(2,1)S(1)}, u32[]{:S(2)}, u32[]{:S(2)}) collective-permute-start(bf16[1024,256]{1,0:T(8,128)(2,1)S(1)} %copy-done.10), channel_id=1, source_target_pairs={{0,32},{32,0},{1,33},{33,1},{2,34},{34,2},{3,35},{35,3},{4,36},{36... | collective-permute-start | bytes 1572872 | tf_op jit(solution)/shard_map/ppermute | solution.py:33
  139.5 24.1 %copy-start.11 = (bf16[1024,256]{1,0:T(8,128)(2,1)}, bf16[1024,256]{1,0:T(8,128)(2,1)S(1)}, u32[]{:S(2)}) copy-start(bf16[1024,256]{1,0:T(8,128)(2,1)S(1)} %collective-permute-done.7.refs_0_) | copy-start | bytes 1572868
  139.5 69.4 %slice-start.2 = ((s8[7340032]{0:T(1024)(128)(4,1)}), s8[4194304]{0:T(1024)(128)(4,1)S(1)}, s32[]{:S(2)}) async-start(s8[7340032]{0:T(1024)(128)(4,1)} %bitcast.30), calls=%async_computation.9 | async-start | bytes 8388608
  157.4 51.6 %slice-start.3 = ((s8[7340032]{0:T(1024)(128)(4,1)}), s8[3145728]{0:T(1024)(128)(4,1)S(1)}, s32[]{:S(2)}) async-start(s8[7340032]{0:T(1024)(128)(4,1)} %bitcast.30), calls=%async_computation.10 | async-start | bytes 6291456
  180.1 28.8 %copy-start.2 = (bf16[256,1024]{1,0:T(8,128)(2,1)S(1)}, bf16[256,1024]{1,0:T(8,128)(2,1)}, u32[]{:S(2)}) copy-start(bf16[256,1024]{1,0:T(8,128)(2,1)} %copy-done.1) | copy-start | bytes 1572868
  211.4 14.9 %collective-permute-start.9 = (bf16[256,1024]{1,0:T(8,128)(2,1)S(1)}, bf16[256,1024]{1,0:T(8,128)(2,1)S(1)}, u32[]{:S(2)}, u32[]{:S(2)}) collective-permute-start(bf16[256,1024]{1,0:T(8,128)(2,1)S(1)} %shard_map.130.refs_4_), channel_id=1, source_target_pairs={{0,64},{64,0},{1,65},{65,1},{2,66},{66,2},{3,67},{67,3},{4,68},{68... | collective-permute-start | bytes 1572872 | tf_op jit(solution)/shard_map/ppermute | solution.py:33
  211.6 24.5 %collective-permute-start.11 = (bf16[256,896]{1,0:T(8,128)(2,1)S(1)}, bf16[256,896]{1,0:T(8,128)(2,1)S(1)}, u32[]{:S(2)}, u32[]{:S(2)}) collective-permute-start(bf16[256,896]{1,0:T(8,128)(2,1)S(1)} %get-tuple-element.77), channel_id=1, source_target_pairs={{0,64},{64,0},{1,65},{65,1},{2,66},{66,2},{3,67},{67,3},{4,68},{68... | collective-permute-start | bytes 1376264 | tf_op jit(solution)/shard_map/ppermute | solution.py:33
  226.3 9.8 %collective-permute-start.10 = (bf16[256,896]{1,0:T(8,128)(2,1)S(1)}, bf16[256,896]{1,0:T(8,128)(2,1)S(1)}, u32[]{:S(2)}, u32[]{:S(2)}) collective-permute-start(bf16[256,896]{1,0:T(8,128)(2,1)S(1)} %get-tuple-element.67), channel_id=1, source_target_pairs={{0,32},{32,0},{1,33},{33,1},{2,34},{34,2},{3,35},{35,3},{4,36},{36... | collective-permute-start | bytes 1376264 | tf_op jit(solution)/shard_map/ppermute | solution.py:33
  226.3 13.0 %collective-permute-start.12 = (bf16[256,1024]{1,0:T(8,128)(2,1)S(1)}, bf16[256,1024]{1,0:T(8,128)(2,1)S(1)}, u32[]{:S(2)}, u32[]{:S(2)}) collective-permute-start(bf16[256,1024]{1,0:T(8,128)(2,1)S(1)} %shard_map.130.refs_4_), channel_id=1, source_target_pairs={{0,32},{32,0},{1,33},{33,1},{2,34},{34,2},{3,35},{35,3},{4,36},{36... | collective-permute-start | bytes 1572872 | tf_op jit(solution)/shard_map/ppermute | solution.py:33
  226.8 12.5 %collective-permute-start.13 = (bf16[256,1024]{1,0:T(8,128)(2,1)S(1)}, bf16[256,1024]{1,0:T(8,128)(2,1)S(1)}, u32[]{:S(2)}, u32[]{:S(2)}) collective-permute-start(bf16[256,1024]{1,0:T(8,128)(2,1)S(1)} %collective-permute-done.9.refs_6_), channel_id=1, source_target_pairs={{0,32},{32,0},{1,33},{33,1},{2,34},{34,2},{3,35},{35,3},{4,36},{36... | collective-permute-start | bytes 1572872 | tf_op jit(solution)/shard_map/ppermute | solution.py:33
  226.8 17.1 %collective-permute-start.14 = (bf16[256,896]{1,0:T(8,128)(2,1)S(1)}, bf16[256,896]{1,0:T(8,128)(2,1)S(1)}, u32[]{:S(2)}, u32[]{:S(2)}) collective-permute-start(bf16[256,896]{1,0:T(8,128)(2,1)S(1)} %get-tuple-element.76), channel_id=1, source_target_pairs={{0,96},{32,64},{64,32},{96,0},{1,97},{33,65},{65,33},{97,1},{2,98}... | collective-permute-start | bytes 1376264 | tf_op jit(solution)/shard_map/ppermute | solution.py:33

commit v12 on v11

--- a/solution.py
+++ b/solution.py
@@ -120,6 +120,31 @@
             pl.BlockSpec((tile, tokens), lambda j: (j, 0)),
         ],
         scratch_shapes=[pltpu.VMEM((tokens, width), bf16)],
+    )
+
+
+def gather_kernel(at_ref, *refs):
+    *weights, out_ref, sems = refs
+    count = out_ref.shape[1]
+    at = pl.multiple_of(at_ref[0], count)
+    copies = [
+        pltpu.make_async_copy(w.at[pl.ds(at, count)], out_ref.at[k], sems.at[k])
+        for k, w in enumerate(weights)
+    ]
+    for copy in copies:
+        copy.start()
+    arrive(copies)
+
+
+def rows_of_each(weights, at, count):
+    anywhere = pl.BlockSpec(memory_space=pl.ANY)
+    return call(
+        gather_kernel,
+        hbm_array((len(weights), count, weights[0].shape[1])),
+        0,
+        [at.reshape(1), *map(in_hbm, weights)],
+        in_specs=[pl.BlockSpec(memory_space=pltpu.SMEM)] + [anywhere] * len(weights),
+        scratch_shapes=[pltpu.SemaphoreType.DMA((len(weights),))],
     )
 
 
@@ -412,7 +437,7 @@
     centered_share = (residual.astype(f32) - bias_share).astype(bf16).T
     pieces = jnp.broadcast_to(centered_share, (shards, share_width, tokens))
     pieces, weights_then = lax.optimization_barrier((pieces, weights))
-    sent = jnp.stack([lax.dynamic_slice_in_dim(w, at, units, axis=0) for w in weights_then])
+    sent = rows_of_each(weights_then, at, units)
     near = swap(sent, OTHER_HALF)
     centered = exchange(pieces, SHARDS).reshape(width, tokens)
 

time: 247 us -> 247 us (level)
  Pallas kernels: 39.6 us -> 42.9 us
    pallas_call x12 -> x13, Pallas kernels: 39.6 us -> 42.9 us  [call(): pl.pallas_call(body, out_shape=outs, cost_estimate=cost, compiler_params=...]
  transfers between devices with their start and end apart: 19 -> 19, of which waited for: 8 -> 8; matrix products, arithmetic and copies ran while one was open for 2% -> 1% of each run, Pallas kernels for 11% -> 13%
where the time goes in v12:
time: 247 us; the launch traced here: 246 us
  waiting for transfers between devices  95.7 us (39%)
  blocking collectives  62.7 us (25%)
  Pallas kernels  42.9 us (17%)
  starting transfers between devices  38.1 us (15%)
  local copies, waits for them, and re-layouts  4.36 us (2%)
    all_to_all x4, waiting for transfers between devices, exchange(): return lax.all_to_all(pieces, axes, split_axis=0, concat_axis=0, tiled=True)  65.5 us
    all_to_all x3, blocking collectives, exchange(): return lax.all_to_all(pieces, axes, split_axis=0, concat_axis=0, tiled=True)  62.7 us
    pallas_call x13, Pallas kernels, call(): pl.pallas_call(body, out_shape=outs, cost_estimate=cost, compiler_params=...  42.9 us
    ppermute x15, waiting for transfers between devices, swap(): lax.ppermute(block, axes, [(i, for_all - 1 - i) for i in range(for_all)])  30.2 us
    all_to_all x4, starting transfers between devices, exchange(): return lax.all_to_all(pieces, axes, split_axis=0, concat_axis=0, tiled=True)  29.7 us
    ppermute x15, starting transfers between devices, swap(): lax.ppermute(block, axes, [(i, for_all - 1 - i) for i in range(for_all)])  8.43 us
  transfers between devices with their start and end apart: 19, of which 8 were waited for; matrix products, arithmetic and copies ran while one was open for 1% of the time, Pallas kernels for 13%

profile of v12, /device:TPU:14, one launch (start us, length us, event | category | flops | bytes accessed | tf_op | source)
XLA Modules:
  0.0 246.5 jit_solution(14079031779707065809)
XLA Ops:
  0.6 0.8 dynamic-slice_convert_fusion
  1.4 0.9 fusion.2
  2.3 1.3 broadcast_in_dim.4
  3.7 10.2 %all-to-all-start = ((bf16[32,112,256]{2,1,0:T(8,128)(2,1)}), bf16[32,112,256]{2,1,0:T(8,128)(2,1)}, u32[]{:S(2)}, u32[]{:S(2)}) async-start(bf16[32,112,256]{2,1,0:T(8,128)(2,1)} %broadcast_in_dim.4), calls=%async_computation | async-start | bytes 3670016 | tf_op jit(solution)/shard_map/all_to_all | solution.py:28
  13.9 0.0 copy-start.13
  13.9 0.0 slice-start
  13.9 3.3 %shard_map.126 = bf16[3,112,3584]{2,1,0:T(8,128)(2,1)} custom-call(s32[1]{0:T(128)} %bitcast.7.at_ref, bf16[224,3584]{1,0:T(8,128)(2,1)} %bitcast.33, bf16[224,3584]{1,0:T(8,128)(2,1)} %bitcast.36, bf16[224,3584]{1,0:T(8,128)(2,1)} %refs_2_.4), custom_call_target="tpu_custom_call" | custom-call | bytes 7225348 | tf_op jit(solution)/shard_map/pallas_call | solution.py:52
  17.2 2.4 collective-permute-start.3
  19.6 18.8 %all-to-all-done = bf16[32,112,256]{2,1,0:T(8,128)(2,1)} async-done(((bf16[32,112,256]{2,1,0:T(8,128)(2,1)}), bf16[32,112,256]{2,1,0:T(8,128)(2,1)}, u32[]{:S(2)}, u32[]{:S(2)}) %all-to-all-start) | async-done | bytes 1835040 | tf_op jit(solution)/shard_map/all_to_all | solution.py:28
  38.4 5.9 %shard_map.122 = (bf16[256,1024]{1,0:T(8,128)(2,1)S(1)}, bf16[1024,256]{1,0:T(8,128)(2,1)}) custom-call(bf16[3584,256]{1,0:T(8,128)(2,1)} %bitcast.4.centered_ref, bf16[3584,1024]{1,0:T(8,128)(2,1)} %weight_ref.3, bf16[1,1024]{1,0:T(2,128)(2,1)S(1)} %reshape.52.bias_ref), custom_call_target="tpu_custom_call" | custom-call | flops 1879048192 | bytes 10225664 | tf_op jit(solution)/shard_map/pallas_call | solution.py:52
  44.4 4.4 %shard_map.123 = bf16[256,3712]{1,0:T(8,128)(2,1)} custom-call(bf16[256,1024]{1,0:T(8,128)(2,1)S(1)} %get-tuple-element.40.latents_ref, bf16[1024,3584]{1,0:T(8,128)(2,1)S(1)} %bitcast.24, bf16[112,256]{1,0:T(8,128)(2,1)S(1)} %bitcast.32), custom_call_target="tpu_custom_call" | custom-call | flops 1879048192 | bytes 9822208 | tf_op jit(solution)/shard_map/pallas_call | solution.py:52
  48.9 6.9 %all-to-all-start.1 = ((bf16[16,16,3712]{2,1,0:T(8,128)(2,1)}), bf16[16,16,3712]{2,1,0:T(8,128)(2,1)S(1)}, u32[]{:S(2)}, u32[]{:S(2)}) async-start(bf16[16,16,3712]{2,1,0:T(8,128)(2,1)} %bitcast.39), calls=%async_computation.1 | async-start | bytes 3801088 | tf_op jit(solution)/shard_map/all_to_all | solution.py:28
  55.8 0.5 collective-permute-start
  56.3 2.6 %constant_dynamic-slice_fusion.1 = (bf16[896,256]{1,0:T(8,128)(2,1)}, bf16[896,256]{1,0:T(8,128)(2,1)}, bf16[896,256]{1,0:T(8,128)(2,1)}, bf16[896,256]{1,0:T(8,128)(2,1)S(1)}) fusion(bf16[3584,256]{1,0:T(8,128)(2,1)} %bitcast.4.centered_ref, s32[]{:T(128)S(6)} %select_n.33, s32[]{:T(128)S(6)} %select_n.32, s32[]{:T(128)S(6)} %select_n.29, s32[]{:T(128)S(6)} %select_n.28), kind=kLoop, calls=%fused_computation.10 | loop fusion | bytes 3670032 | tf_op jit(solution)/shard_map/dynamic_slice | solution.py:452
  58.9 21.1 %all-to-all-done.1.pieces_ref = bf16[16,16,3712]{2,1,0:T(8,128)(2,1)S(1)} async-done(((bf16[16,16,3712]{2,1,0:T(8,128)(2,1)}), bf16[16,16,3712]{2,1,0:T(8,128)(2,1)S(1)}, u32[]{:S(2)}, u32[]{:S(2)}) %all-to-all-start.1) | async-done | bytes 1900576 | tf_op jit(solution)/shard_map/all_to_all | solution.py:28
  80.0 0.6 shard_map.124
  80.7 0.8 collective-permute-start.2
  81.5 5.4 %collective-permute-done.2.partner_ref = bf16[8,5632]{1,0:T(8,128)(2,1)S(1)} collective-permute-done((bf16[8,5632]{1,0:T(8,128)(2,1)S(1)}, bf16[8,5632]{1,0:T(8,128)(2,1)S(1)}, u32[]{:S(2)}, u32[]{:S(2)}) %collective-permute-start.2) | collective-permute-done | bytes 90144 | tf_op jit(solution)/shard_map/ppermute | solution.py:33
  86.9 1.1 shard_map.125
  88.0 3.0 %collective-permute-done.3.refs_3_ = bf16[3,112,3584]{2,1,0:T(8,128)(2,1)} collective-permute-done((bf16[3,112,3584]{2,1,0:T(8,128)(2,1)}, bf16[3,112,3584]{2,1,0:T(8,128)(2,1)}, u32[]{:S(2)}, u32[]{:S(2)}) %collective-permute-start.3) | collective-permute-done | bytes 2408480 | tf_op jit(solution)/shard_map/ppermute | solution.py:33
  91.0 6.6 %all-to-all-start.2 = ((bf16[16,8,3584]{2,1,0:T(8,128)(2,1)}), bf16[16,8,3584]{2,1,0:T(8,128)(2,1)S(1)}, u32[]{:S(2)}, u32[]{:S(2)}) async-start(bf16[16,8,3584]{2,1,0:T(8,128)(2,1)} %get-tuple-element.52), calls=%async_computation.2 | async-start | bytes 1835008 | tf_op jit(solution)/shard_map/all_to_all | solution.py:28
  97.6 1.3 collective-permute-start.5
  98.9 13.4 %all-to-all-done.2 = bf16[16,8,3584]{2,1,0:T(8,128)(2,1)S(1)} async-done(((bf16[16,8,3584]{2,1,0:T(8,128)(2,1)}), bf16[16,8,3584]{2,1,0:T(8,128)(2,1)S(1)}, u32[]{:S(2)}, u32[]{:S(2)}) %all-to-all-start.2) | async-done | bytes 917536 | tf_op jit(solution)/shard_map/all_to_all | solution.py:28
  112.3 6.5 %shard_map.127 = (bf16[128,3584]{1,0:T(8,128)(2,1)}, f32[128,448]{1,0:T(8,128)}, f32[128,448]{1,0:T(8,128)}) custom-call(bf16[128,3584]{1,0:T(8,128)(2,1)S(1)} %bitcast.29, bf16[224,3584]{1,0:T(8,128)(2,1)} %bitcast.34, bf16[224,3584]{1,0:T(8,128)(2,1)} %bitcast.37, bf16[224,3584]{1,0:T(8,128)(2,1)} %refs_2_.4, ...), custom_call_target="tpu_custom_call" | custom-call | flops 1233125376 | bytes 11927552 | tf_op jit(solution)/shard_map/pallas_call | solution.py:52
  118.9 5.9 %all-to-all-start.3 = ((bf16[16,8,3584]{2,1,0:T(8,128)(2,1)}), bf16[16,8,3584]{2,1,0:T(8,128)(2,1)S(1)}, u32[]{:S(2)}, u32[]{:S(2)}) async-start(bf16[16,8,3584]{2,1,0:T(8,128)(2,1)} %bitcast.40), calls=%async_computation.3 | async-start | bytes 1835008 | tf_op jit(solution)/shard_map/all_to_all | solution.py:28
  124.9 0.1 collective-permute-start.6
  125.0 0.5 collective-permute-start.8
  125.5 0.1 collective-permute-start.7
  125.7 0.1 reshape.60.target_ref
  125.8 12.1 %all-to-all-done.3.pieces_ref = bf16[16,8,3584]{2,1,0:T(8,128)(2,1)S(1)} async-done(((bf16[16,8,3584]{2,1,0:T(8,128)(2,1)}), bf16[16,8,3584]{2,1,0:T(8,128)(2,1)S(1)}, u32[]{:S(2)}, u32[]{:S(2)}) %all-to-all-start.3) | async-done | bytes 917536 | tf_op jit(solution)/shard_map/all_to_all | solution.py:28
  137.9 1.4 shard_map.128
  139.3 0.0 slice-start.2
  139.3 17.8 %all_to_all.35 = bf16[16,8,3584]{2,1,0:T(8,128)(2,1)S(1)} all-to-all(bf16[16,8,3584]{2,1,0:T(8,128)(2,1)} %get-tuple-element.63), channel_id=1, replica_groups=mesh['batch_0'=2,'batch_1'=2,'tensor_0'=4,'tensor_1'=2,'latent'=4] {'ten..., dimensions={0} | all-to-all | bytes 1835008 | tf_op jit(solution)/shard_map/all_to_all | solution.py:28
  157.1 6.2 %shard_map.129 = bf16[128,3584]{1,0:T(8,128)(2,1)S(1)} custom-call(bf16[128,3584]{1,0:T(8,128)(2,1)S(1)} %bitcast.30, bf16[224,3584]{1,0:T(8,128)(2,1)} %bitcast.35, bf16[224,3584]{1,0:T(8,128)(2,1)} %bitcast.38, bf16[224,3584]{1,0:T(8,128)(2,1)} %refs_2_.4, bf16[3,112,3584]{2,1,0:T(8,128)(2,1)} %collective-permute-done.3.refs_3_, ...), custom_call_target="tpu_custom_call" | custom-call | flops 1233125376 | bytes 11927552 | tf_op jit(solution)/shard_map/pallas_call | solution.py:52
  163.4 16.1 %all_to_all.36.pieces_ref = bf16[16,8,3584]{2,1,0:T(8,128)(2,1)S(1)} all-to-all(bf16[16,8,3584]{2,1,0:T(8,128)(2,1)S(1)} %bitcast.31), channel_id=1, replica_groups=mesh['batch_0'=2,'batch_1'=2,'tensor_0'=4,'tensor_1'=2,'latent'=4] {'ten..., dimensions={0} | all-to-all | bytes 1835008 | tf_op jit(solution)/shard_map/all_to_all | solution.py:28
  179.5 0.4 shard_map.130
  179.9 28.8 %all_to_all.37 = bf16[32,8,3584]{2,1,0:T(8,128)(2,1)S(1)} all-to-all(bf16[32,8,3584]{2,1,0:T(8,128)(2,1)S(1)} %shard_map.130), channel_id=1, replica_groups=mesh['batch_0'=2,'batch_1'=2,'tensor_0'=4,'tensor_1'=2,'latent'=4] {'ten..., dimensions={0} | all-to-all | bytes 3670016 | tf_op jit(solution)/shard_map/all_to_all | solution.py:28
  208.7 2.4 shard_map.131.refs_4_
  211.1 0.1 collective-permute-start.9
  211.2 0.2 constant_dynamic-slice_fusion
  211.4 2.1 collective-permute-start.11
  213.5 12.6 %collective-permute-done.9.refs_6_ = bf16[256,1024]{1,0:T(8,128)(2,1)S(1)} collective-permute-done((bf16[256,1024]{1,0:T(8,128)(2,1)S(1)}, bf16[256,1024]{1,0:T(8,128)(2,1)S(1)}, u32[]{:S(2)}, u32[]{:S(2)}) %collective-permute-start.9) | collective-permute-done | bytes 524320 | tf_op jit(solution)/shard_map/ppermute | solution.py:33
  226.1 0.5 collective-permute-start.12
  226.6 0.1 collective-permute-start.14
  226.7 9.2 %collective-permute-done.11.refs_5_ = bf16[256,896]{1,0:T(8,128)(2,1)S(1)} collective-permute-done((bf16[256,896]{1,0:T(8,128)(2,1)S(1)}, bf16[256,896]{1,0:T(8,128)(2,1)S(1)}, u32[]{:S(2)}, u32[]{:S(2)}) %collective-permute-start.11) | collective-permute-done | bytes 458784 | tf_op jit(solution)/shard_map/ppermute | solution.py:33
  235.9 3.1 %shard_map.132.refs_2_ = f32[1024,896]{1,0:T(8,128)S(1)} custom-call(bf16[1024,256]{1,0:T(8,128)(2,1)} %get-tuple-element.60.refs_0_, bf16[1024,256]{1,0:T(8,128)(2,1)} %collective-permute-done.6.refs_1_, bf16[1024,256]{1,0:T(8,128)(2,1)} %copy-done.6, bf16[256,896]{1,0:T(8,128)(2,1)S(1)} %get-tuple-element.79.refs_3_, ...), custom_call_target="tpu_custom_call" | custom-call | flops 1409286144 | bytes 6619136 | tf_op jit(solution)/shard_map/pallas_call | solution.py:52
  239.1 4.7 %shard_map.133 = bf16[896,1024]{1,0:T(8,128)(2,1)} custom-call(bf16[896,256]{1,0:T(8,128)(2,1)} %get-tuple-element.80.refs_0_, bf16[896,256]{1,0:T(8,128)(2,1)} %collective-permute-done.8.refs_1_, bf16[896,256]{1,0:T(8,128)(2,1)} %collective-permute-done.5.refs_2_, bf16[896,256]{1,0:T(8,128)(2,1)} %collective-permute-done.1.refs_3_, ...), custom_call_target="tpu_custom_call" | custom-call | flops 1879048192 | bytes 5767168 | tf_op jit(solution)/shard_map/pallas_call | solution.py:52
  243.7 2.8 %shard_map.134 = bf16[1024,896]{1,0:T(8,128)(2,1)} custom-call(bf16[1024,256]{1,0:T(8,128)(2,1)} %copy-done.8, bf16[256,896]{1,0:T(8,128)(2,1)S(1)} %collective-permute-done.14.refs_1_, f32[1024,896]{1,0:T(8,128)S(1)} %shard_map.132.refs_2_), custom_call_target="tpu_custom_call" | custom-call | flops 469762048 | bytes 6488064 | tf_op jit(solution)/shard_map/pallas_call | solution.py:52
  (59 shorter events, 0.2 us)
Async XLA Ops:
  3.7 34.8 %all-to-all-start = ((bf16[32,112,256]{2,1,0:T(8,128)(2,1)}), bf16[32,112,256]{2,1,0:T(8,128)(2,1)}, u32[]{:S(2)}, u32[]{:S(2)}) async-start(bf16[32,112,256]{2,1,0:T(8,128)(2,1)} %broadcast_in_dim.4), calls=%async_computation | async-start | bytes 3670016 | tf_op jit(solution)/shard_map/all_to_all | solution.py:28
  13.9 5.7 %copy-start.13 = (bf16[1024]{0:T(1024)(128)(2,1)S(1)}, bf16[1024]{0:T(1024)(128)(2,1)}, u32[]{:S(2)}) copy-start(bf16[1024]{0:T(1024)(128)(2,1)} %param.14) | copy-start | bytes 6148
  13.9 30.5 %slice-start = ((s8[7340032]{0:T(1024)(128)(4,1)}), s8[3145728]{0:T(1024)(128)(4,1)S(1)}, s32[]{:S(2)}) async-start(s8[7340032]{0:T(1024)(128)(4,1)} %bitcast.23), calls=%async_computation.7 | async-start | bytes 6291456
  17.2 73.8 %collective-permute-start.3 = (bf16[3,112,3584]{2,1,0:T(8,128)(2,1)}, bf16[3,112,3584]{2,1,0:T(8,128)(2,1)}, u32[]{:S(2)}, u32[]{:S(2)}) collective-permute-start(bf16[3,112,3584]{2,1,0:T(8,128)(2,1)} %shard_map.126), channel_id=1, source_target_pairs={{0,68},{4,64},{64,4},{68,0},{1,69},{5,65},{65,5},{69,1},{2,70},{6,... | collective-permute-start | bytes 7225352 | tf_op jit(solution)/shard_map/ppermute | solution.py:33
  38.4 6.0 %slice-start.1 = ((s8[7340032]{0:T(1024)(128)(4,1)}), s8[4194304]{0:T(1024)(128)(4,1)S(1)}, s32[]{:S(2)}) async-start(s8[7340032]{0:T(1024)(128)(4,1)} %bitcast.23), calls=%async_computation.8 | async-start | bytes 8388608
  38.4 6.0 %copy-start.3 = (bf16[256,112]{0,1:T(8,128)(2,1)S(1)}, bf16[256,112]{0,1:T(8,128)(2,1)}, u32[]{:S(2)}) copy-start(bf16[256,112]{0,1:T(8,128)(2,1)} %param.12) | copy-start | bytes 172036
  44.4 4.5 %copy-start.1 = (bf16[256,1024]{1,0:T(8,128)(2,1)}, bf16[256,1024]{1,0:T(8,128)(2,1)S(1)}, u32[]{:S(2)}) copy-start(bf16[256,1024]{1,0:T(8,128)(2,1)S(1)} %get-tuple-element.40.latents_ref) | copy-start | bytes 1572868
  48.9 6.9 %copy-start.4 = (bf16[1024,256]{1,0:T(8,128)(2,1)S(1)}, bf16[1024,256]{1,0:T(8,128)(2,1)}, u32[]{:S(2)}) copy-start(bf16[1024,256]{1,0:T(8,128)(2,1)} %get-tuple-element.60.refs_0_) | copy-start | bytes 1572868
  48.9 31.1 %all-to-all-start.1 = ((bf16[16,16,3712]{2,1,0:T(8,128)(2,1)}), bf16[16,16,3712]{2,1,0:T(8,128)(2,1)S(1)}, u32[]{:S(2)}, u32[]{:S(2)}) async-start(bf16[16,16,3712]{2,1,0:T(8,128)(2,1)} %bitcast.39), calls=%async_computation.1 | async-start | bytes 3801088 | tf_op jit(solution)/shard_map/all_to_all | solution.py:28
  55.8 24.9 %collective-permute-start = (bf16[1024,256]{1,0:T(8,128)(2,1)S(1)}, bf16[1024,256]{1,0:T(8,128)(2,1)S(1)}, u32[]{:S(2)}, u32[]{:S(2)}) collective-permute-start(bf16[1024,256]{1,0:T(8,128)(2,1)S(1)} %copy-done.4), channel_id=1, source_target_pairs={{0,64},{64,0},{1,65},{65,1},{2,66},{66,2},{3,67},{67,3},{4,68},{68... | collective-permute-start | bytes 1572872 | tf_op jit(solution)/shard_map/ppermute | solution.py:33
  58.9 22.6 %copy-start.10 = (bf16[3584]{0:T(1024)(128)(2,1)S(1)}, bf16[3584]{0:T(1024)(128)(2,1)}, u32[]{:S(2)}) copy-start(bf16[3584]{0:T(1024)(128)(2,1)} %param.16) | copy-start | bytes 21508
  58.9 22.6 %copy-start.11 = (bf16[3584]{0:T(1024)(128)(2,1)S(1)}, bf16[3584]{0:T(1024)(128)(2,1)}, u32[]{:S(2)}) copy-start(bf16[3584]{0:T(1024)(128)(2,1)} %param.17) | copy-start | bytes 21508
  58.9 21.8 %collective-permute-start.1 = (bf16[896,256]{1,0:T(8,128)(2,1)S(1)}, bf16[896,256]{1,0:T(8,128)(2,1)}, u32[]{:S(2)}, u32[]{:S(2)}) collective-permute-start(bf16[896,256]{1,0:T(8,128)(2,1)S(1)} %get-tuple-element.83), channel_id=1, source_target_pairs={{0,96},{32,64},{64,32},{96,0},{1,97},{33,65},{65,33},{97,1},{2,98}... | collective-permute-start | bytes 1376264 | tf_op jit(solution)/shard_map/ppermute | solution.py:33
  80.7 10.4 %copy-start.6 = (bf16[1024,256]{1,0:T(8,128)(2,1)}, bf16[1024,256]{1,0:T(8,128)(2,1)S(1)}, u32[]{:S(2)}) copy-start(bf16[1024,256]{1,0:T(8,128)(2,1)S(1)} %collective-permute-done.refs_2_) | copy-start | bytes 1572868
  80.7 6.2 %collective-permute-start.2 = (bf16[8,5632]{1,0:T(8,128)(2,1)S(1)}, bf16[8,5632]{1,0:T(8,128)(2,1)S(1)}, u32[]{:S(2)}, u32[]{:S(2)}) collective-permute-start(bf16[8,5632]{1,0:T(8,128)(2,1)S(1)} %get-tuple-element.47), channel_id=1, source_target_pairs={{0,4},{4,0},{1,5},{5,1},{2,6},{6,2},{3,7},{7,3},{8,12},{12,8},{9,1... | collective-permute-start | bytes 270344 | tf_op jit(solution)/shard_map/ppermute | solution.py:33
  91.0 21.3 %collective-permute-start.4 = (bf16[3,112,3584]{2,1,0:T(8,128)(2,1)}, bf16[3,112,3584]{2,1,0:T(8,128)(2,1)S(1)}, u32[]{:S(2)}, u32[]{:S(2)}) collective-permute-start(bf16[3,112,3584]{2,1,0:T(8,128)(2,1)} %collective-permute-done.3.refs_3_), channel_id=1, source_target_pairs={{0,32},{32,0},{1,33},{33,1},{2,34},{34,2},{3,35},{35,3},{4,36},{36... | collective-permute-start | bytes 7225352 | tf_op jit(solution)/shard_map/ppermute | solution.py:33
  91.0 21.3 %all-to-all-start.2 = ((bf16[16,8,3584]{2,1,0:T(8,128)(2,1)}), bf16[16,8,3584]{2,1,0:T(8,128)(2,1)S(1)}, u32[]{:S(2)}, u32[]{:S(2)}) async-start(bf16[16,8,3584]{2,1,0:T(8,128)(2,1)} %get-tuple-element.52), calls=%async_computation.2 | async-start | bytes 1835008 | tf_op jit(solution)/shard_map/all_to_all | solution.py:28
  97.6 21.3 %collective-permute-start.5 = (bf16[896,256]{1,0:T(8,128)(2,1)}, bf16[896,256]{1,0:T(8,128)(2,1)}, u32[]{:S(2)}, u32[]{:S(2)}) collective-permute-start(bf16[896,256]{1,0:T(8,128)(2,1)} %get-tuple-element.82), channel_id=1, source_target_pairs={{0,64},{64,0},{1,65},{65,1},{2,66},{66,2},{3,67},{67,3},{4,68},{68... | collective-permute-start | bytes 1376264 | tf_op jit(solution)/shard_map/ppermute | solution.py:33
  112.3 6.5 %copy-start = (bf16[3,112,3584]{2,1,0:T(8,128)(2,1)}, bf16[3,112,3584]{2,1,0:T(8,128)(2,1)S(1)}, u32[]{:S(2)}) copy-start(bf16[3,112,3584]{2,1,0:T(8,128)(2,1)S(1)} %collective-permute-done.4.refs_4_) | copy-start | bytes 7225348
  118.9 6.0 %copy-start.12 = (bf16[3584]{0:T(1024)(128)(2,1)S(1)}, bf16[3584]{0:T(1024)(128)(2,1)}, u32[]{:S(2)}) copy-start(bf16[3584]{0:T(1024)(128)(2,1)} %param.18) | copy-start | bytes 21508
  118.9 6.0 %copy-start.5 = (bf16[1024,256]{1,0:T(8,128)(2,1)S(1)}, bf16[1024,256]{1,0:T(8,128)(2,1)}, u32[]{:S(2)}) copy-start(bf16[1024,256]{1,0:T(8,128)(2,1)} %get-tuple-element.60.refs_0_) | copy-start | bytes 1572868
  118.9 6.7 %copy-start.9 = (bf16[16,8,128]{2,1,0:T(8,128)(2,1)S(1)}, bf16[16,8,128]{2,1,0:T(8,128)(2,1)}, u32[]{:S(2)}) copy-start(bf16[16,8,128]{2,1,0:T(8,128)(2,1)} %get-tuple-element.57) | copy-start | bytes 98308
  118.9 6.6 %copy-start.7 = (bf16[1024,256]{1,0:T(8,128)(2,1)S(1)}, bf16[1024,256]{1,0:T(8,128)(2,1)}, u32[]{:S(2)}) copy-start(bf16[1024,256]{1,0:T(8,128)(2,1)} %copy-done.6) | copy-start | bytes 1572868
  118.9 19.0 %all-to-all-start.3 = ((bf16[16,8,3584]{2,1,0:T(8,128)(2,1)}), bf16[16,8,3584]{2,1,0:T(8,128)(2,1)S(1)}, u32[]{:S(2)}, u32[]{:S(2)}) async-start(bf16[16,8,3584]{2,1,0:T(8,128)(2,1)} %bitcast.40), calls=%async_computation.3 | async-start | bytes 1835008 | tf_op jit(solution)/shard_map/all_to_all | solution.py:28
  124.9 14.4 %collective-permute-start.6 = (bf16[1024,256]{1,0:T(8,128)(2,1)S(1)}, bf16[1024,256]{1,0:T(8,128)(2,1)}, u32[]{:S(2)}, u32[]{:S(2)}) collective-permute-start(bf16[1024,256]{1,0:T(8,128)(2,1)S(1)} %copy-done.5), channel_id=1, source_target_pairs={{0,32},{32,0},{1,33},{33,1},{2,34},{34,2},{3,35},{35,3},{4,36},{36... | collective-permute-start | bytes 1572872 | tf_op jit(solution)/shard_map/ppermute | solution.py:33
  125.0 14.3 %collective-permute-start.8 = (bf16[896,256]{1,0:T(8,128)(2,1)}, bf16[896,256]{1,0:T(8,128)(2,1)}, u32[]{:S(2)}, u32[]{:S(2)}) collective-permute-start(bf16[896,256]{1,0:T(8,128)(2,1)} %get-tuple-element.81), channel_id=1, source_target_pairs={{0,32},{32,0},{1,33},{33,1},{2,34},{34,2},{3,35},{35,3},{4,36},{36... | collective-permute-start | bytes 1376264 | tf_op jit(solution)/shard_map/ppermute | solution.py:33
  125.5 13.8 %collective-permute-start.7 = (bf16[1024,256]{1,0:T(8,128)(2,1)S(1)}, bf16[1024,256]{1,0:T(8,128)(2,1)S(1)}, u32[]{:S(2)}, u32[]{:S(2)}) collective-permute-start(bf16[1024,256]{1,0:T(8,128)(2,1)S(1)} %copy-done.7), channel_id=1, source_target_pairs={{0,32},{32,0},{1,33},{33,1},{2,34},{34,2},{3,35},{35,3},{4,36},{36... | collective-permute-start | bytes 1572872 | tf_op jit(solution)/shard_map/ppermute | solution.py:33
  139.3 24.1 %copy-start.8 = (bf16[1024,256]{1,0:T(8,128)(2,1)}, bf16[1024,256]{1,0:T(8,128)(2,1)S(1)}, u32[]{:S(2)}) copy-start(bf16[1024,256]{1,0:T(8,128)(2,1)S(1)} %collective-permute-done.7.refs_0_) | copy-start | bytes 1572868
  139.3 69.4 %slice-start.2 = ((s8[7340032]{0:T(1024)(128)(4,1)}), s8[4194304]{0:T(1024)(128)(4,1)S(1)}, s32[]{:S(2)}) async-start(s8[7340032]{0:T(1024)(128)(4,1)} %bitcast.25), calls=%async_computation.9 | async-start | bytes 8388608
  157.1 51.6 %slice-start.3 = ((s8[7340032]{0:T(1024)(128)(4,1)}), s8[3145728]{0:T(1024)(128)(4,1)S(1)}, s32[]{:S(2)}) async-start(s8[7340032]{0:T(1024)(128)(4,1)} %bitcast.25), calls=%async_computation.10 | async-start | bytes 6291456
  179.9 28.8 %copy-start.2 = (bf16[256,1024]{1,0:T(8,128)(2,1)S(1)}, bf16[256,1024]{1,0:T(8,128)(2,1)}, u32[]{:S(2)}) copy-start(bf16[256,1024]{1,0:T(8,128)(2,1)} %copy-done.1) | copy-start | bytes 1572868
  211.1 14.9 %collective-permute-start.9 = (bf16[256,1024]{1,0:T(8,128)(2,1)S(1)}, bf16[256,1024]{1,0:T(8,128)(2,1)S(1)}, u32[]{:S(2)}, u32[]{:S(2)}) collective-permute-start(bf16[256,1024]{1,0:T(8,128)(2,1)S(1)} %shard_map.131.refs_4_), channel_id=1, source_target_pairs={{0,64},{64,0},{1,65},{65,1},{2,66},{66,2},{3,67},{67,3},{4,68},{68... | collective-permute-start | bytes 1572872 | tf_op jit(solution)/shard_map/ppermute | solution.py:33
  211.4 24.5 %collective-permute-start.11 = (bf16[256,896]{1,0:T(8,128)(2,1)S(1)}, bf16[256,896]{1,0:T(8,128)(2,1)S(1)}, u32[]{:S(2)}, u32[]{:S(2)}) collective-permute-start(bf16[256,896]{1,0:T(8,128)(2,1)S(1)} %get-tuple-element.77), channel_id=1, source_target_pairs={{0,64},{64,0},{1,65},{65,1},{2,66},{66,2},{3,67},{67,3},{4,68},{68... | collective-permute-start | bytes 1376264 | tf_op jit(solution)/shard_map/ppermute | solution.py:33
  226.1 9.8 %collective-permute-start.10 = (bf16[256,896]{1,0:T(8,128)(2,1)S(1)}, bf16[256,896]{1,0:T(8,128)(2,1)S(1)}, u32[]{:S(2)}, u32[]{:S(2)}) collective-permute-start(bf16[256,896]{1,0:T(8,128)(2,1)S(1)} %get-tuple-element.67), channel_id=1, source_target_pairs={{0,32},{32,0},{1,33},{33,1},{2,34},{34,2},{3,35},{35,3},{4,36},{36... | collective-permute-start | bytes 1376264 | tf_op jit(solution)/shard_map/ppermute | solution.py:33
  226.1 13.0 %collective-permute-start.12 = (bf16[256,1024]{1,0:T(8,128)(2,1)S(1)}, bf16[256,1024]{1,0:T(8,128)(2,1)S(1)}, u32[]{:S(2)}, u32[]{:S(2)}) collective-permute-start(bf16[256,1024]{1,0:T(8,128)(2,1)S(1)} %shard_map.131.refs_4_), channel_id=1, source_target_pairs={{0,32},{32,0},{1,33},{33,1},{2,34},{34,2},{3,35},{35,3},{4,36},{36... | collective-permute-start | bytes 1572872 | tf_op jit(solution)/shard_map/ppermute | solution.py:33
  226.6 12.5 %collective-permute-start.13 = (bf16[256,1024]{1,0:T(8,128)(2,1)S(1)}, bf16[256,1024]{1,0:T(8,128)(2,1)S(1)}, u32[]{:S(2)}, u32[]{:S(2)}) collective-permute-start(bf16[256,1024]{1,0:T(8,128)(2,1)S(1)} %collective-permute-done.9.refs_6_), channel_id=1, source_target_pairs={{0,32},{32,0},{1,33},{33,1},{2,34},{34,2},{3,35},{35,3},{4,36},{36... | collective-permute-start | bytes 1572872 | tf_op jit(solution)/shard_map/ppermute | solution.py:33
  226.6 17.1 %collective-permute-start.14 = (bf16[256,896]{1,0:T(8,128)(2,1)S(1)}, bf16[256,896]{1,0:T(8,128)(2,1)S(1)}, u32[]{:S(2)}, u32[]{:S(2)}) collective-permute-start(bf16[256,896]{1,0:T(8,128)(2,1)S(1)} %get-tuple-element.76), channel_id=1, source_target_pairs={{0,96},{32,64},{64,32},{96,0},{1,97},{33,65},{65,33},{97,1},{2,98}... | collective-permute-start | bytes 1376264 | tf_op jit(solution)/shard_map/ppermute | solution.py:33

commit v13 on v12

--- a/solution.py
+++ b/solution.py
@@ -263,14 +263,14 @@
 
 
 def fetches(refs, weights_ref, sems, order):
-    *own, near, far = refs
+    own, near, far = refs[:3], refs[3], refs[4:]
     units, more = own[0].shape[0], near.shape[1]
     copies = []
     for k in order:
         rows = weights_ref.at[k]
         pairs = [(own[k], rows.at[pl.ds(0, units)])]
         pairs += [(near.at[k], rows.at[pl.ds(units, more)])]
-        pairs += [(far.at[k], rows.at[pl.ds(units + more, more)])]
+        pairs += [(far[k], rows.at[pl.ds(units + more, more)])]
         copies.append([pltpu.make_async_copy(*p, sems.at[k, i]) for i, p in enumerate(pairs)])
     for copy in sum(copies, []):
         copy.start()
@@ -283,10 +283,10 @@
 
 
 def forward_kernel(rows_ref, *refs):
-    out_ref, gelu_ref, slope_ref, weights_ref, sems = refs[5:]
+    out_ref, gelu_ref, slope_ref, weights_ref, sems = refs[7:]
     root = 0.7978845608028654
     cube = 0.044715
-    gate, up, down = fetches(refs[:5], weights_ref, sems, (0, 1, 2))
+    gate, up, down = fetches(refs[:7], weights_ref, sems, (0, 1, 2))
     rows = rows_ref[...]
     arrive(gate)
     gate_value = product_t(rows, weights_ref[0])
@@ -307,8 +307,8 @@
 
 
 def backward_kernel(rows_ref, *refs):
-    gelu_ref, slope_ref, out_ref, weights_ref, sems = refs[5:]
-    down, gate, up = fetches(refs[:5], weights_ref, sems, (2, 0, 1))
+    gelu_ref, slope_ref, out_ref, weights_ref, sems = refs[7:]
+    down, gate, up = fetches(refs[:7], weights_ref, sems, (2, 0, 1))
     arrive(down)
     grad_hidden = product_t(rows_ref[...], weights_ref[2])
     grad_gate = (grad_hidden * slope_ref[...]).astype(bf16)
@@ -330,8 +330,8 @@
         body,
         outs,
         6 * rows.shape[0] * width * units,
-        [rows, *map(in_hbm, weights), in_hbm(near), far, *map(in_hbm, saved)],
-        in_specs=[WHOLE] + [anywhere] * 5 + [pl.BlockSpec()] * len(saved),
+        [rows, *map(in_hbm, weights), in_hbm(near), *far, *map(in_hbm, saved)],
+        in_specs=[WHOLE] + [anywhere] * 7 + [pl.BlockSpec()] * len(saved),
         scratch_shapes=[pltpu.VMEM((3, units, width), bf16), pltpu.SemaphoreType.DMA((3, 3))],
     )
 
@@ -477,8 +477,8 @@
     targets = targets.reshape(own_tokens, *(lax.axis_size(a) for a in OWNERS), share_width)
     own_target = jnp.swapaxes(targets, 2, 3).reshape(own_tokens, width)
 
-    pieces, near = lax.optimization_barrier((pieces, near))
-    far = swap(near, BATCH[1])
+    _, near = lax.optimization_barrier((pieces, near))
+    far = [swap(near[k], BATCH[1]) for k in range(len(weights))]
     normed_input = all_tokens(pieces, HALF)
     rows = half * own_tokens
     hidden = gate.shape[0] + 2 * units
@@ -504,7 +504,7 @@
     )
     grad_output = all_tokens(pieces, HALF)
     partial_input = with_weights(
-        backward_kernel, array((rows, width)), grad_output, weights, near, in_hbm(far), saved
+        backward_kernel, array((rows, width)), grad_output, weights, near, far, saved
     )
     (pieces,) = local(
         input_kernel, [everyone], [to_owners(partial_input, HALF), recon, grad_result, gain_in]

time: 247 us -> 241 us (0.976)
  waiting for transfers between devices: 95.7 us -> 82.4 us
  local copies, waits for them, and re-layouts: 4.36 us -> 10.5 us
    all_to_all x4, waiting for transfers between devices: 65.5 us -> 51.8 us  [exchange(): return lax.all_to_all(pieces, axes, split_axis=0, concat_axis=0, tiled=True)]
    ppermute x15 -> x17, waiting for transfers between devices: 30.2 us -> 30.6 us  [swap(): lax.ppermute(block, axes, [(i, for_all - 1 - i) for i in range(for_all)])]
    ppermute x15 -> x17, starting transfers between devices: 8.43 us -> 8.33 us  [swap(): lax.ppermute(block, axes, [(i, for_all - 1 - i) for i in range(for_all)])]
  transfers between devices with their start and end apart: 19 -> 21, of which waited for: 8 -> 10; matrix products, arithmetic and copies ran while one was open for 1% -> 4% of each run, Pallas kernels for 13% -> 13%
where the time goes in v13:
time: 241 us; the launch traced here: 240 us
  waiting for transfers between devices  82.4 us (34%)
  blocking collectives  64 us (27%)
  Pallas kernels  41.4 us (17%)
  starting transfers between devices  37.1 us (15%)
  local copies, waits for them, and re-layouts  10.5 us (4%)
  other arithmetic  3.83 us (2%)
    all_to_all x3, blocking collectives, exchange(): return lax.all_to_all(pieces, axes, split_axis=0, concat_axis=0, tiled=True)  64 us
    all_to_all x4, waiting for transfers between devices, exchange(): return lax.all_to_all(pieces, axes, split_axis=0, concat_axis=0, tiled=True)  51.8 us
    pallas_call x13, Pallas kernels, call(): pl.pallas_call(body, out_shape=outs, cost_estimate=cost, compiler_params=...  41.4 us
    ppermute x17, waiting for transfers between devices, swap(): lax.ppermute(block, axes, [(i, for_all - 1 - i) for i in range(for_all)])  30.6 us
    all_to_all x4, starting transfers between devices, exchange(): return lax.all_to_all(pieces, axes, split_axis=0, concat_axis=0, tiled=True)  28.8 us
    ppermute x17, starting transfers between devices, swap(): lax.ppermute(block, axes, [(i, for_all - 1 - i) for i in range(for_all)])  8.33 us
  transfers between devices with their start and end apart: 21, of which 10 were waited for; matrix products, arithmetic and copies ran while one was open for 4% of the time, Pallas kernels for 13%

profile of v13, /device:TPU:14, one launch (start us, length us, event | category | flops | bytes accessed | tf_op | source)
XLA Modules:
  0.0 240.2 jit_solution(5186067428053974871)
XLA Ops:
  0.6 0.8 dynamic-slice_convert_fusion
  1.4 0.9 fusion.2
  2.3 1.3 broadcast_in_dim.4
  3.7 10.2 %all-to-all-start = ((bf16[32,112,256]{2,1,0:T(8,128)(2,1)}), bf16[32,112,256]{2,1,0:T(8,128)(2,1)}, u32[]{:S(2)}, u32[]{:S(2)}) async-start(bf16[32,112,256]{2,1,0:T(8,128)(2,1)} %broadcast_in_dim.4), calls=%async_computation | async-start | bytes 3670016 | tf_op jit(solution)/shard_map/all_to_all | solution.py:28
  13.9 3.3 %shard_map.126 = bf16[3,112,3584]{2,1,0:T(8,128)(2,1)} custom-call(s32[1]{0:T(128)} %bitcast.8.at_ref, bf16[224,3584]{1,0:T(8,128)(2,1)} %bitcast.39, bf16[224,3584]{1,0:T(8,128)(2,1)} %bitcast.42, bf16[224,3584]{1,0:T(8,128)(2,1)} %refs_2_.4), custom_call_target="tpu_custom_call" | custom-call | bytes 7225348 | tf_op jit(solution)/shard_map/pallas_call | solution.py:52
  17.2 2.4 collective-permute-start.3
  19.6 18.8 %all-to-all-done = bf16[32,112,256]{2,1,0:T(8,128)(2,1)} async-done(((bf16[32,112,256]{2,1,0:T(8,128)(2,1)}), bf16[32,112,256]{2,1,0:T(8,128)(2,1)}, u32[]{:S(2)}, u32[]{:S(2)}) %all-to-all-start) | async-done | bytes 1835040 | tf_op jit(solution)/shard_map/all_to_all | solution.py:28
  38.4 5.9 %shard_map.122 = (bf16[256,1024]{1,0:T(8,128)(2,1)S(1)}, bf16[1024,256]{1,0:T(8,128)(2,1)}) custom-call(bf16[3584,256]{1,0:T(8,128)(2,1)} %bitcast.4.centered_ref, bf16[3584,1024]{1,0:T(8,128)(2,1)} %weight_ref.3, bf16[1,1024]{1,0:T(2,128)(2,1)S(1)} %reshape.52.bias_ref), custom_call_target="tpu_custom_call" | custom-call | flops 1879048192 | bytes 10225664 | tf_op jit(solution)/shard_map/pallas_call | solution.py:52
  44.4 4.4 %shard_map.123 = bf16[256,3712]{1,0:T(8,128)(2,1)} custom-call(bf16[256,1024]{1,0:T(8,128)(2,1)S(1)} %get-tuple-element.39.latents_ref, bf16[1024,3584]{1,0:T(8,128)(2,1)S(1)} %bitcast.30, bf16[112,256]{1,0:T(8,128)(2,1)S(1)} %bitcast.38), custom_call_target="tpu_custom_call" | custom-call | flops 1879048192 | bytes 9822208 | tf_op jit(solution)/shard_map/pallas_call | solution.py:52
  48.9 6.9 %all-to-all-start.1 = ((bf16[16,16,3712]{2,1,0:T(8,128)(2,1)}), bf16[16,16,3712]{2,1,0:T(8,128)(2,1)S(1)}, u32[]{:S(2)}, u32[]{:S(2)}) async-start(bf16[16,16,3712]{2,1,0:T(8,128)(2,1)} %bitcast.45), calls=%async_computation.1 | async-start | bytes 3801088 | tf_op jit(solution)/shard_map/all_to_all | solution.py:28
  55.8 0.5 collective-permute-start
  56.3 2.7 %constant_dynamic-slice_fusion.1 = (bf16[896,256]{1,0:T(8,128)(2,1)}, bf16[896,256]{1,0:T(8,128)(2,1)}, bf16[896,256]{1,0:T(8,128)(2,1)}, bf16[896,256]{1,0:T(8,128)(2,1)}) fusion(bf16[3584,256]{1,0:T(8,128)(2,1)} %bitcast.4.centered_ref, s32[]{:T(128)S(6)} %select_n.33, s32[]{:T(128)S(6)} %select_n.32, s32[]{:T(128)S(6)} %select_n.29, s32[]{:T(128)S(6)} %select_n.28), kind=kLoop, calls=%fused_computation.13 | loop fusion | bytes 3670032 | tf_op jit(solution)/shard_map/dynamic_slice | solution.py:452
  59.0 21.0 %all-to-all-done.1.pieces_ref = bf16[16,16,3712]{2,1,0:T(8,128)(2,1)S(1)} async-done(((bf16[16,16,3712]{2,1,0:T(8,128)(2,1)}), bf16[16,16,3712]{2,1,0:T(8,128)(2,1)S(1)}, u32[]{:S(2)}, u32[]{:S(2)}) %all-to-all-start.1) | async-done | bytes 1900576 | tf_op jit(solution)/shard_map/all_to_all | solution.py:28
  80.0 0.6 shard_map.124
  80.7 0.8 collective-permute-start.2
  81.5 5.4 %collective-permute-done.2.partner_ref = bf16[8,5632]{1,0:T(8,128)(2,1)S(1)} collective-permute-done((bf16[8,5632]{1,0:T(8,128)(2,1)S(1)}, bf16[8,5632]{1,0:T(8,128)(2,1)S(1)}, u32[]{:S(2)}, u32[]{:S(2)}) %collective-permute-start.2) | collective-permute-done | bytes 90144 | tf_op jit(solution)/shard_map/ppermute | solution.py:33
  86.9 1.1 shard_map.125
  88.0 5.9 %all-to-all-start.2 = ((bf16[16,8,3584]{2,1,0:T(8,128)(2,1)}), bf16[16,8,3584]{2,1,0:T(8,128)(2,1)S(1)}, u32[]{:S(2)}, u32[]{:S(2)}) async-start(bf16[16,8,3584]{2,1,0:T(8,128)(2,1)} %get-tuple-element.47), calls=%async_computation.2 | async-start | bytes 1835008 | tf_op jit(solution)/shard_map/all_to_all | solution.py:28
  93.9 1.8 slice_bitcast_fusion
  96.3 0.5 collective-permute-start.7
  96.9 1.2 collective-permute-done.4.refs_4_
  98.0 1.1 collective-permute-done.5.refs_5_
  99.2 1.1 collective-permute-done.6.refs_6_
  100.3 4.9 %all-to-all-done.2 = bf16[16,8,3584]{2,1,0:T(8,128)(2,1)S(1)} async-done(((bf16[16,8,3584]{2,1,0:T(8,128)(2,1)}), bf16[16,8,3584]{2,1,0:T(8,128)(2,1)S(1)}, u32[]{:S(2)}, u32[]{:S(2)}) %all-to-all-start.2) | async-done | bytes 917536 | tf_op jit(solution)/shard_map/all_to_all | solution.py:28
  105.3 5.7 %shard_map.127 = (bf16[128,3584]{1,0:T(8,128)(2,1)}, f32[128,448]{1,0:T(8,128)}, f32[128,448]{1,0:T(8,128)}) custom-call(bf16[128,3584]{1,0:T(8,128)(2,1)S(1)} %bitcast.35, bf16[224,3584]{1,0:T(8,128)(2,1)} %bitcast.40, bf16[224,3584]{1,0:T(8,128)(2,1)} %bitcast.43, bf16[224,3584]{1,0:T(8,128)(2,1)} %refs_2_.4, ...), custom_call_target="tpu_custom_call" | custom-call | flops 1233125376 | bytes 11927552 | tf_op jit(solution)/shard_map/pallas_call | solution.py:52
  110.9 5.8 %all-to-all-start.3 = ((bf16[16,8,3584]{2,1,0:T(8,128)(2,1)}), bf16[16,8,3584]{2,1,0:T(8,128)(2,1)S(1)}, u32[]{:S(2)}, u32[]{:S(2)}) async-start(bf16[16,8,3584]{2,1,0:T(8,128)(2,1)} %bitcast.46), calls=%async_computation.3 | async-start | bytes 1835008 | tf_op jit(solution)/shard_map/all_to_all | solution.py:28
  116.7 0.6 reshape.61.gain_ref
  117.3 0.5 collective-permute-start.10
  117.9 0.6 copy-done.6
  118.5 1.4 pad_maximum_fusion
  119.9 0.8 rev.4
  120.7 0.8 fusion.1
  121.5 0.6 copy.15
  122.1 1.0 reshape.60.target_ref
  123.1 7.1 %all-to-all-done.3.pieces_ref = bf16[16,8,3584]{2,1,0:T(8,128)(2,1)S(1)} async-done(((bf16[16,8,3584]{2,1,0:T(8,128)(2,1)}), bf16[16,8,3584]{2,1,0:T(8,128)(2,1)S(1)}, u32[]{:S(2)}, u32[]{:S(2)}) %all-to-all-start.3) | async-done | bytes 917536 | tf_op jit(solution)/shard_map/all_to_all | solution.py:28
  130.3 0.7 copy-done.2
  131.0 1.4 shard_map.128
  132.4 18.0 %all_to_all.35 = bf16[16,8,3584]{2,1,0:T(8,128)(2,1)S(1)} all-to-all(bf16[16,8,3584]{2,1,0:T(8,128)(2,1)} %get-tuple-element.61), channel_id=1, replica_groups=mesh['batch_0'=2,'batch_1'=2,'tensor_0'=4,'tensor_1'=2,'latent'=4] {'ten..., dimensions={0} | all-to-all | bytes 1835008 | tf_op jit(solution)/shard_map/all_to_all | solution.py:28
  150.3 5.6 %shard_map.129 = bf16[128,3584]{1,0:T(8,128)(2,1)S(1)} custom-call(bf16[128,3584]{1,0:T(8,128)(2,1)S(1)} %bitcast.36, bf16[224,3584]{1,0:T(8,128)(2,1)} %bitcast.41, bf16[224,3584]{1,0:T(8,128)(2,1)} %bitcast.44, bf16[224,3584]{1,0:T(8,128)(2,1)} %refs_2_.4, bf16[3,112,3584]{2,1,0:T(8,128)(2,1)} %collective-permute-done.3.refs_3_, ...), custom_call_target="tpu_custom_call" | custom-call | flops 1233125376 | bytes 11927552 | tf_op jit(solution)/shard_map/pallas_call | solution.py:52
  155.9 16.1 %all_to_all.36.pieces_ref = bf16[16,8,3584]{2,1,0:T(8,128)(2,1)S(1)} all-to-all(bf16[16,8,3584]{2,1,0:T(8,128)(2,1)S(1)} %bitcast.37), channel_id=1, replica_groups=mesh['batch_0'=2,'batch_1'=2,'tensor_0'=4,'tensor_1'=2,'latent'=4] {'ten..., dimensions={0} | all-to-all | bytes 1835008 | tf_op jit(solution)/shard_map/all_to_all | solution.py:28
  172.4 29.9 %all_to_all.37 = bf16[32,8,3584]{2,1,0:T(8,128)(2,1)S(1)} all-to-all(bf16[32,8,3584]{2,1,0:T(8,128)(2,1)S(1)} %shard_map.130), channel_id=1, replica_groups=mesh['batch_0'=2,'batch_1'=2,'tensor_0'=4,'tensor_1'=2,'latent'=4] {'ten..., dimensions={0} | all-to-all | bytes 3670016 | tf_op jit(solution)/shard_map/all_to_all | solution.py:28
  202.4 2.4 %shard_map.131.refs_4_ = bf16[256,1024]{1,0:T(8,128)(2,1)S(1)} custom-call(bf16[256,3584]{1,0:T(8,128)(2,1)S(1)} %bitcast.33, bf16[1024,3584]{1,0:T(8,128)(2,1)S(1)} %bitcast.32, bf16[256,1024]{1,0:T(8,128)(2,1)S(1)} %copy-done.1), custom_call_target="tpu_custom_call" | custom-call | flops 1879048192 | bytes 10223616 | tf_op jit(solution)/shard_map/pallas_call | solution.py:52
  205.1 2.0 collective-permute-start.13
  207.1 12.6 %collective-permute-done.11.refs_6_ = bf16[256,1024]{1,0:T(8,128)(2,1)S(1)} collective-permute-done((bf16[256,1024]{1,0:T(8,128)(2,1)S(1)}, bf16[256,1024]{1,0:T(8,128)(2,1)S(1)}, u32[]{:S(2)}, u32[]{:S(2)}) %collective-permute-start.11) | collective-permute-done | bytes 524320 | tf_op jit(solution)/shard_map/ppermute | solution.py:33
  220.5 9.1 %collective-permute-done.13.refs_5_ = bf16[256,896]{1,0:T(8,128)(2,1)S(1)} collective-permute-done((bf16[256,896]{1,0:T(8,128)(2,1)S(1)}, bf16[256,896]{1,0:T(8,128)(2,1)S(1)}, u32[]{:S(2)}, u32[]{:S(2)}) %collective-permute-start.13) | collective-permute-done | bytes 458784 | tf_op jit(solution)/shard_map/ppermute | solution.py:33
  229.6 3.1 %shard_map.132.refs_2_ = f32[1024,896]{1,0:T(8,128)S(1)} custom-call(bf16[1024,256]{1,0:T(8,128)(2,1)} %get-tuple-element.58.refs_0_, bf16[1024,256]{1,0:T(8,128)(2,1)} %collective-permute-done.8.refs_1_, bf16[1024,256]{1,0:T(8,128)(2,1)} %copy-done.5, bf16[256,896]{1,0:T(8,128)(2,1)S(1)} %get-tuple-element.80.refs_3_, ...), custom_call_target="tpu_custom_call" | custom-call | flops 1409286144 | bytes 6619136 | tf_op jit(solution)/shard_map/pallas_call | solution.py:52
  232.7 4.7 %shard_map.133 = bf16[896,1024]{1,0:T(8,128)(2,1)} custom-call(bf16[896,256]{1,0:T(8,128)(2,1)} %get-tuple-element.81.refs_0_, bf16[896,256]{1,0:T(8,128)(2,1)} %collective-permute-done.10.refs_1_, bf16[896,256]{1,0:T(8,128)(2,1)} %collective-permute-done.7.refs_2_, bf16[896,256]{1,0:T(8,128)(2,1)} %collective-permute-done.1.refs_3_, ...), custom_call_target="tpu_custom_call" | custom-call | flops 1879048192 | bytes 5767168 | tf_op jit(solution)/shard_map/pallas_call | solution.py:52
  237.4 2.8 %shard_map.134 = bf16[1024,896]{1,0:T(8,128)(2,1)} custom-call(bf16[1024,256]{1,0:T(8,128)(2,1)} %collective-permute-done.9.refs_0_, bf16[256,896]{1,0:T(8,128)(2,1)S(1)} %collective-permute-done.16.refs_1_, f32[1024,896]{1,0:T(8,128)S(1)} %shard_map.132.refs_2_), custom_call_target="tpu_custom_call" | custom-call | flops 469762048 | bytes 6488064 | tf_op jit(solution)/shard_map/pallas_call | solution.py:52
  (58 shorter events, 2.3 us)
Async XLA Ops:
  3.7 34.8 %all-to-all-start = ((bf16[32,112,256]{2,1,0:T(8,128)(2,1)}), bf16[32,112,256]{2,1,0:T(8,128)(2,1)}, u32[]{:S(2)}, u32[]{:S(2)}) async-start(bf16[32,112,256]{2,1,0:T(8,128)(2,1)} %broadcast_in_dim.4), calls=%async_computation | async-start | bytes 3670016 | tf_op jit(solution)/shard_map/all_to_all | solution.py:28
  13.9 5.7 %copy-start.10 = (bf16[1024]{0:T(1024)(128)(2,1)S(1)}, bf16[1024]{0:T(1024)(128)(2,1)}, u32[]{:S(2)}) copy-start(bf16[1024]{0:T(1024)(128)(2,1)} %param.14) | copy-start | bytes 6148
  13.9 30.5 %slice-start = ((s8[7340032]{0:T(1024)(128)(4,1)}), s8[3145728]{0:T(1024)(128)(4,1)S(1)}, s32[]{:S(2)}) async-start(s8[7340032]{0:T(1024)(128)(4,1)} %bitcast.29), calls=%async_computation.7 | async-start | bytes 6291456
  17.2 76.6 %collective-permute-start.3 = (bf16[3,112,3584]{2,1,0:T(8,128)(2,1)}, bf16[3,112,3584]{2,1,0:T(8,128)(2,1)}, u32[]{:S(2)}, u32[]{:S(2)}) collective-permute-start(bf16[3,112,3584]{2,1,0:T(8,128)(2,1)} %shard_map.126), channel_id=1, source_target_pairs={{0,68},{4,64},{64,4},{68,0},{1,69},{5,65},{65,5},{69,1},{2,70},{6,... | collective-permute-start | bytes 7225352 | tf_op jit(solution)/shard_map/ppermute | solution.py:33
  38.4 6.0 %slice-start.1 = ((s8[7340032]{0:T(1024)(128)(4,1)}), s8[4194304]{0:T(1024)(128)(4,1)S(1)}, s32[]{:S(2)}) async-start(s8[7340032]{0:T(1024)(128)(4,1)} %bitcast.29), calls=%async_computation.8 | async-start | bytes 8388608
  38.4 6.0 %copy-start.3 = (bf16[256,112]{0,1:T(8,128)(2,1)S(1)}, bf16[256,112]{0,1:T(8,128)(2,1)}, u32[]{:S(2)}) copy-start(bf16[256,112]{0,1:T(8,128)(2,1)} %param.12) | copy-start | bytes 172036
  44.4 4.5 %copy-start = (bf16[256,1024]{1,0:T(8,128)(2,1)}, bf16[256,1024]{1,0:T(8,128)(2,1)S(1)}, u32[]{:S(2)}) copy-start(bf16[256,1024]{1,0:T(8,128)(2,1)S(1)} %get-tuple-element.39.latents_ref) | copy-start | bytes 1572868
  48.9 6.9 %copy-start.4 = (bf16[1024,256]{1,0:T(8,128)(2,1)S(1)}, bf16[1024,256]{1,0:T(8,128)(2,1)}, u32[]{:S(2)}) copy-start(bf16[1024,256]{1,0:T(8,128)(2,1)} %get-tuple-element.58.refs_0_) | copy-start | bytes 1572868
  48.9 31.1 %all-to-all-start.1 = ((bf16[16,16,3712]{2,1,0:T(8,128)(2,1)}), bf16[16,16,3712]{2,1,0:T(8,128)(2,1)S(1)}, u32[]{:S(2)}, u32[]{:S(2)}) async-start(bf16[16,16,3712]{2,1,0:T(8,128)(2,1)} %bitcast.45), calls=%async_computation.1 | async-start | bytes 3801088 | tf_op jit(solution)/shard_map/all_to_all | solution.py:28
  55.8 24.9 %collective-permute-start = (bf16[1024,256]{1,0:T(8,128)(2,1)S(1)}, bf16[1024,256]{1,0:T(8,128)(2,1)S(1)}, u32[]{:S(2)}, u32[]{:S(2)}) collective-permute-start(bf16[1024,256]{1,0:T(8,128)(2,1)S(1)} %copy-done.4), channel_id=1, source_target_pairs={{0,64},{64,0},{1,65},{65,1},{2,66},{66,2},{3,67},{67,3},{4,68},{68... | collective-permute-start | bytes 1572872 | tf_op jit(solution)/shard_map/ppermute | solution.py:33
  59.0 22.5 %copy-start.7 = (bf16[3584]{0:T(1024)(128)(2,1)S(1)}, bf16[3584]{0:T(1024)(128)(2,1)}, u32[]{:S(2)}) copy-start(bf16[3584]{0:T(1024)(128)(2,1)} %param.16) | copy-start | bytes 21508
  59.0 22.5 %copy-start.8 = (bf16[3584]{0:T(1024)(128)(2,1)S(1)}, bf16[3584]{0:T(1024)(128)(2,1)}, u32[]{:S(2)}) copy-start(bf16[3584]{0:T(1024)(128)(2,1)} %param.17) | copy-start | bytes 21508
  59.0 21.6 %collective-permute-start.1 = (bf16[896,256]{1,0:T(8,128)(2,1)}, bf16[896,256]{1,0:T(8,128)(2,1)}, u32[]{:S(2)}, u32[]{:S(2)}) collective-permute-start(bf16[896,256]{1,0:T(8,128)(2,1)} %get-tuple-element.84), channel_id=1, source_target_pairs={{0,96},{32,64},{64,32},{96,0},{1,97},{33,65},{65,33},{97,1},{2,98}... | collective-permute-start | bytes 1376264 | tf_op jit(solution)/shard_map/ppermute | solution.py:33
  80.7 7.3 %copy-start.5 = (bf16[1024,256]{1,0:T(8,128)(2,1)}, bf16[1024,256]{1,0:T(8,128)(2,1)S(1)}, u32[]{:S(2)}) copy-start(bf16[1024,256]{1,0:T(8,128)(2,1)S(1)} %collective-permute-done.refs_2_) | copy-start | bytes 1572868
  80.7 6.2 %collective-permute-start.2 = (bf16[8,5632]{1,0:T(8,128)(2,1)S(1)}, bf16[8,5632]{1,0:T(8,128)(2,1)S(1)}, u32[]{:S(2)}, u32[]{:S(2)}) collective-permute-start(bf16[8,5632]{1,0:T(8,128)(2,1)S(1)} %get-tuple-element.46), channel_id=1, source_target_pairs={{0,4},{4,0},{1,5},{5,1},{2,6},{6,2},{3,7},{7,3},{8,12},{12,8},{9,1... | collective-permute-start | bytes 270344 | tf_op jit(solution)/shard_map/ppermute | solution.py:33
  88.0 17.2 %all-to-all-start.2 = ((bf16[16,8,3584]{2,1,0:T(8,128)(2,1)}), bf16[16,8,3584]{2,1,0:T(8,128)(2,1)S(1)}, u32[]{:S(2)}, u32[]{:S(2)}) async-start(bf16[16,8,3584]{2,1,0:T(8,128)(2,1)} %get-tuple-element.47), calls=%async_computation.2 | async-start | bytes 1835008 | tf_op jit(solution)/shard_map/all_to_all | solution.py:28
  95.7 2.4 collective-permute-start.4
  95.8 3.4 %collective-permute-start.5 = (bf16[112,3584]{1,0:T(8,128)(2,1)S(1)}, bf16[112,3584]{1,0:T(8,128)(2,1)S(1)}, u32[]{:S(2)}, u32[]{:S(2)}) collective-permute-start(bf16[112,3584]{1,0:T(8,128)(2,1)S(1)} %get-tuple-element.75), channel_id=1, source_target_pairs={{0,32},{32,0},{1,33},{33,1},{2,34},{34,2},{3,35},{35,3},{4,36},{36... | collective-permute-start | bytes 2408456 | tf_op jit(solution)/shard_map/ppermute | solution.py:33
  96.2 4.1 %collective-permute-start.6 = (bf16[112,3584]{1,0:T(8,128)(2,1)S(1)}, bf16[112,3584]{1,0:T(8,128)(2,1)S(1)}, u32[]{:S(2)}, u32[]{:S(2)}) collective-permute-start(bf16[112,3584]{1,0:T(8,128)(2,1)S(1)} %get-tuple-element.74), channel_id=1, source_target_pairs={{0,32},{32,0},{1,33},{33,1},{2,34},{34,2},{3,35},{35,3},{4,36},{36... | collective-permute-start | bytes 2408456 | tf_op jit(solution)/shard_map/ppermute | solution.py:33
  96.3 14.6 %collective-permute-start.7 = (bf16[896,256]{1,0:T(8,128)(2,1)}, bf16[896,256]{1,0:T(8,128)(2,1)}, u32[]{:S(2)}, u32[]{:S(2)}) collective-permute-start(bf16[896,256]{1,0:T(8,128)(2,1)} %get-tuple-element.83), channel_id=1, source_target_pairs={{0,64},{64,0},{1,65},{65,1},{2,66},{66,2},{3,67},{67,3},{4,68},{68... | collective-permute-start | bytes 1376264 | tf_op jit(solution)/shard_map/ppermute | solution.py:33
  110.9 5.8 %copy-start.9 = (bf16[3584]{0:T(1024)(128)(2,1)S(1)}, bf16[3584]{0:T(1024)(128)(2,1)}, u32[]{:S(2)}) copy-start(bf16[3584]{0:T(1024)(128)(2,1)} %param.18) | copy-start | bytes 21508
  110.9 19.3 %all-to-all-start.3 = ((bf16[16,8,3584]{2,1,0:T(8,128)(2,1)}), bf16[16,8,3584]{2,1,0:T(8,128)(2,1)S(1)}, u32[]{:S(2)}, u32[]{:S(2)}) async-start(bf16[16,8,3584]{2,1,0:T(8,128)(2,1)} %bitcast.46), calls=%async_computation.3 | async-start | bytes 1835008 | tf_op jit(solution)/shard_map/all_to_all | solution.py:28
  117.3 15.0 %collective-permute-start.8 = (bf16[1024,256]{1,0:T(8,128)(2,1)}, bf16[1024,256]{1,0:T(8,128)(2,1)}, u32[]{:S(2)}, u32[]{:S(2)}) collective-permute-start(bf16[1024,256]{1,0:T(8,128)(2,1)} %get-tuple-element.58.refs_0_), channel_id=1, source_target_pairs={{0,32},{32,0},{1,33},{33,1},{2,34},{34,2},{3,35},{35,3},{4,36},{36... | collective-permute-start | bytes 1572872 | tf_op jit(solution)/shard_map/ppermute | solution.py:33
  117.3 15.0 %collective-permute-start.10 = (bf16[896,256]{1,0:T(8,128)(2,1)}, bf16[896,256]{1,0:T(8,128)(2,1)}, u32[]{:S(2)}, u32[]{:S(2)}) collective-permute-start(bf16[896,256]{1,0:T(8,128)(2,1)} %get-tuple-element.82), channel_id=1, source_target_pairs={{0,32},{32,0},{1,33},{33,1},{2,34},{34,2},{3,35},{35,3},{4,36},{36... | collective-permute-start | bytes 1376264 | tf_op jit(solution)/shard_map/ppermute | solution.py:33
  117.9 14.5 %collective-permute-start.9 = (bf16[1024,256]{1,0:T(8,128)(2,1)}, bf16[1024,256]{1,0:T(8,128)(2,1)}, u32[]{:S(2)}, u32[]{:S(2)}) collective-permute-start(bf16[1024,256]{1,0:T(8,128)(2,1)} %copy-done.5), channel_id=1, source_target_pairs={{0,32},{32,0},{1,33},{33,1},{2,34},{34,2},{3,35},{35,3},{4,36},{36... | collective-permute-start | bytes 1572872 | tf_op jit(solution)/shard_map/ppermute | solution.py:33
  117.9 0.6 copy-start.6
  130.3 0.7 copy-start.2
  132.3 70.0 %slice-start.2 = ((s8[7340032]{0:T(1024)(128)(4,1)}), s8[4194304]{0:T(1024)(128)(4,1)S(1)}, s32[]{:S(2)}) async-start(s8[7340032]{0:T(1024)(128)(4,1)} %bitcast.31), calls=%async_computation.9 | async-start | bytes 8388608
  150.3 52.0 %slice-start.3 = ((s8[7340032]{0:T(1024)(128)(4,1)}), s8[3145728]{0:T(1024)(128)(4,1)S(1)}, s32[]{:S(2)}) async-start(s8[7340032]{0:T(1024)(128)(4,1)} %bitcast.31), calls=%async_computation.10 | async-start | bytes 6291456
  172.4 30.0 %copy-start.1 = (bf16[256,1024]{1,0:T(8,128)(2,1)S(1)}, bf16[256,1024]{1,0:T(8,128)(2,1)}, u32[]{:S(2)}) copy-start(bf16[256,1024]{1,0:T(8,128)(2,1)} %copy-done) | copy-start | bytes 1572868
  204.8 14.9 %collective-permute-start.11 = (bf16[256,1024]{1,0:T(8,128)(2,1)S(1)}, bf16[256,1024]{1,0:T(8,128)(2,1)S(1)}, u32[]{:S(2)}, u32[]{:S(2)}) collective-permute-start(bf16[256,1024]{1,0:T(8,128)(2,1)S(1)} %shard_map.131.refs_4_), channel_id=1, source_target_pairs={{0,64},{64,0},{1,65},{65,1},{2,66},{66,2},{3,67},{67,3},{4,68},{68... | collective-permute-start | bytes 1572872 | tf_op jit(solution)/shard_map/ppermute | solution.py:33
  205.1 24.4 %collective-permute-start.13 = (bf16[256,896]{1,0:T(8,128)(2,1)S(1)}, bf16[256,896]{1,0:T(8,128)(2,1)S(1)}, u32[]{:S(2)}, u32[]{:S(2)}) collective-permute-start(bf16[256,896]{1,0:T(8,128)(2,1)S(1)} %get-tuple-element.78), channel_id=1, source_target_pairs={{0,64},{64,0},{1,65},{65,1},{2,66},{66,2},{3,67},{67,3},{4,68},{68... | collective-permute-start | bytes 1376264 | tf_op jit(solution)/shard_map/ppermute | solution.py:33
  219.7 9.8 %collective-permute-start.12 = (bf16[256,896]{1,0:T(8,128)(2,1)S(1)}, bf16[256,896]{1,0:T(8,128)(2,1)S(1)}, u32[]{:S(2)}, u32[]{:S(2)}) collective-permute-start(bf16[256,896]{1,0:T(8,128)(2,1)S(1)} %get-tuple-element.65), channel_id=1, source_target_pairs={{0,32},{32,0},{1,33},{33,1},{2,34},{34,2},{3,35},{35,3},{4,36},{36... | collective-permute-start | bytes 1376264 | tf_op jit(solution)/shard_map/ppermute | solution.py:33
  219.7 13.0 %collective-permute-start.14 = (bf16[256,1024]{1,0:T(8,128)(2,1)S(1)}, bf16[256,1024]{1,0:T(8,128)(2,1)S(1)}, u32[]{:S(2)}, u32[]{:S(2)}) collective-permute-start(bf16[256,1024]{1,0:T(8,128)(2,1)S(1)} %shard_map.131.refs_4_), channel_id=1, source_target_pairs={{0,32},{32,0},{1,33},{33,1},{2,34},{34,2},{3,35},{35,3},{4,36},{36... | collective-permute-start | bytes 1572872 | tf_op jit(solution)/shard_map/ppermute | solution.py:33
  220.2 12.5 %collective-permute-start.15 = (bf16[256,1024]{1,0:T(8,128)(2,1)S(1)}, bf16[256,1024]{1,0:T(8,128)(2,1)S(1)}, u32[]{:S(2)}, u32[]{:S(2)}) collective-permute-start(bf16[256,1024]{1,0:T(8,128)(2,1)S(1)} %collective-permute-done.11.refs_6_), channel_id=1, source_target_pairs={{0,32},{32,0},{1,33},{33,1},{2,34},{34,2},{3,35},{35,3},{4,36},{36... | collective-permute-start | bytes 1572872 | tf_op jit(solution)/shard_map/ppermute | solution.py:33
  220.2 17.1 %collective-permute-start.16 = (bf16[256,896]{1,0:T(8,128)(2,1)S(1)}, bf16[256,896]{1,0:T(8,128)(2,1)S(1)}, u32[]{:S(2)}, u32[]{:S(2)}) collective-permute-start(bf16[256,896]{1,0:T(8,128)(2,1)S(1)} %get-tuple-element.77), channel_id=1, source_target_pairs={{0,96},{32,64},{64,32},{96,0},{1,97},{33,65},{65,33},{97,1},{2,98}... | collective-permute-start | bytes 1376264 | tf_op jit(solution)/shard_map/ppermute | solution.py:33

commit v14 on v13

--- a/solution.py
+++ b/solution.py
@@ -464,9 +464,7 @@
         [side, pieces],
         in_specs=[pl.BlockSpec(memory_space=pltpu.SMEM), WHOLE],
     )
-    sent, far_latents, centered_blocks[3] = lax.optimization_barrier(
-        (sent, far_latents, centered_blocks[3])
-    )
+    sent, far_latents = lax.optimization_barrier((sent, far_latents))
     partner = swap(sent, SHARDS[1])
     pieces, recon = local(
         recon_kernel, [half_of_them, own_rows], [own_sum, partner, bias, gain_in]
@@ -499,8 +497,8 @@
     )
     latent_blocks = [turned_latents, swap(turned_latents, BATCH[1])]
     latent_blocks += [far_latents, swap(far_latents, BATCH[1])]
-    pieces, latent_blocks, centered_blocks[1] = lax.optimization_barrier(
-        (pieces, latent_blocks, centered_blocks[1])
+    pieces, latent_blocks, centered_blocks[1::2] = lax.optimization_barrier(
+        (pieces, latent_blocks, centered_blocks[1::2])
     )
     grad_output = all_tokens(pieces, HALF)
     partial_input = with_weights(

time: 241 us -> 248 us (1.029)
  blocking collectives: 64 us -> 67.2 us
    all_to_all x3, blocking collectives: 64 us -> 67.2 us  [exchange(): return lax.all_to_all(pieces, axes, split_axis=0, concat_axis=0, tiled=True)]
  transfers between devices with their start and end apart: 21 -> 21, of which waited for: 10 -> 9; matrix products, arithmetic and copies ran while one was open for 4% -> 5% of each run, Pallas kernels for 13% -> 12%
where the time goes in v14:
time: 248 us; the launch traced here: 247 us
  waiting for transfers between devices  83 us (33%)
  blocking collectives  67.2 us (27%)
  Pallas kernels  41.4 us (17%)
  starting transfers between devices  39.1 us (16%)
  local copies, waits for them, and re-layouts  11.9 us (5%)
  other arithmetic  3.86 us (2%)
    all_to_all x3, blocking collectives, exchange(): return lax.all_to_all(pieces, axes, split_axis=0, concat_axis=0, tiled=True)  67.2 us
    all_to_all x4, waiting for transfers between devices, exchange(): return lax.all_to_all(pieces, axes, split_axis=0, concat_axis=0, tiled=True)  51.3 us
    pallas_call x13, Pallas kernels, call(): pl.pallas_call(body, out_shape=outs, cost_estimate=cost, compiler_params=...  41.4 us
    ppermute x17, waiting for transfers between devices, swap(): lax.ppermute(block, axes, [(i, for_all - 1 - i) for i in range(for_all)])  31.7 us
    all_to_all x4, starting transfers between devices, exchange(): return lax.all_to_all(pieces, axes, split_axis=0, concat_axis=0, tiled=True)  30.2 us
    ppermute x17, starting transfers between devices, swap(): lax.ppermute(block, axes, [(i, for_all - 1 - i) for i in range(for_all)])  8.89 us
  transfers between devices with their start and end apart: 21, of which 9 were waited for; matrix products, arithmetic and copies ran while one was open for 5% of the time, Pallas kernels for 12%

profile of v14, /device:TPU:14, one launch (start us, length us, event | category | flops | bytes accessed | tf_op | source)
XLA Modules:
  0.0 247.3 jit_solution(11531241149890053522)
XLA Ops:
  0.6 0.8 dynamic-slice_convert_fusion
  1.4 0.9 fusion.2
  2.3 1.3 broadcast_in_dim.4
  3.7 10.2 %all-to-all-start = ((bf16[32,112,256]{2,1,0:T(8,128)(2,1)}), bf16[32,112,256]{2,1,0:T(8,128)(2,1)}, u32[]{:S(2)}, u32[]{:S(2)}) async-start(bf16[32,112,256]{2,1,0:T(8,128)(2,1)} %broadcast_in_dim.4), calls=%async_computation | async-start | bytes 3670016 | tf_op jit(solution)/shard_map/all_to_all | solution.py:28
  13.9 3.3 %shard_map.126 = bf16[3,112,3584]{2,1,0:T(8,128)(2,1)} custom-call(s32[1]{0:T(128)} %bitcast.8.at_ref, bf16[224,3584]{1,0:T(8,128)(2,1)} %bitcast.39, bf16[224,3584]{1,0:T(8,128)(2,1)} %bitcast.42, bf16[224,3584]{1,0:T(8,128)(2,1)} %refs_2_.4), custom_call_target="tpu_custom_call" | custom-call | bytes 7225348 | tf_op jit(solution)/shard_map/pallas_call | solution.py:52
  17.2 2.4 collective-permute-start.2
  19.6 18.8 %all-to-all-done = bf16[32,112,256]{2,1,0:T(8,128)(2,1)} async-done(((bf16[32,112,256]{2,1,0:T(8,128)(2,1)}), bf16[32,112,256]{2,1,0:T(8,128)(2,1)}, u32[]{:S(2)}, u32[]{:S(2)}) %all-to-all-start) | async-done | bytes 1835040 | tf_op jit(solution)/shard_map/all_to_all | solution.py:28
  38.4 5.9 %shard_map.122 = (bf16[256,1024]{1,0:T(8,128)(2,1)S(1)}, bf16[1024,256]{1,0:T(8,128)(2,1)}) custom-call(bf16[3584,256]{1,0:T(8,128)(2,1)} %bitcast.4.centered_ref, bf16[3584,1024]{1,0:T(8,128)(2,1)} %weight_ref.3, bf16[1,1024]{1,0:T(2,128)(2,1)S(1)} %reshape.52.bias_ref), custom_call_target="tpu_custom_call" | custom-call | flops 1879048192 | bytes 10225664 | tf_op jit(solution)/shard_map/pallas_call | solution.py:52
  44.4 4.4 %shard_map.123 = bf16[256,3712]{1,0:T(8,128)(2,1)} custom-call(bf16[256,1024]{1,0:T(8,128)(2,1)S(1)} %get-tuple-element.39.latents_ref, bf16[1024,3584]{1,0:T(8,128)(2,1)S(1)} %bitcast.30, bf16[112,256]{1,0:T(8,128)(2,1)S(1)} %bitcast.38), custom_call_target="tpu_custom_call" | custom-call | flops 1879048192 | bytes 9822208 | tf_op jit(solution)/shard_map/pallas_call | solution.py:52
  48.9 6.9 %all-to-all-start.1 = ((bf16[16,16,3712]{2,1,0:T(8,128)(2,1)}), bf16[16,16,3712]{2,1,0:T(8,128)(2,1)S(1)}, u32[]{:S(2)}, u32[]{:S(2)}) async-start(bf16[16,16,3712]{2,1,0:T(8,128)(2,1)} %bitcast.45), calls=%async_computation.1 | async-start | bytes 3801088 | tf_op jit(solution)/shard_map/all_to_all | solution.py:28
  55.8 0.5 collective-permute-start
  56.3 23.7 %all-to-all-done.1.pieces_ref = bf16[16,16,3712]{2,1,0:T(8,128)(2,1)S(1)} async-done(((bf16[16,16,3712]{2,1,0:T(8,128)(2,1)}), bf16[16,16,3712]{2,1,0:T(8,128)(2,1)S(1)}, u32[]{:S(2)}, u32[]{:S(2)}) %all-to-all-start.1) | async-done | bytes 1900576 | tf_op jit(solution)/shard_map/all_to_all | solution.py:28
  80.0 0.6 shard_map.124
  80.7 0.7 collective-permute-start.1
  81.4 5.4 %collective-permute-done.1.partner_ref = bf16[8,5632]{1,0:T(8,128)(2,1)S(1)} collective-permute-done((bf16[8,5632]{1,0:T(8,128)(2,1)S(1)}, bf16[8,5632]{1,0:T(8,128)(2,1)S(1)}, u32[]{:S(2)}, u32[]{:S(2)}) %collective-permute-start.1) | collective-permute-done | bytes 90144 | tf_op jit(solution)/shard_map/ppermute | solution.py:33
  86.8 1.1 shard_map.125
  87.9 5.9 %all-to-all-start.2 = ((bf16[16,8,3584]{2,1,0:T(8,128)(2,1)}), bf16[16,8,3584]{2,1,0:T(8,128)(2,1)S(1)}, u32[]{:S(2)}, u32[]{:S(2)}) async-start(bf16[16,8,3584]{2,1,0:T(8,128)(2,1)} %get-tuple-element.46), calls=%async_computation.2 | async-start | bytes 1835008 | tf_op jit(solution)/shard_map/all_to_all | solution.py:28
  93.8 3.1 %slice_bitcast_fusion = (bf16[112,3584]{1,0:T(8,128)(2,1)}, bf16[112,3584]{1,0:T(8,128)(2,1)}, bf16[112,3584]{1,0:T(8,128)(2,1)}) fusion(bf16[3,112,3584]{2,1,0:T(8,128)(2,1)} %collective-permute-done.2.refs_3_), kind=kLoop, calls=%fused_computation | loop fusion | bytes 4816896 | tf_op jit(solution)/shard_map/squeeze | solution.py:479
  96.9 0.5 collective-permute-start.4
  97.4 2.7 %constant_dynamic-slice_fusion.1 = (bf16[896,256]{1,0:T(8,128)(2,1)}, bf16[896,256]{1,0:T(8,128)(2,1)}, bf16[896,256]{1,0:T(8,128)(2,1)}, bf16[896,256]{1,0:T(8,128)(2,1)}) fusion(bf16[3584,256]{1,0:T(8,128)(2,1)} %bitcast.4.centered_ref, s32[]{:T(128)S(6)} %select_n.33, s32[]{:T(128)S(6)} %select_n.32, s32[]{:T(128)S(6)} %select_n.31, s32[]{:T(128)S(6)} %select_n.28), kind=kLoop, calls=%fused_computation.13 | loop fusion | bytes 3670032 | tf_op jit(solution)/shard_map/dynamic_slice | solution.py:452
  100.1 0.5 collective-permute-start.6
  100.7 1.0 collective-permute-done.5.refs_6_
  101.7 2.3 all-to-all-done.2
  104.0 5.7 %shard_map.127 = (bf16[128,3584]{1,0:T(8,128)(2,1)}, f32[128,448]{1,0:T(8,128)}, f32[128,448]{1,0:T(8,128)}) custom-call(bf16[128,3584]{1,0:T(8,128)(2,1)S(1)} %bitcast.35, bf16[224,3584]{1,0:T(8,128)(2,1)} %bitcast.40, bf16[224,3584]{1,0:T(8,128)(2,1)} %bitcast.43, bf16[224,3584]{1,0:T(8,128)(2,1)} %refs_2_.4, ...), custom_call_target="tpu_custom_call" | custom-call | flops 1233125376 | bytes 11927552 | tf_op jit(solution)/shard_map/pallas_call | solution.py:52
  109.6 3.7 %collective-permute-done.6.refs_2_ = bf16[896,256]{1,0:T(8,128)(2,1)} collective-permute-done((bf16[896,256]{1,0:T(8,128)(2,1)}, bf16[896,256]{1,0:T(8,128)(2,1)}, u32[]{:S(2)}, u32[]{:S(2)}) %collective-permute-start.6) | collective-permute-done | bytes 458784 | tf_op jit(solution)/shard_map/ppermute | solution.py:33
  113.4 7.2 %all-to-all-start.3 = ((bf16[16,8,3584]{2,1,0:T(8,128)(2,1)}), bf16[16,8,3584]{2,1,0:T(8,128)(2,1)S(1)}, u32[]{:S(2)}, u32[]{:S(2)}) async-start(bf16[16,8,3584]{2,1,0:T(8,128)(2,1)} %bitcast.46), calls=%async_computation.3 | async-start | bytes 1835008 | tf_op jit(solution)/shard_map/all_to_all | solution.py:28
  120.6 0.6 reshape.61.gain_ref
  121.2 0.6 collective-permute-start.10
  122.4 0.6 copy-done.6
  123.0 1.4 pad_maximum_fusion
  124.4 0.8 rev.4
  125.2 0.8 fusion.1
  126.0 0.7 copy.15
  126.7 1.0 reshape.60.target_ref
  127.7 6.5 %all-to-all-done.3.pieces_ref = bf16[16,8,3584]{2,1,0:T(8,128)(2,1)S(1)} async-done(((bf16[16,8,3584]{2,1,0:T(8,128)(2,1)}), bf16[16,8,3584]{2,1,0:T(8,128)(2,1)S(1)}, u32[]{:S(2)}, u32[]{:S(2)}) %all-to-all-start.3) | async-done | bytes 917536 | tf_op jit(solution)/shard_map/all_to_all | solution.py:28
  134.2 0.7 copy-done.2
  134.9 1.4 shard_map.128
  136.3 19.1 %all_to_all.35 = bf16[16,8,3584]{2,1,0:T(8,128)(2,1)S(1)} all-to-all(bf16[16,8,3584]{2,1,0:T(8,128)(2,1)} %get-tuple-element.61), channel_id=1, replica_groups=mesh['batch_0'=2,'batch_1'=2,'tensor_0'=4,'tensor_1'=2,'latent'=4] {'ten..., dimensions={0} | all-to-all | bytes 1835008 | tf_op jit(solution)/shard_map/all_to_all | solution.py:28
  155.5 5.6 %shard_map.129 = bf16[128,3584]{1,0:T(8,128)(2,1)S(1)} custom-call(bf16[128,3584]{1,0:T(8,128)(2,1)S(1)} %bitcast.36, bf16[224,3584]{1,0:T(8,128)(2,1)} %bitcast.41, bf16[224,3584]{1,0:T(8,128)(2,1)} %bitcast.44, bf16[224,3584]{1,0:T(8,128)(2,1)} %refs_2_.4, bf16[3,112,3584]{2,1,0:T(8,128)(2,1)} %collective-permute-done.2.refs_3_, ...), custom_call_target="tpu_custom_call" | custom-call | flops 1233125376 | bytes 11927552 | tf_op jit(solution)/shard_map/pallas_call | solution.py:52
  161.0 17.2 %all_to_all.36.pieces_ref = bf16[16,8,3584]{2,1,0:T(8,128)(2,1)S(1)} all-to-all(bf16[16,8,3584]{2,1,0:T(8,128)(2,1)S(1)} %bitcast.37), channel_id=1, replica_groups=mesh['batch_0'=2,'batch_1'=2,'tensor_0'=4,'tensor_1'=2,'latent'=4] {'ten..., dimensions={0} | all-to-all | bytes 1835008 | tf_op jit(solution)/shard_map/all_to_all | solution.py:28
  178.6 30.9 %all_to_all.37 = bf16[32,8,3584]{2,1,0:T(8,128)(2,1)S(1)} all-to-all(bf16[32,8,3584]{2,1,0:T(8,128)(2,1)S(1)} %shard_map.130), channel_id=1, replica_groups=mesh['batch_0'=2,'batch_1'=2,'tensor_0'=4,'tensor_1'=2,'latent'=4] {'ten..., dimensions={0} | all-to-all | bytes 3670016 | tf_op jit(solution)/shard_map/all_to_all | solution.py:28
  209.6 2.4 shard_map.131.refs_4_
  212.5 1.8 collective-permute-start.13
  214.3 12.6 %collective-permute-done.11.refs_6_ = bf16[256,1024]{1,0:T(8,128)(2,1)S(1)} collective-permute-done((bf16[256,1024]{1,0:T(8,128)(2,1)S(1)}, bf16[256,1024]{1,0:T(8,128)(2,1)S(1)}, u32[]{:S(2)}, u32[]{:S(2)}) %collective-permute-start.11) | collective-permute-done | bytes 524320 | tf_op jit(solution)/shard_map/ppermute | solution.py:33
  227.8 8.9 %collective-permute-done.13.refs_5_ = bf16[256,896]{1,0:T(8,128)(2,1)S(1)} collective-permute-done((bf16[256,896]{1,0:T(8,128)(2,1)S(1)}, bf16[256,896]{1,0:T(8,128)(2,1)S(1)}, u32[]{:S(2)}, u32[]{:S(2)}) %collective-permute-start.13) | collective-permute-done | bytes 458784 | tf_op jit(solution)/shard_map/ppermute | solution.py:33
  236.7 3.1 %shard_map.132.refs_2_ = f32[1024,896]{1,0:T(8,128)S(1)} custom-call(bf16[1024,256]{1,0:T(8,128)(2,1)} %get-tuple-element.58.refs_0_, bf16[1024,256]{1,0:T(8,128)(2,1)} %collective-permute-done.7.refs_1_, bf16[1024,256]{1,0:T(8,128)(2,1)} %copy-done.5, bf16[256,896]{1,0:T(8,128)(2,1)S(1)} %get-tuple-element.80.refs_3_, ...), custom_call_target="tpu_custom_call" | custom-call | flops 1409286144 | bytes 6619136 | tf_op jit(solution)/shard_map/pallas_call | solution.py:52
  239.9 4.7 %shard_map.133 = bf16[896,1024]{1,0:T(8,128)(2,1)} custom-call(bf16[896,256]{1,0:T(8,128)(2,1)} %get-tuple-element.81.refs_0_, bf16[896,256]{1,0:T(8,128)(2,1)} %collective-permute-done.9.refs_1_, bf16[896,256]{1,0:T(8,128)(2,1)} %collective-permute-done.6.refs_2_, bf16[896,256]{1,0:T(8,128)(2,1)} %collective-permute-done.10.refs_3_, ...), custom_call_target="tpu_custom_call" | custom-call | flops 1879048192 | bytes 5767168 | tf_op jit(solution)/shard_map/pallas_call | solution.py:52
  244.6 2.8 %shard_map.134 = bf16[1024,896]{1,0:T(8,128)(2,1)} custom-call(bf16[1024,256]{1,0:T(8,128)(2,1)} %collective-permute-done.8.refs_0_, bf16[256,896]{1,0:T(8,128)(2,1)S(1)} %collective-permute-done.16.refs_1_, f32[1024,896]{1,0:T(8,128)S(1)} %shard_map.132.refs_2_), custom_call_target="tpu_custom_call" | custom-call | flops 469762048 | bytes 6488064 | tf_op jit(solution)/shard_map/pallas_call | solution.py:52
  (58 shorter events, 2.5 us)
Async XLA Ops:
  3.7 34.8 %all-to-all-start = ((bf16[32,112,256]{2,1,0:T(8,128)(2,1)}), bf16[32,112,256]{2,1,0:T(8,128)(2,1)}, u32[]{:S(2)}, u32[]{:S(2)}) async-start(bf16[32,112,256]{2,1,0:T(8,128)(2,1)} %broadcast_in_dim.4), calls=%async_computation | async-start | bytes 3670016 | tf_op jit(solution)/shard_map/all_to_all | solution.py:28
  13.9 5.7 %copy-start.10 = (bf16[1024]{0:T(1024)(128)(2,1)S(1)}, bf16[1024]{0:T(1024)(128)(2,1)}, u32[]{:S(2)}) copy-start(bf16[1024]{0:T(1024)(128)(2,1)} %param.14) | copy-start | bytes 6148
  13.9 30.5 %slice-start = ((s8[7340032]{0:T(1024)(128)(4,1)}), s8[3145728]{0:T(1024)(128)(4,1)S(1)}, s32[]{:S(2)}) async-start(s8[7340032]{0:T(1024)(128)(4,1)} %bitcast.29), calls=%async_computation.7 | async-start | bytes 6291456
  17.2 76.5 %collective-permute-start.2 = (bf16[3,112,3584]{2,1,0:T(8,128)(2,1)}, bf16[3,112,3584]{2,1,0:T(8,128)(2,1)}, u32[]{:S(2)}, u32[]{:S(2)}) collective-permute-start(bf16[3,112,3584]{2,1,0:T(8,128)(2,1)} %shard_map.126), channel_id=1, source_target_pairs={{0,68},{4,64},{64,4},{68,0},{1,69},{5,65},{65,5},{69,1},{2,70},{6,... | collective-permute-start | bytes 7225352 | tf_op jit(solution)/shard_map/ppermute | solution.py:33
  38.4 6.0 %slice-start.1 = ((s8[7340032]{0:T(1024)(128)(4,1)}), s8[4194304]{0:T(1024)(128)(4,1)S(1)}, s32[]{:S(2)}) async-start(s8[7340032]{0:T(1024)(128)(4,1)} %bitcast.29), calls=%async_computation.8 | async-start | bytes 8388608
  38.4 6.0 %copy-start.3 = (bf16[256,112]{0,1:T(8,128)(2,1)S(1)}, bf16[256,112]{0,1:T(8,128)(2,1)}, u32[]{:S(2)}) copy-start(bf16[256,112]{0,1:T(8,128)(2,1)} %param.12) | copy-start | bytes 172036
  44.4 4.5 %copy-start = (bf16[256,1024]{1,0:T(8,128)(2,1)}, bf16[256,1024]{1,0:T(8,128)(2,1)S(1)}, u32[]{:S(2)}) copy-start(bf16[256,1024]{1,0:T(8,128)(2,1)S(1)} %get-tuple-element.39.latents_ref) | copy-start | bytes 1572868
  48.9 6.9 %copy-start.4 = (bf16[1024,256]{1,0:T(8,128)(2,1)S(1)}, bf16[1024,256]{1,0:T(8,128)(2,1)}, u32[]{:S(2)}) copy-start(bf16[1024,256]{1,0:T(8,128)(2,1)} %get-tuple-element.58.refs_0_) | copy-start | bytes 1572868
  48.9 31.1 %all-to-all-start.1 = ((bf16[16,16,3712]{2,1,0:T(8,128)(2,1)}), bf16[16,16,3712]{2,1,0:T(8,128)(2,1)S(1)}, u32[]{:S(2)}, u32[]{:S(2)}) async-start(bf16[16,16,3712]{2,1,0:T(8,128)(2,1)} %bitcast.45), calls=%async_computation.1 | async-start | bytes 3801088 | tf_op jit(solution)/shard_map/all_to_all | solution.py:28
  55.8 25.6 %copy-start.7 = (bf16[3584]{0:T(1024)(128)(2,1)S(1)}, bf16[3584]{0:T(1024)(128)(2,1)}, u32[]{:S(2)}) copy-start(bf16[3584]{0:T(1024)(128)(2,1)} %param.16) | copy-start | bytes 21508
  55.8 25.6 %copy-start.8 = (bf16[3584]{0:T(1024)(128)(2,1)S(1)}, bf16[3584]{0:T(1024)(128)(2,1)}, u32[]{:S(2)}) copy-start(bf16[3584]{0:T(1024)(128)(2,1)} %param.17) | copy-start | bytes 21508
  55.8 24.8 %collective-permute-start = (bf16[1024,256]{1,0:T(8,128)(2,1)S(1)}, bf16[1024,256]{1,0:T(8,128)(2,1)S(1)}, u32[]{:S(2)}, u32[]{:S(2)}) collective-permute-start(bf16[1024,256]{1,0:T(8,128)(2,1)S(1)} %copy-done.4), channel_id=1, source_target_pairs={{0,64},{64,0},{1,65},{65,1},{2,66},{66,2},{3,67},{67,3},{4,68},{68... | collective-permute-start | bytes 1572872 | tf_op jit(solution)/shard_map/ppermute | solution.py:33
  80.7 7.3 %copy-start.5 = (bf16[1024,256]{1,0:T(8,128)(2,1)}, bf16[1024,256]{1,0:T(8,128)(2,1)S(1)}, u32[]{:S(2)}) copy-start(bf16[1024,256]{1,0:T(8,128)(2,1)S(1)} %collective-permute-done.refs_2_) | copy-start | bytes 1572868
  80.7 6.1 %collective-permute-start.1 = (bf16[8,5632]{1,0:T(8,128)(2,1)S(1)}, bf16[8,5632]{1,0:T(8,128)(2,1)S(1)}, u32[]{:S(2)}, u32[]{:S(2)}) collective-permute-start(bf16[8,5632]{1,0:T(8,128)(2,1)S(1)} %get-tuple-element.45), channel_id=1, source_target_pairs={{0,4},{4,0},{1,5},{5,1},{2,6},{6,2},{3,7},{7,3},{8,12},{12,8},{9,1... | collective-permute-start | bytes 270344 | tf_op jit(solution)/shard_map/ppermute | solution.py:33
  87.9 16.0 %all-to-all-start.2 = ((bf16[16,8,3584]{2,1,0:T(8,128)(2,1)}), bf16[16,8,3584]{2,1,0:T(8,128)(2,1)S(1)}, u32[]{:S(2)}, u32[]{:S(2)}) async-start(bf16[16,8,3584]{2,1,0:T(8,128)(2,1)} %get-tuple-element.46), calls=%async_computation.2 | async-start | bytes 1835008 | tf_op jit(solution)/shard_map/all_to_all | solution.py:28
  96.9 3.8 %collective-permute-start.3 = (bf16[112,3584]{1,0:T(8,128)(2,1)}, bf16[112,3584]{1,0:T(8,128)(2,1)S(1)}, u32[]{:S(2)}, u32[]{:S(2)}) collective-permute-start(bf16[112,3584]{1,0:T(8,128)(2,1)} %get-tuple-element.76), channel_id=1, source_target_pairs={{0,32},{32,0},{1,33},{33,1},{2,34},{34,2},{3,35},{35,3},{4,36},{36... | collective-permute-start | bytes 2408456 | tf_op jit(solution)/shard_map/ppermute | solution.py:33
  96.9 3.8 %collective-permute-start.4 = (bf16[112,3584]{1,0:T(8,128)(2,1)}, bf16[112,3584]{1,0:T(8,128)(2,1)S(1)}, u32[]{:S(2)}, u32[]{:S(2)}) collective-permute-start(bf16[112,3584]{1,0:T(8,128)(2,1)} %get-tuple-element.75), channel_id=1, source_target_pairs={{0,32},{32,0},{1,33},{33,1},{2,34},{34,2},{3,35},{35,3},{4,36},{36... | collective-permute-start | bytes 2408456 | tf_op jit(solution)/shard_map/ppermute | solution.py:33
  97.4 4.3 %collective-permute-start.5 = (bf16[112,3584]{1,0:T(8,128)(2,1)}, bf16[112,3584]{1,0:T(8,128)(2,1)S(1)}, u32[]{:S(2)}, u32[]{:S(2)}) collective-permute-start(bf16[112,3584]{1,0:T(8,128)(2,1)} %get-tuple-element.74), channel_id=1, source_target_pairs={{0,32},{32,0},{1,33},{33,1},{2,34},{34,2},{3,35},{35,3},{4,36},{36... | collective-permute-start | bytes 2408456 | tf_op jit(solution)/shard_map/ppermute | solution.py:33
  100.1 13.2 %collective-permute-start.6 = (bf16[896,256]{1,0:T(8,128)(2,1)}, bf16[896,256]{1,0:T(8,128)(2,1)}, u32[]{:S(2)}, u32[]{:S(2)}) collective-permute-start(bf16[896,256]{1,0:T(8,128)(2,1)} %get-tuple-element.84), channel_id=1, source_target_pairs={{0,64},{64,0},{1,65},{65,1},{2,66},{66,2},{3,67},{67,3},{4,68},{68... | collective-permute-start | bytes 1376264 | tf_op jit(solution)/shard_map/ppermute | solution.py:33
  109.6 11.0 %copy-start.9 = (bf16[3584]{0:T(1024)(128)(2,1)S(1)}, bf16[3584]{0:T(1024)(128)(2,1)}, u32[]{:S(2)}) copy-start(bf16[3584]{0:T(1024)(128)(2,1)} %param.18) | copy-start | bytes 21508
  113.4 20.8 %all-to-all-start.3 = ((bf16[16,8,3584]{2,1,0:T(8,128)(2,1)}), bf16[16,8,3584]{2,1,0:T(8,128)(2,1)S(1)}, u32[]{:S(2)}, u32[]{:S(2)}) async-start(bf16[16,8,3584]{2,1,0:T(8,128)(2,1)} %bitcast.46), calls=%async_computation.3 | async-start | bytes 1835008 | tf_op jit(solution)/shard_map/all_to_all | solution.py:28
  121.2 15.1 %collective-permute-start.7 = (bf16[1024,256]{1,0:T(8,128)(2,1)}, bf16[1024,256]{1,0:T(8,128)(2,1)}, u32[]{:S(2)}, u32[]{:S(2)}) collective-permute-start(bf16[1024,256]{1,0:T(8,128)(2,1)} %get-tuple-element.58.refs_0_), channel_id=1, source_target_pairs={{0,32},{32,0},{1,33},{33,1},{2,34},{34,2},{3,35},{35,3},{4,36},{36... | collective-permute-start | bytes 1572872 | tf_op jit(solution)/shard_map/ppermute | solution.py:33
  121.2 15.1 %collective-permute-start.10 = (bf16[896,256]{1,0:T(8,128)(2,1)}, bf16[896,256]{1,0:T(8,128)(2,1)}, u32[]{:S(2)}, u32[]{:S(2)}) collective-permute-start(bf16[896,256]{1,0:T(8,128)(2,1)} %get-tuple-element.82), channel_id=1, source_target_pairs={{0,96},{32,64},{64,32},{96,0},{1,97},{33,65},{65,33},{97,1},{2,98}... | collective-permute-start | bytes 1376264 | tf_op jit(solution)/shard_map/ppermute | solution.py:33
  121.9 14.4 %collective-permute-start.9 = (bf16[896,256]{1,0:T(8,128)(2,1)}, bf16[896,256]{1,0:T(8,128)(2,1)}, u32[]{:S(2)}, u32[]{:S(2)}) collective-permute-start(bf16[896,256]{1,0:T(8,128)(2,1)} %get-tuple-element.83), channel_id=1, source_target_pairs={{0,32},{32,0},{1,33},{33,1},{2,34},{34,2},{3,35},{35,3},{4,36},{36... | collective-permute-start | bytes 1376264 | tf_op jit(solution)/shard_map/ppermute | solution.py:33
  121.9 14.5 %collective-permute-start.8 = (bf16[1024,256]{1,0:T(8,128)(2,1)}, bf16[1024,256]{1,0:T(8,128)(2,1)}, u32[]{:S(2)}, u32[]{:S(2)}) collective-permute-start(bf16[1024,256]{1,0:T(8,128)(2,1)} %copy-done.5), channel_id=1, source_target_pairs={{0,32},{32,0},{1,33},{33,1},{2,34},{34,2},{3,35},{35,3},{4,36},{36... | collective-permute-start | bytes 1572872 | tf_op jit(solution)/shard_map/ppermute | solution.py:33
  122.4 0.6 copy-start.6
  134.2 0.7 copy-start.2
  136.3 73.2 %slice-start.2 = ((s8[7340032]{0:T(1024)(128)(4,1)}), s8[4194304]{0:T(1024)(128)(4,1)S(1)}, s32[]{:S(2)}) async-start(s8[7340032]{0:T(1024)(128)(4,1)} %bitcast.31), calls=%async_computation.9 | async-start | bytes 8388608
  155.5 54.1 %slice-start.3 = ((s8[7340032]{0:T(1024)(128)(4,1)}), s8[3145728]{0:T(1024)(128)(4,1)S(1)}, s32[]{:S(2)}) async-start(s8[7340032]{0:T(1024)(128)(4,1)} %bitcast.31), calls=%async_computation.10 | async-start | bytes 6291456
  178.6 30.9 %copy-start.1 = (bf16[256,1024]{1,0:T(8,128)(2,1)S(1)}, bf16[256,1024]{1,0:T(8,128)(2,1)}, u32[]{:S(2)}) copy-start(bf16[256,1024]{1,0:T(8,128)(2,1)} %copy-done) | copy-start | bytes 1572868
  212.0 14.9 %collective-permute-start.11 = (bf16[256,1024]{1,0:T(8,128)(2,1)S(1)}, bf16[256,1024]{1,0:T(8,128)(2,1)S(1)}, u32[]{:S(2)}, u32[]{:S(2)}) collective-permute-start(bf16[256,1024]{1,0:T(8,128)(2,1)S(1)} %shard_map.131.refs_4_), channel_id=1, source_target_pairs={{0,64},{64,0},{1,65},{65,1},{2,66},{66,2},{3,67},{67,3},{4,68},{68... | collective-permute-start | bytes 1572872 | tf_op jit(solution)/shard_map/ppermute | solution.py:33
  212.5 24.2 %collective-permute-start.13 = (bf16[256,896]{1,0:T(8,128)(2,1)S(1)}, bf16[256,896]{1,0:T(8,128)(2,1)S(1)}, u32[]{:S(2)}, u32[]{:S(2)}) collective-permute-start(bf16[256,896]{1,0:T(8,128)(2,1)S(1)} %get-tuple-element.78), channel_id=1, source_target_pairs={{0,64},{64,0},{1,65},{65,1},{2,66},{66,2},{3,67},{67,3},{4,68},{68... | collective-permute-start | bytes 1376264 | tf_op jit(solution)/shard_map/ppermute | solution.py:33
  226.9 9.8 %collective-permute-start.12 = (bf16[256,896]{1,0:T(8,128)(2,1)S(1)}, bf16[256,896]{1,0:T(8,128)(2,1)S(1)}, u32[]{:S(2)}, u32[]{:S(2)}) collective-permute-start(bf16[256,896]{1,0:T(8,128)(2,1)S(1)} %get-tuple-element.65), channel_id=1, source_target_pairs={{0,32},{32,0},{1,33},{33,1},{2,34},{34,2},{3,35},{35,3},{4,36},{36... | collective-permute-start | bytes 1376264 | tf_op jit(solution)/shard_map/ppermute | solution.py:33
  226.9 13.0 %collective-permute-start.14 = (bf16[256,1024]{1,0:T(8,128)(2,1)S(1)}, bf16[256,1024]{1,0:T(8,128)(2,1)S(1)}, u32[]{:S(2)}, u32[]{:S(2)}) collective-permute-start(bf16[256,1024]{1,0:T(8,128)(2,1)S(1)} %shard_map.131.refs_4_), channel_id=1, source_target_pairs={{0,32},{32,0},{1,33},{33,1},{2,34},{34,2},{3,35},{35,3},{4,36},{36... | collective-permute-start | bytes 1572872 | tf_op jit(solution)/shard_map/ppermute | solution.py:33
  227.4 12.5 %collective-permute-start.15 = (bf16[256,1024]{1,0:T(8,128)(2,1)S(1)}, bf16[256,1024]{1,0:T(8,128)(2,1)S(1)}, u32[]{:S(2)}, u32[]{:S(2)}) collective-permute-start(bf16[256,1024]{1,0:T(8,128)(2,1)S(1)} %collective-permute-done.11.refs_6_), channel_id=1, source_target_pairs={{0,32},{32,0},{1,33},{33,1},{2,34},{34,2},{3,35},{35,3},{4,36},{36... | collective-permute-start | bytes 1572872 | tf_op jit(solution)/shard_map/ppermute | solution.py:33
  227.4 17.1 %collective-permute-start.16 = (bf16[256,896]{1,0:T(8,128)(2,1)S(1)}, bf16[256,896]{1,0:T(8,128)(2,1)S(1)}, u32[]{:S(2)}, u32[]{:S(2)}) collective-permute-start(bf16[256,896]{1,0:T(8,128)(2,1)S(1)} %get-tuple-element.77), channel_id=1, source_target_pairs={{0,96},{32,64},{64,32},{96,0},{1,97},{33,65},{65,33},{97,1},{2,98}... | collective-permute-start | bytes 1376264 | tf_op jit(solution)/shard_map/ppermute | solution.py:33

commit v15 on v14

--- a/solution.py
+++ b/solution.py
@@ -466,6 +466,7 @@
     )
     sent, far_latents = lax.optimization_barrier((sent, far_latents))
     partner = swap(sent, SHARDS[1])
+    partner, centered_blocks[3] = lax.optimization_barrier((partner, centered_blocks[3]))
     pieces, recon = local(
         recon_kernel, [half_of_them, own_rows], [own_sum, partner, bias, gain_in]
     )
@@ -497,8 +498,8 @@
     )
     latent_blocks = [turned_latents, swap(turned_latents, BATCH[1])]
     latent_blocks += [far_latents, swap(far_latents, BATCH[1])]
-    pieces, latent_blocks, centered_blocks[1::2] = lax.optimization_barrier(
-        (pieces, latent_blocks, centered_blocks[1::2])
+    pieces, latent_blocks, centered_blocks[1] = lax.optimization_barrier(
+        (pieces, latent_blocks, centered_blocks[1])
     )
     grad_output = all_tokens(pieces, HALF)
     partial_input = with_weights(

time: 248 us -> 241 us (0.972)
  blocking collectives: 67.2 us -> 64 us
    all_to_all x3, blocking collectives: 67.2 us -> 64 us  [exchange(): return lax.all_to_all(pieces, axes, split_axis=0, concat_axis=0, tiled=True)]
  transfers between devices with their start and end apart: 21 -> 21, of which waited for: 9 -> 10; matrix products, arithmetic and copies ran while one was open for 5% -> 4% of each run, Pallas kernels for 12% -> 13%
where the time goes in v15:
time: 241 us; the launch traced here: 240 us
  waiting for transfers between devices  81.2 us (34%)
  blocking collectives  64 us (27%)
  Pallas kernels  41.4 us (17%)
  starting transfers between devices  38.2 us (16%)
  local copies, waits for them, and re-layouts  10.5 us (4%)
  other arithmetic  3.83 us (2%)
    all_to_all x3, blocking collectives, exchange(): return lax.all_to_all(pieces, axes, split_axis=0, concat_axis=0, tiled=True)  64 us
    all_to_all x4, waiting for transfers between devices, exchange(): return lax.all_to_all(pieces, axes, split_axis=0, concat_axis=0, tiled=True)  50.6 us
    pallas_call x13, Pallas kernels, call(): pl.pallas_call(body, out_shape=outs, cost_estimate=cost, compiler_params=...  41.4 us
    ppermute x17, waiting for transfers between devices, swap(): lax.ppermute(block, axes, [(i, for_all - 1 - i) for i in range(for_all)])  30.6 us
    all_to_all x4, starting transfers between devices, exchange(): return lax.all_to_all(pieces, axes, split_axis=0, concat_axis=0, tiled=True)  30 us
    ppermute x17, starting transfers between devices, swap(): lax.ppermute(block, axes, [(i, for_all - 1 - i) for i in range(for_all)])  8.25 us
  transfers between devices with their start and end apart: 21, of which 10 were waited for; matrix products, arithmetic and copies ran while one was open for 4% of the time, Pallas kernels for 13%

profile of v15, /device:TPU:14, one launch (start us, length us, event | category | flops | bytes accessed | tf_op | source)
XLA Modules:
  0.0 240.1 jit_solution(16232118877308488742)
XLA Ops:
  0.6 0.8 dynamic-slice_convert_fusion
  1.4 0.9 fusion.2
  2.3 1.3 broadcast_in_dim.4
  3.7 10.2 %all-to-all-start = ((bf16[32,112,256]{2,1,0:T(8,128)(2,1)}), bf16[32,112,256]{2,1,0:T(8,128)(2,1)}, u32[]{:S(2)}, u32[]{:S(2)}) async-start(bf16[32,112,256]{2,1,0:T(8,128)(2,1)} %broadcast_in_dim.4), calls=%async_computation | async-start | bytes 3670016 | tf_op jit(solution)/shard_map/all_to_all | solution.py:28
  13.9 3.3 %shard_map.126 = bf16[3,112,3584]{2,1,0:T(8,128)(2,1)} custom-call(s32[1]{0:T(128)} %bitcast.8.at_ref, bf16[224,3584]{1,0:T(8,128)(2,1)} %bitcast.39, bf16[224,3584]{1,0:T(8,128)(2,1)} %bitcast.42, bf16[224,3584]{1,0:T(8,128)(2,1)} %refs_2_.4), custom_call_target="tpu_custom_call" | custom-call | bytes 7225348 | tf_op jit(solution)/shard_map/pallas_call | solution.py:52
  17.2 2.4 collective-permute-start.3
  19.6 18.8 %all-to-all-done = bf16[32,112,256]{2,1,0:T(8,128)(2,1)} async-done(((bf16[32,112,256]{2,1,0:T(8,128)(2,1)}), bf16[32,112,256]{2,1,0:T(8,128)(2,1)}, u32[]{:S(2)}, u32[]{:S(2)}) %all-to-all-start) | async-done | bytes 1835040 | tf_op jit(solution)/shard_map/all_to_all | solution.py:28
  38.4 5.9 %shard_map.122 = (bf16[256,1024]{1,0:T(8,128)(2,1)S(1)}, bf16[1024,256]{1,0:T(8,128)(2,1)}) custom-call(bf16[3584,256]{1,0:T(8,128)(2,1)} %bitcast.4.centered_ref, bf16[3584,1024]{1,0:T(8,128)(2,1)} %weight_ref.3, bf16[1,1024]{1,0:T(2,128)(2,1)S(1)} %reshape.52.bias_ref), custom_call_target="tpu_custom_call" | custom-call | flops 1879048192 | bytes 10225664 | tf_op jit(solution)/shard_map/pallas_call | solution.py:52
  44.4 4.4 %shard_map.123 = bf16[256,3712]{1,0:T(8,128)(2,1)} custom-call(bf16[256,1024]{1,0:T(8,128)(2,1)S(1)} %get-tuple-element.40.latents_ref, bf16[1024,3584]{1,0:T(8,128)(2,1)S(1)} %bitcast.30, bf16[112,256]{1,0:T(8,128)(2,1)S(1)} %bitcast.38), custom_call_target="tpu_custom_call" | custom-call | flops 1879048192 | bytes 9822208 | tf_op jit(solution)/shard_map/pallas_call | solution.py:52
  48.9 6.9 %all-to-all-start.1 = ((bf16[16,16,3712]{2,1,0:T(8,128)(2,1)}), bf16[16,16,3712]{2,1,0:T(8,128)(2,1)S(1)}, u32[]{:S(2)}, u32[]{:S(2)}) async-start(bf16[16,16,3712]{2,1,0:T(8,128)(2,1)} %bitcast.45), calls=%async_computation.1 | async-start | bytes 3801088 | tf_op jit(solution)/shard_map/all_to_all | solution.py:28
  55.8 0.5 collective-permute-start
  56.3 2.7 %constant_dynamic-slice_fusion.1 = (bf16[896,256]{1,0:T(8,128)(2,1)}, bf16[896,256]{1,0:T(8,128)(2,1)}, bf16[896,256]{1,0:T(8,128)(2,1)}, bf16[896,256]{1,0:T(8,128)(2,1)}) fusion(bf16[3584,256]{1,0:T(8,128)(2,1)} %bitcast.4.centered_ref, s32[]{:T(128)S(6)} %select_n.33, s32[]{:T(128)S(6)} %select_n.32, s32[]{:T(128)S(6)} %select_n.29, s32[]{:T(128)S(6)} %select_n.28), kind=kLoop, calls=%fused_computation.13 | loop fusion | bytes 3670032 | tf_op jit(solution)/shard_map/dynamic_slice | solution.py:452
  59.0 21.0 %all-to-all-done.1.pieces_ref = bf16[16,16,3712]{2,1,0:T(8,128)(2,1)S(1)} async-done(((bf16[16,16,3712]{2,1,0:T(8,128)(2,1)}), bf16[16,16,3712]{2,1,0:T(8,128)(2,1)S(1)}, u32[]{:S(2)}, u32[]{:S(2)}) %all-to-all-start.1) | async-done | bytes 1900576 | tf_op jit(solution)/shard_map/all_to_all | solution.py:28
  80.0 0.6 shard_map.124
  80.7 0.7 collective-permute-start.1
  81.4 5.4 %collective-permute-done.1.partner_ref = bf16[8,5632]{1,0:T(8,128)(2,1)S(1)} collective-permute-done((bf16[8,5632]{1,0:T(8,128)(2,1)S(1)}, bf16[8,5632]{1,0:T(8,128)(2,1)S(1)}, u32[]{:S(2)}, u32[]{:S(2)}) %collective-permute-start.1) | collective-permute-done | bytes 90144 | tf_op jit(solution)/shard_map/ppermute | solution.py:33
  86.8 1.1 shard_map.125
  87.9 5.9 %all-to-all-start.2 = ((bf16[16,8,3584]{2,1,0:T(8,128)(2,1)}), bf16[16,8,3584]{2,1,0:T(8,128)(2,1)S(1)}, u32[]{:S(2)}, u32[]{:S(2)}) async-start(bf16[16,8,3584]{2,1,0:T(8,128)(2,1)} %get-tuple-element.49), calls=%async_computation.2 | async-start | bytes 1835008 | tf_op jit(solution)/shard_map/all_to_all | solution.py:28
  93.8 1.8 slice_bitcast_fusion
  96.3 0.5 collective-permute-start.7
  96.8 1.2 collective-permute-done.4.refs_4_
  98.0 1.1 collective-permute-done.5.refs_5_
  99.1 1.1 collective-permute-done.6.refs_6_
  100.3 3.7 %all-to-all-done.2 = bf16[16,8,3584]{2,1,0:T(8,128)(2,1)S(1)} async-done(((bf16[16,8,3584]{2,1,0:T(8,128)(2,1)}), bf16[16,8,3584]{2,1,0:T(8,128)(2,1)S(1)}, u32[]{:S(2)}, u32[]{:S(2)}) %all-to-all-start.2) | async-done | bytes 917536 | tf_op jit(solution)/shard_map/all_to_all | solution.py:28
  104.0 5.7 %shard_map.127 = (bf16[128,3584]{1,0:T(8,128)(2,1)}, f32[128,448]{1,0:T(8,128)}, f32[128,448]{1,0:T(8,128)}) custom-call(bf16[128,3584]{1,0:T(8,128)(2,1)S(1)} %bitcast.35, bf16[224,3584]{1,0:T(8,128)(2,1)} %bitcast.40, bf16[224,3584]{1,0:T(8,128)(2,1)} %bitcast.43, bf16[224,3584]{1,0:T(8,128)(2,1)} %refs_2_.4, ...), custom_call_target="tpu_custom_call" | custom-call | flops 1233125376 | bytes 11927552 | tf_op jit(solution)/shard_map/pallas_call | solution.py:52
  109.7 7.0 %all-to-all-start.3 = ((bf16[16,8,3584]{2,1,0:T(8,128)(2,1)}), bf16[16,8,3584]{2,1,0:T(8,128)(2,1)S(1)}, u32[]{:S(2)}, u32[]{:S(2)}) async-start(bf16[16,8,3584]{2,1,0:T(8,128)(2,1)} %bitcast.46), calls=%async_computation.3 | async-start | bytes 1835008 | tf_op jit(solution)/shard_map/all_to_all | solution.py:28
  116.7 0.6 reshape.61.gain_ref
  117.8 0.6 copy-done.6
  118.4 1.4 pad_maximum_fusion
  119.8 0.8 rev.4
  120.6 0.8 fusion.1
  121.4 0.6 copy.15
  122.1 1.0 reshape.60.target_ref
  123.1 7.1 %all-to-all-done.3.pieces_ref = bf16[16,8,3584]{2,1,0:T(8,128)(2,1)S(1)} async-done(((bf16[16,8,3584]{2,1,0:T(8,128)(2,1)}), bf16[16,8,3584]{2,1,0:T(8,128)(2,1)S(1)}, u32[]{:S(2)}, u32[]{:S(2)}) %all-to-all-start.3) | async-done | bytes 917536 | tf_op jit(solution)/shard_map/all_to_all | solution.py:28
  130.2 0.7 copy-done.2
  130.9 1.4 shard_map.128
  132.3 18.0 %all_to_all.35 = bf16[16,8,3584]{2,1,0:T(8,128)(2,1)S(1)} all-to-all(bf16[16,8,3584]{2,1,0:T(8,128)(2,1)} %get-tuple-element.63), channel_id=1, replica_groups=mesh['batch_0'=2,'batch_1'=2,'tensor_0'=4,'tensor_1'=2,'latent'=4] {'ten..., dimensions={0} | all-to-all | bytes 1835008 | tf_op jit(solution)/shard_map/all_to_all | solution.py:28
  150.3 5.6 %shard_map.129 = bf16[128,3584]{1,0:T(8,128)(2,1)S(1)} custom-call(bf16[128,3584]{1,0:T(8,128)(2,1)S(1)} %bitcast.36, bf16[224,3584]{1,0:T(8,128)(2,1)} %bitcast.41, bf16[224,3584]{1,0:T(8,128)(2,1)} %bitcast.44, bf16[224,3584]{1,0:T(8,128)(2,1)} %refs_2_.4, bf16[3,112,3584]{2,1,0:T(8,128)(2,1)} %collective-permute-done.3.refs_3_, ...), custom_call_target="tpu_custom_call" | custom-call | flops 1233125376 | bytes 11927552 | tf_op jit(solution)/shard_map/pallas_call | solution.py:52
  155.8 16.1 %all_to_all.36.pieces_ref = bf16[16,8,3584]{2,1,0:T(8,128)(2,1)S(1)} all-to-all(bf16[16,8,3584]{2,1,0:T(8,128)(2,1)S(1)} %bitcast.37), channel_id=1, replica_groups=mesh['batch_0'=2,'batch_1'=2,'tensor_0'=4,'tensor_1'=2,'latent'=4] {'ten..., dimensions={0} | all-to-all | bytes 1835008 | tf_op jit(solution)/shard_map/all_to_all | solution.py:28
  172.3 29.9 %all_to_all.37 = bf16[32,8,3584]{2,1,0:T(8,128)(2,1)S(1)} all-to-all(bf16[32,8,3584]{2,1,0:T(8,128)(2,1)S(1)} %shard_map.130), channel_id=1, replica_groups=mesh['batch_0'=2,'batch_1'=2,'tensor_0'=4,'tensor_1'=2,'latent'=4] {'ten..., dimensions={0} | all-to-all | bytes 3670016 | tf_op jit(solution)/shard_map/all_to_all | solution.py:28
  202.3 2.4 %shard_map.131.refs_4_ = bf16[256,1024]{1,0:T(8,128)(2,1)S(1)} custom-call(bf16[256,3584]{1,0:T(8,128)(2,1)S(1)} %bitcast.33, bf16[1024,3584]{1,0:T(8,128)(2,1)S(1)} %bitcast.32, bf16[256,1024]{1,0:T(8,128)(2,1)S(1)} %copy-done.1), custom_call_target="tpu_custom_call" | custom-call | flops 1879048192 | bytes 10223616 | tf_op jit(solution)/shard_map/pallas_call | solution.py:52
  205.1 2.0 collective-permute-start.13
  207.0 12.6 %collective-permute-done.11.refs_6_ = bf16[256,1024]{1,0:T(8,128)(2,1)S(1)} collective-permute-done((bf16[256,1024]{1,0:T(8,128)(2,1)S(1)}, bf16[256,1024]{1,0:T(8,128)(2,1)S(1)}, u32[]{:S(2)}, u32[]{:S(2)}) %collective-permute-start.11) | collective-permute-done | bytes 524320 | tf_op jit(solution)/shard_map/ppermute | solution.py:33
  219.6 0.5 collective-permute-start.14
  220.4 9.1 %collective-permute-done.13.refs_5_ = bf16[256,896]{1,0:T(8,128)(2,1)S(1)} collective-permute-done((bf16[256,896]{1,0:T(8,128)(2,1)S(1)}, bf16[256,896]{1,0:T(8,128)(2,1)S(1)}, u32[]{:S(2)}, u32[]{:S(2)}) %collective-permute-start.13) | collective-permute-done | bytes 458784 | tf_op jit(solution)/shard_map/ppermute | solution.py:33
  229.5 3.1 %shard_map.132.refs_2_ = f32[1024,896]{1,0:T(8,128)S(1)} custom-call(bf16[1024,256]{1,0:T(8,128)(2,1)} %get-tuple-element.60.refs_0_, bf16[1024,256]{1,0:T(8,128)(2,1)} %collective-permute-done.8.refs_1_, bf16[1024,256]{1,0:T(8,128)(2,1)} %copy-done.5, bf16[256,896]{1,0:T(8,128)(2,1)S(1)} %get-tuple-element.82.refs_3_, ...), custom_call_target="tpu_custom_call" | custom-call | flops 1409286144 | bytes 6619136 | tf_op jit(solution)/shard_map/pallas_call | solution.py:52
  232.6 4.7 %shard_map.133 = bf16[896,1024]{1,0:T(8,128)(2,1)} custom-call(bf16[896,256]{1,0:T(8,128)(2,1)} %get-tuple-element.83.refs_0_, bf16[896,256]{1,0:T(8,128)(2,1)} %collective-permute-done.10.refs_1_, bf16[896,256]{1,0:T(8,128)(2,1)} %collective-permute-done.7.refs_2_, bf16[896,256]{1,0:T(8,128)(2,1)} %collective-permute-done.2.refs_3_, ...), custom_call_target="tpu_custom_call" | custom-call | flops 1879048192 | bytes 5767168 | tf_op jit(solution)/shard_map/pallas_call | solution.py:52
  237.3 2.8 %shard_map.134 = bf16[1024,896]{1,0:T(8,128)(2,1)} custom-call(bf16[1024,256]{1,0:T(8,128)(2,1)} %collective-permute-done.9.refs_0_, bf16[256,896]{1,0:T(8,128)(2,1)S(1)} %collective-permute-done.16.refs_1_, f32[1024,896]{1,0:T(8,128)S(1)} %shard_map.132.refs_2_), custom_call_target="tpu_custom_call" | custom-call | flops 469762048 | bytes 6488064 | tf_op jit(solution)/shard_map/pallas_call | solution.py:52
  (58 shorter events, 2.3 us)
Async XLA Ops:
  3.7 34.8 %all-to-all-start = ((bf16[32,112,256]{2,1,0:T(8,128)(2,1)}), bf16[32,112,256]{2,1,0:T(8,128)(2,1)}, u32[]{:S(2)}, u32[]{:S(2)}) async-start(bf16[32,112,256]{2,1,0:T(8,128)(2,1)} %broadcast_in_dim.4), calls=%async_computation | async-start | bytes 3670016 | tf_op jit(solution)/shard_map/all_to_all | solution.py:28
  13.9 5.7 %copy-start.10 = (bf16[1024]{0:T(1024)(128)(2,1)S(1)}, bf16[1024]{0:T(1024)(128)(2,1)}, u32[]{:S(2)}) copy-start(bf16[1024]{0:T(1024)(128)(2,1)} %param.14) | copy-start | bytes 6148
  13.9 30.5 %slice-start = ((s8[7340032]{0:T(1024)(128)(4,1)}), s8[3145728]{0:T(1024)(128)(4,1)S(1)}, s32[]{:S(2)}) async-start(s8[7340032]{0:T(1024)(128)(4,1)} %bitcast.29), calls=%async_computation.7 | async-start | bytes 6291456
  17.2 76.5 %collective-permute-start.3 = (bf16[3,112,3584]{2,1,0:T(8,128)(2,1)}, bf16[3,112,3584]{2,1,0:T(8,128)(2,1)}, u32[]{:S(2)}, u32[]{:S(2)}) collective-permute-start(bf16[3,112,3584]{2,1,0:T(8,128)(2,1)} %shard_map.126), channel_id=1, source_target_pairs={{0,68},{4,64},{64,4},{68,0},{1,69},{5,65},{65,5},{69,1},{2,70},{6,... | collective-permute-start | bytes 7225352 | tf_op jit(solution)/shard_map/ppermute | solution.py:33
  38.4 6.0 %slice-start.1 = ((s8[7340032]{0:T(1024)(128)(4,1)}), s8[4194304]{0:T(1024)(128)(4,1)S(1)}, s32[]{:S(2)}) async-start(s8[7340032]{0:T(1024)(128)(4,1)} %bitcast.29), calls=%async_computation.8 | async-start | bytes 8388608
  38.4 6.0 %copy-start.3 = (bf16[256,112]{0,1:T(8,128)(2,1)S(1)}, bf16[256,112]{0,1:T(8,128)(2,1)}, u32[]{:S(2)}) copy-start(bf16[256,112]{0,1:T(8,128)(2,1)} %param.12) | copy-start | bytes 172036
  44.4 4.5 %copy-start = (bf16[256,1024]{1,0:T(8,128)(2,1)}, bf16[256,1024]{1,0:T(8,128)(2,1)S(1)}, u32[]{:S(2)}) copy-start(bf16[256,1024]{1,0:T(8,128)(2,1)S(1)} %get-tuple-element.40.latents_ref) | copy-start | bytes 1572868
  48.9 6.9 %copy-start.4 = (bf16[1024,256]{1,0:T(8,128)(2,1)S(1)}, bf16[1024,256]{1,0:T(8,128)(2,1)}, u32[]{:S(2)}) copy-start(bf16[1024,256]{1,0:T(8,128)(2,1)} %get-tuple-element.60.refs_0_) | copy-start | bytes 1572868
  48.9 31.1 %all-to-all-start.1 = ((bf16[16,16,3712]{2,1,0:T(8,128)(2,1)}), bf16[16,16,3712]{2,1,0:T(8,128)(2,1)S(1)}, u32[]{:S(2)}, u32[]{:S(2)}) async-start(bf16[16,16,3712]{2,1,0:T(8,128)(2,1)} %bitcast.45), calls=%async_computation.1 | async-start | bytes 3801088 | tf_op jit(solution)/shard_map/all_to_all | solution.py:28
  55.8 24.9 %collective-permute-start = (bf16[1024,256]{1,0:T(8,128)(2,1)S(1)}, bf16[1024,256]{1,0:T(8,128)(2,1)S(1)}, u32[]{:S(2)}, u32[]{:S(2)}) collective-permute-start(bf16[1024,256]{1,0:T(8,128)(2,1)S(1)} %copy-done.4), channel_id=1, source_target_pairs={{0,64},{64,0},{1,65},{65,1},{2,66},{66,2},{3,67},{67,3},{4,68},{68... | collective-permute-start | bytes 1572872 | tf_op jit(solution)/shard_map/ppermute | solution.py:33
  59.0 22.4 %copy-start.7 = (bf16[3584]{0:T(1024)(128)(2,1)S(1)}, bf16[3584]{0:T(1024)(128)(2,1)}, u32[]{:S(2)}) copy-start(bf16[3584]{0:T(1024)(128)(2,1)} %param.16) | copy-start | bytes 21508
  59.0 22.4 %copy-start.8 = (bf16[3584]{0:T(1024)(128)(2,1)S(1)}, bf16[3584]{0:T(1024)(128)(2,1)}, u32[]{:S(2)}) copy-start(bf16[3584]{0:T(1024)(128)(2,1)} %param.17) | copy-start | bytes 21508
  59.0 22.4 %collective-permute-start.2 = (bf16[896,256]{1,0:T(8,128)(2,1)}, bf16[896,256]{1,0:T(8,128)(2,1)}, u32[]{:S(2)}, u32[]{:S(2)}) collective-permute-start(bf16[896,256]{1,0:T(8,128)(2,1)} %get-tuple-element.86), channel_id=1, source_target_pairs={{0,96},{32,64},{64,32},{96,0},{1,97},{33,65},{65,33},{97,1},{2,98}... | collective-permute-start | bytes 1376264 | tf_op jit(solution)/shard_map/ppermute | solution.py:33
  80.7 7.3 %copy-start.5 = (bf16[1024,256]{1,0:T(8,128)(2,1)}, bf16[1024,256]{1,0:T(8,128)(2,1)S(1)}, u32[]{:S(2)}) copy-start(bf16[1024,256]{1,0:T(8,128)(2,1)S(1)} %collective-permute-done.refs_2_) | copy-start | bytes 1572868
  80.7 6.1 %collective-permute-start.1 = (bf16[8,5632]{1,0:T(8,128)(2,1)S(1)}, bf16[8,5632]{1,0:T(8,128)(2,1)S(1)}, u32[]{:S(2)}, u32[]{:S(2)}) collective-permute-start(bf16[8,5632]{1,0:T(8,128)(2,1)S(1)} %get-tuple-element.46), channel_id=1, source_target_pairs={{0,4},{4,0},{1,5},{5,1},{2,6},{6,2},{3,7},{7,3},{8,12},{12,8},{9,1... | collective-permute-start | bytes 270344 | tf_op jit(solution)/shard_map/ppermute | solution.py:33
  87.9 16.0 %all-to-all-start.2 = ((bf16[16,8,3584]{2,1,0:T(8,128)(2,1)}), bf16[16,8,3584]{2,1,0:T(8,128)(2,1)S(1)}, u32[]{:S(2)}, u32[]{:S(2)}) async-start(bf16[16,8,3584]{2,1,0:T(8,128)(2,1)} %get-tuple-element.49), calls=%async_computation.2 | async-start | bytes 1835008 | tf_op jit(solution)/shard_map/all_to_all | solution.py:28
  95.6 2.4 collective-permute-start.4
  95.7 3.4 %collective-permute-start.5 = (bf16[112,3584]{1,0:T(8,128)(2,1)S(1)}, bf16[112,3584]{1,0:T(8,128)(2,1)S(1)}, u32[]{:S(2)}, u32[]{:S(2)}) collective-permute-start(bf16[112,3584]{1,0:T(8,128)(2,1)S(1)} %get-tuple-element.77), channel_id=1, source_target_pairs={{0,32},{32,0},{1,33},{33,1},{2,34},{34,2},{3,35},{35,3},{4,36},{36... | collective-permute-start | bytes 2408456 | tf_op jit(solution)/shard_map/ppermute | solution.py:33
  96.2 4.1 %collective-permute-start.6 = (bf16[112,3584]{1,0:T(8,128)(2,1)S(1)}, bf16[112,3584]{1,0:T(8,128)(2,1)S(1)}, u32[]{:S(2)}, u32[]{:S(2)}) collective-permute-start(bf16[112,3584]{1,0:T(8,128)(2,1)S(1)} %get-tuple-element.76), channel_id=1, source_target_pairs={{0,32},{32,0},{1,33},{33,1},{2,34},{34,2},{3,35},{35,3},{4,36},{36... | collective-permute-start | bytes 2408456 | tf_op jit(solution)/shard_map/ppermute | solution.py:33
  96.3 13.4 %collective-permute-start.7 = (bf16[896,256]{1,0:T(8,128)(2,1)}, bf16[896,256]{1,0:T(8,128)(2,1)}, u32[]{:S(2)}, u32[]{:S(2)}) collective-permute-start(bf16[896,256]{1,0:T(8,128)(2,1)} %get-tuple-element.85), channel_id=1, source_target_pairs={{0,64},{64,0},{1,65},{65,1},{2,66},{66,2},{3,67},{67,3},{4,68},{68... | collective-permute-start | bytes 1376264 | tf_op jit(solution)/shard_map/ppermute | solution.py:33
  109.6 7.0 %copy-start.9 = (bf16[3584]{0:T(1024)(128)(2,1)S(1)}, bf16[3584]{0:T(1024)(128)(2,1)}, u32[]{:S(2)}) copy-start(bf16[3584]{0:T(1024)(128)(2,1)} %param.18) | copy-start | bytes 21508
  109.7 20.5 %all-to-all-start.3 = ((bf16[16,8,3584]{2,1,0:T(8,128)(2,1)}), bf16[16,8,3584]{2,1,0:T(8,128)(2,1)S(1)}, u32[]{:S(2)}, u32[]{:S(2)}) async-start(bf16[16,8,3584]{2,1,0:T(8,128)(2,1)} %bitcast.46), calls=%async_computation.3 | async-start | bytes 1835008 | tf_op jit(solution)/shard_map/all_to_all | solution.py:28
  117.3 15.0 %collective-permute-start.8 = (bf16[1024,256]{1,0:T(8,128)(2,1)}, bf16[1024,256]{1,0:T(8,128)(2,1)}, u32[]{:S(2)}, u32[]{:S(2)}) collective-permute-start(bf16[1024,256]{1,0:T(8,128)(2,1)} %get-tuple-element.60.refs_0_), channel_id=1, source_target_pairs={{0,32},{32,0},{1,33},{33,1},{2,34},{34,2},{3,35},{35,3},{4,36},{36... | collective-permute-start | bytes 1572872 | tf_op jit(solution)/shard_map/ppermute | solution.py:33
  117.3 15.0 %collective-permute-start.10 = (bf16[896,256]{1,0:T(8,128)(2,1)}, bf16[896,256]{1,0:T(8,128)(2,1)}, u32[]{:S(2)}, u32[]{:S(2)}) collective-permute-start(bf16[896,256]{1,0:T(8,128)(2,1)} %get-tuple-element.84), channel_id=1, source_target_pairs={{0,32},{32,0},{1,33},{33,1},{2,34},{34,2},{3,35},{35,3},{4,36},{36... | collective-permute-start | bytes 1376264 | tf_op jit(solution)/shard_map/ppermute | solution.py:33
  117.8 14.5 %collective-permute-start.9 = (bf16[1024,256]{1,0:T(8,128)(2,1)}, bf16[1024,256]{1,0:T(8,128)(2,1)}, u32[]{:S(2)}, u32[]{:S(2)}) collective-permute-start(bf16[1024,256]{1,0:T(8,128)(2,1)} %copy-done.5), channel_id=1, source_target_pairs={{0,32},{32,0},{1,33},{33,1},{2,34},{34,2},{3,35},{35,3},{4,36},{36... | collective-permute-start | bytes 1572872 | tf_op jit(solution)/shard_map/ppermute | solution.py:33
  117.8 0.6 copy-start.6
  130.2 0.7 copy-start.2
  132.3 70.0 %slice-start.2 = ((s8[7340032]{0:T(1024)(128)(4,1)}), s8[4194304]{0:T(1024)(128)(4,1)S(1)}, s32[]{:S(2)}) async-start(s8[7340032]{0:T(1024)(128)(4,1)} %bitcast.31), calls=%async_computation.9 | async-start | bytes 8388608
  150.3 52.0 %slice-start.3 = ((s8[7340032]{0:T(1024)(128)(4,1)}), s8[3145728]{0:T(1024)(128)(4,1)S(1)}, s32[]{:S(2)}) async-start(s8[7340032]{0:T(1024)(128)(4,1)} %bitcast.31), calls=%async_computation.10 | async-start | bytes 6291456
  172.3 30.0 %copy-start.1 = (bf16[256,1024]{1,0:T(8,128)(2,1)S(1)}, bf16[256,1024]{1,0:T(8,128)(2,1)}, u32[]{:S(2)}) copy-start(bf16[256,1024]{1,0:T(8,128)(2,1)} %copy-done) | copy-start | bytes 1572868
  204.7 14.9 %collective-permute-start.11 = (bf16[256,1024]{1,0:T(8,128)(2,1)S(1)}, bf16[256,1024]{1,0:T(8,128)(2,1)S(1)}, u32[]{:S(2)}, u32[]{:S(2)}) collective-permute-start(bf16[256,1024]{1,0:T(8,128)(2,1)S(1)} %shard_map.131.refs_4_), channel_id=1, source_target_pairs={{0,64},{64,0},{1,65},{65,1},{2,66},{66,2},{3,67},{67,3},{4,68},{68... | collective-permute-start | bytes 1572872 | tf_op jit(solution)/shard_map/ppermute | solution.py:33
  205.1 24.4 %collective-permute-start.13 = (bf16[256,896]{1,0:T(8,128)(2,1)S(1)}, bf16[256,896]{1,0:T(8,128)(2,1)S(1)}, u32[]{:S(2)}, u32[]{:S(2)}) collective-permute-start(bf16[256,896]{1,0:T(8,128)(2,1)S(1)} %get-tuple-element.80), channel_id=1, source_target_pairs={{0,64},{64,0},{1,65},{65,1},{2,66},{66,2},{3,67},{67,3},{4,68},{68... | collective-permute-start | bytes 1376264 | tf_op jit(solution)/shard_map/ppermute | solution.py:33
  219.6 9.8 %collective-permute-start.12 = (bf16[256,896]{1,0:T(8,128)(2,1)S(1)}, bf16[256,896]{1,0:T(8,128)(2,1)S(1)}, u32[]{:S(2)}, u32[]{:S(2)}) collective-permute-start(bf16[256,896]{1,0:T(8,128)(2,1)S(1)} %get-tuple-element.67), channel_id=1, source_target_pairs={{0,32},{32,0},{1,33},{33,1},{2,34},{34,2},{3,35},{35,3},{4,36},{36... | collective-permute-start | bytes 1376264 | tf_op jit(solution)/shard_map/ppermute | solution.py:33
  219.6 13.0 %collective-permute-start.14 = (bf16[256,1024]{1,0:T(8,128)(2,1)S(1)}, bf16[256,1024]{1,0:T(8,128)(2,1)S(1)}, u32[]{:S(2)}, u32[]{:S(2)}) collective-permute-start(bf16[256,1024]{1,0:T(8,128)(2,1)S(1)} %shard_map.131.refs_4_), channel_id=1, source_target_pairs={{0,32},{32,0},{1,33},{33,1},{2,34},{34,2},{3,35},{35,3},{4,36},{36... | collective-permute-start | bytes 1572872 | tf_op jit(solution)/shard_map/ppermute | solution.py:33
  220.2 12.5 %collective-permute-start.15 = (bf16[256,1024]{1,0:T(8,128)(2,1)S(1)}, bf16[256,1024]{1,0:T(8,128)(2,1)S(1)}, u32[]{:S(2)}, u32[]{:S(2)}) collective-permute-start(bf16[256,1024]{1,0:T(8,128)(2,1)S(1)} %collective-permute-done.11.refs_6_), channel_id=1, source_target_pairs={{0,32},{32,0},{1,33},{33,1},{2,34},{34,2},{3,35},{35,3},{4,36},{36... | collective-permute-start | bytes 1572872 | tf_op jit(solution)/shard_map/ppermute | solution.py:33
  220.2 17.1 %collective-permute-start.16 = (bf16[256,896]{1,0:T(8,128)(2,1)S(1)}, bf16[256,896]{1,0:T(8,128)(2,1)S(1)}, u32[]{:S(2)}, u32[]{:S(2)}) collective-permute-start(bf16[256,896]{1,0:T(8,128)(2,1)S(1)} %get-tuple-element.79), channel_id=1, source_target_pairs={{0,96},{32,64},{64,32},{96,0},{1,97},{33,65},{65,33},{97,1},{2,98}... | collective-permute-start | bytes 1376264 | tf_op jit(solution)/shard_map/ppermute | solution.py:33
